TPU v7x, 256 devices: a whole 4x4x8 slice. The times are simulated.
256 devices in a mesh: pass: 32 (over x, z), head: 8 (over y, core).
Axes of the slice: x: 4, y: 4, z: 8, core: 2. Of those that a mesh axis runs over, the one named last changes fastest.
Arguments:
- queries: bfloat16 [12288, 8192], P('pass', 'head'), may hold values from -4.5 to 4.5
- own_kv: bfloat16 [12288, 8, 256], P('pass', 'head'), may hold values from -4.5 to 4.5
- passage_cache: bfloat16 [512, 512, 8, 256], P('pass', None, 'head'), may hold values from -4.5 to 4.5
- out_weight: bfloat16 [8192, 4096], P('head', 'pass'), may hold values from -3.5 to 3.5
- lists: int32 [96, 8], replicated, may hold values from 0 to 511, as said below
- passage_slot: int32 [512], replicated, may hold values from 0 to 511, as said below
- question_slot: int32 [96], replicated, may hold values from 0 to 95, as said below
Outputs:
- attended: bfloat16 [12288, 4096], P('pass', 'head')
Inputs may be any that keep to these rules, and one draw needn't show every extreme that they name: Each question lists 8 different passages. The listed passages of the 3 questions at slots d * 3 to d * 3 + 2 are all different, and at most 1 of them have their cache rows in one aligned block of 16 rows; some block holds exactly 1 of them. `passage_slot`: A permutation. `question_slot`: A permutation.
All inputs are finite; a program needn't handle non-finite values.
Results may differ from a plain program's by a relative error of at most 0.014.
Values may be sent and summed in bfloat16 or wider, within the bound.
No kernel may reach another device: no remote copies, remote signals or barrier semaphores. Data moves between devices by JAX's collectives and lax.ppermute only.
A program may use at most 128 MiB of HBM per device.

v0:
```python
import jax
import jax.numpy as jnp
from jax import lax
from jax.sharding import PartitionSpec as P

H = 64
KVH = 8
HD = 128
LQ = 128
TOPP = 8


def attend(query, keys, values, causal):
    heads = query.shape[1]
    rows = query.shape[0] * heads
    flat = query.reshape(rows, query.shape[2])
    scores = lax.dot_general(
        flat, keys, (((1,), (1,)), ((), ())), preferred_element_type=jnp.float32
    )
    scores = scores * query.shape[2] ** (-0.5)
    if causal:
        token = lax.broadcasted_iota(jnp.int32, scores.shape, 0) // heads
        column = lax.broadcasted_iota(jnp.int32, scores.shape, 1)
        scores = jnp.where(column <= token, scores, -1e30)
    row_max = jnp.max(scores, axis=1, keepdims=True)
    weights = jnp.exp(scores - row_max)
    row_total = jnp.sum(weights, axis=1, keepdims=True)
    mixed = (
        jnp.dot(weights.astype(jnp.bfloat16), values, preferred_element_type=jnp.float32)
        / row_total
    )
    level = row_max + jnp.log(row_total)
    return (
        mixed.astype(jnp.bfloat16).reshape(query.shape[0], heads * query.shape[2]),
        level.reshape(query.shape[0], heads),
    )


def attend_block(query_block, cache_block, causal):
    outputs, levels = ([], [])
    mixed, level = attend(query_block[:, 0], cache_block[:, 0, :HD], cache_block[:, 0, HD:], causal)
    outputs.append(mixed)
    levels.append(level)
    return (jnp.concatenate(outputs, axis=1), jnp.concatenate(levels, axis=1))


def request_tables(lists, passage_slot, question_slot, per_device, pass_dev):
    slot_count = question_slot.shape[0]
    slot_ids = jnp.arange(slot_count, dtype=jnp.int32)
    holder = (question_slot[None, :] == slot_ids[:, None]).astype(jnp.int32)
    chosen = jnp.sum(holder[:, :, None] * lists[None, :, :], axis=1)
    catalog = jnp.arange(passage_slot.shape[0], dtype=jnp.int32)
    picked = (chosen[:, :, None] == catalog[None, None, :]).astype(jnp.int32)
    cache_rows = jnp.sum(picked * passage_slot[None, None, :], axis=2)
    cache_rows = cache_rows.reshape(slot_count // per_device, per_device * TOPP)
    owners = cache_rows // pass_dev
    local_rows = cache_rows % pass_dev
    count = owners.shape[1]
    earlier = lax.broadcasted_iota(jnp.int32, (count, count), 1) < lax.broadcasted_iota(
        jnp.int32, (count, count), 0
    )
    same_owner = owners[:, :, None] == owners[:, None, :]
    ranks = jnp.sum((same_owner & earlier[None]).astype(jnp.int32), axis=2)
    return (owners, local_rows, ranks)


def body(queries, own_kv, passage_cache, out_weight, lists, passage_slot, question_slot):
    shards = lax.axis_size("pass")
    my_index = lax.axis_index("pass")
    per_device = queries.shape[0] // LQ
    pass_dev = passage_cache.shape[0]
    local_heads = own_kv.shape[1]
    group = H // KVH
    head_cols = queries.shape[1]
    entries = per_device * TOPP
    most = (entries + shards - 1) // shards
    owners, local_rows, ranks = request_tables(
        lists, passage_slot, question_slot, per_device, pass_dev
    )
    blocks = queries.reshape(per_device, LQ, local_heads, group, HD)
    slot_ids = jnp.arange(most, dtype=jnp.int32)
    entry_ids = jnp.arange(entries, dtype=jnp.int32)
    my_owner = lax.dynamic_index_in_dim(owners, my_index, 0, keepdims=False)
    my_rank = lax.dynamic_index_in_dim(ranks, my_index, 0, keepdims=False)
    match = (
        (owners == my_index)[:, :, None] & (ranks[:, :, None] == slot_ids[None, None, :])
    ).astype(jnp.int32)
    send_row = jnp.sum(match * local_rows[:, :, None], axis=1)
    send_tag = jnp.sum(match * (entry_ids + 1)[None, :, None], axis=1) - 1
    outgoing = jnp.take(passage_cache, send_row, axis=0)
    cache_items = lax.all_to_all(outgoing, "pass", split_axis=0, concat_axis=0, tiled=True)
    tags = lax.all_to_all(send_tag, "pass", split_axis=0, concat_axis=0, tiled=True)
    leading = tags.shape
    flat_cache = cache_items.reshape((-1,) + cache_items.shape[2:])
    flat_tags = tags.reshape(-1)

    def one_item(pair):
        cache_block, tag = pair
        question = jnp.maximum(tag, 0) // TOPP
        query_block = lax.dynamic_index_in_dim(blocks, question, 0, keepdims=False)
        return attend_block(query_block, cache_block, False)

    on_mixed, levels = lax.map(one_item, (flat_cache, flat_tags), batch_size=8)
    arrived = on_mixed.reshape(leading + on_mixed.shape[1:])
    arrived_levels = levels.reshape(leading + levels.shape[1:])
    place = my_owner * most + my_rank
    flat_out = arrived.reshape((shards * most,) + arrived.shape[2:])
    flat_levels = arrived_levels.reshape((shards * most,) + arrived_levels.shape[2:])
    passage_out = jnp.take(flat_out, place, axis=0).reshape(per_device, TOPP, LQ, head_cols)
    passage_levels = jnp.take(flat_levels, place, axis=0).reshape(
        per_device, TOPP, LQ, local_heads * group
    )
    own_out, own_levels = ([], [])
    for question in range(per_device):
        own_block = own_kv[question * LQ : (question + 1) * LQ]
        mixed, level = attend_block(blocks[question], own_block, True)
        own_out.append(mixed)
        own_levels.append(level)
    all_out = jnp.concatenate([passage_out, jnp.stack(own_out)[:, None]], axis=1)
    all_levels = jnp.concatenate([passage_levels, jnp.stack(own_levels)[:, None]], axis=1)
    peak = jnp.max(all_levels, axis=1, keepdims=True)
    overall = peak + jnp.log(jnp.sum(jnp.exp(all_levels - peak), axis=1, keepdims=True))
    share = jnp.exp(all_levels - overall)
    shaped = all_out.reshape(per_device, TOPP + 1, LQ, local_heads * group, HD).astype(jnp.float32)
    context = (
        jnp.sum(shaped * share[..., None], axis=1)
        .reshape(per_device * LQ, head_cols)
        .astype(jnp.bfloat16)
    )
    partial_value = jnp.dot(
        context,
        lax.all_gather(out_weight, "pass", axis=1, tiled=True),
        preferred_element_type=jnp.float32,
    )
    result = lax.psum_scatter(
        partial_value.astype(jnp.bfloat16), "head", scatter_dimension=1, tiled=True
    )
    return result


def solution(mesh):
    in_specs = (
        P("pass", "head"),
        P("pass", "head", None),
        P("pass", None, "head", None),
        P("head", "pass"),
        P(),
        P(),
        P(),
    )
    out_specs = P("pass", "head")
    return jax.shard_map(body, mesh=mesh, in_specs=in_specs, out_specs=out_specs, check_vma=False)
```

profile of v0, /device:TPU:1, one launch (start us, length us, event | category | flops | bytes accessed | tf_op | source)
XLA Modules:
  0.0 487.9 jit_solution(13711640160814067652)
XLA Ops:
  13.4 11.9 %all-to-all-start = ((s32[32,1,1]{2,1,0:T(1,128)}), s32[32,1,1]{2,1,0:T(1,128)S(1)}, u32[]{:S(2)}, u32[]{:S(2)}) async-start(s32[32,1,1]{2,1,0:T(1,128)} %copy.68), calls=%async_computation | async-start | bytes 32768 | tf_op jit(solution)/shard_map/all_to_all | solution.py:92
  25.9 7.2 %gather_fusion.1 = bf16[32,512,256]{2,1,0:T(8,128)(2,1)} fusion(bf16[16,512,256]{2,1,0:T(8,128)(2,1)} %bitcast.117, s32[1024]{0:T(1024)S(1)} %pad_clamp_fusion.1), kind=kCustom, calls=%fused_computation.1 | custom fusion | bytes 16777344 | tf_op jit(solution)/shard_map/jit(_take)/gather | solution.py:90
  33.0 7.5 %bitcast_select_fusion.1 = bf16[32,1,512,1,256]{4,2,3,1,0:T(8,128)(2,1)} fusion(bf16[32,512,256]{2,1,0:T(8,128)(2,1)} %gather_fusion.1, pred[32]{0:T(512)(128)(4,1)S(1)} %compare_and_fusion), kind=kLoop, calls=%fused_computation.30 | loop fusion | flops 4194304 | bytes 16777248 | tf_op jit(solution)/shard_map/jit(_take)/select_n | solution.py:90
  40.5 9.5 %all-to-all-start.1 = ((bf16[32,1,512,1,256]{4,2,3,1,0:T(8,128)(2,1)}), bf16[32,1,512,1,256]{4,2,3,1,0:T(8,128)(2,1)}, u32[]{:S(2)}, u32[]{:S(2)}) async-start(bf16[32,1,512,1,256]{4,2,3,1,0:T(8,128)(2,1)} %bitcast_select_fusion.1), calls=%async_computation.1 | async-start | bytes 16777216 | tf_op jit(solution)/shard_map/all_to_all | solution.py:91
  58.4 203.7 %all-to-all-done.1 = bf16[32,1,512,1,256]{4,2,3,1,0:T(8,128)(2,1)} async-done(((bf16[32,1,512,1,256]{4,2,3,1,0:T(8,128)(2,1)}), bf16[32,1,512,1,256]{4,2,3,1,0:T(8,128)(2,1)}, u32[]{:S(2)}, u32[]{:S(2)}) %all-to-all-start.1) | async-done | bytes 8388640 | tf_op jit(solution)/shard_map/all_to_all | solution.py:91
  262.1 146.1 %while.14 = (s32[]{:T(128)}, bf16[4,8,128,1024]{3,2,1,0:T(8,128)(2,1)}, f32[4,8,128,8]{2,3,1,0:T(8,128)S(1)}, s32[4,8]{1,0:T(4,128)}, bf16[3,128,1,8,128]{4,1,3,...) while((s32[]{:T(128)}, bf16[4,8,128,1024]{3,2,1,0:T(8,128)(2,1)}, ...), condition=%wide.region_9.10_spmd, body=%wide.region_6.9_spmd.sunk | while | flops 2183127040 | bytes 90899360 | solution.py:103
  265.6 7.1 %multiply_reduce_fusion.4 = (f32[8,1024]{1,0:T(8,128)S(1)}, f32[8,1024,512]{1,2,0:T(8,128)}) fusion(bf16[8,512,1,256]{3,1,0,2:T(8,128)(2,1)S(1)} %dynamic-slice_bitcast_fusion.2, bf16[8,128,8,128]{3,1,2,0:T(8,128)(2,1)S(1)} %gather_fusion), kind=kOutput, calls=%fused_computation.5.clone.1 | convolution fusion | flops 1082122240 | bytes 19955712 | tf_op jit(solution)/shard_map/while/body/eval_jaxpr/vmap()/dot_general | solution.py:17
  272.7 8.8 %fusion.82 = f32[8,1024]{1,0:T(8,128)S(1)} fusion(f32[8,1024,512]{1,2,0:T(8,128)} %get-tuple-element.186, f32[8,1024]{1,0:T(8,128)S(1)} %get-tuple-element.187), kind=kLoop, calls=%fused_computation.6.clone.1 | loop fusion | flops 12574720 | bytes 16842752 | tf_op jit(solution)/shard_map/while/body/eval_jaxpr/vmap()/reduce_sum | solution.py:27
  285.3 9.2 %divide_convert_fusion.2 = bf16[8,1024,128]{2,1,0:T(8,128)(2,1)} fusion(f32[8,1024]{1,0:T(8,128)} %copy-done.3, f32[8,1024,512]{1,2,0:T(8,128)} %get-tuple-element.186, f32[8,1024]{1,0:T(8,128)} %copy-done.2, bf16[8,512,1,256]{3,1,0,2:T(8,128)(2,1)S(1)} %copy-done.1), kind=kOutput, calls=%fused_computation.11.clone.1 | convolution fusion | flops 1088421888 | bytes 19988480 | tf_op jit(solution)/shard_map/while/body/eval_jaxpr/vmap()/dot_general | solution.py:29
  294.4 2.8 broadcast_in_dim.101
  302.3 7.1 %multiply_reduce_fusion.4 = (f32[8,1024]{1,0:T(8,128)S(1)}, f32[8,1024,512]{1,2,0:T(8,128)}) fusion(bf16[8,512,1,256]{3,1,0,2:T(8,128)(2,1)S(1)} %dynamic-slice_bitcast_fusion.2, bf16[8,128,8,128]{3,1,2,0:T(8,128)(2,1)S(1)} %gather_fusion), kind=kOutput, calls=%fused_computation.5.clone.1 | convolution fusion | flops 1082122240 | bytes 19955712 | tf_op jit(solution)/shard_map/while/body/eval_jaxpr/vmap()/dot_general | solution.py:17
  309.3 8.7 %fusion.82 = f32[8,1024]{1,0:T(8,128)S(1)} fusion(f32[8,1024,512]{1,2,0:T(8,128)} %get-tuple-element.186, f32[8,1024]{1,0:T(8,128)S(1)} %get-tuple-element.187), kind=kLoop, calls=%fused_computation.6.clone.1 | loop fusion | flops 12574720 | bytes 16842752 | tf_op jit(solution)/shard_map/while/body/eval_jaxpr/vmap()/reduce_sum | solution.py:27
  321.9 9.0 %divide_convert_fusion.2 = bf16[8,1024,128]{2,1,0:T(8,128)(2,1)} fusion(f32[8,1024]{1,0:T(8,128)} %copy-done.3, f32[8,1024,512]{1,2,0:T(8,128)} %get-tuple-element.186, f32[8,1024]{1,0:T(8,128)} %copy-done.2, bf16[8,512,1,256]{3,1,0,2:T(8,128)(2,1)S(1)} %copy-done.1), kind=kOutput, calls=%fused_computation.11.clone.1 | convolution fusion | flops 1088421888 | bytes 19988480 | tf_op jit(solution)/shard_map/while/body/eval_jaxpr/vmap()/dot_general | solution.py:29
  338.8 7.1 %multiply_reduce_fusion.4 = (f32[8,1024]{1,0:T(8,128)S(1)}, f32[8,1024,512]{1,2,0:T(8,128)}) fusion(bf16[8,512,1,256]{3,1,0,2:T(8,128)(2,1)S(1)} %dynamic-slice_bitcast_fusion.2, bf16[8,128,8,128]{3,1,2,0:T(8,128)(2,1)S(1)} %gather_fusion), kind=kOutput, calls=%fused_computation.5.clone.1 | convolution fusion | flops 1082122240 | bytes 19955712 | tf_op jit(solution)/shard_map/while/body/eval_jaxpr/vmap()/dot_general | solution.py:17
  345.8 8.7 %fusion.82 = f32[8,1024]{1,0:T(8,128)S(1)} fusion(f32[8,1024,512]{1,2,0:T(8,128)} %get-tuple-element.186, f32[8,1024]{1,0:T(8,128)S(1)} %get-tuple-element.187), kind=kLoop, calls=%fused_computation.6.clone.1 | loop fusion | flops 12574720 | bytes 16842752 | tf_op jit(solution)/shard_map/while/body/eval_jaxpr/vmap()/reduce_sum | solution.py:27
  358.3 9.0 %divide_convert_fusion.2 = bf16[8,1024,128]{2,1,0:T(8,128)(2,1)} fusion(f32[8,1024]{1,0:T(8,128)} %copy-done.3, f32[8,1024,512]{1,2,0:T(8,128)} %get-tuple-element.186, f32[8,1024]{1,0:T(8,128)} %copy-done.2, bf16[8,512,1,256]{3,1,0,2:T(8,128)(2,1)S(1)} %copy-done.1), kind=kOutput, calls=%fused_computation.11.clone.1 | convolution fusion | flops 1088421888 | bytes 19988480 | tf_op jit(solution)/shard_map/while/body/eval_jaxpr/vmap()/dot_general | solution.py:29
  375.2 7.1 %multiply_reduce_fusion.4 = (f32[8,1024]{1,0:T(8,128)S(1)}, f32[8,1024,512]{1,2,0:T(8,128)}) fusion(bf16[8,512,1,256]{3,1,0,2:T(8,128)(2,1)S(1)} %dynamic-slice_bitcast_fusion.2, bf16[8,128,8,128]{3,1,2,0:T(8,128)(2,1)S(1)} %gather_fusion), kind=kOutput, calls=%fused_computation.5.clone.1 | convolution fusion | flops 1082122240 | bytes 19955712 | tf_op jit(solution)/shard_map/while/body/eval_jaxpr/vmap()/dot_general | solution.py:17
  382.2 8.7 %fusion.82 = f32[8,1024]{1,0:T(8,128)S(1)} fusion(f32[8,1024,512]{1,2,0:T(8,128)} %get-tuple-element.186, f32[8,1024]{1,0:T(8,128)S(1)} %get-tuple-element.187), kind=kLoop, calls=%fused_computation.6.clone.1 | loop fusion | flops 12574720 | bytes 16842752 | tf_op jit(solution)/shard_map/while/body/eval_jaxpr/vmap()/reduce_sum | solution.py:27
  394.8 9.0 %divide_convert_fusion.2 = bf16[8,1024,128]{2,1,0:T(8,128)(2,1)} fusion(f32[8,1024]{1,0:T(8,128)} %copy-done.3, f32[8,1024,512]{1,2,0:T(8,128)} %get-tuple-element.186, f32[8,1024]{1,0:T(8,128)} %copy-done.2, bf16[8,512,1,256]{3,1,0,2:T(8,128)(2,1)S(1)} %copy-done.1), kind=kOutput, calls=%fused_computation.11.clone.1 | convolution fusion | flops 1088421888 | bytes 19988480 | tf_op jit(solution)/shard_map/while/body/eval_jaxpr/vmap()/dot_general | solution.py:29
  410.1 7.9 %gather_fusion.2 = bf16[24,128,1024]{2,1,0:T(8,128)(2,1)} fusion(bf16[32,128,1024]{2,1,0:T(8,128)(2,1)} %bitcast.118, s32[1024]{0:T(1024)S(1)} %pad_clamp_fusion), kind=kCustom, calls=%fused_computation.2 | custom fusion | bytes 12583008 | tf_op jit(solution)/shard_map/jit(_take)/gather | solution.py:109
  418.0 4.4 copy.87
  423.5 5.2 %multiply_reduce_fusion.1 = bf16[3,128,8,128]{3,2,1,0:T(8,128)(2,1)S(1)} fusion(bf16[1,1,128,8,128]{4,3,2,1,0:T(8,128)(2,1)S(1)} %copy-done.7, bf16[1,1,128,8,128]{4,3,2,1,0:T(8,128)(2,1)S(1)} %copy-done.6, bf16[1,1,128,8,128]{4,3,2,1,0:T(8,128)(2,1)S(1)} %copy-done.5, bf16[3,8,128,8,128]{4,3,2,1,0:T(8,128)(2,1)S(1)} %broadcast_select_fusion, ...), kind=kLoop, calls=%fused_computation.29 | loop fusion | flops 34996224 | bytes 7974912 | tf_op jit(solution)/shard_map/reduce_sum | solution.py:126
  428.8 8.2 %convolution_convert_fusion = bf16[384,4096]{1,0:T(8,128)(2,1)} fusion(bf16[1024,4096]{1,0:T(8,128)(2,1)} %all-gather.2.cloned.1.call-done, bf16[48,8,8,128]{3,2,1,0:T(8,128)(2,1)S(1)} %bitcast.121), kind=kOutput, calls=%fused_computation.32 | convolution fusion | flops 3222798336 | bytes 12320768 | tf_op jit(solution)/shard_map/dot_general | solution.py:130
  437.0 44.1 %reduce-scatter.2.cloned.1.call-done = bf16[384,512]{1,0:T(8,128)(2,1)} async-done(((bf16[384,4096]{1,0:T(8,128)(2,1)}), bf16[384,512]{1,0:T(8,128)(2,1)}) %reduce-scatter.2.cloned.1.call-update) | async-done | bytes 393232 | tf_op jit(solution)/shard_map/reduce_scatter | solution.py:135
  (150 shorter events, 62.2 us)
Async XLA Ops:
  13.4 27.1 %all-to-all-start = ((s32[32,1,1]{2,1,0:T(1,128)}), s32[32,1,1]{2,1,0:T(1,128)S(1)}, u32[]{:S(2)}, u32[]{:S(2)}) async-start(s32[32,1,1]{2,1,0:T(1,128)} %copy.68), calls=%async_computation | async-start | bytes 32768 | tf_op jit(solution)/shard_map/all_to_all | solution.py:92
  40.5 10.3 %copy-start.4 = (bf16[384,1024]{1,0:T(8,128)(2,1)S(1)}, bf16[384,1024]{1,0:T(8,128)(2,1)}, u32[]{:S(2)}) copy-start(bf16[384,1024]{1,0:T(8,128)(2,1)} %param.9) | copy-start | bytes 2359300
  40.5 11.2 %copy-start.9 = (bf16[384,1,256]{2,0,1:T(8,128)(2,1)S(1)}, bf16[384,1,256]{2,0,1:T(8,128)(2,1)}, u32[]{:S(2)}) copy-start(bf16[384,1,256]{2,0,1:T(8,128)(2,1)} %param.10) | copy-start | bytes 589828
  40.5 221.6 %all-to-all-start.1 = ((bf16[32,1,512,1,256]{4,2,3,1,0:T(8,128)(2,1)}), bf16[32,1,512,1,256]{4,2,3,1,0:T(8,128)(2,1)}, u32[]{:S(2)}, u32[]{:S(2)}) async-start(bf16[32,1,512,1,256]{4,2,3,1,0:T(8,128)(2,1)} %bitcast_select_fusion.1), calls=%async_computation.1 | async-start | bytes 16777216 | tf_op jit(solution)/shard_map/all_to_all | solution.py:91
  50.0 378.7 %all-gather.2.cloned.1.call-start = ((), (), s32[]{:S(2)}) async-start(), calls=%async_computation.3 | async-start | bytes 8650752 | tf_op jit(solution)/shard_map/all_gather | solution.py:132
  50.8 430.3 %reduce-scatter.2.cloned.1.call-start = ((), (), s32[]{:S(2)}) async-start(), calls=%async_computation.4 | async-start | bytes 3538944 | tf_op jit(solution)/shard_map/reduce_scatter | solution.py:135
  265.6 7.1 %copy-start = (bf16[8,512,1,256]{3,1,0,2:T(8,128)(2,1)}, bf16[8,512,1,256]{3,1,0,2:T(8,128)(2,1)S(1)}, u32[]{:S(2)}) copy-start(bf16[8,512,1,256]{3,1,0,2:T(8,128)(2,1)S(1)} %dynamic-slice_bitcast_fusion.2) | copy-start | bytes 6291460 | tf_op jit(solution)/shard_map/while
  272.7 8.8 %copy-start.2 = (f32[8,1024]{1,0:T(8,128)}, f32[8,1024]{1,0:T(8,128)S(1)}, u32[]{:S(2)}) copy-start(f32[8,1024]{1,0:T(8,128)S(1)} %get-tuple-element.187) | copy-start | bytes 98308 | tf_op jit(solution)/shard_map/while
  272.7 12.6 %copy-start.1 = (bf16[8,512,1,256]{3,1,0,2:T(8,128)(2,1)S(1)}, bf16[8,512,1,256]{3,1,0,2:T(8,128)(2,1)}, u32[]{:S(2)}) copy-start(bf16[8,512,1,256]{3,1,0,2:T(8,128)(2,1)} %copy-done) | copy-start | bytes 6291460 | tf_op jit(solution)/shard_map/while
  281.5 0.6 copy-start.3
  302.3 7.1 %copy-start = (bf16[8,512,1,256]{3,1,0,2:T(8,128)(2,1)}, bf16[8,512,1,256]{3,1,0,2:T(8,128)(2,1)S(1)}, u32[]{:S(2)}) copy-start(bf16[8,512,1,256]{3,1,0,2:T(8,128)(2,1)S(1)} %dynamic-slice_bitcast_fusion.2) | copy-start | bytes 6291460 | tf_op jit(solution)/shard_map/while
  309.3 8.7 %copy-start.2 = (f32[8,1024]{1,0:T(8,128)}, f32[8,1024]{1,0:T(8,128)S(1)}, u32[]{:S(2)}) copy-start(f32[8,1024]{1,0:T(8,128)S(1)} %get-tuple-element.187) | copy-start | bytes 98308 | tf_op jit(solution)/shard_map/while
  309.3 12.5 %copy-start.1 = (bf16[8,512,1,256]{3,1,0,2:T(8,128)(2,1)S(1)}, bf16[8,512,1,256]{3,1,0,2:T(8,128)(2,1)}, u32[]{:S(2)}) copy-start(bf16[8,512,1,256]{3,1,0,2:T(8,128)(2,1)} %copy-done) | copy-start | bytes 6291460 | tf_op jit(solution)/shard_map/while
  338.8 7.1 %copy-start = (bf16[8,512,1,256]{3,1,0,2:T(8,128)(2,1)}, bf16[8,512,1,256]{3,1,0,2:T(8,128)(2,1)S(1)}, u32[]{:S(2)}) copy-start(bf16[8,512,1,256]{3,1,0,2:T(8,128)(2,1)S(1)} %dynamic-slice_bitcast_fusion.2) | copy-start | bytes 6291460 | tf_op jit(solution)/shard_map/while
  345.8 8.7 %copy-start.2 = (f32[8,1024]{1,0:T(8,128)}, f32[8,1024]{1,0:T(8,128)S(1)}, u32[]{:S(2)}) copy-start(f32[8,1024]{1,0:T(8,128)S(1)} %get-tuple-element.187) | copy-start | bytes 98308 | tf_op jit(solution)/shard_map/while
  345.8 12.5 %copy-start.1 = (bf16[8,512,1,256]{3,1,0,2:T(8,128)(2,1)S(1)}, bf16[8,512,1,256]{3,1,0,2:T(8,128)(2,1)}, u32[]{:S(2)}) copy-start(bf16[8,512,1,256]{3,1,0,2:T(8,128)(2,1)} %copy-done) | copy-start | bytes 6291460 | tf_op jit(solution)/shard_map/while
  375.2 7.1 %copy-start = (bf16[8,512,1,256]{3,1,0,2:T(8,128)(2,1)}, bf16[8,512,1,256]{3,1,0,2:T(8,128)(2,1)S(1)}, u32[]{:S(2)}) copy-start(bf16[8,512,1,256]{3,1,0,2:T(8,128)(2,1)S(1)} %dynamic-slice_bitcast_fusion.2) | copy-start | bytes 6291460 | tf_op jit(solution)/shard_map/while
  382.2 8.7 %copy-start.2 = (f32[8,1024]{1,0:T(8,128)}, f32[8,1024]{1,0:T(8,128)S(1)}, u32[]{:S(2)}) copy-start(f32[8,1024]{1,0:T(8,128)S(1)} %get-tuple-element.187) | copy-start | bytes 98308 | tf_op jit(solution)/shard_map/while
  382.2 12.5 %copy-start.1 = (bf16[8,512,1,256]{3,1,0,2:T(8,128)(2,1)S(1)}, bf16[8,512,1,256]{3,1,0,2:T(8,128)(2,1)}, u32[]{:S(2)}) copy-start(bf16[8,512,1,256]{3,1,0,2:T(8,128)(2,1)} %copy-done) | copy-start | bytes 6291460 | tf_op jit(solution)/shard_map/while
  390.9 0.6 copy-start.3
  418.0 4.5 copy-start.8
  422.4 1.0 copy-start.5
  422.4 1.0 copy-start.6
  422.4 1.1 copy-start.7
  (2 other events, 1.2 us)
Sparse Core Ops, SparseCore 0:
  53.3 238.9 all-gather.1
  437.1 43.9 reduce-scatter.1
where the time goes:
time: 491 us; the launch traced here: 488 us
  waiting for transfers between devices  249 us (51%)
  matrix products  76.5 us (16%)
  local copies, waits for them, and re-layouts  65.5 us (13%)
  other arithmetic  61.8 us (13%)
  starting transfers between devices  21.5 us (4%)
  between operations  13.8 us (3%)
    all_to_all x1, waiting for transfers between devices, body(): lax.all_to_all(outgoing, 'pass', split_axis=0, concat_axis=0, tiled=True)  204 us
    reduce_scatter x1, waiting for transfers between devices, body(): lax.psum_scatter(partial_value.astype(jnp.bfloat16), 'head', scatter_dime...  44.1 us
    dot_general x7, matrix products, attend(): jnp.dot(weights.astype(jnp.bfloat16), values, preferred_element_type=jnp....  39.3 us
    reduce_sum x7, other arithmetic, attend(): row_total = jnp.sum(weights, axis=1, keepdims=True)  35.1 us
    dot_general x7, matrix products, attend(): lax.dot_general(flat, keys, (((1,), (1,)), ((), ())), preferred_element_t...  29 us
    dynamic_update_slice x12, local copies, waits for them, and re-layouts, body(): on_mixed, levels = lax.map(one_item, (flat_cache, flat_tags), batch_size=8)  12.6 us
    all_to_all x1, starting transfers between devices, body(): lax.all_to_all(send_tag, 'pass', split_axis=0, concat_axis=0, tiled=True)  11.9 us
    broadcast_in_dim x4, local copies, waits for them, and re-layouts, body(): on_mixed, levels = lax.map(one_item, (flat_cache, flat_tags), batch_size=8)  11.3 us
  transfers between devices with their start and end apart: 4, of which 2 were waited for; matrix products, arithmetic and copies ran while one was open for 38% of the time, Pallas kernels for 0%

commit v1 on v0

v1 whole, which is shorter than its diff:
```python
import functools
import math

import jax
import jax.numpy as jnp
from jax import lax
from jax.experimental import pallas as pl
from jax.experimental.pallas import tpu as pltpu
from jax.sharding import Mesh, PartitionSpec as P

HD = 128
GROUP = 8
LQ = 128
PLEN = 512
TOPP = 8
NX, NZ, NY, NC = 4, 8, 4, 2
ROWS = GROUP * LQ
SCALE = math.log2(math.e) / math.sqrt(HD)
NEG = -1e30
WIDTH = 512
VMEM_LIMIT = 50 << 20

FAR_SENT = (3, -3, 4)
FAR_HERE = (2, -2)
NEAR = (0, 1, -1)


def request_tables(lists, passage_slot, question_slot, per_device, pass_dev):
    slot_count = question_slot.shape[0]
    slot_ids = jnp.arange(slot_count, dtype=jnp.int32)
    holder = (question_slot[None, :] == slot_ids[:, None]).astype(jnp.int32)
    chosen = jnp.sum(holder[:, :, None] * lists[None, :, :], axis=1)
    catalog = jnp.arange(passage_slot.shape[0], dtype=jnp.int32)
    picked = (chosen[:, :, None] == catalog[None, None, :]).astype(jnp.int32)
    cache_rows = jnp.sum(picked * passage_slot[None, None, :], axis=2)
    cache_rows = cache_rows.reshape(slot_count // per_device, per_device * TOPP)
    return cache_rows // pass_dev, cache_rows % pass_dev


def row_copy(rows_ref, cache_ref, out_ref):
    out_ref[...] = cache_ref[...]


def take_rows(cache, rows):
    n = rows.shape[0]
    block = (1,) + cache.shape[1:]
    return pl.pallas_call(
        row_copy,
        out_shape=jax.ShapeDtypeStruct((n,) + cache.shape[1:], cache.dtype),
        grid_spec=pltpu.PrefetchScalarGridSpec(
            num_scalar_prefetch=1,
            grid=(n,),
            in_specs=[pl.BlockSpec(block, lambda i, rows_ref: (rows_ref[i], 0, 0))],
            out_specs=pl.BlockSpec(block, lambda i, rows_ref: (i, 0, 0)),
        ),
        name="take_rows",
    )(rows, cache)


def absorb(keys, values_t, query_ref, group, cols, acc, top, total, causal=False):
    which, lane = group
    scores = lax.dot_general(
        keys,
        query_ref[lane, cols, :],
        (((1,), (1,)), ((), ())),
        preferred_element_type=jnp.float32,
    )
    if causal:
        key = lax.broadcasted_iota(jnp.int32, scores.shape, 0)
        token = lax.broadcasted_iota(jnp.int32, scores.shape, 1)
        scores = jnp.where(key <= token, scores, NEG)
    old = top[which, :, cols]
    new = jnp.maximum(old, jnp.max(scores, axis=0, keepdims=True))
    weights = jnp.exp2((scores - new) * SCALE)
    keep = jnp.exp2((old - new) * SCALE)
    top[which, :, cols] = new
    total[which, :, cols] = total[which, :, cols] * keep + jnp.sum(weights, axis=0, keepdims=True)
    acc[which, :, cols] = acc[which, :, cols] * keep + jnp.dot(
        values_t, weights.astype(jnp.bfloat16), preferred_element_type=jnp.float32
    )


def start(acc, top, total):
    acc[...] = jnp.zeros_like(acc)
    top[...] = jnp.full_like(top, NEG)
    total[...] = jnp.zeros_like(total)


def absorb_all(tag_ref, first, kv_ref, count, pick, query_ref, base, acc, top, total):
    def step(i, carry):
        tag = tag_ref[first + i]

        @pl.when(tag >= 0)
        def _():
            index = pick(i)
            keys = kv_ref[(*index, slice(None), slice(0, HD))]
            values_t = kv_ref[(*index, slice(None), slice(HD, 2 * HD))].T
            for part in range(ROWS // WIDTH):
                cols = pl.ds(part * WIDTH, WIDTH)
                absorb(keys, values_t, query_ref, (base + tag, tag), cols, acc, top, total)

        return carry

    lax.fori_loop(0, count, step, 0)


def finish(out_ref, level_ref, base, acc, top, total):
    for j in range(out_ref.shape[0]):
        sums = jnp.maximum(total[base + j], 1e-30)
        out_ref[j] = (acc[base + j] / sums).astype(jnp.bfloat16)
        level_ref[j] = top[base + j] * SCALE + jnp.log2(sums)


def far_kernel(tags, q_up, q_down, here, up3, down3, up4, down4, o_up, l_up, o_down, l_down, *state):
    start(*state)
    n = q_up.shape[0]
    absorb_all(tags, 0, here, 4, lambda i: (i, 0), q_up, 0, *state)
    absorb_all(tags, 4, here, 4, lambda i: (i, 1), q_down, n, *state)
    absorb_all(tags, 8, up3, 4, lambda i: (i,), q_up, 0, *state)
    absorb_all(tags, 12, down3, 4, lambda i: (i,), q_down, n, *state)
    absorb_all(tags, 16, up4, 2, lambda i: (i,), q_up, 0, *state)
    absorb_all(tags, 18, down4, 2, lambda i: (i,), q_down, n, *state)
    finish(o_up, l_up, 0, *state)
    finish(o_down, l_down, n, *state)


def near_kernel(
    tags, q_own, q_up, q_down, here, own, o_own, l_own, o_up, l_up, o_down, l_down, *state
):
    start(*state)
    n = q_own.shape[0]
    for j in range(n):
        rows = slice(j * LQ, (j + 1) * LQ)
        keys = own[rows, 0:HD]
        values_t = own[rows, HD : 2 * HD].T
        for part in range(GROUP):
            cols = pl.ds(part * LQ, LQ)
            absorb(keys, values_t, q_own, (j, j), cols, *state, causal=True)
    absorb_all(tags, 0, here, 4, lambda i: (i, 0), q_own, 0, *state)
    absorb_all(tags, 4, here, 4, lambda i: (i, 1), q_up, n, *state)
    absorb_all(tags, 8, here, 4, lambda i: (i, 2), q_down, 2 * n, *state)
    finish(o_own, l_own, 0, *state)
    finish(o_up, l_up, n, *state)
    finish(o_down, l_down, 2 * n, *state)


def attention(kernel, name, tags, arrays, n, sides, items):
    out = []
    for _ in range(sides):
        out.append(jax.ShapeDtypeStruct((n, HD, ROWS), jnp.bfloat16))
        out.append(jax.ShapeDtypeStruct((n, 1, ROWS), jnp.float32))
    vmem = pl.BlockSpec(memory_space=pltpu.VMEM)
    return pl.pallas_call(
        kernel,
        out_shape=tuple(out),
        in_specs=[pl.BlockSpec(memory_space=pltpu.SMEM)] + [vmem] * len(arrays),
        out_specs=(vmem,) * len(out),
        scratch_shapes=[
            pltpu.VMEM((sides * n, HD, ROWS), jnp.float32),
            pltpu.VMEM((sides * n, 1, ROWS), jnp.float32),
            pltpu.VMEM((sides * n, 1, ROWS), jnp.float32),
        ],
        compiler_params=pltpu.CompilerParams(vmem_limit_bytes=VMEM_LIMIT),
        cost_estimate=pl.CostEstimate(
            flops=items * 4 * ROWS * PLEN * HD * 2,
            bytes_accessed=items * PLEN * 2 * HD * 2,
            transcendentals=items * ROWS * PLEN,
        ),
        name=name,
    )(tags, *arrays)


def merge(pairs):
    level = pairs[0][1]
    for _, other in pairs[1:]:
        level = jnp.maximum(level, other)
    shares = [jnp.exp2(l - level) for _, l in pairs]
    whole = functools.reduce(jnp.add, shares)
    mixed = functools.reduce(
        jnp.add, [o.astype(jnp.float32) * s for (o, _), s in zip(pairs, shares)]
    )
    return mixed / whole, level + jnp.log2(whole)


def hop_kernel(o_a, l_a, o_b, l_b, o_c, l_c, o_d, l_d, o_up, l_up, o_down, l_down):
    for j in range(o_a.shape[0]):
        mixed, level = merge([(o_a[j], l_a[j]), (o_b[j], l_b[j])])
        o_up[j] = mixed.astype(jnp.bfloat16)
        l_up[j] = level
        mixed, level = merge([(o_c[j], l_c[j]), (o_d[j], l_d[j])])
        o_down[j] = mixed.astype(jnp.bfloat16)
        l_down[j] = level


def last_kernel(o_a, l_a, o_b, l_b, o_c, l_c, out_ref):
    for j in range(o_a.shape[0]):
        mixed, _ = merge([(o_a[j], l_a[j]), (o_b[j], l_b[j]), (o_c[j], l_c[j])])
        for part in range(GROUP):
            cols = slice(part * LQ, (part + 1) * LQ)
            out_ref[j * LQ : (j + 1) * LQ, part * HD : (part + 1) * HD] = mixed[:, cols].T.astype(
                jnp.bfloat16
            )


def in_vmem(kernel, name, out, *arrays):
    vmem = pl.BlockSpec(memory_space=pltpu.VMEM)
    return pl.pallas_call(
        kernel,
        out_shape=out,
        in_specs=[vmem] * len(arrays),
        out_specs=jax.tree.map(lambda _: vmem, out),
        compiler_params=pltpu.CompilerParams(vmem_limit_bytes=VMEM_LIMIT),
        name=name,
    )(*arrays)


def project_kernel(context_ref, weight_ref, out_ref):
    weight = jnp.concatenate([weight_ref[0], weight_ref[1]], axis=1)
    out_ref[...] = jnp.dot(
        context_ref[...], weight, preferred_element_type=jnp.float32
    ).astype(jnp.bfloat16)


def project(context, weight):
    blocks, rows, cols = weight.shape
    return pl.pallas_call(
        project_kernel,
        out_shape=jax.ShapeDtypeStruct((context.shape[0], blocks * cols), jnp.bfloat16),
        grid=(blocks // 2,),
        in_specs=[
            pl.BlockSpec(context.shape, lambda i: (0, 0)),
            pl.BlockSpec((2, rows, cols), lambda i: (i, 0, 0)),
        ],
        out_specs=pl.BlockSpec((context.shape[0], 2 * cols), lambda i: (0, i)),
        compiler_params=pltpu.CompilerParams(vmem_limit_bytes=VMEM_LIMIT),
        name="project",
    )(context, weight)


def along(array, axis, size, shift):
    pairs = [(i, (i + shift) % size) for i in range(size)]
    return jax.tree.map(lambda a: lax.ppermute(a, axis, pairs), array)


def over_x(items):
    return lax.all_to_all(items, "x", split_axis=0, concat_axis=0, tiled=True)


def body(queries, own_kv, passage_cache, out_weight, lists, passage_slot, question_slot):
    x, z = lax.axis_index("x"), lax.axis_index("z")
    per_device = queries.shape[0] // LQ
    pass_dev = passage_cache.shape[0]
    cache = passage_cache.reshape(pass_dev, PLEN, 2 * HD)
    own = own_kv.reshape(per_device * LQ, 2 * HD)

    weight = lax.all_gather(out_weight, "z", axis=0)
    weight = lax.all_gather(weight, "x", axis=0)
    weight = weight.reshape(NX * NZ, out_weight.shape[0], out_weight.shape[1])

    q_own = queries.reshape(per_device, LQ, GROUP, HD).transpose(0, 2, 1, 3)
    q_own = q_own.reshape(per_device, ROWS, HD)
    q_up = along(q_own, "z", NZ, -1)
    q_down = along(q_own, "z", NZ, 1)
    q_up2 = along(q_up, "z", NZ, -1)
    q_down2 = along(q_down, "z", NZ, 1)

    owners, local_rows = request_tables(lists, passage_slot, question_slot, per_device, pass_dev)
    mine = jnp.sum(jnp.where(owners == x * NZ + z, local_rows, 0), axis=1).reshape(NX, NZ)
    sent = jnp.array(FAR_SENT + FAR_HERE + NEAR, jnp.int32)
    target_z = (z + sent) % NZ
    rows = jnp.sum(
        jnp.where(target_z[None, :, None] == jnp.arange(NZ)[None, None, :], mine[:, None, :], 0),
        axis=2,
    )

    def items_for(first, count):
        picked = rows[:, first : first + count].reshape(NX * count)
        return over_x(take_rows(cache, picked).reshape(NX, count, PLEN, 2 * HD))

    moved = items_for(0, 3)
    far_here = items_for(3, 2)
    near_here = items_for(5, 3)
    up3 = along(moved[:, 0], "z", NZ, 1)
    down3 = along(moved[:, 1], "z", NZ, -1)
    up4 = along(moved[0:2, 2], "z", NZ, 2)
    down4 = along(moved[2:4, 2], "z", NZ, -2)

    four, low, high = range(NX), (0, 1), (2, 3)
    slots = (
        [(2, i, 0) for i in four]
        + [(-2, i, 0) for i in four]
        + [(2, i, -1) for i in four]
        + [(-2, i, 1) for i in four]
        + [(2, i, -2) for i in low]
        + [(-2, i, 2) for i in high]
        + [(0, i, 0) for i in four]
        + [(1, i, 0) for i in four]
        + [(-1, i, 0) for i in four]
    )
    slot_question = (z + jnp.array([s[0] for s in slots], jnp.int32)) % NZ
    slot_owner = jnp.array([s[1] for s in slots], jnp.int32) * NZ + (
        z + jnp.array([s[2] for s in slots], jnp.int32)
    ) % NZ
    column = lax.dynamic_index_in_dim(owners.reshape(NX, NZ, -1), x, 0, keepdims=False)
    number = jnp.arange(column.shape[1], dtype=jnp.int32) // TOPP + 1
    hit = (slot_question[:, None, None] == jnp.arange(NZ)[None, :, None]) & (
        slot_owner[:, None, None] == column[None, :, :]
    )
    tags = jnp.sum(jnp.where(hit, number[None, None, :], 0), axis=(1, 2)) - 1

    far = attention(
        far_kernel,
        "far",
        tags[:20],
        [q_up2, q_down2, far_here, up3, down3, up4, down4],
        per_device,
        2,
        15,
    )
    o_near = attention(
        near_kernel,
        "near",
        tags[20:],
        [q_own, q_up, q_down, near_here, own],
        per_device,
        3,
        10,
    )
    back_up = along(far[0:2], "z", NZ, 1)
    back_down = along(far[2:4], "z", NZ, -1)
    shapes = tuple(jax.ShapeDtypeStruct(a.shape, a.dtype) for a in far)
    hop = in_vmem(hop_kernel, "hop", shapes, *o_near[2:4], *back_up, *o_near[4:6], *back_down)
    home_up = along(hop[0:2], "z", NZ, 1)
    home_down = along(hop[2:4], "z", NZ, -1)
    context = in_vmem(
        last_kernel,
        "last",
        jax.ShapeDtypeStruct(queries.shape, jnp.bfloat16),
        *o_near[0:2],
        *home_up,
        *home_down,
    )
    partial_value = project(context, weight)
    return lax.psum_scatter(partial_value, ("y", "core"), scatter_dimension=1, tiled=True)


def solution(mesh):
    grid = Mesh(mesh.devices.reshape(NX, NZ, NY, NC), ("x", "z", "y", "core"))
    on_pass, on_head = ("x", "z"), ("y", "core")
    in_specs = (
        P(on_pass, on_head),
        P(on_pass, on_head, None),
        P(on_pass, None, on_head, None),
        P(on_head, on_pass),
        P(),
        P(),
        P(),
    )
    out_specs = P(on_pass, on_head)
    return jax.shard_map(body, mesh=grid, in_specs=in_specs, out_specs=out_specs, check_vma=False)
```

time: 491 us -> 384 us (0.78)
  Pallas kernels: 0 us -> 80.5 us
  matrix products: 76.5 us -> 0 us
  local copies, waits for them, and re-layouts: 65.5 us -> 8.26 us
  other arithmetic: 61.8 us -> 6.86 us
  starting transfers between devices: 21.5 us -> 43.4 us
  waiting for transfers between devices: 249 us -> 229 us
    all_to_all x2 -> x3, waiting for transfers between devices: 204 us -> 92.7 us  [over_x(): return lax.all_to_all(items, 'x', split_axis=0, concat_axis=0, tiled=True)]
    pallas_call x0 -> x8, Pallas kernels: none -> 80.5 us  [the longest x2 40.7 us: attention(): pl.pallas_call(kernel, out_shape=tuple(out), in_specs=[pl.BlockSpec(memor...]
    dot_general x15 -> x0, matrix products: 76.5 us -> none  [the longest x7 39.3 us: attend(): jnp.dot(weights.astype(jnp.bfloat16), values, preferred_element_type=jnp....]
    ppermute x0 -> x16, waiting for transfers between devices: none -> 49.4 us  [along(): return jax.tree.map(lambda a: lax.ppermute(a, axis, pairs), array)]
    all_gather x1 -> x2, waiting for transfers between devices: 0.02 us -> 43.1 us  [the longest x1 43.1 us: body(): weight = lax.all_gather(out_weight, 'z', axis=0)]
    reduce_sum x13 -> x4, other arithmetic: 40.8 us -> 0.51 us  [the longest x2 0.26 us: body(): jnp.sum(jnp.where(owners == x * NZ + z, local_rows, 0), axis=1)]
    ppermute x0 -> x16, starting transfers between devices: none -> 30 us  [along(): return jax.tree.map(lambda a: lax.ppermute(a, axis, pairs), array)]
    gather x7 -> x0, local copies, waits for them, and re-layouts: 19.4 us -> none  [the longest x1 7.88 us: body(): jnp.take(flat_out, place, axis=0).reshape(per_device, TOPP, LQ, head_cols)]
  transfers between devices with their start and end apart: 4 -> 22, of which waited for: 2 -> 8; matrix products, arithmetic and copies ran while one was open for 38% -> 3% of each run, Pallas kernels for 0% -> 18%
where the time goes in v1:
time: 384 us; the launch traced here: 381 us
  waiting for transfers between devices  229 us (60%)
  Pallas kernels  80.5 us (21%)
  starting transfers between devices  43.4 us (11%)
  between operations  13.4 us (3%)
  local copies, waits for them, and re-layouts  8.26 us (2%)
  other arithmetic  6.86 us (2%)
    all_to_all x3, waiting for transfers between devices, over_x(): return lax.all_to_all(items, 'x', split_axis=0, concat_axis=0, tiled=True)  92.7 us
    ppermute x16, waiting for transfers between devices, along(): return jax.tree.map(lambda a: lax.ppermute(a, axis, pairs), array)  49.4 us
    all_gather x1, waiting for transfers between devices, body(): weight = lax.all_gather(out_weight, 'z', axis=0)  43.1 us
    reduce_scatter x1, waiting for transfers between devices, body(): lax.psum_scatter(partial_value, ('y', 'core'), scatter_dimension=1, tiled...  43 us
    pallas_call x2, Pallas kernels, attention(): pl.pallas_call(kernel, out_shape=tuple(out), in_specs=[pl.BlockSpec(memor...  40.7 us
    ppermute x16, starting transfers between devices, along(): return jax.tree.map(lambda a: lax.ppermute(a, axis, pairs), array)  30 us
    pallas_call x3, Pallas kernels, take_rows(): pl.pallas_call(row_copy, out_shape=jax.ShapeDtypeStruct((n,) + cache.shap...  23.7 us
    pallas_call x1, Pallas kernels, project(): pl.pallas_call(project_kernel, out_shape=jax.ShapeDtypeStruct((context.sh...  13.5 us
  transfers between devices with their start and end apart: 22, of which 8 were waited for; matrix products, arithmetic and copies ran while one was open for 3% of the time, Pallas kernels for 18%

profile of v1, /device:TPU:1, one launch (start us, length us, event | category | flops | bytes accessed | tf_op | source)
XLA Modules:
  0.0 381.4 jit_solution(5376814417857245276)
XLA Ops:
  7.3 43.1 %all-gather.5.cloned.1.call-done = bf16[8192,128]{1,0:T(8,128)(2,1)} async-done(((bf16[1024,128]{1,0:T(8,128)(2,1)}), bf16[8192,128]{1,0:T(8,128)(2,1)}) %all-gather.5.cloned.1.call-update) | async-done | bytes 2097168 | tf_op jit(solution)/shard_map/all_gather | solution.py:256
  51.1 2.4 multiply_reduce_fusion
  53.5 2.5 select_reduce_fusion
  58.0 6.4 %take_rows.4 = bf16[8,512,256]{2,1,0:T(8,128)(2,1)} custom-call(s32[8]{0:T(128)} %reshape.131.rows_ref, bf16[16,512,256]{2,1,0:T(8,128)(2,1)} %bitcast.36), custom_call_target="tpu_custom_call" | custom-call | tf_op jit(solution)/shard_map/take_rows/pallas_call | solution.py:47
  64.4 3.9 %all-to-all-start.1 = ((bf16[4,2,512,256]{3,2,1,0:T(8,128)(2,1)}), bf16[4,2,512,256]{3,2,1,0:T(8,128)(2,1)S(1)}, u32[]{:S(2)}, u32[]{:S(2)}) async-start(bf16[4,2,512,256]{3,2,1,0:T(8,128)(2,1)} %bitcast.41), calls=%async_computation.1 | async-start | bytes 4194304 | tf_op jit(solution)/shard_map/all_to_all | solution.py:246
  69.0 8.6 %take_rows.5 = bf16[12,512,256]{2,1,0:T(8,128)(2,1)} custom-call(s32[12]{0:T(128)} %reshape.133.rows_ref, bf16[16,512,256]{2,1,0:T(8,128)(2,1)} %bitcast.37), custom_call_target="tpu_custom_call" | custom-call | tf_op jit(solution)/shard_map/take_rows/pallas_call | solution.py:47
  77.6 37.8 %all-to-all-done.1.here = bf16[4,2,512,256]{3,2,1,0:T(8,128)(2,1)S(1)} async-done(((bf16[4,2,512,256]{3,2,1,0:T(8,128)(2,1)}), bf16[4,2,512,256]{3,2,1,0:T(8,128)(2,1)S(1)}, u32[]{:S(2)}, u32[]{:S(2)}) %all-to-all-start.1) | async-done | bytes 2097184 | tf_op jit(solution)/shard_map/all_to_all | solution.py:246
  116.8 4.6 %all-to-all-start.2 = ((bf16[4,3,512,256]{3,2,1,0:T(8,128)(2,1)}), bf16[4,3,512,256]{3,2,1,0:T(8,128)(2,1)}, u32[]{:S(2)}, u32[]{:S(2)}) async-start(bf16[4,3,512,256]{3,2,1,0:T(8,128)(2,1)} %bitcast.40), calls=%async_computation.2 | async-start | bytes 6291456 | tf_op jit(solution)/shard_map/all_to_all | solution.py:246
  124.1 8.7 %take_rows.3 = bf16[12,512,256]{2,1,0:T(8,128)(2,1)} custom-call(s32[12]{0:T(128)} %reshape.127.rows_ref, bf16[16,512,256]{2,1,0:T(8,128)(2,1)} %bitcast.38), custom_call_target="tpu_custom_call" | custom-call | tf_op jit(solution)/shard_map/take_rows/pallas_call | solution.py:47
  132.7 2.3 collective-permute-done.q_up
  136.3 54.9 %all-to-all-done.2 = bf16[4,3,512,256]{3,2,1,0:T(8,128)(2,1)} async-done(((bf16[4,3,512,256]{3,2,1,0:T(8,128)(2,1)}), bf16[4,3,512,256]{3,2,1,0:T(8,128)(2,1)}, u32[]{:S(2)}, u32[]{:S(2)}) %all-to-all-start.2) | async-done | bytes 3145760 | tf_op jit(solution)/shard_map/all_to_all | solution.py:246
  191.2 4.7 %all-to-all-start = ((bf16[4,3,512,256]{3,2,1,0:T(8,128)(2,1)}), bf16[4,3,512,256]{3,2,1,0:T(8,128)(2,1)}, u32[]{:S(2)}, u32[]{:S(2)}) async-start(bf16[4,3,512,256]{3,2,1,0:T(8,128)(2,1)} %bitcast.39), calls=%async_computation | async-start | bytes 6291456 | tf_op jit(solution)/shard_map/all_to_all | solution.py:246
  197.8 2.7 collective-permute-start.5
  202.0 3.6 collective-permute-start.7
  205.6 34.8 %collective-permute-done.3.q_down = bf16[3,1024,128]{2,1,0:T(8,128)(2,1)S(1)} collective-permute-done((bf16[3,1024,128]{2,1,0:T(8,128)(2,1)}, bf16[3,1024,128]{2,1,0:T(8,128)(2,1)S(1)}, u32[]{:S(2)}, u32[]{:S(2)}) %collective-permute-start.3) | collective-permute-done | bytes 786464 | tf_op jit(solution)/shard_map/ppermute | solution.py:242
  240.5 4.6 %collective-permute-done.6.up4 = bf16[2,512,256]{2,1,0:T(8,128)(2,1)S(1)} collective-permute-done((bf16[2,512,256]{2,1,0:T(8,128)(2,1)S(1)}, bf16[2,512,256]{2,1,0:T(8,128)(2,1)S(1)}, u32[]{:S(2)}, u32[]{:S(2)}) %collective-permute-start.6) | collective-permute-done | bytes 524320 | tf_op jit(solution)/shard_map/ppermute | solution.py:242
  246.4 23.2 %far.1 = (bf16[3,128,1024]{2,1,0:T(8,128)(2,1)S(1)}, f32[3,1,1024]{2,1,0:T(1,128)S(1)}, bf16[3,128,1024]{2,1,0:T(8,128)(2,1)S(1)}, f32[3,1,1024]{2,1,0:T(1,128)S(1)}) custom-call(s32[20]{0:T(128)S(1)} %bitcast.35, bf16[3,1024,128]{2,1,0:T(8,128)(2,1)S(1)} %collective-permute-done.2.q_up, bf16[3,1024,128]{2,1,0:T(8,128)(2,1)} %copy-done.8, ...), custom_call_target="tpu_custom_call" | custom-call | flops 8053063680 | bytes 3932160 | tf_op jit(solution)/shard_map/far/pallas_call | solution.py:153
  269.7 10.2 %collective-permute-start.10 = (bf16[3,128,1024]{2,1,0:T(8,128)(2,1)S(1)}, bf16[3,128,1024]{2,1,0:T(8,128)(2,1)}, u32[]{:S(2)}, u32[]{:S(2)}) collective-permute-start(bf16[3,128,1024]{2,1,0:T(8,128)(2,1)S(1)} %get-tuple-element.27), channel_id=1, source_target_pairs={{0,56},{8,0},{16,8},{24,16},{32,24},{40,32},{48,40},{56,48},{1,57}... | collective-permute-start | bytes 2359304 | tf_op jit(solution)/shard_map/ppermute | solution.py:242
  283.5 17.5 %near.1 = (bf16[3,128,1024]{2,1,0:T(8,128)(2,1)S(1)}, f32[3,1,1024]{2,1,0:T(1,128)S(1)}, bf16[3,128,1024]{2,1,0:T(8,128)(2,1)S(1)}, f32[3,1,1024]{2,1,0:T(1,128)...) custom-call(s32[12]{0:T(128)S(1)} %slice.27.tags, bf16[3,1024,128]{2,1,0:T(8,128)(2,1)S(1)} %bitcast.33, ...), custom_call_target="tpu_custom_call" | custom-call | flops 5368709120 | bytes 2621440 | tf_op jit(solution)/shard_map/near/pallas_call | solution.py:153
  304.2 3.1 collective-permute-start.14
  307.4 2.7 collective-permute-start.15
  310.0 7.5 %collective-permute-done.13.l_b = f32[3,1,1024]{2,1,0:T(1,128)S(1)} collective-permute-done((f32[3,1,1024]{2,1,0:T(1,128)S(1)}, f32[3,1,1024]{2,1,0:T(1,128)S(1)}, u32[]{:S(2)}, u32[]{:S(2)}) %collective-permute-start.13) | collective-permute-done | bytes 12320 | tf_op jit(solution)/shard_map/ppermute | solution.py:242
  318.3 13.5 %project.1 = bf16[384,4096]{1,0:T(8,128)(2,1)} custom-call(bf16[384,1024]{1,0:T(8,128)(2,1)S(1)} %last.1.context_ref, bf16[32,1024,128]{2,1,0:T(8,128)(2,1)} %all-gather.7.cloned.1.call-done.weight_ref), custom_call_target="tpu_custom_call" | custom-call | tf_op jit(solution)/shard_map/project/pallas_call | solution.py:226
  331.8 43.0 %reduce-scatter.2.cloned.1.call-done = bf16[384,512]{1,0:T(8,128)(2,1)} async-done(((bf16[384,4096]{1,0:T(8,128)(2,1)}), bf16[384,512]{1,0:T(8,128)(2,1)}) %reduce-scatter.2.cloned.1.call-update) | async-done | bytes 393232 | tf_op jit(solution)/shard_map/reduce_scatter | solution.py:344
  (78 shorter events, 21.5 us)
Async XLA Ops:
  6.5 43.8 %all-gather.5.cloned.1.call-start = ((), (), s32[]{:S(2)}) async-start(), calls=%async_computation.5 | async-start | bytes 2359296 | tf_op jit(solution)/shard_map/all_gather | solution.py:256
  7.3 311.0 %all-gather.7.cloned.1.call-start = ((), (), s32[]{:S(2)}) async-start(), calls=%async_computation.6 | async-start | bytes 10485760 | tf_op jit(solution)/shard_map/all_gather | solution.py:257
  64.4 51.0 %all-to-all-start.1 = ((bf16[4,2,512,256]{3,2,1,0:T(8,128)(2,1)}), bf16[4,2,512,256]{3,2,1,0:T(8,128)(2,1)S(1)}, u32[]{:S(2)}, u32[]{:S(2)}) async-start(bf16[4,2,512,256]{3,2,1,0:T(8,128)(2,1)} %bitcast.41), calls=%async_computation.1 | async-start | bytes 4194304 | tf_op jit(solution)/shard_map/all_to_all | solution.py:246
  115.4 6.0 %copy-start.2 = (bf16[384,1024]{1,0:T(8,128)(2,1)S(1)}, bf16[384,1024]{1,0:T(8,128)(2,1)}, u32[]{:S(2)}) copy-start(bf16[384,1024]{1,0:T(8,128)(2,1)} %param.11) | copy-start | bytes 2359300
  116.8 74.4 %all-to-all-start.2 = ((bf16[4,3,512,256]{3,2,1,0:T(8,128)(2,1)}), bf16[4,3,512,256]{3,2,1,0:T(8,128)(2,1)}, u32[]{:S(2)}, u32[]{:S(2)}) async-start(bf16[4,3,512,256]{3,2,1,0:T(8,128)(2,1)} %bitcast.40), calls=%async_computation.2 | async-start | bytes 6291456 | tf_op jit(solution)/shard_map/all_to_all | solution.py:246
  121.8 13.2 %collective-permute-start = (bf16[3,1024,128]{2,1,0:T(8,128)(2,1)S(1)}, bf16[3,1024,128]{2,1,0:T(8,128)(2,1)}, u32[]{:S(2)}, u32[]{:S(2)}) collective-permute-start(bf16[3,1024,128]{2,1,0:T(8,128)(2,1)S(1)} %bitcast.31), channel_id=1, source_target_pairs={{0,56},{8,0},{16,8},{24,16},{32,24},{40,32},{48,40},{56,48},{1,57}... | collective-permute-start | bytes 2359304 | tf_op jit(solution)/shard_map/ppermute | solution.py:242
  121.9 78.6 %collective-permute-start.1 = (bf16[3,1024,128]{2,1,0:T(8,128)(2,1)S(1)}, bf16[3,1024,128]{2,1,0:T(8,128)(2,1)}, u32[]{:S(2)}, u32[]{:S(2)}) collective-permute-start(bf16[3,1024,128]{2,1,0:T(8,128)(2,1)S(1)} %bitcast.32), channel_id=1, source_target_pairs={{0,8},{8,16},{16,24},{24,32},{32,40},{40,48},{48,56},{56,0},{1,9},... | collective-permute-start | bytes 2359304 | tf_op jit(solution)/shard_map/ppermute | solution.py:242
  135.1 66.9 %collective-permute-start.2 = (bf16[3,1024,128]{2,1,0:T(8,128)(2,1)}, bf16[3,1024,128]{2,1,0:T(8,128)(2,1)S(1)}, u32[]{:S(2)}, u32[]{:S(2)}) collective-permute-start(bf16[3,1024,128]{2,1,0:T(8,128)(2,1)} %collective-permute-done.q_up), channel_id=1, source_target_pairs={{0,56},{8,0},{16,8},{24,16},{32,24},{40,32},{48,40},{56,48},{1,57}... | collective-permute-start | bytes 2359304 | tf_op jit(solution)/shard_map/ppermute | solution.py:242
  191.2 92.3 %all-to-all-start = ((bf16[4,3,512,256]{3,2,1,0:T(8,128)(2,1)}), bf16[4,3,512,256]{3,2,1,0:T(8,128)(2,1)}, u32[]{:S(2)}, u32[]{:S(2)}) async-start(bf16[4,3,512,256]{3,2,1,0:T(8,128)(2,1)} %bitcast.39), calls=%async_computation | async-start | bytes 6291456 | tf_op jit(solution)/shard_map/all_to_all | solution.py:246
  196.0 178.9 %reduce-scatter.2.cloned.1.call-start = ((), (), s32[]{:S(2)}) async-start(), calls=%async_computation.4 | async-start | bytes 3538944 | tf_op jit(solution)/shard_map/reduce_scatter | solution.py:344
  197.7 47.4 %collective-permute-start.4 = (bf16[4,512,256]{2,1,0:T(8,128)(2,1)S(1)}, bf16[4,512,256]{2,1,0:T(8,128)(2,1)S(1)}, u32[]{:S(2)}, u32[]{:S(2)}) collective-permute-start(bf16[4,512,256]{2,1,0:T(8,128)(2,1)S(1)} %get-tuple-element.36), channel_id=1, source_target_pairs={{0,8},{8,16},{16,24},{24,32},{32,40},{40,48},{48,56},{56,0},{1,9},... | collective-permute-start | bytes 3145736 | tf_op jit(solution)/shard_map/ppermute | solution.py:242
  197.8 47.3 %collective-permute-start.5 = (bf16[4,512,256]{2,1,0:T(8,128)(2,1)S(1)}, bf16[4,512,256]{2,1,0:T(8,128)(2,1)S(1)}, u32[]{:S(2)}, u32[]{:S(2)}) collective-permute-start(bf16[4,512,256]{2,1,0:T(8,128)(2,1)S(1)} %get-tuple-element.35), channel_id=1, source_target_pairs={{0,56},{8,0},{16,8},{24,16},{32,24},{40,32},{48,40},{56,48},{1,57}... | collective-permute-start | bytes 3145736 | tf_op jit(solution)/shard_map/ppermute | solution.py:242
  200.5 40.0 %collective-permute-start.3 = (bf16[3,1024,128]{2,1,0:T(8,128)(2,1)}, bf16[3,1024,128]{2,1,0:T(8,128)(2,1)S(1)}, u32[]{:S(2)}, u32[]{:S(2)}) collective-permute-start(bf16[3,1024,128]{2,1,0:T(8,128)(2,1)} %collective-permute-done.1.q_down), channel_id=1, source_target_pairs={{0,8},{8,16},{16,24},{24,32},{32,40},{40,48},{48,56},{56,0},{1,9},... | collective-permute-start | bytes 2359304 | tf_op jit(solution)/shard_map/ppermute | solution.py:242
  201.9 43.3 %collective-permute-start.6 = (bf16[2,512,256]{2,1,0:T(8,128)(2,1)S(1)}, bf16[2,512,256]{2,1,0:T(8,128)(2,1)S(1)}, u32[]{:S(2)}, u32[]{:S(2)}) collective-permute-start(bf16[2,512,256]{2,1,0:T(8,128)(2,1)S(1)} %get-tuple-element.34), channel_id=1, source_target_pairs={{0,16},{8,24},{16,32},{24,40},{32,48},{40,56},{48,0},{56,8},{1,17}... | collective-permute-start | bytes 1572872 | tf_op jit(solution)/shard_map/ppermute | solution.py:242
  202.0 43.2 %collective-permute-start.7 = (bf16[2,512,256]{2,1,0:T(8,128)(2,1)S(1)}, bf16[2,512,256]{2,1,0:T(8,128)(2,1)S(1)}, u32[]{:S(2)}, u32[]{:S(2)}) collective-permute-start(bf16[2,512,256]{2,1,0:T(8,128)(2,1)S(1)} %get-tuple-element.33), channel_id=1, source_target_pairs={{0,48},{8,56},{16,0},{24,8},{32,16},{40,24},{48,32},{56,40},{1,49}... | collective-permute-start | bytes 1572872 | tf_op jit(solution)/shard_map/ppermute | solution.py:242
  246.4 37.0 %copy-start = (bf16[384,1,256]{2,0,1:T(8,128)(2,1)S(1)}, bf16[384,1,256]{2,0,1:T(8,128)(2,1)}, u32[]{:S(2)}) copy-start(bf16[384,1,256]{2,0,1:T(8,128)(2,1)} %param.12) | copy-start | bytes 589828
  269.7 31.3 %collective-permute-start.10 = (bf16[3,128,1024]{2,1,0:T(8,128)(2,1)S(1)}, bf16[3,128,1024]{2,1,0:T(8,128)(2,1)}, u32[]{:S(2)}, u32[]{:S(2)}) collective-permute-start(bf16[3,128,1024]{2,1,0:T(8,128)(2,1)S(1)} %get-tuple-element.27), channel_id=1, source_target_pairs={{0,56},{8,0},{16,8},{24,16},{32,24},{40,32},{48,40},{56,48},{1,57}... | collective-permute-start | bytes 2359304 | tf_op jit(solution)/shard_map/ppermute | solution.py:242
  279.9 21.1 %collective-permute-start.8 = (bf16[3,128,1024]{2,1,0:T(8,128)(2,1)S(1)}, bf16[3,128,1024]{2,1,0:T(8,128)(2,1)S(1)}, u32[]{:S(2)}, u32[]{:S(2)}) collective-permute-start(bf16[3,128,1024]{2,1,0:T(8,128)(2,1)S(1)} %get-tuple-element.23), channel_id=1, source_target_pairs={{0,8},{8,16},{16,24},{24,32},{32,40},{40,48},{48,56},{56,0},{1,9},... | collective-permute-start | bytes 2359304 | tf_op jit(solution)/shard_map/ppermute | solution.py:242
  281.8 19.1 %collective-permute-start.11 = (f32[3,1,1024]{2,1,0:T(1,128)S(1)}, f32[3,1,1024]{2,1,0:T(1,128)S(1)}, u32[]{:S(2)}, u32[]{:S(2)}) collective-permute-start(f32[3,1,1024]{2,1,0:T(1,128)S(1)} %get-tuple-element.28), channel_id=1, source_target_pairs={{0,56},{8,0},{16,8},{24,16},{32,24},{40,32},{48,40},{56,48},{1,57}... | collective-permute-start | bytes 36872 | tf_op jit(solution)/shard_map/ppermute | solution.py:242
  282.7 18.3 %collective-permute-start.9 = (f32[3,1,1024]{2,1,0:T(1,128)S(1)}, f32[3,1,1024]{2,1,0:T(1,128)S(1)}, u32[]{:S(2)}, u32[]{:S(2)}) collective-permute-start(f32[3,1,1024]{2,1,0:T(1,128)S(1)} %get-tuple-element.24), channel_id=1, source_target_pairs={{0,8},{8,16},{16,24},{24,32},{32,40},{40,48},{48,56},{56,0},{1,9},... | collective-permute-start | bytes 36872 | tf_op jit(solution)/shard_map/ppermute | solution.py:242
  302.9 14.7 %collective-permute-start.12 = (bf16[3,128,1024]{2,1,0:T(8,128)(2,1)S(1)}, bf16[3,128,1024]{2,1,0:T(8,128)(2,1)S(1)}, u32[]{:S(2)}, u32[]{:S(2)}) collective-permute-start(bf16[3,128,1024]{2,1,0:T(8,128)(2,1)S(1)} %get-tuple-element.29), channel_id=1, source_target_pairs={{0,8},{8,16},{16,24},{24,32},{32,40},{40,48},{48,56},{56,0},{1,9},... | collective-permute-start | bytes 2359304 | tf_op jit(solution)/shard_map/ppermute | solution.py:242
  304.2 13.4 %collective-permute-start.14 = (bf16[3,128,1024]{2,1,0:T(8,128)(2,1)S(1)}, bf16[3,128,1024]{2,1,0:T(8,128)(2,1)S(1)}, u32[]{:S(2)}, u32[]{:S(2)}) collective-permute-start(bf16[3,128,1024]{2,1,0:T(8,128)(2,1)S(1)} %get-tuple-element.31), channel_id=1, source_target_pairs={{0,56},{8,0},{16,8},{24,16},{32,24},{40,32},{48,40},{56,48},{1,57}... | collective-permute-start | bytes 2359304 | tf_op jit(solution)/shard_map/ppermute | solution.py:242
  307.4 10.2 %collective-permute-start.13 = (f32[3,1,1024]{2,1,0:T(1,128)S(1)}, f32[3,1,1024]{2,1,0:T(1,128)S(1)}, u32[]{:S(2)}, u32[]{:S(2)}) collective-permute-start(f32[3,1,1024]{2,1,0:T(1,128)S(1)} %get-tuple-element.30), channel_id=1, source_target_pairs={{0,8},{8,16},{16,24},{24,32},{32,40},{40,48},{48,56},{56,0},{1,9},... | collective-permute-start | bytes 36872 | tf_op jit(solution)/shard_map/ppermute | solution.py:242
  307.4 10.2 %collective-permute-start.15 = (f32[3,1,1024]{2,1,0:T(1,128)S(1)}, f32[3,1,1024]{2,1,0:T(1,128)S(1)}, u32[]{:S(2)}, u32[]{:S(2)}) collective-permute-start(f32[3,1,1024]{2,1,0:T(1,128)S(1)} %get-tuple-element.32), channel_id=1, source_target_pairs={{0,56},{8,0},{16,8},{24,16},{32,24},{40,32},{48,40},{56,48},{1,57}... | collective-permute-start | bytes 36872 | tf_op jit(solution)/shard_map/ppermute | solution.py:242
  (7 other events, 21.9 us)
Sparse Core Ops, SparseCore 0:
  9.1 41.1 all-gather.4
  52.2 143.2 all-gather.6
  331.9 42.8 reduce-scatter.1

commit v2 on v1

--- a/solution.py
+++ b/solution.py
@@ -136,9 +136,9 @@
         for part in range(GROUP):
             cols = pl.ds(part * LQ, LQ)
             absorb(keys, values_t, q_own, (j, j), cols, *state, causal=True)
-    absorb_all(tags, 0, here, 4, lambda i: (i, 0), q_own, 0, *state)
-    absorb_all(tags, 4, here, 4, lambda i: (i, 1), q_up, n, *state)
-    absorb_all(tags, 8, here, 4, lambda i: (i, 2), q_down, 2 * n, *state)
+    absorb_all(tags, 0, here, 4, lambda i: (i, 2), q_own, 0, *state)
+    absorb_all(tags, 4, here, 4, lambda i: (i, 3), q_up, n, *state)
+    absorb_all(tags, 8, here, 4, lambda i: (i, 4), q_down, 2 * n, *state)
     finish(o_own, l_own, 0, *state)
     finish(o_up, l_up, n, *state)
     finish(o_down, l_down, 2 * n, *state)
@@ -214,29 +214,6 @@
     )(*arrays)
 
 
-def project_kernel(context_ref, weight_ref, out_ref):
-    weight = jnp.concatenate([weight_ref[0], weight_ref[1]], axis=1)
-    out_ref[...] = jnp.dot(
-        context_ref[...], weight, preferred_element_type=jnp.float32
-    ).astype(jnp.bfloat16)
-
-
-def project(context, weight):
-    blocks, rows, cols = weight.shape
-    return pl.pallas_call(
-        project_kernel,
-        out_shape=jax.ShapeDtypeStruct((context.shape[0], blocks * cols), jnp.bfloat16),
-        grid=(blocks // 2,),
-        in_specs=[
-            pl.BlockSpec(context.shape, lambda i: (0, 0)),
-            pl.BlockSpec((2, rows, cols), lambda i: (i, 0, 0)),
-        ],
-        out_specs=pl.BlockSpec((context.shape[0], 2 * cols), lambda i: (0, i)),
-        compiler_params=pltpu.CompilerParams(vmem_limit_bytes=VMEM_LIMIT),
-        name="project",
-    )(context, weight)
-
-
 def along(array, axis, size, shift):
     pairs = [(i, (i + shift) % size) for i in range(size)]
     return jax.tree.map(lambda a: lax.ppermute(a, axis, pairs), array)
@@ -253,16 +230,12 @@
     cache = passage_cache.reshape(pass_dev, PLEN, 2 * HD)
     own = own_kv.reshape(per_device * LQ, 2 * HD)
 
-    weight = lax.all_gather(out_weight, "z", axis=0)
-    weight = lax.all_gather(weight, "x", axis=0)
-    weight = weight.reshape(NX * NZ, out_weight.shape[0], out_weight.shape[1])
+    weight = lax.all_gather(out_weight, ("x", "z"), axis=1, tiled=True)
 
     q_own = queries.reshape(per_device, LQ, GROUP, HD).transpose(0, 2, 1, 3)
     q_own = q_own.reshape(per_device, ROWS, HD)
     q_up = along(q_own, "z", NZ, -1)
     q_down = along(q_own, "z", NZ, 1)
-    q_up2 = along(q_up, "z", NZ, -1)
-    q_down2 = along(q_down, "z", NZ, 1)
 
     owners, local_rows = request_tables(lists, passage_slot, question_slot, per_device, pass_dev)
     mine = jnp.sum(jnp.where(owners == x * NZ + z, local_rows, 0), axis=1).reshape(NX, NZ)
@@ -275,11 +248,13 @@
 
     def items_for(first, count):
         picked = rows[:, first : first + count].reshape(NX * count)
-        return over_x(take_rows(cache, picked).reshape(NX, count, PLEN, 2 * HD))
-
-    moved = items_for(0, 3)
-    far_here = items_for(3, 2)
-    near_here = items_for(5, 3)
+        return take_rows(cache, picked).reshape(NX, count, PLEN, 2 * HD)
+
+    moved = over_x(items_for(0, 3))
+    here, moved, q_up, q_down = lax.optimization_barrier((items_for(3, 5), moved, q_up, q_down))
+    here = over_x(here)
+    q_up2 = along(q_up, "z", NZ, -1)
+    q_down2 = along(q_down, "z", NZ, 1)
     up3 = along(moved[:, 0], "z", NZ, 1)
     down3 = along(moved[:, 1], "z", NZ, -1)
     up4 = along(moved[0:2, 2], "z", NZ, 2)
@@ -312,7 +287,7 @@
         far_kernel,
         "far",
         tags[:20],
-        [q_up2, q_down2, far_here, up3, down3, up4, down4],
+        [q_up2, q_down2, here, up3, down3, up4, down4],
         per_device,
         2,
         15,
@@ -321,7 +296,7 @@
         near_kernel,
         "near",
         tags[20:],
-        [q_own, q_up, q_down, near_here, own],
+        [q_own, q_up, q_down, here, own],
         per_device,
         3,
         10,
@@ -340,7 +315,8 @@
         *home_up,
         *home_down,
     )
-    partial_value = project(context, weight)
+    partial_value = jnp.dot(context, weight, preferred_element_type=jnp.float32)
+    partial_value = partial_value.astype(jnp.bfloat16)
     return lax.psum_scatter(partial_value, ("y", "core"), scatter_dimension=1, tiled=True)
 
 

time: 384 us -> 308 us (0.80)
  waiting for transfers between devices: 229 us -> 169 us
  Pallas kernels: 80.5 us -> 59 us
  matrix products: 0 us -> 8.17 us
    all_to_all x3 -> x2, waiting for transfers between devices: 92.7 us -> 7.49 us  [over_x(): return lax.all_to_all(items, 'x', split_axis=0, concat_axis=0, tiled=True)]
    ppermute x16, waiting for transfers between devices: 49.4 us -> 121 us  [along(): return jax.tree.map(lambda a: lax.ppermute(a, axis, pairs), array)]
    all_gather x2 -> x1, waiting for transfers between devices: 43.1 us -> 0.02 us  [body(): weight = lax.all_gather(out_weight, ('x', 'z'), axis=1, tiled=True)]
    pallas_call x1 -> x0, Pallas kernels: 13.5 us -> none  [project(): pl.pallas_call(project_kernel, out_shape=jax.ShapeDtypeStruct((context.sh...]
    dot_general x0 -> x1, matrix products: none -> 8.17 us  [body(): partial_value = jnp.dot(context, weight, preferred_element_type=jnp.float32)]
    pallas_call x2, Pallas kernels: 40.7 us -> 35.2 us  [attention(): pl.pallas_call(kernel, out_shape=tuple(out), in_specs=[pl.BlockSpec(memor...]
    all_to_all x3 -> x2, starting transfers between devices: 13.3 us -> 10.6 us  [over_x(): return lax.all_to_all(items, 'x', split_axis=0, concat_axis=0, tiled=True)]
    pallas_call x3 -> x2, Pallas kernels: 23.7 us -> 21.3 us  [take_rows(): pl.pallas_call(row_copy, out_shape=jax.ShapeDtypeStruct((n,) + cache.shap...]
  transfers between devices with their start and end apart: 22 -> 20, of which waited for: 8 -> 8; matrix products, arithmetic and copies ran while one was open for 3% -> 4% of each run, Pallas kernels for 18% -> 19%
where the time goes in v2:
time: 308 us; the launch traced here: 305 us
  waiting for transfers between devices  169 us (55%)
  Pallas kernels  59 us (19%)
  starting transfers between devices  41.4 us (13%)
  between operations  13.6 us (4%)
  matrix products  8.17 us (3%)
  local copies, waits for them, and re-layouts  7.38 us (2%)
  other arithmetic  6.87 us (2%)
    ppermute x16, waiting for transfers between devices, along(): return jax.tree.map(lambda a: lax.ppermute(a, axis, pairs), array)  121 us
    reduce_scatter x1, waiting for transfers between devices, body(): lax.psum_scatter(partial_value, ('y', 'core'), scatter_dimension=1, tiled...  39.7 us
    pallas_call x2, Pallas kernels, attention(): pl.pallas_call(kernel, out_shape=tuple(out), in_specs=[pl.BlockSpec(memor...  35.2 us
    ppermute x16, starting transfers between devices, along(): return jax.tree.map(lambda a: lax.ppermute(a, axis, pairs), array)  30.8 us
    pallas_call x2, Pallas kernels, take_rows(): pl.pallas_call(row_copy, out_shape=jax.ShapeDtypeStruct((n,) + cache.shap...  21.3 us
    all_to_all x2, starting transfers between devices, over_x(): return lax.all_to_all(items, 'x', split_axis=0, concat_axis=0, tiled=True)  10.6 us
    dot_general x1, matrix products, body(): partial_value = jnp.dot(context, weight, preferred_element_type=jnp.float32)  8.17 us
    all_to_all x2, waiting for transfers between devices, over_x(): return lax.all_to_all(items, 'x', split_axis=0, concat_axis=0, tiled=True)  7.49 us
  transfers between devices with their start and end apart: 20, of which 8 were waited for; matrix products, arithmetic and copies ran while one was open for 4% of the time, Pallas kernels for 19%

profile of v2, /device:TPU:1, one launch (start us, length us, event | category | flops | bytes accessed | tf_op | source)
XLA Modules:
  0.0 305.2 jit_solution(1072799400442566524)
XLA Ops:
  7.9 2.4 multiply_reduce_fusion
  10.3 2.5 select_reduce_fusion
  14.8 8.1 %take_rows.3 = bf16[12,512,256]{2,1,0:T(8,128)(2,1)} custom-call(s32[12]{0:T(128)} %reshape.121.rows_ref, bf16[16,512,256]{2,1,0:T(8,128)(2,1)} %bitcast.30), custom_call_target="tpu_custom_call" | custom-call | tf_op jit(solution)/shard_map/take_rows/pallas_call | solution.py:47
  22.9 5.5 %all-to-all-start = ((bf16[4,3,512,256]{3,2,1,0:T(8,128)(2,1)}), bf16[4,3,512,256]{3,2,1,0:T(8,128)(2,1)}, u32[]{:S(2)}, u32[]{:S(2)}) async-start(bf16[4,3,512,256]{3,2,1,0:T(8,128)(2,1)} %bitcast.32), calls=%async_computation | async-start | bytes 6291456 | tf_op jit(solution)/shard_map/all_to_all | solution.py:223
  28.8 6.2 %collective-permute-start = (bf16[3,1024,128]{2,1,0:T(8,128)(2,1)S(1)}, bf16[3,1024,128]{2,1,0:T(8,128)(2,1)S(1)}, u32[]{:S(2)}, u32[]{:S(2)}) collective-permute-start(bf16[3,1024,128]{2,1,0:T(8,128)(2,1)S(1)} %bitcast.24), channel_id=1, source_target_pairs={{0,56},{8,0},{16,8},{24,16},{32,24},{40,32},{48,40},{56,48},{1,57}... | collective-permute-start | bytes 2359304 | tf_op jit(solution)/shard_map/ppermute | solution.py:219
  35.7 13.2 %take_rows.2 = bf16[20,512,256]{2,1,0:T(8,128)(2,1)} custom-call(s32[20]{0:T(128)} %reshape.118.rows_ref, bf16[16,512,256]{2,1,0:T(8,128)(2,1)} %bitcast.31), custom_call_target="tpu_custom_call" | custom-call | tf_op jit(solution)/shard_map/take_rows/pallas_call | solution.py:47
  48.9 7.1 %collective-permute-done.q_up = bf16[3,1024,128]{2,1,0:T(8,128)(2,1)S(1)} collective-permute-done((bf16[3,1024,128]{2,1,0:T(8,128)(2,1)S(1)}, bf16[3,1024,128]{2,1,0:T(8,128)(2,1)S(1)}, u32[]{:S(2)}, u32[]{:S(2)}) %collective-permute-start) | collective-permute-done | bytes 786464 | tf_op jit(solution)/shard_map/ppermute | solution.py:219
  56.0 5.2 %collective-permute-done.1.q_down = bf16[3,1024,128]{2,1,0:T(8,128)(2,1)S(1)} collective-permute-done((bf16[3,1024,128]{2,1,0:T(8,128)(2,1)S(1)}, bf16[3,1024,128]{2,1,0:T(8,128)(2,1)S(1)}, u32[]{:S(2)}, u32[]{:S(2)}) %collective-permute-start.1) | collective-permute-done | bytes 786464 | tf_op jit(solution)/shard_map/ppermute | solution.py:219
  61.2 7.5 %all-to-all-done = bf16[4,3,512,256]{3,2,1,0:T(8,128)(2,1)} async-done(((bf16[4,3,512,256]{3,2,1,0:T(8,128)(2,1)}), bf16[4,3,512,256]{3,2,1,0:T(8,128)(2,1)}, u32[]{:S(2)}, u32[]{:S(2)}) %all-to-all-start) | async-done | bytes 3145760 | tf_op jit(solution)/shard_map/all_to_all | solution.py:223
  68.7 5.1 %all-to-all-start.1 = ((bf16[4,5,512,256]{3,2,1,0:T(8,128)(2,1)}), bf16[4,5,512,256]{3,2,1,0:T(8,128)(2,1)}, u32[]{:S(2)}, u32[]{:S(2)}) async-start(bf16[4,5,512,256]{3,2,1,0:T(8,128)(2,1)} %bitcast.29), calls=%async_computation.1 | async-start | bytes 10485760 | tf_op jit(solution)/shard_map/all_to_all | solution.py:223
  74.0 3.2 %slice_bitcast_fusion = (bf16[4,512,256]{2,1,0:T(8,128)(2,1)}, bf16[4,512,256]{2,1,0:T(8,128)(2,1)}) fusion(bf16[4,3,512,256]{3,2,1,0:T(8,128)(2,1)} %all-to-all-done), kind=kLoop, calls=%fused_computation.3 | loop fusion | bytes 4194304 | tf_op jit(solution)/shard_map/squeeze | solution.py:259
  77.2 2.4 collective-permute-start.4
  85.4 66.0 %collective-permute-done.6.up4 = bf16[2,512,256]{2,1,0:T(8,128)(2,1)S(1)} collective-permute-done((bf16[2,512,256]{2,1,0:T(8,128)(2,1)S(1)}, bf16[2,512,256]{2,1,0:T(8,128)(2,1)S(1)}, u32[]{:S(2)}, u32[]{:S(2)}) %collective-permute-start.6) | collective-permute-done | bytes 524320 | tf_op jit(solution)/shard_map/ppermute | solution.py:219
  151.4 2.0 collective-permute-start.7
  153.6 26.1 %collective-permute-done.7.down4 = bf16[2,512,256]{2,1,0:T(8,128)(2,1)S(1)} collective-permute-done((bf16[2,512,256]{2,1,0:T(8,128)(2,1)S(1)}, bf16[2,512,256]{2,1,0:T(8,128)(2,1)S(1)}, u32[]{:S(2)}, u32[]{:S(2)}) %collective-permute-start.7) | collective-permute-done | bytes 524320 | tf_op jit(solution)/shard_map/ppermute | solution.py:219
  179.7 18.2 %far.1 = (bf16[3,128,1024]{2,1,0:T(8,128)(2,1)S(1)}, f32[3,1,1024]{2,1,0:T(1,128)S(1)}, bf16[3,128,1024]{2,1,0:T(8,128)(2,1)S(1)}, f32[3,1,1024]{2,1,0:T(1,128)S(1)}) custom-call(s32[20]{0:T(128)S(1)} %bitcast.28, bf16[3,1024,128]{2,1,0:T(8,128)(2,1)S(1)} %collective-permute-done.2.q_up, bf16[3,1024,128]{2,1,0:T(8,128)(2,1)} %collective-permute-done.3.q_down, ...), custom_call_target="tpu_custom_call" | custom-call | flops 8053063680 | bytes 3932160 | tf_op jit(solution)/shard_map/far/pallas_call | solution.py:153
  200.7 3.7 %collective-permute-start.9 = (f32[3,1,1024]{2,1,0:T(1,128)S(1)}, f32[3,1,1024]{2,1,0:T(1,128)S(1)}, u32[]{:S(2)}, u32[]{:S(2)}) collective-permute-start(f32[3,1,1024]{2,1,0:T(1,128)S(1)} %get-tuple-element.32), channel_id=1, source_target_pairs={{0,8},{8,16},{16,24},{24,32},{32,40},{40,48},{48,56},{56,0},{1,9},... | collective-permute-start | bytes 36872 | tf_op jit(solution)/shard_map/ppermute | solution.py:219
  204.4 16.9 %near.1 = (bf16[3,128,1024]{2,1,0:T(8,128)(2,1)S(1)}, f32[3,1,1024]{2,1,0:T(1,128)S(1)}, bf16[3,128,1024]{2,1,0:T(8,128)(2,1)S(1)}, f32[3,1,1024]{2,1,0:T(1,128)...) custom-call(s32[12]{0:T(128)S(1)} %slice.24.tags, bf16[3,1024,128]{2,1,0:T(8,128)(2,1)S(1)} %bitcast.26, ...), custom_call_target="tpu_custom_call" | custom-call | flops 5368709120 | bytes 2621440 | tf_op jit(solution)/shard_map/near/pallas_call | solution.py:153
  224.3 5.1 %collective-permute-start.12 = (bf16[3,128,1024]{2,1,0:T(8,128)(2,1)S(1)}, bf16[3,128,1024]{2,1,0:T(8,128)(2,1)S(1)}, u32[]{:S(2)}, u32[]{:S(2)}) collective-permute-start(bf16[3,128,1024]{2,1,0:T(8,128)(2,1)S(1)} %get-tuple-element.37), channel_id=1, source_target_pairs={{0,8},{8,16},{16,24},{24,32},{32,40},{40,48},{48,56},{56,0},{1,9},... | collective-permute-start | bytes 2359304 | tf_op jit(solution)/shard_map/ppermute | solution.py:219
  229.4 4.0 %collective-permute-start.13 = (f32[3,1,1024]{2,1,0:T(1,128)S(1)}, f32[3,1,1024]{2,1,0:T(1,128)S(1)}, u32[]{:S(2)}, u32[]{:S(2)}) collective-permute-start(f32[3,1,1024]{2,1,0:T(1,128)S(1)} %get-tuple-element.38), channel_id=1, source_target_pairs={{0,8},{8,16},{16,24},{24,32},{32,40},{40,48},{48,56},{56,0},{1,9},... | collective-permute-start | bytes 36872 | tf_op jit(solution)/shard_map/ppermute | solution.py:219
  233.4 10.0 %collective-permute-done.13.l_b = f32[3,1,1024]{2,1,0:T(1,128)S(1)} collective-permute-done((f32[3,1,1024]{2,1,0:T(1,128)S(1)}, f32[3,1,1024]{2,1,0:T(1,128)S(1)}, u32[]{:S(2)}, u32[]{:S(2)}) %collective-permute-start.13) | collective-permute-done | bytes 12320 | tf_op jit(solution)/shard_map/ppermute | solution.py:219
  243.4 6.3 %collective-permute-done.15.l_c = f32[3,1,1024]{2,1,0:T(1,128)S(1)} collective-permute-done((f32[3,1,1024]{2,1,0:T(1,128)S(1)}, f32[3,1,1024]{2,1,0:T(1,128)S(1)}, u32[]{:S(2)}, u32[]{:S(2)}) %collective-permute-start.15) | collective-permute-done | bytes 12320 | tf_op jit(solution)/shard_map/ppermute | solution.py:219
  250.4 8.2 %convolution_convert_fusion = bf16[384,4096]{1,0:T(8,128)(2,1)} fusion(bf16[384,1024]{1,0:T(8,128)(2,1)S(1)} %last.1, bf16[1024,4096]{1,0:T(8,128)(2,1)} %all-gather.2.cloned.1.call-done), kind=kOutput, calls=%fused_computation | convolution fusion | flops 3222798336 | bytes 12320768 | tf_op jit(solution)/shard_map/dot_general | solution.py:318
  258.6 39.7 %reduce-scatter.2.cloned.1.call-done = bf16[384,512]{1,0:T(8,128)(2,1)} async-done(((bf16[384,4096]{1,0:T(8,128)(2,1)}), bf16[384,512]{1,0:T(8,128)(2,1)}) %reduce-scatter.2.cloned.1.call-update) | async-done | bytes 393232 | tf_op jit(solution)/shard_map/reduce_scatter | solution.py:320
  (68 shorter events, 16.8 us)
Async XLA Ops:
  6.5 243.8 %all-gather.2.cloned.1.call-start = ((), (), s32[]{:S(2)}) async-start(), calls=%async_computation.3 | async-start | bytes 8650752 | tf_op jit(solution)/shard_map/all_gather | solution.py:233
  22.9 45.8 %all-to-all-start = ((bf16[4,3,512,256]{3,2,1,0:T(8,128)(2,1)}), bf16[4,3,512,256]{3,2,1,0:T(8,128)(2,1)}, u32[]{:S(2)}, u32[]{:S(2)}) async-start(bf16[4,3,512,256]{3,2,1,0:T(8,128)(2,1)} %bitcast.32), calls=%async_computation | async-start | bytes 6291456 | tf_op jit(solution)/shard_map/all_to_all | solution.py:223
  28.8 27.2 %collective-permute-start = (bf16[3,1024,128]{2,1,0:T(8,128)(2,1)S(1)}, bf16[3,1024,128]{2,1,0:T(8,128)(2,1)S(1)}, u32[]{:S(2)}, u32[]{:S(2)}) collective-permute-start(bf16[3,1024,128]{2,1,0:T(8,128)(2,1)S(1)} %bitcast.24), channel_id=1, source_target_pairs={{0,56},{8,0},{16,8},{24,16},{32,24},{40,32},{48,40},{56,48},{1,57}... | collective-permute-start | bytes 2359304 | tf_op jit(solution)/shard_map/ppermute | solution.py:219
  35.0 26.2 %collective-permute-start.1 = (bf16[3,1024,128]{2,1,0:T(8,128)(2,1)S(1)}, bf16[3,1024,128]{2,1,0:T(8,128)(2,1)S(1)}, u32[]{:S(2)}, u32[]{:S(2)}) collective-permute-start(bf16[3,1024,128]{2,1,0:T(8,128)(2,1)S(1)} %bitcast.25), channel_id=1, source_target_pairs={{0,8},{8,16},{16,24},{24,32},{32,40},{40,48},{48,56},{56,0},{1,9},... | collective-permute-start | bytes 2359304 | tf_op jit(solution)/shard_map/ppermute | solution.py:219
  56.0 12.7 %copy-start.6 = (bf16[3,1024,128]{2,1,0:T(8,128)(2,1)}, bf16[3,1024,128]{2,1,0:T(8,128)(2,1)S(1)}, u32[]{:S(2)}) copy-start(bf16[3,1024,128]{2,1,0:T(8,128)(2,1)S(1)} %collective-permute-done.q_up) | copy-start | bytes 2359300
  68.7 111.0 %all-to-all-start.1 = ((bf16[4,5,512,256]{3,2,1,0:T(8,128)(2,1)}), bf16[4,5,512,256]{3,2,1,0:T(8,128)(2,1)}, u32[]{:S(2)}, u32[]{:S(2)}) async-start(bf16[4,5,512,256]{3,2,1,0:T(8,128)(2,1)} %bitcast.29), calls=%async_computation.1 | async-start | bytes 10485760 | tf_op jit(solution)/shard_map/all_to_all | solution.py:223
  73.8 224.5 %reduce-scatter.2.cloned.1.call-start = ((), (), s32[]{:S(2)}) async-start(), calls=%async_computation.4 | async-start | bytes 3538944 | tf_op jit(solution)/shard_map/reduce_scatter | solution.py:320
  74.0 11.4 %copy-start.3 = (s32[32]{0:T(128)S(1)}, s32[32]{0:T(128)}, u32[]{:S(2)}) copy-start(s32[32]{0:T(128)} %constant.97.clone) | copy-start | bytes 388
  74.0 11.4 %copy-start.4 = (s32[32]{0:T(128)S(1)}, s32[32]{0:T(128)}, u32[]{:S(2)}) copy-start(s32[32]{0:T(128)} %constant.102) | copy-start | bytes 388
  77.2 102.5 %collective-permute-start.4 = (bf16[4,512,256]{2,1,0:T(8,128)(2,1)}, bf16[4,512,256]{2,1,0:T(8,128)(2,1)}, u32[]{:S(2)}, u32[]{:S(2)}) collective-permute-start(bf16[4,512,256]{2,1,0:T(8,128)(2,1)} %get-tuple-element.44), channel_id=1, source_target_pairs={{0,8},{8,16},{16,24},{24,32},{32,40},{40,48},{48,56},{56,0},{1,9},... | collective-permute-start | bytes 3145736 | tf_op jit(solution)/shard_map/ppermute | solution.py:219
  79.6 100.1 %collective-permute-start.5 = (bf16[4,512,256]{2,1,0:T(8,128)(2,1)}, bf16[4,512,256]{2,1,0:T(8,128)(2,1)}, u32[]{:S(2)}, u32[]{:S(2)}) collective-permute-start(bf16[4,512,256]{2,1,0:T(8,128)(2,1)} %get-tuple-element.43), channel_id=1, source_target_pairs={{0,56},{8,0},{16,8},{24,16},{32,24},{40,32},{48,40},{56,48},{1,57}... | collective-permute-start | bytes 3145736 | tf_op jit(solution)/shard_map/ppermute | solution.py:219
  82.8 68.6 %collective-permute-start.6 = (bf16[2,512,256]{2,1,0:T(8,128)(2,1)S(1)}, bf16[2,512,256]{2,1,0:T(8,128)(2,1)S(1)}, u32[]{:S(2)}, u32[]{:S(2)}) collective-permute-start(bf16[2,512,256]{2,1,0:T(8,128)(2,1)S(1)} %get-tuple-element.42), channel_id=1, source_target_pairs={{0,16},{8,24},{16,32},{24,40},{32,48},{40,56},{48,0},{56,8},{1,17}... | collective-permute-start | bytes 1572872 | tf_op jit(solution)/shard_map/ppermute | solution.py:219
  83.6 96.1 %collective-permute-start.2 = (bf16[3,1024,128]{2,1,0:T(8,128)(2,1)}, bf16[3,1024,128]{2,1,0:T(8,128)(2,1)S(1)}, u32[]{:S(2)}, u32[]{:S(2)}) collective-permute-start(bf16[3,1024,128]{2,1,0:T(8,128)(2,1)} %copy-done.6), channel_id=1, source_target_pairs={{0,56},{8,0},{16,8},{24,16},{32,24},{40,32},{48,40},{56,48},{1,57}... | collective-permute-start | bytes 2359304 | tf_op jit(solution)/shard_map/ppermute | solution.py:219
  84.9 94.8 %collective-permute-start.3 = (bf16[3,1024,128]{2,1,0:T(8,128)(2,1)}, bf16[3,1024,128]{2,1,0:T(8,128)(2,1)}, u32[]{:S(2)}, u32[]{:S(2)}) collective-permute-start(bf16[3,1024,128]{2,1,0:T(8,128)(2,1)} %copy-done.7), channel_id=1, source_target_pairs={{0,8},{8,16},{16,24},{24,32},{32,40},{40,48},{48,56},{56,0},{1,9},... | collective-permute-start | bytes 2359304 | tf_op jit(solution)/shard_map/ppermute | solution.py:219
  151.4 28.2 %collective-permute-start.7 = (bf16[2,512,256]{2,1,0:T(8,128)(2,1)S(1)}, bf16[2,512,256]{2,1,0:T(8,128)(2,1)S(1)}, u32[]{:S(2)}, u32[]{:S(2)}) collective-permute-start(bf16[2,512,256]{2,1,0:T(8,128)(2,1)S(1)} %get-tuple-element.41), channel_id=1, source_target_pairs={{0,48},{8,56},{16,0},{24,8},{32,16},{40,24},{48,32},{56,40},{1,49}... | collective-permute-start | bytes 1572872 | tf_op jit(solution)/shard_map/ppermute | solution.py:219
  179.7 24.8 %copy-start = (bf16[384,1,256]{2,0,1:T(8,128)(2,1)S(1)}, bf16[384,1,256]{2,0,1:T(8,128)(2,1)}, u32[]{:S(2)}) copy-start(bf16[384,1,256]{2,0,1:T(8,128)(2,1)} %param.12) | copy-start | bytes 589828
  197.9 23.5 %collective-permute-start.8 = (bf16[3,128,1024]{2,1,0:T(8,128)(2,1)S(1)}, bf16[3,128,1024]{2,1,0:T(8,128)(2,1)S(1)}, u32[]{:S(2)}, u32[]{:S(2)}) collective-permute-start(bf16[3,128,1024]{2,1,0:T(8,128)(2,1)S(1)} %get-tuple-element.31), channel_id=1, source_target_pairs={{0,8},{8,16},{16,24},{24,32},{32,40},{40,48},{48,56},{56,0},{1,9},... | collective-permute-start | bytes 2359304 | tf_op jit(solution)/shard_map/ppermute | solution.py:219
  199.8 21.6 %collective-permute-start.10 = (bf16[3,128,1024]{2,1,0:T(8,128)(2,1)S(1)}, bf16[3,128,1024]{2,1,0:T(8,128)(2,1)S(1)}, u32[]{:S(2)}, u32[]{:S(2)}) collective-permute-start(bf16[3,128,1024]{2,1,0:T(8,128)(2,1)S(1)} %get-tuple-element.35), channel_id=1, source_target_pairs={{0,56},{8,0},{16,8},{24,16},{32,24},{40,32},{48,40},{56,48},{1,57}... | collective-permute-start | bytes 2359304 | tf_op jit(solution)/shard_map/ppermute | solution.py:219
  200.7 20.6 %collective-permute-start.9 = (f32[3,1,1024]{2,1,0:T(1,128)S(1)}, f32[3,1,1024]{2,1,0:T(1,128)S(1)}, u32[]{:S(2)}, u32[]{:S(2)}) collective-permute-start(f32[3,1,1024]{2,1,0:T(1,128)S(1)} %get-tuple-element.32), channel_id=1, source_target_pairs={{0,8},{8,16},{16,24},{24,32},{32,40},{40,48},{48,56},{56,0},{1,9},... | collective-permute-start | bytes 36872 | tf_op jit(solution)/shard_map/ppermute | solution.py:219
  204.4 17.0 %collective-permute-start.11 = (f32[3,1,1024]{2,1,0:T(1,128)S(1)}, f32[3,1,1024]{2,1,0:T(1,128)S(1)}, u32[]{:S(2)}, u32[]{:S(2)}) collective-permute-start(f32[3,1,1024]{2,1,0:T(1,128)S(1)} %get-tuple-element.36), channel_id=1, source_target_pairs={{0,56},{8,0},{16,8},{24,16},{32,24},{40,32},{48,40},{56,48},{1,57}... | collective-permute-start | bytes 36872 | tf_op jit(solution)/shard_map/ppermute | solution.py:219
  224.3 25.4 %collective-permute-start.12 = (bf16[3,128,1024]{2,1,0:T(8,128)(2,1)S(1)}, bf16[3,128,1024]{2,1,0:T(8,128)(2,1)S(1)}, u32[]{:S(2)}, u32[]{:S(2)}) collective-permute-start(bf16[3,128,1024]{2,1,0:T(8,128)(2,1)S(1)} %get-tuple-element.37), channel_id=1, source_target_pairs={{0,8},{8,16},{16,24},{24,32},{32,40},{40,48},{48,56},{56,0},{1,9},... | collective-permute-start | bytes 2359304 | tf_op jit(solution)/shard_map/ppermute | solution.py:219
  229.4 20.3 %collective-permute-start.14 = (bf16[3,128,1024]{2,1,0:T(8,128)(2,1)S(1)}, bf16[3,128,1024]{2,1,0:T(8,128)(2,1)S(1)}, u32[]{:S(2)}, u32[]{:S(2)}) collective-permute-start(bf16[3,128,1024]{2,1,0:T(8,128)(2,1)S(1)} %get-tuple-element.39), channel_id=1, source_target_pairs={{0,56},{8,0},{16,8},{24,16},{32,24},{40,32},{48,40},{56,48},{1,57}... | collective-permute-start | bytes 2359304 | tf_op jit(solution)/shard_map/ppermute | solution.py:219
  229.4 14.0 %collective-permute-start.13 = (f32[3,1,1024]{2,1,0:T(1,128)S(1)}, f32[3,1,1024]{2,1,0:T(1,128)S(1)}, u32[]{:S(2)}, u32[]{:S(2)}) collective-permute-start(f32[3,1,1024]{2,1,0:T(1,128)S(1)} %get-tuple-element.38), channel_id=1, source_target_pairs={{0,8},{8,16},{16,24},{24,32},{32,40},{40,48},{48,56},{56,0},{1,9},... | collective-permute-start | bytes 36872 | tf_op jit(solution)/shard_map/ppermute | solution.py:219
  233.4 16.3 %collective-permute-start.15 = (f32[3,1,1024]{2,1,0:T(1,128)S(1)}, f32[3,1,1024]{2,1,0:T(1,128)S(1)}, u32[]{:S(2)}, u32[]{:S(2)}) collective-permute-start(f32[3,1,1024]{2,1,0:T(1,128)S(1)} %get-tuple-element.40), channel_id=1, source_target_pairs={{0,56},{8,0},{16,8},{24,16},{32,24},{40,32},{48,40},{56,48},{1,57}... | collective-permute-start | bytes 36872 | tf_op jit(solution)/shard_map/ppermute | solution.py:219
  (4 other events, 25.4 us)
Sparse Core Ops, SparseCore 0:
  9.8 165.0 all-gather.1
  258.7 39.5 reduce-scatter.1

commit v3 on v2

v3 whole, which is shorter than its diff:
```python
import functools
import math

import jax
import jax.numpy as jnp
from jax import lax
from jax.experimental import pallas as pl
from jax.experimental.pallas import tpu as pltpu
from jax.sharding import Mesh, PartitionSpec as P

HD = 128
GROUP = 8
LQ = 128
PLEN = 512
TOPP = 8
NX, NZ, NY, NC = 4, 8, 4, 2
ROWS = GROUP * LQ
SCALE = math.log2(math.e) / math.sqrt(HD)
NEG = -1e30
WIDTH = 512
PACK = 16
VMEM_LIMIT = 50 << 20

STAY = (0, 1, -1, 2, -2)
MOVE = (3, -3, 4)


def request_tables(lists, passage_slot, question_slot, per_device, pass_dev):
    slot_count = question_slot.shape[0]
    slot_ids = jnp.arange(slot_count, dtype=jnp.int32)
    holder = (question_slot[None, :] == slot_ids[:, None]).astype(jnp.int32)
    chosen = jnp.sum(holder[:, :, None] * lists[None, :, :], axis=1)
    catalog = jnp.arange(passage_slot.shape[0], dtype=jnp.int32)
    picked = (chosen[:, :, None] == catalog[None, None, :]).astype(jnp.int32)
    cache_rows = jnp.sum(picked * passage_slot[None, None, :], axis=2)
    cache_rows = cache_rows.reshape(slot_count // per_device, per_device * TOPP)
    return cache_rows // pass_dev, cache_rows % pass_dev


def row_copies(rows_ref, cache_ref, *refs):
    outs, sems = refs[:-1], refs[-1]
    copies = []
    for out_ref in outs:
        for i in range(out_ref.shape[0]):
            n = len(copies)
            copies.append(
                pltpu.make_async_copy(cache_ref.at[rows_ref[n]], out_ref.at[i], sems.at[n])
            )
    for copy in copies:
        copy.start()
    for copy in copies:
        copy.wait()


def take_rows(cache, rows, counts):
    anywhere = pl.BlockSpec(memory_space=pl.ANY)
    return pl.pallas_call(
        row_copies,
        out_shape=tuple(jax.ShapeDtypeStruct((n,) + cache.shape[1:], cache.dtype) for n in counts),
        in_specs=[pl.BlockSpec(memory_space=pltpu.SMEM), anywhere],
        out_specs=(anywhere,) * len(counts),
        scratch_shapes=[pltpu.SemaphoreType.DMA((sum(counts),))],
        name="take_rows",
    )(rows, cache)


def absorb(keys, values_t, query_ref, group, cols, acc, top, total, causal=False):
    which, lane = group
    scores = lax.dot_general(
        keys,
        query_ref[lane, cols, :],
        (((1,), (1,)), ((), ())),
        preferred_element_type=jnp.float32,
    )
    if causal:
        key = lax.broadcasted_iota(jnp.int32, scores.shape, 0)
        token = lax.broadcasted_iota(jnp.int32, scores.shape, 1)
        scores = jnp.where(key <= token, scores, NEG)
    old = top[which, :, cols]
    new = jnp.maximum(old, jnp.max(scores, axis=0, keepdims=True))
    weights = jnp.exp2((scores - new) * SCALE)
    keep = jnp.exp2((old - new) * SCALE)
    top[which, :, cols] = new
    total[which, :, cols] = total[which, :, cols] * keep + jnp.sum(weights, axis=0, keepdims=True)
    acc[which, :, cols] = acc[which, :, cols] * keep + jnp.dot(
        values_t, weights.astype(jnp.bfloat16), preferred_element_type=jnp.float32
    )


def start(acc, top, total):
    acc[...] = jnp.zeros_like(acc)
    top[...] = jnp.full_like(top, NEG)
    total[...] = jnp.zeros_like(total)


def absorb_all(tag_ref, first, kv_ref, count, pick, query_ref, base, acc, top, total):
    def step(i, carry):
        tag = tag_ref[first + i]

        @pl.when(tag >= 0)
        def _():
            index = pick(i)
            keys = kv_ref[(*index, slice(None), slice(0, HD))]
            values_t = kv_ref[(*index, slice(None), slice(HD, 2 * HD))].T
            for part in range(ROWS // WIDTH):
                cols = pl.ds(part * WIDTH, WIDTH)
                absorb(keys, values_t, query_ref, (base + tag, tag), cols, acc, top, total)

        return carry

    lax.fori_loop(0, count, step, 0)


def pack(level):
    parts = []
    for _ in range(3):
        part = level.astype(jnp.bfloat16).astype(jnp.float32)
        parts.append(part)
        level = level - part
    parts.append(jnp.zeros((PACK - 3, level.shape[1]), jnp.float32))
    return jnp.concatenate(parts, axis=0).astype(jnp.bfloat16)


def store(out_ref, j, mixed, level):
    out_ref[j, 0:HD, :] = mixed.astype(jnp.bfloat16)
    out_ref[j, HD : HD + PACK, :] = pack(level)


def load(ref, j):
    parts = ref[j, HD : HD + PACK, :].astype(jnp.float32)
    level = parts[0:1] + parts[1:2] + parts[2:3]
    return ref[j, 0:HD, :].astype(jnp.float32), level


def state_of(group, acc, top, total):
    sums = jnp.maximum(total[group], 1e-30)
    return acc[group] / sums, top[group] * SCALE + jnp.log2(sums)


def merge(pairs):
    level = pairs[0][1]
    for _, other in pairs[1:]:
        level = jnp.maximum(level, other)
    shares = [jnp.exp2(l - level) for _, l in pairs]
    whole = functools.reduce(jnp.add, shares)
    mixed = functools.reduce(jnp.add, [o * s for (o, _), s in zip(pairs, shares)])
    return mixed / whole, level + jnp.log2(whole)


def stay_kernel(tags, here, own, q0, q1, q2, q3, q4, o0, o1, o2, o3, o4, *state):
    start(*state)
    n = q0.shape[0]
    for j in range(n):
        rows = slice(j * LQ, (j + 1) * LQ)
        keys = own[rows, 0:HD]
        values_t = own[rows, HD : 2 * HD].T
        for part in range(GROUP):
            cols = pl.ds(part * LQ, LQ)
            absorb(keys, values_t, q0, (j, j), cols, *state, causal=True)
    for k, query in enumerate((q0, q1, q2, q3, q4)):
        absorb_all(tags, k * NX, here, NX, lambda i, k=k: (i, k), query, k * n, *state)
    for k, out_ref in enumerate((o0, o1, o2, o3, o4)):
        for j in range(n):
            store(out_ref, j, *state_of(k * n + j, *state))


def move_kernel(tags, moved, q_up, q_down, so_far_up, so_far_down, o_up, o_down, *state):
    start(*state)
    n = q_up.shape[0]
    absorb_all(tags, 0, moved, NX, lambda i: (i, 0), q_up, 0, *state)
    absorb_all(tags, 4, moved, NX, lambda i: (i, 1), q_down, n, *state)
    absorb_all(tags, 8, moved, NX, lambda i: (i, 2), q_up, 0, *state)
    absorb_all(tags, 12, moved, NX, lambda i: (i, 2), q_down, n, *state)
    for j in range(n):
        store(o_up, j, *merge([state_of(j, *state), load(so_far_up, j)]))
        store(o_down, j, *merge([state_of(n + j, *state), load(so_far_down, j)]))


def attention(kernel, name, tags, arrays, n, groups, outs, items):
    vmem = pl.BlockSpec(memory_space=pltpu.VMEM)
    return pl.pallas_call(
        kernel,
        out_shape=(jax.ShapeDtypeStruct((n, HD + PACK, ROWS), jnp.bfloat16),) * outs,
        in_specs=[pl.BlockSpec(memory_space=pltpu.SMEM)] + [vmem] * len(arrays),
        out_specs=(vmem,) * outs,
        scratch_shapes=[
            pltpu.VMEM((groups * n, HD, ROWS), jnp.float32),
            pltpu.VMEM((groups * n, 1, ROWS), jnp.float32),
            pltpu.VMEM((groups * n, 1, ROWS), jnp.float32),
        ],
        compiler_params=pltpu.CompilerParams(vmem_limit_bytes=VMEM_LIMIT),
        cost_estimate=pl.CostEstimate(
            flops=items * 4 * ROWS * PLEN * HD * 2,
            bytes_accessed=items * PLEN * 2 * HD * 2,
            transcendentals=items * ROWS * PLEN,
        ),
        name=name,
    )(tags, *arrays)


def hop_kernel(near_up, back_up, near_down, back_down, o_up, o_down):
    for j in range(near_up.shape[0]):
        store(o_up, j, *merge([load(near_up, j), load(back_up, j)]))
        store(o_down, j, *merge([load(near_down, j), load(back_down, j)]))


def last_kernel(own, home_up, home_down, out_ref):
    for j in range(own.shape[0]):
        mixed, _ = merge([load(own, j), load(home_up, j), load(home_down, j)])
        for part in range(GROUP):
            cols = slice(part * LQ, (part + 1) * LQ)
            out_ref[j * LQ : (j + 1) * LQ, part * HD : (part + 1) * HD] = mixed[:, cols].T.astype(
                jnp.bfloat16
            )


def in_vmem(kernel, name, out, *arrays):
    vmem = pl.BlockSpec(memory_space=pltpu.VMEM)
    return pl.pallas_call(
        kernel,
        out_shape=out,
        in_specs=[vmem] * len(arrays),
        out_specs=jax.tree.map(lambda _: vmem, out),
        compiler_params=pltpu.CompilerParams(vmem_limit_bytes=VMEM_LIMIT),
        name=name,
    )(*arrays)


def along_z(array, shift):
    return lax.ppermute(array, "z", [(i, (i + shift) % NZ) for i in range(NZ)])


def over_x(items):
    return lax.all_to_all(items, "x", split_axis=0, concat_axis=0, tiled=True)


def body(queries, own_kv, passage_cache, out_weight, lists, passage_slot, question_slot):
    x, z = lax.axis_index("x"), lax.axis_index("z")
    per_device = queries.shape[0] // LQ
    pass_dev = passage_cache.shape[0]
    cache = passage_cache.reshape(pass_dev, PLEN, 2 * HD)
    own = own_kv.reshape(per_device * LQ, 2 * HD)

    q_own = queries.reshape(per_device, LQ, GROUP, HD).transpose(0, 2, 1, 3)
    q_own = q_own.reshape(per_device, ROWS, HD)
    q_up = along_z(q_own, -1)
    q_down = along_z(q_own, 1)
    owners, local_rows = request_tables(lists, passage_slot, question_slot, per_device, pass_dev)
    mine = jnp.sum(jnp.where(owners == x * NZ + z, local_rows, 0), axis=1).reshape(NX, NZ)
    target_z = (z + jnp.array(STAY + MOVE, jnp.int32)) % NZ
    rows = jnp.sum(
        jnp.where(target_z[None, :, None] == jnp.arange(NZ)[None, None, :], mine[:, None, :], 0),
        axis=2,
    )
    stay = len(STAY)
    (here,) = take_rows(cache, rows[:, :stay].reshape(-1), (NX * stay,))
    here = over_x(here.reshape(NX, stay, PLEN, 2 * HD))
    moving = take_rows(cache, rows[:, stay:].T.reshape(-1), (4, 4, 2, 2))
    (up3, down3, up4, down4), q_up, q_down = lax.optimization_barrier((moving, q_up, q_down))
    up3 = along_z(up3, 1)
    down3 = along_z(down3, -1)
    up4 = along_z(up4, 2)
    down4 = along_z(down4, -2)
    moved = jnp.stack([up3, down3, jnp.concatenate([up4, down4], axis=0)], axis=1)
    moved, here, out_weight = lax.optimization_barrier((moved, here, out_weight))
    moved = over_x(moved)
    weight = lax.all_gather(out_weight, "z", axis=1, tiled=True)
    q_up2 = along_z(q_up, -1)
    q_down2 = along_z(q_down, 1)

    four = range(NX)
    slots = (
        [(d, i, 0) for d in STAY for i in four]
        + [(2, i, -1) for i in four]
        + [(-2, i, 1) for i in four]
        + [(2, i, -2) for i in four]
        + [(-2, i, 2) for i in four]
    )
    count = len(slots)
    slot_question = (z + jnp.array([s[0] for s in slots], jnp.int32)) % NZ
    slot_owner = jnp.array([s[1] for s in slots], jnp.int32) * NZ + (
        z + jnp.array([s[2] for s in slots], jnp.int32)
    ) % NZ
    index = jnp.arange(count)
    absent = jnp.where(x < 2, index >= count - NX, (index >= count - 2 * NX) & (index < count - NX))
    column = lax.dynamic_index_in_dim(owners.reshape(NX, NZ, -1), x, 0, keepdims=False)
    number = jnp.arange(column.shape[1], dtype=jnp.int32) // TOPP + 1
    hit = (slot_question[:, None, None] == jnp.arange(NZ)[None, :, None]) & (
        slot_owner[:, None, None] == column[None, :, :]
    )
    tags = jnp.sum(jnp.where(hit, number[None, None, :], 0), axis=(1, 2)) - 1
    tags = jnp.where(absent, -1, tags)

    split = NX * stay
    own_part, near_up, near_down, far_up, far_down = attention(
        stay_kernel,
        "stay",
        tags[:split],
        [here, own, q_own, q_up, q_down, q_up2, q_down2],
        per_device,
        stay,
        stay,
        17,
    )
    weight, moved, far_up, far_down = lax.optimization_barrier((weight, moved, far_up, far_down))
    weight = lax.all_gather(weight, "x", axis=1, tiled=True)
    far_up, far_down = attention(
        move_kernel,
        "move",
        tags[split:],
        [moved, q_up2, q_down2, far_up, far_down],
        per_device,
        2,
        2,
        9,
    )
    shape = jax.ShapeDtypeStruct(own_part.shape, own_part.dtype)
    hop_up, hop_down = in_vmem(
        hop_kernel,
        "hop",
        (shape, shape),
        near_up,
        along_z(far_up, 1),
        near_down,
        along_z(far_down, -1),
    )
    context = in_vmem(
        last_kernel,
        "last",
        jax.ShapeDtypeStruct(queries.shape, jnp.bfloat16),
        own_part,
        along_z(hop_up, 1),
        along_z(hop_down, -1),
    )
    partial_value = jnp.dot(context, weight, preferred_element_type=jnp.float32)
    partial_value = partial_value.astype(jnp.bfloat16)
    return lax.psum_scatter(partial_value, ("y", "core"), scatter_dimension=1, tiled=True)


def solution(mesh):
    grid = Mesh(mesh.devices.reshape(NX, NZ, NY, NC), ("x", "z", "y", "core"))
    on_pass, on_head = ("x", "z"), ("y", "core")
    in_specs = (
        P(on_pass, on_head),
        P(on_pass, on_head, None),
        P(on_pass, None, on_head, None),
        P(on_head, on_pass),
        P(),
        P(),
        P(),
    )
    out_specs = P(on_pass, on_head)
    return jax.shard_map(body, mesh=grid, in_specs=in_specs, out_specs=out_specs, check_vma=False)
```

time: 308 us -> 539 us (1.75)
  Pallas kernels: 59 us -> 304 us
  starting transfers between devices: 41.4 us -> 30.3 us
    pallas_call x4, Pallas kernels: 56.5 us -> 301 us  [the longest x2 258 us: take_rows(): pl.pallas_call(row_copies, out_shape=tuple((jax.ShapeDtypeStruct((n,) + c...]
    all_gather x1 -> x2, waiting for transfers between devices: 0.02 us -> 34.7 us  [the longest x1 34.7 us: body(): weight = lax.all_gather(weight, 'x', axis=1, tiled=True)]
    ppermute x16 -> x12, waiting for transfers between devices: 121 us -> 94.5 us  [along_z(): return lax.ppermute(array, 'z', [(i, (i + shift) % NZ) for i in range(NZ)])]
    ppermute x16 -> x12, starting transfers between devices: 30.8 us -> 19.9 us  [along_z(): return lax.ppermute(array, 'z', [(i, (i + shift) % NZ) for i in range(NZ)])]
    all_to_all x2, waiting for transfers between devices: 7.49 us -> 0.01 us  [over_x(): return lax.all_to_all(items, 'x', split_axis=0, concat_axis=0, tiled=True)]
  transfers between devices with their start and end apart: 20 -> 17, of which waited for: 8 -> 7; matrix products, arithmetic and copies ran while one was open for 4% -> 1% of each run, Pallas kernels for 19% -> 27%
where the time goes in v3:
time: 539 us; the launch traced here: 536 us
  Pallas kernels  304 us (56%)
  waiting for transfers between devices  166 us (31%)
  starting transfers between devices  30.3 us (6%)
  between operations  13.4 us (2%)
  other arithmetic  9.03 us (2%)
  matrix products  8.16 us (2%)
    pallas_call x2, Pallas kernels, take_rows(): pl.pallas_call(row_copies, out_shape=tuple((jax.ShapeDtypeStruct((n,) + c...  258 us
    ppermute x12, waiting for transfers between devices, along_z(): return lax.ppermute(array, 'z', [(i, (i + shift) % NZ) for i in range(NZ)])  94.5 us
    pallas_call x2, Pallas kernels, attention(): pl.pallas_call(kernel, out_shape=(jax.ShapeDtypeStruct((n, HD + PACK, ROW...  43 us
    reduce_scatter x1, waiting for transfers between devices, body(): lax.psum_scatter(partial_value, ('y', 'core'), scatter_dimension=1, tiled...  36.7 us
    all_gather x1, waiting for transfers between devices, body(): weight = lax.all_gather(weight, 'x', axis=1, tiled=True)  34.7 us
    ppermute x12, starting transfers between devices, along_z(): return lax.ppermute(array, 'z', [(i, (i + shift) % NZ) for i in range(NZ)])  19.9 us
  transfers between devices with their start and end apart: 17, of which 7 were waited for; matrix products, arithmetic and copies ran while one was open for 1% of the time, Pallas kernels for 27%

profile of v3, /device:TPU:1, one launch (start us, length us, event | category | flops | bytes accessed | tf_op | source)
XLA Modules:
  0.0 536.0 jit_solution(9896693908444183460)
XLA Ops:
  7.2 2.4 multiply_reduce_fusion
  9.6 2.5 select_reduce_fusion
  14.0 160.8 %take_rows.3 = bf16[20,512,256]{2,1,0:T(8,128)(2,1)} custom-call(s32[20]{0:T(128)} %reshape.117.rows_ref, bf16[16,512,256]{2,1,0:T(8,128)(2,1)} %bitcast.27), custom_call_target="tpu_custom_call" | custom-call | tf_op jit(solution)/shard_map/take_rows/pallas_call | solution.py:57
  174.8 5.2 all-to-all-start
  180.5 6.5 %collective-permute-start = (bf16[3,1024,128]{2,1,0:T(8,128)(2,1)S(1)}, bf16[3,1024,128]{2,1,0:T(8,128)(2,1)S(1)}, u32[]{:S(2)}, u32[]{:S(2)}) collective-permute-start(bf16[3,1024,128]{2,1,0:T(8,128)(2,1)S(1)} %bitcast.21), channel_id=1, source_target_pairs={{0,56},{8,0},{16,8},{24,16},{32,24},{40,32},{48,40},{56,48},{1,57}... | collective-permute-start | bytes 2359304 | tf_op jit(solution)/shard_map/ppermute | solution.py:230
  187.7 97.2 %take_rows.2 = (bf16[4,512,256]{2,1,0:T(8,128)(2,1)}, bf16[4,512,256]{2,1,0:T(8,128)(2,1)}, bf16[2,512,256]{2,1,0:T(8,128)(2,1)}, bf16[2,512,256]{2,1,0:T(8,128)(2,1)}) custom-call(s32[12]{0:T(128)} %reshape.113.rows_ref, bf16[16,512,256]{2,1,0:T(8,128)(2,1)} %bitcast.28), custom_call_target="tpu_custom_call" | custom-call | tf_op jit(solution)/shard_map/take_rows/pallas_call | solution.py:57
  285.0 2.7 collective-permute-start.3
  287.8 3.6 collective-permute-start.5
  291.3 42.1 %collective-permute-done.4 = bf16[2,512,256]{2,1,0:T(8,128)(2,1)S(1)} collective-permute-done((bf16[2,512,256]{2,1,0:T(8,128)(2,1)}, bf16[2,512,256]{2,1,0:T(8,128)(2,1)S(1)}, u32[]{:S(2)}, u32[]{:S(2)}) %collective-permute-start.4) | collective-permute-done | bytes 524320 | tf_op jit(solution)/shard_map/ppermute | solution.py:230
  333.6 2.1 pad_maximum_fusion
  335.7 4.9 all-to-all-start.1
  340.9 1.5 collective-permute-start.7
  342.5 20.6 %collective-permute-done.6.q3.q_up = bf16[3,1024,128]{2,1,0:T(8,128)(2,1)S(1)} collective-permute-done((bf16[3,1024,128]{2,1,0:T(8,128)(2,1)S(1)}, bf16[3,1024,128]{2,1,0:T(8,128)(2,1)S(1)}, u32[]{:S(2)}, u32[]{:S(2)}) %collective-permute-start.6) | collective-permute-done | bytes 786464 | tf_op jit(solution)/shard_map/ppermute | solution.py:230
  363.1 1.4 collective-permute-done.7.q4.q_down
  365.4 28.5 %stay.1 = (bf16[3,144,1024]{2,1,0:T(8,128)(2,1)}, bf16[3,144,1024]{2,1,0:T(8,128)(2,1)}, bf16[3,144,1024]{2,1,0:T(8,128)(2,1)}, bf16[3,144,1024]{2,1,0:T(8,128)(2,1)}, bf16[3,144,1024]{2,1,0:T(8,128)(2,1)}) custom-call(s32[20]{0:T(128)S(1)} %bitcast.25, bf16[4,5,512,256]{3,2,1,0:T(8,128)(2,1)} %all-to-all-done.here, bf16[384,256]{1,0:T(8,128)(2,1)S(1)} %bitcast.24, ...), custom_call_target="tpu_custom_call" | custom-call | flops 9126805504 | bytes 4456448 | tf_op jit(solution)/shard_map/stay/pallas_call | solution.py:181
  395.5 14.5 %move.1 = (bf16[3,144,1024]{2,1,0:T(8,128)(2,1)S(1)}, bf16[3,144,1024]{2,1,0:T(8,128)(2,1)S(1)}) custom-call(s32[16]{0:T(128)S(1)} %slice.15.tags, bf16[4,3,512,256]{3,2,1,0:T(8,128)(2,1)} %all-to-all-done.1.moved, bf16[3,1024,128]{2,1,0:T(8,128)(2,1)S(1)} %collective-permute-done.6.q3.q_up, bf16[3,1024,128]{2,1,0:T(8,128)(2,1)S(1)} %copy-done.3, ...), custom_call_target="tpu_custom_call" | custom-call | flops 4831838208 | bytes 2359296 | tf_op jit(solution)/shard_map/move/pallas_call | solution.py:181
  410.0 2.7 collective-permute-start.9
  412.7 16.4 %collective-permute-done.8.back_up = bf16[3,144,1024]{2,1,0:T(8,128)(2,1)S(1)} collective-permute-done((bf16[3,144,1024]{2,1,0:T(8,128)(2,1)S(1)}, bf16[3,144,1024]{2,1,0:T(8,128)(2,1)S(1)}, u32[]{:S(2)}, u32[]{:S(2)}) %collective-permute-start.8) | collective-permute-done | bytes 884768 | tf_op jit(solution)/shard_map/ppermute | solution.py:230
  430.1 2.3 hop.1
  433.7 1.5 collective-permute-start.11
  435.3 13.9 %collective-permute-done.10.home_up = bf16[3,144,1024]{2,1,0:T(8,128)(2,1)S(1)} collective-permute-done((bf16[3,144,1024]{2,1,0:T(8,128)(2,1)S(1)}, bf16[3,144,1024]{2,1,0:T(8,128)(2,1)S(1)}, u32[]{:S(2)}, u32[]{:S(2)}) %collective-permute-start.10) | collective-permute-done | bytes 884768 | tf_op jit(solution)/shard_map/ppermute | solution.py:230
  449.9 34.7 %all-gather.5.cloned.1.call-done = bf16[1024,4096]{1,0:T(8,128)(2,1)} async-done(((bf16[1024,1024]{1,0:T(8,128)(2,1)}), bf16[1024,4096]{1,0:T(8,128)(2,1)}) %all-gather.5.cloned.1.call-update) | async-done | bytes 8388624 | tf_op jit(solution)/shard_map/all_gather | solution.py:306
  484.6 8.2 %convolution_convert_fusion = bf16[384,4096]{1,0:T(8,128)(2,1)} fusion(bf16[384,1024]{1,0:T(8,128)(2,1)S(1)} %last.1, bf16[1024,4096]{1,0:T(8,128)(2,1)} %all-gather.5.cloned.1.call-done), kind=kOutput, calls=%fused_computation | convolution fusion | flops 3222798336 | bytes 12320768 | tf_op jit(solution)/shard_map/dot_general | solution.py:335
  492.7 36.7 %reduce-scatter.2.cloned.1.call-done = bf16[384,512]{1,0:T(8,128)(2,1)} async-done(((bf16[384,4096]{1,0:T(8,128)(2,1)}), bf16[384,512]{1,0:T(8,128)(2,1)}) %reduce-scatter.2.cloned.1.call-update) | async-done | bytes 393232 | tf_op jit(solution)/shard_map/reduce_scatter | solution.py:337
  (68 shorter events, 9.8 us)
Async XLA Ops:
  174.8 5.3 copy-start.6
  174.8 160.8 %all-to-all-start = ((bf16[4,5,512,256]{3,2,1,0:T(8,128)(2,1)}), bf16[4,5,512,256]{3,2,1,0:T(8,128)(2,1)}, u32[]{:S(2)}, u32[]{:S(2)}) async-start(bf16[4,5,512,256]{3,2,1,0:T(8,128)(2,1)} %bitcast.26), calls=%async_computation | async-start | bytes 10485760 | tf_op jit(solution)/shard_map/all_to_all | solution.py:234
  180.0 213.9 %all-gather.3.cloned.1.call-start = ((), (), s32[]{:S(2)}) async-start(), calls=%async_computation.3 | async-start | bytes 2359296 | tf_op jit(solution)/shard_map/all_gather | solution.py:267
  180.5 104.4 %collective-permute-start = (bf16[3,1024,128]{2,1,0:T(8,128)(2,1)S(1)}, bf16[3,1024,128]{2,1,0:T(8,128)(2,1)S(1)}, u32[]{:S(2)}, u32[]{:S(2)}) collective-permute-start(bf16[3,1024,128]{2,1,0:T(8,128)(2,1)S(1)} %bitcast.21), channel_id=1, source_target_pairs={{0,56},{8,0},{16,8},{24,16},{32,24},{40,32},{48,40},{56,48},{1,57}... | collective-permute-start | bytes 2359304 | tf_op jit(solution)/shard_map/ppermute | solution.py:230
  186.9 98.0 %collective-permute-start.1 = (bf16[3,1024,128]{2,1,0:T(8,128)(2,1)S(1)}, bf16[3,1024,128]{2,1,0:T(8,128)(2,1)S(1)}, u32[]{:S(2)}, u32[]{:S(2)}) collective-permute-start(bf16[3,1024,128]{2,1,0:T(8,128)(2,1)S(1)} %bitcast.22), channel_id=1, source_target_pairs={{0,8},{8,16},{16,24},{24,32},{32,40},{40,48},{48,56},{56,0},{1,9},... | collective-permute-start | bytes 2359304 | tf_op jit(solution)/shard_map/ppermute | solution.py:230
  284.9 48.7 %collective-permute-start.2 = (bf16[4,512,256]{2,1,0:T(8,128)(2,1)}, bf16[4,512,256]{2,1,0:T(8,128)(2,1)S(1)}, u32[]{:S(2)}, u32[]{:S(2)}) collective-permute-start(bf16[4,512,256]{2,1,0:T(8,128)(2,1)} %get-tuple-element.35), channel_id=1, source_target_pairs={{0,8},{8,16},{16,24},{24,32},{32,40},{40,48},{48,56},{56,0},{1,9},... | collective-permute-start | bytes 3145736 | tf_op jit(solution)/shard_map/ppermute | solution.py:230
  285.0 48.6 %collective-permute-start.3 = (bf16[4,512,256]{2,1,0:T(8,128)(2,1)}, bf16[4,512,256]{2,1,0:T(8,128)(2,1)S(1)}, u32[]{:S(2)}, u32[]{:S(2)}) collective-permute-start(bf16[4,512,256]{2,1,0:T(8,128)(2,1)} %get-tuple-element.36), channel_id=1, source_target_pairs={{0,56},{8,0},{16,8},{24,16},{32,24},{40,32},{48,40},{56,48},{1,57}... | collective-permute-start | bytes 3145736 | tf_op jit(solution)/shard_map/ppermute | solution.py:230
  287.7 45.7 %collective-permute-start.4 = (bf16[2,512,256]{2,1,0:T(8,128)(2,1)}, bf16[2,512,256]{2,1,0:T(8,128)(2,1)S(1)}, u32[]{:S(2)}, u32[]{:S(2)}) collective-permute-start(bf16[2,512,256]{2,1,0:T(8,128)(2,1)} %get-tuple-element.37), channel_id=1, source_target_pairs={{0,16},{8,24},{16,32},{24,40},{32,48},{40,56},{48,0},{56,8},{1,17}... | collective-permute-start | bytes 1572872 | tf_op jit(solution)/shard_map/ppermute | solution.py:230
  287.8 45.7 %collective-permute-start.5 = (bf16[2,512,256]{2,1,0:T(8,128)(2,1)}, bf16[2,512,256]{2,1,0:T(8,128)(2,1)S(1)}, u32[]{:S(2)}, u32[]{:S(2)}) collective-permute-start(bf16[2,512,256]{2,1,0:T(8,128)(2,1)} %get-tuple-element.38), channel_id=1, source_target_pairs={{0,48},{8,56},{16,0},{24,8},{32,16},{40,24},{48,32},{56,40},{1,49}... | collective-permute-start | bytes 1572872 | tf_op jit(solution)/shard_map/ppermute | solution.py:230
  335.7 6.7 %copy-start.7 = (s32[36]{0:T(128)S(1)}, s32[36]{0:T(128)}, u32[]{:S(2)}) copy-start(s32[36]{0:T(128)} %constant.104.clone) | copy-start | bytes 436
  335.7 6.6 %copy-start.8 = (s32[36]{0:T(128)S(1)}, s32[36]{0:T(128)}, u32[]{:S(2)}) copy-start(s32[36]{0:T(128)} %constant.106.clone) | copy-start | bytes 436
  335.7 6.6 %copy-start.9 = (s32[36]{0:T(128)S(1)}, s32[36]{0:T(128)}, u32[]{:S(2)}) copy-start(s32[36]{0:T(128)} %constant.109) | copy-start | bytes 436
  335.7 29.7 %copy-start.4 = (bf16[384,1,256]{2,0,1:T(8,128)(2,1)S(1)}, bf16[384,1,256]{2,0,1:T(8,128)(2,1)}, u32[]{:S(2)}) copy-start(bf16[384,1,256]{2,0,1:T(8,128)(2,1)} %param.12) | copy-start | bytes 589828
  335.7 58.2 %all-to-all-start.1 = ((bf16[4,3,512,256]{3,2,1,0:T(8,128)(2,1)}), bf16[4,3,512,256]{3,2,1,0:T(8,128)(2,1)}, u32[]{:S(2)}, u32[]{:S(2)}) async-start(bf16[4,3,512,256]{3,2,1,0:T(8,128)(2,1)} %pad_maximum_fusion), calls=%async_computation.1 | async-start | bytes 6291456 | tf_op jit(solution)/shard_map/all_to_all | solution.py:234
  340.6 143.9 %all-gather.5.cloned.1.call-start = ((), (), s32[]{:S(2)}) async-start(), calls=%async_computation.4 | async-start | bytes 10485760 | tf_op jit(solution)/shard_map/all_gather | solution.py:306
  340.8 22.3 %collective-permute-start.6 = (bf16[3,1024,128]{2,1,0:T(8,128)(2,1)S(1)}, bf16[3,1024,128]{2,1,0:T(8,128)(2,1)S(1)}, u32[]{:S(2)}, u32[]{:S(2)}) collective-permute-start(bf16[3,1024,128]{2,1,0:T(8,128)(2,1)S(1)} %collective-permute-done.q1), channel_id=1, source_target_pairs={{0,56},{8,0},{16,8},{24,16},{32,24},{40,32},{48,40},{56,48},{1,57}... | collective-permute-start | bytes 2359304 | tf_op jit(solution)/shard_map/ppermute | solution.py:230
  340.9 23.6 %collective-permute-start.7 = (bf16[3,1024,128]{2,1,0:T(8,128)(2,1)S(1)}, bf16[3,1024,128]{2,1,0:T(8,128)(2,1)S(1)}, u32[]{:S(2)}, u32[]{:S(2)}) collective-permute-start(bf16[3,1024,128]{2,1,0:T(8,128)(2,1)S(1)} %collective-permute-done.1.q2), channel_id=1, source_target_pairs={{0,8},{8,16},{16,24},{24,32},{32,40},{40,48},{48,56},{56,0},{1,9},... | collective-permute-start | bytes 2359304 | tf_op jit(solution)/shard_map/ppermute | solution.py:230
  394.0 135.5 %reduce-scatter.2.cloned.1.call-start = ((), (), s32[]{:S(2)}) async-start(), calls=%async_computation.5 | async-start | bytes 3538944 | tf_op jit(solution)/shard_map/reduce_scatter | solution.py:337
  395.5 34.7 %copy-start = (bf16[3,144,1024]{2,1,0:T(8,128)(2,1)S(1)}, bf16[3,144,1024]{2,1,0:T(8,128)(2,1)}, u32[]{:S(2)}) copy-start(bf16[3,144,1024]{2,1,0:T(8,128)(2,1)} %get-tuple-element.43.near_up) | copy-start | bytes 2654212
  409.9 39.2 %copy-start.1 = (bf16[3,144,1024]{2,1,0:T(8,128)(2,1)S(1)}, bf16[3,144,1024]{2,1,0:T(8,128)(2,1)}, u32[]{:S(2)}) copy-start(bf16[3,144,1024]{2,1,0:T(8,128)(2,1)} %get-tuple-element.42.own) | copy-start | bytes 2654212
  409.9 19.2 %collective-permute-start.8 = (bf16[3,144,1024]{2,1,0:T(8,128)(2,1)S(1)}, bf16[3,144,1024]{2,1,0:T(8,128)(2,1)S(1)}, u32[]{:S(2)}, u32[]{:S(2)}) collective-permute-start(bf16[3,144,1024]{2,1,0:T(8,128)(2,1)S(1)} %get-tuple-element.51), channel_id=1, source_target_pairs={{0,8},{8,16},{16,24},{24,32},{32,40},{40,48},{48,56},{56,0},{1,9},... | collective-permute-start | bytes 2654216 | tf_op jit(solution)/shard_map/ppermute | solution.py:230
  410.0 19.1 %collective-permute-start.9 = (bf16[3,144,1024]{2,1,0:T(8,128)(2,1)S(1)}, bf16[3,144,1024]{2,1,0:T(8,128)(2,1)S(1)}, u32[]{:S(2)}, u32[]{:S(2)}) collective-permute-start(bf16[3,144,1024]{2,1,0:T(8,128)(2,1)S(1)} %get-tuple-element.53), channel_id=1, source_target_pairs={{0,56},{8,0},{16,8},{24,16},{32,24},{40,32},{48,40},{56,48},{1,57}... | collective-permute-start | bytes 2654216 | tf_op jit(solution)/shard_map/ppermute | solution.py:230
  432.5 16.7 %collective-permute-start.10 = (bf16[3,144,1024]{2,1,0:T(8,128)(2,1)S(1)}, bf16[3,144,1024]{2,1,0:T(8,128)(2,1)S(1)}, u32[]{:S(2)}, u32[]{:S(2)}) collective-permute-start(bf16[3,144,1024]{2,1,0:T(8,128)(2,1)S(1)} %get-tuple-element.54), channel_id=1, source_target_pairs={{0,8},{8,16},{16,24},{24,32},{32,40},{40,48},{48,56},{56,0},{1,9},... | collective-permute-start | bytes 2654216 | tf_op jit(solution)/shard_map/ppermute | solution.py:230
  433.7 15.5 %collective-permute-start.11 = (bf16[3,144,1024]{2,1,0:T(8,128)(2,1)S(1)}, bf16[3,144,1024]{2,1,0:T(8,128)(2,1)S(1)}, u32[]{:S(2)}, u32[]{:S(2)}) collective-permute-start(bf16[3,144,1024]{2,1,0:T(8,128)(2,1)S(1)} %get-tuple-element.55), channel_id=1, source_target_pairs={{0,56},{8,0},{16,8},{24,16},{32,24},{40,32},{48,40},{56,48},{1,57}... | collective-permute-start | bytes 2654216 | tf_op jit(solution)/shard_map/ppermute | solution.py:230
  (3 other events, 3.0 us)
Sparse Core Ops, SparseCore 0:
  335.8 51.0 all-gather.2
  394.1 90.4 all-gather.4
  492.9 36.5 reduce-scatter.1

commit v4 on v3

--- a/solution.py
+++ b/solution.py
@@ -38,28 +38,37 @@
 
 
 def row_copies(rows_ref, cache_ref, *refs):
-    outs, sems = refs[:-1], refs[-1]
-    copies = []
-    for out_ref in outs:
-        for i in range(out_ref.shape[0]):
-            n = len(copies)
-            copies.append(
-                pltpu.make_async_copy(cache_ref.at[rows_ref[n]], out_ref.at[i], sems.at[n])
-            )
-    for copy in copies:
-        copy.start()
-    for copy in copies:
-        copy.wait()
+    outs, (buffer, read_sems, write_sems) = refs[:-3], refs[-3:]
+    places = [out_ref.at[i] for out_ref in outs for i in range(out_ref.shape[0])]
+    reads, writes = [], []
+    for n, place in enumerate(places):
+        reads.append(
+            pltpu.make_async_copy(cache_ref.at[rows_ref[n]], buffer.at[n], read_sems.at[n])
+        )
+        writes.append(pltpu.make_async_copy(buffer.at[n], place, write_sems.at[n]))
+    for read in reads:
+        read.start()
+    for read, write in zip(reads, writes):
+        read.wait()
+        write.start()
+    for write in writes:
+        write.wait()
 
 
 def take_rows(cache, rows, counts):
     anywhere = pl.BlockSpec(memory_space=pl.ANY)
+    total = sum(counts)
     return pl.pallas_call(
         row_copies,
         out_shape=tuple(jax.ShapeDtypeStruct((n,) + cache.shape[1:], cache.dtype) for n in counts),
         in_specs=[pl.BlockSpec(memory_space=pltpu.SMEM), anywhere],
         out_specs=(anywhere,) * len(counts),
-        scratch_shapes=[pltpu.SemaphoreType.DMA((sum(counts),))],
+        scratch_shapes=[
+            pltpu.VMEM((total,) + cache.shape[1:], cache.dtype),
+            pltpu.SemaphoreType.DMA((total,)),
+            pltpu.SemaphoreType.DMA((total,)),
+        ],
+        compiler_params=pltpu.CompilerParams(vmem_limit_bytes=VMEM_LIMIT),
         name="take_rows",
     )(rows, cache)
 
@@ -93,22 +102,31 @@
     total[...] = jnp.zeros_like(total)
 
 
-def absorb_all(tag_ref, first, kv_ref, count, pick, query_ref, base, acc, top, total):
+def fetches(items_ref, picks, buffer, sems):
+    return [
+        pltpu.make_async_copy(items_ref.at[i, k], buffer.at[n], sems.at[n])
+        for n, (i, k) in enumerate(picks)
+    ]
+
+
+def absorb_all(tag_ref, first, copies, slot, buffer, query_ref, base, acc, top, total):
+    for copy in copies:
+        copy.wait()
+
     def step(i, carry):
         tag = tag_ref[first + i]
 
         @pl.when(tag >= 0)
         def _():
-            index = pick(i)
-            keys = kv_ref[(*index, slice(None), slice(0, HD))]
-            values_t = kv_ref[(*index, slice(None), slice(HD, 2 * HD))].T
+            keys = buffer[slot + i, :, 0:HD]
+            values_t = buffer[slot + i, :, HD : 2 * HD].T
             for part in range(ROWS // WIDTH):
                 cols = pl.ds(part * WIDTH, WIDTH)
                 absorb(keys, values_t, query_ref, (base + tag, tag), cols, acc, top, total)
 
         return carry
 
-    lax.fori_loop(0, count, step, 0)
+    lax.fori_loop(0, NX, step, 0)
 
 
 def pack(level):
@@ -147,71 +165,127 @@
     return mixed / whole, level + jnp.log2(whole)
 
 
-def stay_kernel(tags, here, own, q0, q1, q2, q3, q4, o0, o1, o2, o3, o4, *state):
+def near_kernel(tags, here, own, q0, q1, q2, o0, o1, o2, buffer, sems, *state):
+    copies = fetches(here, [(i, k) for k in range(3) for i in range(NX)], buffer, sems)
+    for copy in copies:
+        copy.start()
     start(*state)
     n = q0.shape[0]
     for j in range(n):
         rows = slice(j * LQ, (j + 1) * LQ)
         keys = own[rows, 0:HD]
         values_t = own[rows, HD : 2 * HD].T
-        for part in range(GROUP):
-            cols = pl.ds(part * LQ, LQ)
+
+        def head(part, carry, j=j, keys=keys, values_t=values_t):
+            cols = pl.ds(pl.multiple_of(part * LQ, LQ), LQ)
             absorb(keys, values_t, q0, (j, j), cols, *state, causal=True)
-    for k, query in enumerate((q0, q1, q2, q3, q4)):
-        absorb_all(tags, k * NX, here, NX, lambda i, k=k: (i, k), query, k * n, *state)
-    for k, out_ref in enumerate((o0, o1, o2, o3, o4)):
+            return carry
+
+        lax.fori_loop(0, GROUP, head, 0)
+    for k, query in enumerate((q0, q1, q2)):
+        slot = k * NX
+        absorb_all(tags, slot, copies[slot : slot + NX], slot, buffer, query, k * n, *state)
+    for k, out_ref in enumerate((o0, o1, o2)):
         for j in range(n):
             store(out_ref, j, *state_of(k * n + j, *state))
 
 
-def move_kernel(tags, moved, q_up, q_down, so_far_up, so_far_down, o_up, o_down, *state):
+def far_kernel(tags, here, q_up, q_down, o_up, o_down, buffer, sems, *state):
+    copies = fetches(here, [(i, k) for k in (3, 4) for i in range(NX)], buffer, sems)
+    for copy in copies:
+        copy.start()
     start(*state)
     n = q_up.shape[0]
-    absorb_all(tags, 0, moved, NX, lambda i: (i, 0), q_up, 0, *state)
-    absorb_all(tags, 4, moved, NX, lambda i: (i, 1), q_down, n, *state)
-    absorb_all(tags, 8, moved, NX, lambda i: (i, 2), q_up, 0, *state)
-    absorb_all(tags, 12, moved, NX, lambda i: (i, 2), q_down, n, *state)
+    absorb_all(tags, 0, copies[0:4], 0, buffer, q_up, 0, *state)
+    absorb_all(tags, 4, copies[4:8], 4, buffer, q_down, n, *state)
+    for j in range(n):
+        store(o_up, j, *state_of(j, *state))
+        store(o_down, j, *state_of(n + j, *state))
+
+
+def move_kernel(
+    tags, moved, q_up, q_down, so_far_up, so_far_down, o_up, o_down, buffer, sems, *state
+):
+    copies = fetches(moved, [(i, k) for k in range(3) for i in range(NX)], buffer, sems)
+    for copy in copies:
+        copy.start()
+    start(*state)
+    n = q_up.shape[0]
+    absorb_all(tags, 0, copies[0:4], 0, buffer, q_up, 0, *state)
+    absorb_all(tags, 4, copies[4:8], 4, buffer, q_down, n, *state)
+    absorb_all(tags, 8, copies[8:12], 8, buffer, q_up, 0, *state)
+    absorb_all(tags, 12, [], 8, buffer, q_down, n, *state)
     for j in range(n):
         store(o_up, j, *merge([state_of(j, *state), load(so_far_up, j)]))
         store(o_down, j, *merge([state_of(n + j, *state), load(so_far_down, j)]))
 
 
-def attention(kernel, name, tags, arrays, n, groups, outs, items):
+def attention(kernel, name, tags, items, arrays, n, groups, slots, work):
     vmem = pl.BlockSpec(memory_space=pltpu.VMEM)
     return pl.pallas_call(
         kernel,
-        out_shape=(jax.ShapeDtypeStruct((n, HD + PACK, ROWS), jnp.bfloat16),) * outs,
-        in_specs=[pl.BlockSpec(memory_space=pltpu.SMEM)] + [vmem] * len(arrays),
-        out_specs=(vmem,) * outs,
+        out_shape=(jax.ShapeDtypeStruct((n, HD + PACK, ROWS), jnp.bfloat16),) * groups,
+        in_specs=[pl.BlockSpec(memory_space=pltpu.SMEM), pl.BlockSpec(memory_space=pl.ANY)]
+        + [vmem] * len(arrays),
+        out_specs=(vmem,) * groups,
         scratch_shapes=[
+            pltpu.VMEM((slots, PLEN, 2 * HD), jnp.bfloat16),
+            pltpu.SemaphoreType.DMA((slots,)),
             pltpu.VMEM((groups * n, HD, ROWS), jnp.float32),
             pltpu.VMEM((groups * n, 1, ROWS), jnp.float32),
             pltpu.VMEM((groups * n, 1, ROWS), jnp.float32),
         ],
         compiler_params=pltpu.CompilerParams(vmem_limit_bytes=VMEM_LIMIT),
         cost_estimate=pl.CostEstimate(
-            flops=items * 4 * ROWS * PLEN * HD * 2,
-            bytes_accessed=items * PLEN * 2 * HD * 2,
-            transcendentals=items * ROWS * PLEN,
+            flops=work * ROWS * PLEN,
+            bytes_accessed=work * PLEN,
+            transcendentals=0,
         ),
         name=name,
-    )(tags, *arrays)
-
-
-def hop_kernel(near_up, back_up, near_down, back_down, o_up, o_down):
-    for j in range(near_up.shape[0]):
-        store(o_up, j, *merge([load(near_up, j), load(back_up, j)]))
-        store(o_down, j, *merge([load(near_down, j), load(back_down, j)]))
-
-
-def last_kernel(own, home_up, home_down, out_ref):
-    for j in range(own.shape[0]):
-        mixed, _ = merge([load(own, j), load(home_up, j), load(home_down, j)])
-        for part in range(GROUP):
-            cols = slice(part * LQ, (part + 1) * LQ)
-            out_ref[j * LQ : (j + 1) * LQ, part * HD : (part + 1) * HD] = mixed[:, cols].T.astype(
+    )(tags, items, *arrays)
+
+
+def last_kernel(*refs):
+    parts, out_ref = refs[:-1], refs[-1]
+    for j in range(parts[0].shape[0]):
+        mixed, _ = merge([load(part, j) for part in parts])
+        for head in range(GROUP):
+            cols = slice(head * LQ, (head + 1) * LQ)
+            out_ref[j * LQ : (j + 1) * LQ, head * HD : (head + 1) * HD] = mixed[:, cols].T.astype(
                 jnp.bfloat16
             )
+
+
+def project_kernel(core_ref, context_ref, weight_ref, out_ref):
+    out_ref[0] = jnp.dot(
+        context_ref[...], weight_ref[...], preferred_element_type=jnp.float32
+    ).astype(jnp.bfloat16)
+
+
+def project(context, weight, core, name):
+    width = weight.shape[1] // (NY * NC)
+    return pl.pallas_call(
+        project_kernel,
+        out_shape=jax.ShapeDtypeStruct((NY, context.shape[0], width), jnp.bfloat16),
+        grid_spec=pltpu.PrefetchScalarGridSpec(
+            num_scalar_prefetch=1,
+            grid=(NY,),
+            in_specs=[
+                pl.BlockSpec(context.shape, lambda i, core_ref: (0, 0)),
+                pl.BlockSpec(
+                    (weight.shape[0], width), lambda i, core_ref: (0, NC * i + core_ref[0])
+                ),
+            ],
+            out_specs=pl.BlockSpec((1, context.shape[0], width), lambda i, core_ref: (i, 0, 0)),
+        ),
+        compiler_params=pltpu.CompilerParams(vmem_limit_bytes=VMEM_LIMIT),
+        cost_estimate=pl.CostEstimate(
+            flops=2 * context.shape[0] * weight.shape[0] * width * NY,
+            bytes_accessed=weight.shape[0] * width * NY * 2,
+            transcendentals=0,
+        ),
+        name=name,
+    )(core.reshape(1), context, weight)
 
 
 def in_vmem(kernel, name, out, *arrays):
@@ -262,9 +336,9 @@
     up4 = along_z(up4, 2)
     down4 = along_z(down4, -2)
     moved = jnp.stack([up3, down3, jnp.concatenate([up4, down4], axis=0)], axis=1)
-    moved, here, out_weight = lax.optimization_barrier((moved, here, out_weight))
+    weight = lax.all_gather(out_weight, "z", axis=1, tiled=True)
+    moved, here, q_up, q_down = lax.optimization_barrier((moved, here, q_up, q_down))
     moved = over_x(moved)
-    weight = lax.all_gather(out_weight, "z", axis=1, tiled=True)
     q_up2 = along_z(q_up, -1)
     q_down2 = along_z(q_down, 1)
 
@@ -292,49 +366,64 @@
     tags = jnp.where(absent, -1, tags)
 
     split = NX * stay
-    own_part, near_up, near_down, far_up, far_down = attention(
-        stay_kernel,
-        "stay",
-        tags[:split],
-        [here, own, q_own, q_up, q_down, q_up2, q_down2],
+    near = attention(
+        near_kernel,
+        "near",
+        tags[: 3 * NX],
+        here,
+        [own, q_own, q_up, q_down],
         per_device,
-        stay,
-        stay,
-        17,
-    )
-    weight, moved, far_up, far_down = lax.optimization_barrier((weight, moved, far_up, far_down))
+        3,
+        3 * NX,
+        10,
+    )
+    near, q_up2, q_down2 = lax.optimization_barrier((near, q_up2, q_down2))
+    own_part, near_up, near_down = near
+    home_up = along_z(near_up, 1)
+    home_down = along_z(near_down, -1)
+    far = attention(
+        far_kernel,
+        "far",
+        tags[3 * NX : split],
+        here,
+        [q_up2, q_down2],
+        per_device,
+        2,
+        2 * NX,
+        6,
+    )
+    weight, moved, far, home_up, home_down = lax.optimization_barrier(
+        (weight, moved, far, home_up, home_down)
+    )
     weight = lax.all_gather(weight, "x", axis=1, tiled=True)
     far_up, far_down = attention(
         move_kernel,
         "move",
         tags[split:],
-        [moved, q_up2, q_down2, far_up, far_down],
+        moved,
+        [q_up2, q_down2, *far],
         per_device,
         2,
-        2,
+        3 * NX,
         9,
-    )
-    shape = jax.ShapeDtypeStruct(own_part.shape, own_part.dtype)
-    hop_up, hop_down = in_vmem(
-        hop_kernel,
-        "hop",
-        (shape, shape),
-        near_up,
-        along_z(far_up, 1),
-        near_down,
-        along_z(far_down, -1),
     )
     context = in_vmem(
         last_kernel,
         "last",
         jax.ShapeDtypeStruct(queries.shape, jnp.bfloat16),
         own_part,
-        along_z(hop_up, 1),
-        along_z(hop_down, -1),
-    )
-    partial_value = jnp.dot(context, weight, preferred_element_type=jnp.float32)
-    partial_value = partial_value.astype(jnp.bfloat16)
-    return lax.psum_scatter(partial_value, ("y", "core"), scatter_dimension=1, tiled=True)
+        home_up,
+        home_down,
+        along_z(far_up, 2),
+        along_z(far_down, -2),
+    )
+    core = lax.axis_index("core")
+    theirs = project(context, weight, 1 - core, "theirs")
+    theirs = lax.ppermute(theirs, "core", [(0, 1), (1, 0)])
+    ours = project(context, weight, core, "ours")
+    chip = (ours.astype(jnp.float32) + theirs.astype(jnp.float32)).astype(jnp.bfloat16)
+    chips = lax.all_to_all(chip, "y", split_axis=0, concat_axis=0, tiled=True)
+    return jnp.sum(chips.astype(jnp.float32), axis=0).astype(jnp.bfloat16)
 
 
 def solution(mesh):

time: 539 us -> 299 us (0.55)
  Pallas kernels: 304 us -> 65.9 us
  blocking collectives: 0 us -> 24.3 us
  waiting for transfers between devices: 166 us -> 147 us
  matrix products: 8.16 us -> 0 us
    pallas_call x2, Pallas kernels: 258 us -> 8.57 us  [take_rows(): pl.pallas_call(row_copies, out_shape=tuple((jax.ShapeDtypeStruct((n,) + c...]
    reduce_scatter x1 -> x0, waiting for transfers between devices: 36.7 us -> none  [body(): lax.psum_scatter(partial_value, ('y', 'core'), scatter_dimension=1, tiled...]
    ppermute x12, waiting for transfers between devices: 94.5 us -> 120 us  [along_z(): return lax.ppermute(array, 'z', [(i, (i + shift) % NZ) for i in range(NZ)])]
    all_to_all x0 -> x1, blocking collectives: none -> 24.3 us  [body(): chips = lax.all_to_all(chip, 'y', split_axis=0, concat_axis=0, tiled=True)]
    pallas_call x0 -> x2, Pallas kernels: none -> 8.55 us  [project(): pl.pallas_call(project_kernel, out_shape=jax.ShapeDtypeStruct((NY, contex...]
    dot_general x1 -> x0, matrix products: 8.16 us -> none  [body(): partial_value = jnp.dot(context, weight, preferred_element_type=jnp.float32)]
    all_gather x1, waiting for transfers between devices: 34.7 us -> 27.2 us  [body(): weight = lax.all_gather(weight, 'x', axis=1, tiled=True)]
    pallas_call x2 -> x3, Pallas kernels: 43 us -> 45.8 us  [attention(): pl.pallas_call(kernel, out_shape=(jax.ShapeDtypeStruct((n, HD + PACK, ROW...]
  transfers between devices with their start and end apart: 17 -> 17, of which waited for: 7 -> 8; matrix products, arithmetic and copies ran while one was open for 1% -> 1% of each run, Pallas kernels for 27% -> 19%
where the time goes in v4:
time: 299 us; the launch traced here: 298 us
  waiting for transfers between devices  147 us (49%)
  Pallas kernels  65.9 us (22%)
  starting transfers between devices  32.8 us (11%)
  blocking collectives  24.3 us (8%)
  between operations  13.7 us (5%)
  other arithmetic  10.5 us (4%)
  local copies, waits for them, and re-layouts  3.85 us (1%)
    ppermute x12, waiting for transfers between devices, along_z(): return lax.ppermute(array, 'z', [(i, (i + shift) % NZ) for i in range(NZ)])  120 us
    pallas_call x3, Pallas kernels, attention(): pl.pallas_call(kernel, out_shape=(jax.ShapeDtypeStruct((n, HD + PACK, ROW...  45.8 us
    all_gather x1, waiting for transfers between devices, body(): weight = lax.all_gather(weight, 'x', axis=1, tiled=True)  27.2 us
    all_to_all x1, blocking collectives, body(): chips = lax.all_to_all(chip, 'y', split_axis=0, concat_axis=0, tiled=True)  24.3 us
    ppermute x12, starting transfers between devices, along_z(): return lax.ppermute(array, 'z', [(i, (i + shift) % NZ) for i in range(NZ)])  21.9 us
    all_to_all x2, starting transfers between devices, over_x(): return lax.all_to_all(items, 'x', split_axis=0, concat_axis=0, tiled=True)  10 us
    pallas_call x2, Pallas kernels, take_rows(): pl.pallas_call(row_copies, out_shape=tuple((jax.ShapeDtypeStruct((n,) + c...  8.57 us
    pallas_call x2, Pallas kernels, project(): pl.pallas_call(project_kernel, out_shape=jax.ShapeDtypeStruct((NY, contex...  8.55 us
  transfers between devices with their start and end apart: 17, of which 8 were waited for; matrix products, arithmetic and copies ran while one was open for 1% of the time, Pallas kernels for 19%

profile of v4, /device:TPU:1, one launch (start us, length us, event | category | flops | bytes accessed | tf_op | source)
XLA Modules:
  0.0 298.3 jit_solution(2865257977133785048)
XLA Ops:
  9.6 2.5 select_reduce_fusion
  13.5 6.0 %take_rows.3 = bf16[20,512,256]{2,1,0:T(8,128)(2,1)} custom-call(s32[20]{0:T(128)S(1)} %reshape.124.rows_ref, bf16[16,512,256]{2,1,0:T(8,128)(2,1)} %bitcast.27), custom_call_target="tpu_custom_call" | custom-call | tf_op jit(solution)/shard_map/take_rows/pallas_call | solution.py:61
  19.5 5.2 %all-to-all-start = ((bf16[4,5,512,256]{3,2,1,0:T(8,128)(2,1)}), bf16[4,5,512,256]{3,2,1,0:T(8,128)(2,1)}, u32[]{:S(2)}, u32[]{:S(2)}) async-start(bf16[4,5,512,256]{3,2,1,0:T(8,128)(2,1)} %bitcast.26), calls=%async_computation | async-start | bytes 10485760 | tf_op jit(solution)/shard_map/all_to_all | solution.py:308
  25.1 6.8 %collective-permute-start = (bf16[3,1024,128]{2,1,0:T(8,128)(2,1)S(1)}, bf16[3,1024,128]{2,1,0:T(8,128)(2,1)}, u32[]{:S(2)}, u32[]{:S(2)}) collective-permute-start(bf16[3,1024,128]{2,1,0:T(8,128)(2,1)S(1)} %bitcast.21), channel_id=1, source_target_pairs={{0,56},{8,0},{16,8},{24,16},{32,24},{40,32},{48,40},{56,48},{1,57}... | collective-permute-start | bytes 2359304 | tf_op jit(solution)/shard_map/ppermute | solution.py:304
  32.2 2.6 take_rows.2
  34.8 16.1 %collective-permute-done.q1 = bf16[3,1024,128]{2,1,0:T(8,128)(2,1)} collective-permute-done((bf16[3,1024,128]{2,1,0:T(8,128)(2,1)S(1)}, bf16[3,1024,128]{2,1,0:T(8,128)(2,1)}, u32[]{:S(2)}, u32[]{:S(2)}) %collective-permute-start) | collective-permute-done | bytes 786464 | tf_op jit(solution)/shard_map/ppermute | solution.py:304
  50.9 3.2 %collective-permute-done.1.q2 = bf16[3,1024,128]{2,1,0:T(8,128)(2,1)} collective-permute-done((bf16[3,1024,128]{2,1,0:T(8,128)(2,1)S(1)}, bf16[3,1024,128]{2,1,0:T(8,128)(2,1)}, u32[]{:S(2)}, u32[]{:S(2)}) %collective-permute-start.1) | collective-permute-done | bytes 786464 | tf_op jit(solution)/shard_map/ppermute | solution.py:304
  54.1 2.7 collective-permute-start.3
  56.8 3.6 %collective-permute-start.5 = (bf16[2,512,256]{2,1,0:T(8,128)(2,1)S(1)}, bf16[2,512,256]{2,1,0:T(8,128)(2,1)S(1)}, u32[]{:S(2)}, u32[]{:S(2)}) collective-permute-start(bf16[2,512,256]{2,1,0:T(8,128)(2,1)S(1)} %get-tuple-element.44), channel_id=1, source_target_pairs={{0,48},{8,56},{16,0},{24,8},{32,16},{40,24},{48,32},{56,40},{1,49}... | collective-permute-start | bytes 1572872 | tf_op jit(solution)/shard_map/ppermute | solution.py:304
  60.4 56.4 %collective-permute-done.4 = bf16[2,512,256]{2,1,0:T(8,128)(2,1)S(1)} collective-permute-done((bf16[2,512,256]{2,1,0:T(8,128)(2,1)S(1)}, bf16[2,512,256]{2,1,0:T(8,128)(2,1)S(1)}, u32[]{:S(2)}, u32[]{:S(2)}) %collective-permute-start.4) | collective-permute-done | bytes 524320 | tf_op jit(solution)/shard_map/ppermute | solution.py:304
  119.0 4.8 %all-to-all-start.1 = ((bf16[4,3,512,256]{3,2,1,0:T(8,128)(2,1)}), bf16[4,3,512,256]{3,2,1,0:T(8,128)(2,1)}, u32[]{:S(2)}, u32[]{:S(2)}) async-start(bf16[4,3,512,256]{3,2,1,0:T(8,128)(2,1)} %pad_maximum_fusion), calls=%async_computation.1 | async-start | bytes 6291456 | tf_op jit(solution)/shard_map/all_to_all | solution.py:308
  125.7 19.7 %near.1 = (bf16[3,144,1024]{2,1,0:T(8,128)(2,1)S(1)}, bf16[3,144,1024]{2,1,0:T(8,128)(2,1)}, bf16[3,144,1024]{2,1,0:T(8,128)(2,1)}) custom-call(s32[12]{0:T(128)S(1)} %bitcast.25, bf16[4,5,512,256]{3,2,1,0:T(8,128)(2,1)} %all-to-all-done.here, bf16[384,256]{1,0:T(8,128)(2,1)S(1)} %bitcast.24, bf16[3,1024,128]{2,1,0:T(8,128)(2,1)S(1)} %bitcast.23, ...), custom_call_target="tpu_custom_call" | custom-call | flops 5242880 | bytes 5120 | tf_op jit(solution)/shard_map/near/pallas_call | solution.py:225
  145.4 3.7 %collective-permute-start.8 = (bf16[3,144,1024]{2,1,0:T(8,128)(2,1)}, bf16[3,144,1024]{2,1,0:T(8,128)(2,1)}, u32[]{:S(2)}, u32[]{:S(2)}) collective-permute-start(bf16[3,144,1024]{2,1,0:T(8,128)(2,1)} %get-tuple-element.59), channel_id=1, source_target_pairs={{0,8},{8,16},{16,24},{24,32},{32,40},{40,48},{48,56},{56,0},{1,9},... | collective-permute-start | bytes 2654216 | tf_op jit(solution)/shard_map/ppermute | solution.py:304
  149.2 9.3 %far.1 = (bf16[3,144,1024]{2,1,0:T(8,128)(2,1)S(1)}, bf16[3,144,1024]{2,1,0:T(8,128)(2,1)S(1)}) custom-call(s32[8]{0:T(128)S(1)} %slice.18.tags, bf16[4,5,512,256]{3,2,1,0:T(8,128)(2,1)} %all-to-all-done.here, bf16[3,1024,128]{2,1,0:T(8,128)(2,1)S(1)} %collective-permute-done.6.q_up, bf16[3,1024,128]{2,1,0:T(8,128)(2,1)S(1)} %collective-permute-done.7.q_down), custom_call_target="tpu_custom_call" | custom-call | flops 3145728 | bytes 3072 | tf_op jit(solution)/shard_map/far/pallas_call | solution.py:225
  160.3 6.2 %collective-permute-done.8.refs_1_ = bf16[3,144,1024]{2,1,0:T(8,128)(2,1)} collective-permute-done((bf16[3,144,1024]{2,1,0:T(8,128)(2,1)}, bf16[3,144,1024]{2,1,0:T(8,128)(2,1)}, u32[]{:S(2)}, u32[]{:S(2)}) %collective-permute-start.8) | collective-permute-done | bytes 884768 | tf_op jit(solution)/shard_map/ppermute | solution.py:304
  166.5 2.4 collective-permute-done.9.refs_2_
  169.0 16.8 %move.1 = (bf16[3,144,1024]{2,1,0:T(8,128)(2,1)}, bf16[3,144,1024]{2,1,0:T(8,128)(2,1)}) custom-call(s32[16]{0:T(128)S(1)} %slice.19.tags, bf16[4,3,512,256]{3,2,1,0:T(8,128)(2,1)} %all-to-all-done.1.moved, bf16[3,1024,128]{2,1,0:T(8,128)(2,1)S(1)} %collective-permute-done.6.q_up, bf16[3,1024,128]{2,1,0:T(8,128)(2,1)S(1)} %collective-permute-done.7.q_down, ...), custom_call_target="tpu_custom_call" | custom-call | flops 4718592 | bytes 4608 | tf_op jit(solution)/shard_map/move/pallas_call | solution.py:225
  189.5 20.7 %collective-permute-done.10.refs_3_ = bf16[3,144,1024]{2,1,0:T(8,128)(2,1)S(1)} collective-permute-done((bf16[3,144,1024]{2,1,0:T(8,128)(2,1)}, bf16[3,144,1024]{2,1,0:T(8,128)(2,1)S(1)}, u32[]{:S(2)}, u32[]{:S(2)}) %collective-permute-start.10) | collective-permute-done | bytes 884768 | tf_op jit(solution)/shard_map/ppermute | solution.py:304
  210.2 14.9 %collective-permute-done.11.refs_4_ = bf16[3,144,1024]{2,1,0:T(8,128)(2,1)S(1)} collective-permute-done((bf16[3,144,1024]{2,1,0:T(8,128)(2,1)}, bf16[3,144,1024]{2,1,0:T(8,128)(2,1)S(1)}, u32[]{:S(2)}, u32[]{:S(2)}) %collective-permute-start.11) | collective-permute-done | bytes 884768 | tf_op jit(solution)/shard_map/ppermute | solution.py:304
  226.0 3.1 %last.1.context_ref = bf16[384,1024]{1,0:T(8,128)(2,1)S(1)} custom-call(bf16[3,144,1024]{2,1,0:T(8,128)(2,1)S(1)} %get-tuple-element.53.refs_0_, bf16[3,144,1024]{2,1,0:T(8,128)(2,1)} %collective-permute-done.8.refs_1_, bf16[3,144,1024]{2,1,0:T(8,128)(2,1)} %collective-permute-done.9.refs_2_, bf16[3,144,1024]{2,1,0:T(8,128)(2,1)} %copy-done.3, ...), custom_call_target="tpu_custom_call" | custom-call | tf_op jit(solution)/shard_map/last/pallas_call | solution.py:293
  229.0 27.2 %all-gather.5.cloned.1.call-done.weight_ref = bf16[1024,4096]{1,0:T(8,128)(2,1)} async-done(((bf16[1024,1024]{1,0:T(8,128)(2,1)}), bf16[1024,4096]{1,0:T(8,128)(2,1)}) %all-gather.5.cloned.1.call-update) | async-done | bytes 8388624 | tf_op jit(solution)/shard_map/all_gather | solution.py:398
  256.2 4.3 %theirs.1 = bf16[4,384,512]{2,1,0:T(8,128)(2,1)S(1)} custom-call(s32[1]{0:T(128)} %bitcast.12.core_ref, bf16[384,1024]{1,0:T(8,128)(2,1)S(1)} %last.1.context_ref, bf16[1024,4096]{1,0:T(8,128)(2,1)} %all-gather.5.cloned.1.call-done.weight_ref), custom_call_target="tpu_custom_call" | custom-call | flops 1610612736 | bytes 4194304 | tf_op jit(solution)/shard_map/theirs/pallas_call | solution.py:267
  261.3 4.3 %ours.1 = bf16[4,384,512]{2,1,0:T(8,128)(2,1)S(1)} custom-call(s32[1]{0:T(128)} %bitcast.core_ref, bf16[384,1024]{1,0:T(8,128)(2,1)S(1)} %last.1.context_ref, bf16[1024,4096]{1,0:T(8,128)(2,1)} %all-gather.5.cloned.1.call-done.weight_ref), custom_call_target="tpu_custom_call" | custom-call | flops 1610612736 | bytes 4194304 | tf_op jit(solution)/shard_map/ours/pallas_call | solution.py:267
  266.0 24.3 %all_to_all.15 = bf16[4,384,512]{2,1,0:T(8,128)(2,1)S(1)} all-to-all(bf16[4,384,512]{2,1,0:T(8,128)(2,1)S(1)} %add_convert_fusion), channel_id=1, replica_groups=mesh['x'=4,'z'=8,'y'=4,'core'=2] {'y'}, dimensions={0} | all-to-all | bytes 3145728 | tf_op jit(solution)/shard_map/all_to_all | solution.py:425
  (70 shorter events, 18.0 us)
Async XLA Ops:
  19.5 5.3 %copy-start.5 = (bf16[384,1024]{1,0:T(8,128)(2,1)S(1)}, bf16[384,1024]{1,0:T(8,128)(2,1)}, u32[]{:S(2)}) copy-start(bf16[384,1024]{1,0:T(8,128)(2,1)} %param.11) | copy-start | bytes 2359300
  19.5 99.5 %all-to-all-start = ((bf16[4,5,512,256]{3,2,1,0:T(8,128)(2,1)}), bf16[4,5,512,256]{3,2,1,0:T(8,128)(2,1)}, u32[]{:S(2)}, u32[]{:S(2)}) async-start(bf16[4,5,512,256]{3,2,1,0:T(8,128)(2,1)} %bitcast.26), calls=%async_computation | async-start | bytes 10485760 | tf_op jit(solution)/shard_map/all_to_all | solution.py:308
  24.7 135.6 %all-gather.3.cloned.1.call-start = ((), (), s32[]{:S(2)}) async-start(), calls=%async_computation.3 | async-start | bytes 2359296 | tf_op jit(solution)/shard_map/all_gather | solution.py:339
  25.1 25.8 %collective-permute-start = (bf16[3,1024,128]{2,1,0:T(8,128)(2,1)S(1)}, bf16[3,1024,128]{2,1,0:T(8,128)(2,1)}, u32[]{:S(2)}, u32[]{:S(2)}) collective-permute-start(bf16[3,1024,128]{2,1,0:T(8,128)(2,1)S(1)} %bitcast.21), channel_id=1, source_target_pairs={{0,56},{8,0},{16,8},{24,16},{32,24},{40,32},{48,40},{56,48},{1,57}... | collective-permute-start | bytes 2359304 | tf_op jit(solution)/shard_map/ppermute | solution.py:304
  31.9 22.2 %collective-permute-start.1 = (bf16[3,1024,128]{2,1,0:T(8,128)(2,1)S(1)}, bf16[3,1024,128]{2,1,0:T(8,128)(2,1)}, u32[]{:S(2)}, u32[]{:S(2)}) collective-permute-start(bf16[3,1024,128]{2,1,0:T(8,128)(2,1)S(1)} %bitcast.22), channel_id=1, source_target_pairs={{0,8},{8,16},{16,24},{24,32},{32,40},{40,48},{48,56},{56,0},{1,9},... | collective-permute-start | bytes 2359304 | tf_op jit(solution)/shard_map/ppermute | solution.py:304
  54.1 62.8 %collective-permute-start.2 = (bf16[4,512,256]{2,1,0:T(8,128)(2,1)S(1)}, bf16[4,512,256]{2,1,0:T(8,128)(2,1)S(1)}, u32[]{:S(2)}, u32[]{:S(2)}) collective-permute-start(bf16[4,512,256]{2,1,0:T(8,128)(2,1)S(1)} %get-tuple-element.41), channel_id=1, source_target_pairs={{0,8},{8,16},{16,24},{24,32},{32,40},{40,48},{48,56},{56,0},{1,9},... | collective-permute-start | bytes 3145736 | tf_op jit(solution)/shard_map/ppermute | solution.py:304
  54.1 62.8 %collective-permute-start.3 = (bf16[4,512,256]{2,1,0:T(8,128)(2,1)S(1)}, bf16[4,512,256]{2,1,0:T(8,128)(2,1)S(1)}, u32[]{:S(2)}, u32[]{:S(2)}) collective-permute-start(bf16[4,512,256]{2,1,0:T(8,128)(2,1)S(1)} %get-tuple-element.42), channel_id=1, source_target_pairs={{0,56},{8,0},{16,8},{24,16},{32,24},{40,32},{48,40},{56,48},{1,57}... | collective-permute-start | bytes 3145736 | tf_op jit(solution)/shard_map/ppermute | solution.py:304
  56.8 60.0 %collective-permute-start.4 = (bf16[2,512,256]{2,1,0:T(8,128)(2,1)S(1)}, bf16[2,512,256]{2,1,0:T(8,128)(2,1)S(1)}, u32[]{:S(2)}, u32[]{:S(2)}) collective-permute-start(bf16[2,512,256]{2,1,0:T(8,128)(2,1)S(1)} %get-tuple-element.43), channel_id=1, source_target_pairs={{0,16},{8,24},{16,32},{24,40},{32,48},{40,56},{48,0},{56,8},{1,17}... | collective-permute-start | bytes 1572872 | tf_op jit(solution)/shard_map/ppermute | solution.py:304
  56.8 60.0 %collective-permute-start.5 = (bf16[2,512,256]{2,1,0:T(8,128)(2,1)S(1)}, bf16[2,512,256]{2,1,0:T(8,128)(2,1)S(1)}, u32[]{:S(2)}, u32[]{:S(2)}) collective-permute-start(bf16[2,512,256]{2,1,0:T(8,128)(2,1)S(1)} %get-tuple-element.44), channel_id=1, source_target_pairs={{0,48},{8,56},{16,0},{24,8},{32,16},{40,24},{48,32},{56,40},{1,49}... | collective-permute-start | bytes 1572872 | tf_op jit(solution)/shard_map/ppermute | solution.py:304
  119.0 6.6 %copy-start.6 = (s32[36]{0:T(128)S(1)}, s32[36]{0:T(128)}, u32[]{:S(2)}) copy-start(s32[36]{0:T(128)} %constant.112.clone) | copy-start | bytes 436
  119.0 6.6 %copy-start.7 = (s32[36]{0:T(128)S(1)}, s32[36]{0:T(128)}, u32[]{:S(2)}) copy-start(s32[36]{0:T(128)} %constant.114.clone) | copy-start | bytes 436
  119.0 6.6 %copy-start.8 = (s32[36]{0:T(128)S(1)}, s32[36]{0:T(128)}, u32[]{:S(2)}) copy-start(s32[36]{0:T(128)} %constant.117) | copy-start | bytes 436
  119.0 6.7 %copy-start.2 = (bf16[384,1,256]{2,0,1:T(8,128)(2,1)S(1)}, bf16[384,1,256]{2,0,1:T(8,128)(2,1)}, u32[]{:S(2)}) copy-start(bf16[384,1,256]{2,0,1:T(8,128)(2,1)} %param.12) | copy-start | bytes 589828
  119.0 49.9 %all-to-all-start.1 = ((bf16[4,3,512,256]{3,2,1,0:T(8,128)(2,1)}), bf16[4,3,512,256]{3,2,1,0:T(8,128)(2,1)}, u32[]{:S(2)}, u32[]{:S(2)}) async-start(bf16[4,3,512,256]{3,2,1,0:T(8,128)(2,1)} %pad_maximum_fusion), calls=%async_computation.1 | async-start | bytes 6291456 | tf_op jit(solution)/shard_map/all_to_all | solution.py:308
  123.8 132.4 %all-gather.5.cloned.1.call-start = ((), (), s32[]{:S(2)}) async-start(), calls=%async_computation.4 | async-start | bytes 10485760 | tf_op jit(solution)/shard_map/all_gather | solution.py:398
  124.0 21.4 %collective-permute-start.6 = (bf16[3,1024,128]{2,1,0:T(8,128)(2,1)}, bf16[3,1024,128]{2,1,0:T(8,128)(2,1)S(1)}, u32[]{:S(2)}, u32[]{:S(2)}) collective-permute-start(bf16[3,1024,128]{2,1,0:T(8,128)(2,1)} %collective-permute-done.q1), channel_id=1, source_target_pairs={{0,56},{8,0},{16,8},{24,16},{32,24},{40,32},{48,40},{56,48},{1,57}... | collective-permute-start | bytes 2359304 | tf_op jit(solution)/shard_map/ppermute | solution.py:304
  124.1 21.4 %collective-permute-start.7 = (bf16[3,1024,128]{2,1,0:T(8,128)(2,1)}, bf16[3,1024,128]{2,1,0:T(8,128)(2,1)S(1)}, u32[]{:S(2)}, u32[]{:S(2)}) collective-permute-start(bf16[3,1024,128]{2,1,0:T(8,128)(2,1)} %collective-permute-done.1.q2), channel_id=1, source_target_pairs={{0,8},{8,16},{16,24},{24,32},{32,40},{40,48},{48,56},{56,0},{1,9},... | collective-permute-start | bytes 2359304 | tf_op jit(solution)/shard_map/ppermute | solution.py:304
  145.4 21.1 %collective-permute-start.8 = (bf16[3,144,1024]{2,1,0:T(8,128)(2,1)}, bf16[3,144,1024]{2,1,0:T(8,128)(2,1)}, u32[]{:S(2)}, u32[]{:S(2)}) collective-permute-start(bf16[3,144,1024]{2,1,0:T(8,128)(2,1)} %get-tuple-element.59), channel_id=1, source_target_pairs={{0,8},{8,16},{16,24},{24,32},{32,40},{40,48},{48,56},{56,0},{1,9},... | collective-permute-start | bytes 2654216 | tf_op jit(solution)/shard_map/ppermute | solution.py:304
  149.1 19.8 %collective-permute-start.9 = (bf16[3,144,1024]{2,1,0:T(8,128)(2,1)}, bf16[3,144,1024]{2,1,0:T(8,128)(2,1)}, u32[]{:S(2)}, u32[]{:S(2)}) collective-permute-start(bf16[3,144,1024]{2,1,0:T(8,128)(2,1)} %get-tuple-element.60), channel_id=1, source_target_pairs={{0,56},{8,0},{16,8},{24,16},{32,24},{40,32},{48,40},{56,48},{1,57}... | collective-permute-start | bytes 2654216 | tf_op jit(solution)/shard_map/ppermute | solution.py:304
  158.4 0.9 copy-start
  185.8 24.4 %collective-permute-start.10 = (bf16[3,144,1024]{2,1,0:T(8,128)(2,1)}, bf16[3,144,1024]{2,1,0:T(8,128)(2,1)S(1)}, u32[]{:S(2)}, u32[]{:S(2)}) collective-permute-start(bf16[3,144,1024]{2,1,0:T(8,128)(2,1)} %get-tuple-element.66), channel_id=1, source_target_pairs={{0,16},{8,24},{16,32},{24,40},{32,48},{40,56},{48,0},{56,8},{1,17}... | collective-permute-start | bytes 2654216 | tf_op jit(solution)/shard_map/ppermute | solution.py:304
  188.1 36.9 %collective-permute-start.11 = (bf16[3,144,1024]{2,1,0:T(8,128)(2,1)}, bf16[3,144,1024]{2,1,0:T(8,128)(2,1)S(1)}, u32[]{:S(2)}, u32[]{:S(2)}) collective-permute-start(bf16[3,144,1024]{2,1,0:T(8,128)(2,1)} %get-tuple-element.67), channel_id=1, source_target_pairs={{0,48},{8,56},{16,0},{24,8},{32,16},{40,24},{48,32},{56,40},{1,49}... | collective-permute-start | bytes 2654216 | tf_op jit(solution)/shard_map/ppermute | solution.py:304
  210.2 14.9 %copy-start.3 = (bf16[3,144,1024]{2,1,0:T(8,128)(2,1)}, bf16[3,144,1024]{2,1,0:T(8,128)(2,1)S(1)}, u32[]{:S(2)}) copy-start(bf16[3,144,1024]{2,1,0:T(8,128)(2,1)S(1)} %collective-permute-done.10.refs_3_) | copy-start | bytes 2654212
  260.5 5.1 %collective-permute-start.12 = (bf16[4,384,512]{2,1,0:T(8,128)(2,1)S(1)}, bf16[4,384,512]{2,1,0:T(8,128)(2,1)S(1)}, u32[]{:S(2)}, u32[]{:S(2)}) collective-permute-start(bf16[4,384,512]{2,1,0:T(8,128)(2,1)S(1)} %theirs.1), channel_id=1, source_target_pairs={{0,1},{1,0},{2,3},{3,2},{4,5},{5,4},{6,7},{7,6},{8,9},{9,8},{10,11... | collective-permute-start | bytes 4718600 | tf_op jit(solution)/shard_map/ppermute | solution.py:422
  (2 other events, 1.8 us)
Sparse Core Ops, SparseCore 0:
  32.1 71.6 all-gather.2
  169.1 87.0 all-gather.4

commit v5 on v4

--- a/solution.py
+++ b/solution.py
@@ -74,10 +74,9 @@
 
 
 def absorb(keys, values_t, query_ref, group, cols, acc, top, total, causal=False):
-    which, lane = group
     scores = lax.dot_general(
         keys,
-        query_ref[lane, cols, :],
+        query_ref[group, cols, :],
         (((1,), (1,)), ((), ())),
         preferred_element_type=jnp.float32,
     )
@@ -85,13 +84,13 @@
         key = lax.broadcasted_iota(jnp.int32, scores.shape, 0)
         token = lax.broadcasted_iota(jnp.int32, scores.shape, 1)
         scores = jnp.where(key <= token, scores, NEG)
-    old = top[which, :, cols]
+    old = top[group, :, cols]
     new = jnp.maximum(old, jnp.max(scores, axis=0, keepdims=True))
     weights = jnp.exp2((scores - new) * SCALE)
     keep = jnp.exp2((old - new) * SCALE)
-    top[which, :, cols] = new
-    total[which, :, cols] = total[which, :, cols] * keep + jnp.sum(weights, axis=0, keepdims=True)
-    acc[which, :, cols] = acc[which, :, cols] * keep + jnp.dot(
+    top[group, :, cols] = new
+    total[group, :, cols] = total[group, :, cols] * keep + jnp.sum(weights, axis=0, keepdims=True)
+    acc[group, :, cols] = acc[group, :, cols] * keep + jnp.dot(
         values_t, weights.astype(jnp.bfloat16), preferred_element_type=jnp.float32
     )
 
@@ -109,24 +108,24 @@
     ]
 
 
-def absorb_all(tag_ref, first, copies, slot, buffer, query_ref, base, acc, top, total):
+def absorb_all(tag_ref, copies, buffer, query_ref, acc, top, total):
     for copy in copies:
         copy.wait()
 
     def step(i, carry):
-        tag = tag_ref[first + i]
+        tag = tag_ref[i]
 
         @pl.when(tag >= 0)
         def _():
-            keys = buffer[slot + i, :, 0:HD]
-            values_t = buffer[slot + i, :, HD : 2 * HD].T
+            keys = buffer[i, :, 0:HD]
+            values_t = buffer[i, :, HD : 2 * HD].T
             for part in range(ROWS // WIDTH):
                 cols = pl.ds(part * WIDTH, WIDTH)
-                absorb(keys, values_t, query_ref, (base + tag, tag), cols, acc, top, total)
+                absorb(keys, values_t, query_ref, tag, cols, acc, top, total)
 
         return carry
 
-    lax.fori_loop(0, NX, step, 0)
+    lax.fori_loop(0, len(copies), step, 0)
 
 
 def pack(level):
@@ -165,12 +164,12 @@
     return mixed / whole, level + jnp.log2(whole)
 
 
-def near_kernel(tags, here, own, q0, q1, q2, o0, o1, o2, buffer, sems, *state):
+def near_kernel(tags, here, own, query, o0, o1, o2, buffer, sems, *state):
     copies = fetches(here, [(i, k) for k in range(3) for i in range(NX)], buffer, sems)
     for copy in copies:
         copy.start()
     start(*state)
-    n = q0.shape[0]
+    n = o0.shape[0]
     for j in range(n):
         rows = slice(j * LQ, (j + 1) * LQ)
         keys = own[rows, 0:HD]
@@ -178,43 +177,35 @@
 
         def head(part, carry, j=j, keys=keys, values_t=values_t):
             cols = pl.ds(pl.multiple_of(part * LQ, LQ), LQ)
-            absorb(keys, values_t, q0, (j, j), cols, *state, causal=True)
+            absorb(keys, values_t, query, j, cols, *state, causal=True)
             return carry
 
         lax.fori_loop(0, GROUP, head, 0)
-    for k, query in enumerate((q0, q1, q2)):
-        slot = k * NX
-        absorb_all(tags, slot, copies[slot : slot + NX], slot, buffer, query, k * n, *state)
+    absorb_all(tags, copies, buffer, query, *state)
     for k, out_ref in enumerate((o0, o1, o2)):
         for j in range(n):
             store(out_ref, j, *state_of(k * n + j, *state))
 
 
-def far_kernel(tags, here, q_up, q_down, o_up, o_down, buffer, sems, *state):
+def far_kernel(tags, here, query, o_up, o_down, buffer, sems, *state):
     copies = fetches(here, [(i, k) for k in (3, 4) for i in range(NX)], buffer, sems)
     for copy in copies:
         copy.start()
     start(*state)
-    n = q_up.shape[0]
-    absorb_all(tags, 0, copies[0:4], 0, buffer, q_up, 0, *state)
-    absorb_all(tags, 4, copies[4:8], 4, buffer, q_down, n, *state)
+    absorb_all(tags, copies, buffer, query, *state)
+    n = o_up.shape[0]
     for j in range(n):
         store(o_up, j, *state_of(j, *state))
         store(o_down, j, *state_of(n + j, *state))
 
 
-def move_kernel(
-    tags, moved, q_up, q_down, so_far_up, so_far_down, o_up, o_down, buffer, sems, *state
-):
+def move_kernel(tags, moved, query, so_far_up, so_far_down, o_up, o_down, buffer, sems, *state):
     copies = fetches(moved, [(i, k) for k in range(3) for i in range(NX)], buffer, sems)
     for copy in copies:
         copy.start()
     start(*state)
-    n = q_up.shape[0]
-    absorb_all(tags, 0, copies[0:4], 0, buffer, q_up, 0, *state)
-    absorb_all(tags, 4, copies[4:8], 4, buffer, q_down, n, *state)
-    absorb_all(tags, 8, copies[8:12], 8, buffer, q_up, 0, *state)
-    absorb_all(tags, 12, [], 8, buffer, q_down, n, *state)
+    absorb_all(tags, copies, buffer, query, *state)
+    n = o_up.shape[0]
     for j in range(n):
         store(o_up, j, *merge([state_of(j, *state), load(so_far_up, j)]))
         store(o_down, j, *merge([state_of(n + j, *state), load(so_far_down, j)]))
@@ -256,36 +247,51 @@
             )
 
 
-def project_kernel(core_ref, context_ref, weight_ref, out_ref):
-    out_ref[0] = jnp.dot(
-        context_ref[...], weight_ref[...], preferred_element_type=jnp.float32
-    ).astype(jnp.bfloat16)
-
-
-def project(context, weight, core, name):
-    width = weight.shape[1] // (NY * NC)
+def project_kernel(place, context_ref, own_ref, before_ref, after_ref, top_ref, bottom_ref, out_ref):
+    x = place[1]
+
+    def put(index, products):
+        out_ref[lax.rem(index, NX)] = functools.reduce(jnp.add, products).astype(jnp.bfloat16)
+
+    def times(cols, weight_ref):
+        return jnp.dot(
+            context_ref[:, cols], weight_ref[...], preferred_element_type=jnp.float32
+        )
+
+    half = top_ref.shape[0]
+    everything = slice(None)
+    put(x, [times(everything, own_ref)])
+    put(x + NX - 1, [times(everything, before_ref)])
+    put(x + 1, [times(everything, after_ref)])
+    put(x + 2, [times(slice(0, half), top_ref), times(slice(half, None), bottom_ref)])
+
+
+def project(context, weights, core, x, name):
+    tile = 256
+    width = weights[0].shape[1] // NC
+    steps = width // tile
+
+    def tiles(weight):
+        return pl.BlockSpec((weight.shape[0], tile), lambda i, place: (0, steps * place[0] + i))
+
     return pl.pallas_call(
         project_kernel,
-        out_shape=jax.ShapeDtypeStruct((NY, context.shape[0], width), jnp.bfloat16),
+        out_shape=jax.ShapeDtypeStruct((NX, context.shape[0], width), jnp.bfloat16),
         grid_spec=pltpu.PrefetchScalarGridSpec(
             num_scalar_prefetch=1,
-            grid=(NY,),
-            in_specs=[
-                pl.BlockSpec(context.shape, lambda i, core_ref: (0, 0)),
-                pl.BlockSpec(
-                    (weight.shape[0], width), lambda i, core_ref: (0, NC * i + core_ref[0])
-                ),
-            ],
-            out_specs=pl.BlockSpec((1, context.shape[0], width), lambda i, core_ref: (i, 0, 0)),
+            grid=(steps,),
+            in_specs=[pl.BlockSpec(context.shape, lambda i, place: (0, 0))]
+            + [tiles(weight) for weight in weights],
+            out_specs=pl.BlockSpec((NX, context.shape[0], tile), lambda i, place: (0, 0, i)),
         ),
         compiler_params=pltpu.CompilerParams(vmem_limit_bytes=VMEM_LIMIT),
         cost_estimate=pl.CostEstimate(
-            flops=2 * context.shape[0] * weight.shape[0] * width * NY,
-            bytes_accessed=weight.shape[0] * width * NY * 2,
+            flops=2 * context.shape[0] * context.shape[1] * width * NX,
+            bytes_accessed=context.shape[1] * width * NX * 2,
             transcendentals=0,
         ),
         name=name,
-    )(core.reshape(1), context, weight)
+    )(jnp.stack([core, x]), context, *weights)
 
 
 def in_vmem(kernel, name, out, *arrays):
@@ -304,6 +310,10 @@
     return lax.ppermute(array, "z", [(i, (i + shift) % NZ) for i in range(NZ)])
 
 
+def along_x(array, shift):
+    return lax.ppermute(array, "x", [(i, (i + shift) % NX) for i in range(NX)])
+
+
 def over_x(items):
     return lax.all_to_all(items, "x", split_axis=0, concat_axis=0, tiled=True)
 
@@ -317,8 +327,6 @@
 
     q_own = queries.reshape(per_device, LQ, GROUP, HD).transpose(0, 2, 1, 3)
     q_own = q_own.reshape(per_device, ROWS, HD)
-    q_up = along_z(q_own, -1)
-    q_down = along_z(q_own, 1)
     owners, local_rows = request_tables(lists, passage_slot, question_slot, per_device, pass_dev)
     mine = jnp.sum(jnp.where(owners == x * NZ + z, local_rows, 0), axis=1).reshape(NX, NZ)
     target_z = (z + jnp.array(STAY + MOVE, jnp.int32)) % NZ
@@ -327,43 +335,45 @@
         axis=2,
     )
     stay = len(STAY)
-    (here,) = take_rows(cache, rows[:, :stay].reshape(-1), (NX * stay,))
+    moving = take_rows(cache, rows[:, stay:].T.reshape(-1), (4, 4, 2, 2))
+    moving, staying = lax.optimization_barrier((moving, rows[:, :stay].reshape(-1)))
+    (here,) = take_rows(cache, staying, (NX * stay,))
     here = over_x(here.reshape(NX, stay, PLEN, 2 * HD))
-    moving = take_rows(cache, rows[:, stay:].T.reshape(-1), (4, 4, 2, 2))
-    (up3, down3, up4, down4), q_up, q_down = lax.optimization_barrier((moving, q_up, q_down))
+    up3, down3, up4, down4 = moving
     up3 = along_z(up3, 1)
     down3 = along_z(down3, -1)
     up4 = along_z(up4, 2)
     down4 = along_z(down4, -2)
-    moved = jnp.stack([up3, down3, jnp.concatenate([up4, down4], axis=0)], axis=1)
-    weight = lax.all_gather(out_weight, "z", axis=1, tiled=True)
-    moved, here, q_up, q_down = lax.optimization_barrier((moved, here, q_up, q_down))
-    moved = over_x(moved)
+    up3, down3, up4, down4, q_own, out_weight = lax.optimization_barrier(
+        (up3, down3, up4, down4, q_own, out_weight)
+    )
+    q_up = along_z(q_own, -1)
+    q_down = along_z(q_own, 1)
     q_up2 = along_z(q_up, -1)
     q_down2 = along_z(q_down, 1)
-
-    four = range(NX)
-    slots = (
-        [(d, i, 0) for d in STAY for i in four]
-        + [(2, i, -1) for i in four]
-        + [(-2, i, 1) for i in four]
-        + [(2, i, -2) for i in four]
-        + [(-2, i, 2) for i in four]
-    )
-    count = len(slots)
-    slot_question = (z + jnp.array([s[0] for s in slots], jnp.int32)) % NZ
-    slot_owner = jnp.array([s[1] for s in slots], jnp.int32) * NZ + (
-        z + jnp.array([s[2] for s in slots], jnp.int32)
-    ) % NZ
-    index = jnp.arange(count)
-    absent = jnp.where(x < 2, index >= count - NX, (index >= count - 2 * NX) & (index < count - NX))
+    weight = lax.all_gather(out_weight, "z", axis=1, tiled=True)
+    moved = jnp.stack([up3, down3, jnp.concatenate([up4, down4], axis=0)], axis=1)
+    moved, here = lax.optimization_barrier((moved, here))
+    moved = over_x(moved)
+
+    slots = [(d, i, 0, k) for k, d in enumerate(STAY[:3]) for i in range(NX)]
+    slots += [(d, i, 0, k) for k, d in enumerate(STAY[3:]) for i in range(NX)]
+    slots += [(2, i, -1, 0) for i in range(NX)]
+    slots += [(-2, i, 1, 1) for i in range(NX)]
+    slots += [(2, i, -2, 0) for i in range(NX)]
+    slots = jnp.array(slots, jnp.int32)
+    last = jnp.arange(slots.shape[0]) >= slots.shape[0] - NX
+    turn = jnp.where(last & (x >= 2), -1, 1)
+    slot_question = (z + slots[:, 0] * turn) % NZ
+    slot_owner = slots[:, 1] * NZ + (z + slots[:, 2] * turn) % NZ
+    base = per_device * jnp.where(turn < 0, 1, slots[:, 3])
     column = lax.dynamic_index_in_dim(owners.reshape(NX, NZ, -1), x, 0, keepdims=False)
     number = jnp.arange(column.shape[1], dtype=jnp.int32) // TOPP + 1
     hit = (slot_question[:, None, None] == jnp.arange(NZ)[None, :, None]) & (
         slot_owner[:, None, None] == column[None, :, :]
     )
     tags = jnp.sum(jnp.where(hit, number[None, None, :], 0), axis=(1, 2)) - 1
-    tags = jnp.where(absent, -1, tags)
+    tags = jnp.where(tags < 0, -1, tags + base)
 
     split = NX * stay
     near = attention(
@@ -371,7 +381,7 @@
         "near",
         tags[: 3 * NX],
         here,
-        [own, q_own, q_up, q_down],
+        [own, jnp.concatenate([q_own, q_up, q_down])],
         per_device,
         3,
         3 * NX,
@@ -381,12 +391,13 @@
     own_part, near_up, near_down = near
     home_up = along_z(near_up, 1)
     home_down = along_z(near_down, -1)
+    q_far = jnp.concatenate([q_up2, q_down2])
     far = attention(
         far_kernel,
         "far",
         tags[3 * NX : split],
         here,
-        [q_up2, q_down2],
+        [q_far],
         per_device,
         2,
         2 * NX,
@@ -395,18 +406,22 @@
     weight, moved, far, home_up, home_down = lax.optimization_barrier(
         (weight, moved, far, home_up, home_down)
     )
-    weight = lax.all_gather(weight, "x", axis=1, tiled=True)
+    before = along_x(weight, 1)
+    after = along_x(weight, -1)
     far_up, far_down = attention(
         move_kernel,
         "move",
         tags[split:],
         moved,
-        [q_up2, q_down2, *far],
+        [q_far, *far],
         per_device,
         2,
         3 * NX,
         9,
     )
+    far_up = along_z(far_up, 2)
+    far_down = along_z(far_down, -2)
+    before, after, far_up, far_down = lax.optimization_barrier((before, after, far_up, far_down))
     context = in_vmem(
         last_kernel,
         "last",
@@ -414,13 +429,15 @@
         own_part,
         home_up,
         home_down,
-        along_z(far_up, 2),
-        along_z(far_down, -2),
+        far_up,
+        far_down,
     )
     core = lax.axis_index("core")
-    theirs = project(context, weight, 1 - core, "theirs")
+    half = weight.shape[0] // 2
+    weights = (weight, before, after, along_x(before[:half], 1), along_x(after[half:], -1))
+    theirs = project(context, weights, 1 - core, x, "theirs")
     theirs = lax.ppermute(theirs, "core", [(0, 1), (1, 0)])
-    ours = project(context, weight, core, "ours")
+    ours = project(context, weights, core, x, "ours")
     chip = (ours.astype(jnp.float32) + theirs.astype(jnp.float32)).astype(jnp.bfloat16)
     chips = lax.all_to_all(chip, "y", split_axis=0, concat_axis=0, tiled=True)
     return jnp.sum(chips.astype(jnp.float32), axis=0).astype(jnp.bfloat16)

time: 299 us -> 295 us (0.987)
  waiting for transfers between devices: 147 us -> 117 us
  starting transfers between devices: 32.8 us -> 45.4 us
  local copies, waits for them, and re-layouts: 3.85 us -> 12.2 us
  other arithmetic: 10.5 us -> 16.2 us
    all_gather x1 -> x0, waiting for transfers between devices: 27.2 us -> none  [body(): weight = lax.all_gather(weight, 'x', axis=1, tiled=True)]
    ppermute x12, waiting for transfers between devices: 120 us -> 97.4 us  [along_z(): return lax.ppermute(array, 'z', [(i, (i + shift) % NZ) for i in range(NZ)])]
    ppermute x0 -> x4, waiting for transfers between devices: none -> 19.1 us  [along_x(): return lax.ppermute(array, 'x', [(i, (i + shift) % NX) for i in range(NX)])]
    ppermute x12, starting transfers between devices: 21.9 us -> 28 us  [along_z(): return lax.ppermute(array, 'z', [(i, (i + shift) % NZ) for i in range(NZ)])]
    ppermute x0 -> x4, starting transfers between devices: none -> 5.79 us  [along_x(): return lax.ppermute(array, 'x', [(i, (i + shift) % NX) for i in range(NX)])]
    unnamed x19 -> x44, local copies, waits for them, and re-layouts: 2.94 us -> 7.79 us
  transfers between devices with their start and end apart: 17 -> 20, of which waited for: 8 -> 9; matrix products, arithmetic and copies ran while one was open for 1% -> 4% of each run, Pallas kernels for 19% -> 18%
where the time goes in v5:
time: 295 us; the launch traced here: 294 us
  waiting for transfers between devices  117 us (40%)
  Pallas kernels  66.4 us (23%)
  starting transfers between devices  45.4 us (15%)
  blocking collectives  23.9 us (8%)
  other arithmetic  16.2 us (5%)
  between operations  13.7 us (5%)
  local copies, waits for them, and re-layouts  12.2 us (4%)
    ppermute x12, waiting for transfers between devices, along_z(): return lax.ppermute(array, 'z', [(i, (i + shift) % NZ) for i in range(NZ)])  97.4 us
    pallas_call x3, Pallas kernels, attention(): pl.pallas_call(kernel, out_shape=(jax.ShapeDtypeStruct((n, HD + PACK, ROW...  44.7 us
    ppermute x12, starting transfers between devices, along_z(): return lax.ppermute(array, 'z', [(i, (i + shift) % NZ) for i in range(NZ)])  28 us
    all_to_all x1, blocking collectives, body(): chips = lax.all_to_all(chip, 'y', split_axis=0, concat_axis=0, tiled=True)  23.9 us
    ppermute x4, waiting for transfers between devices, along_x(): return lax.ppermute(array, 'x', [(i, (i + shift) % NX) for i in range(NX)])  19.1 us
    all_to_all x2, starting transfers between devices, over_x(): return lax.all_to_all(items, 'x', split_axis=0, concat_axis=0, tiled=True)  10.1 us
    pallas_call x2, Pallas kernels, project(): pl.pallas_call(project_kernel, out_shape=jax.ShapeDtypeStruct((NX, contex...  9.9 us
    pallas_call x2, Pallas kernels, take_rows(): pl.pallas_call(row_copies, out_shape=tuple((jax.ShapeDtypeStruct((n,) + c...  8.7 us
  transfers between devices with their start and end apart: 20, of which 9 were waited for; matrix products, arithmetic and copies ran while one was open for 4% of the time, Pallas kernels for 18%

profile of v5, /device:TPU:1, one launch (start us, length us, event | category | flops | bytes accessed | tf_op | source)
XLA Modules:
  0.0 294.3 jit_solution(240706585766816818)
XLA Ops:
  16.6 5.9 %take_rows.3 = bf16[20,512,256]{2,1,0:T(8,128)(2,1)} custom-call(s32[20]{0:T(128)S(1)} %reshape.163.rows_ref, bf16[16,512,256]{2,1,0:T(8,128)(2,1)} %bitcast.24), custom_call_target="tpu_custom_call" | custom-call | tf_op jit(solution)/shard_map/take_rows/pallas_call | solution.py:61
  22.5 5.3 %all-to-all-start = ((bf16[4,5,512,256]{3,2,1,0:T(8,128)(2,1)}), bf16[4,5,512,256]{3,2,1,0:T(8,128)(2,1)}, u32[]{:S(2)}, u32[]{:S(2)}) async-start(bf16[4,5,512,256]{3,2,1,0:T(8,128)(2,1)} %bitcast.22), calls=%async_computation | async-start | bytes 10485760 | tf_op jit(solution)/shard_map/all_to_all | solution.py:318
  30.3 3.7 %collective-permute-start.1 = (bf16[4,512,256]{2,1,0:T(8,128)(2,1)S(1)}, bf16[4,512,256]{2,1,0:T(8,128)(2,1)S(1)}, u32[]{:S(2)}, u32[]{:S(2)}) collective-permute-start(bf16[4,512,256]{2,1,0:T(8,128)(2,1)S(1)} %get-tuple-element.49), channel_id=1, source_target_pairs={{0,56},{8,0},{16,8},{24,16},{32,24},{40,32},{48,40},{56,48},{1,57}... | collective-permute-start | bytes 3145736 | tf_op jit(solution)/shard_map/ppermute | solution.py:310
  34.0 3.6 %collective-permute-start.3 = (bf16[2,512,256]{2,1,0:T(8,128)(2,1)S(1)}, bf16[2,512,256]{2,1,0:T(8,128)(2,1)S(1)}, u32[]{:S(2)}, u32[]{:S(2)}) collective-permute-start(bf16[2,512,256]{2,1,0:T(8,128)(2,1)S(1)} %get-tuple-element.51), channel_id=1, source_target_pairs={{0,48},{8,56},{16,0},{24,8},{32,16},{40,24},{48,32},{56,40},{1,49}... | collective-permute-start | bytes 1572872 | tf_op jit(solution)/shard_map/ppermute | solution.py:310
  39.9 29.6 %collective-permute-done.2 = bf16[2,512,256]{2,1,0:T(8,128)(2,1)S(1)} collective-permute-done((bf16[2,512,256]{2,1,0:T(8,128)(2,1)S(1)}, bf16[2,512,256]{2,1,0:T(8,128)(2,1)S(1)}, u32[]{:S(2)}, u32[]{:S(2)}) %collective-permute-start.2) | collective-permute-done | bytes 524320 | tf_op jit(solution)/shard_map/ppermute | solution.py:310
  69.5 8.9 %collective-permute-done.3 = bf16[2,512,256]{2,1,0:T(8,128)(2,1)S(1)} collective-permute-done((bf16[2,512,256]{2,1,0:T(8,128)(2,1)S(1)}, bf16[2,512,256]{2,1,0:T(8,128)(2,1)S(1)}, u32[]{:S(2)}, u32[]{:S(2)}) %collective-permute-start.3) | collective-permute-done | bytes 524320 | tf_op jit(solution)/shard_map/ppermute | solution.py:310
  80.7 3.6 %collective-permute-start.4 = (bf16[3,1024,128]{2,1,0:T(8,128)(2,1)}, bf16[3,1024,128]{2,1,0:T(8,128)(2,1)S(1)}, u32[]{:S(2)}, u32[]{:S(2)}) collective-permute-start(bf16[3,1024,128]{2,1,0:T(8,128)(2,1)} %bitcast.25), channel_id=1, source_target_pairs={{0,56},{8,0},{16,8},{24,16},{32,24},{40,32},{48,40},{56,48},{1,57}... | collective-permute-start | bytes 2359304 | tf_op jit(solution)/shard_map/ppermute | solution.py:310
  87.7 4.8 %all-to-all-start.1 = ((bf16[4,3,512,256]{3,2,1,0:T(8,128)(2,1)}), bf16[4,3,512,256]{3,2,1,0:T(8,128)(2,1)}, u32[]{:S(2)}, u32[]{:S(2)}) async-start(bf16[4,3,512,256]{3,2,1,0:T(8,128)(2,1)} %pad_maximum_fusion), calls=%async_computation.1 | async-start | bytes 6291456 | tf_op jit(solution)/shard_map/all_to_all | solution.py:318
  92.7 10.2 %collective-permute-done.4 = bf16[3,1024,128]{2,1,0:T(8,128)(2,1)S(1)} collective-permute-done((bf16[3,1024,128]{2,1,0:T(8,128)(2,1)}, bf16[3,1024,128]{2,1,0:T(8,128)(2,1)S(1)}, u32[]{:S(2)}, u32[]{:S(2)}) %collective-permute-start.4) | collective-permute-done | bytes 786464 | tf_op jit(solution)/shard_map/ppermute | solution.py:310
  102.8 3.4 %collective-permute-start.6 = (bf16[3,1024,128]{2,1,0:T(8,128)(2,1)S(1)}, bf16[3,1024,128]{2,1,0:T(8,128)(2,1)S(1)}, u32[]{:S(2)}, u32[]{:S(2)}) collective-permute-start(bf16[3,1024,128]{2,1,0:T(8,128)(2,1)S(1)} %collective-permute-done.4), channel_id=1, source_target_pairs={{0,56},{8,0},{16,8},{24,16},{32,24},{40,32},{48,40},{56,48},{1,57}... | collective-permute-start | bytes 2359304 | tf_op jit(solution)/shard_map/ppermute | solution.py:310
  109.3 21.2 %near.1 = (bf16[3,144,1024]{2,1,0:T(8,128)(2,1)S(1)}, bf16[3,144,1024]{2,1,0:T(8,128)(2,1)}, bf16[3,144,1024]{2,1,0:T(8,128)(2,1)}) custom-call(s32[12]{0:T(128)S(1)} %get-tuple-element.84.tags, bf16[4,5,512,256]{3,2,1,0:T(8,128)(2,1)} %all-to-all-done.here, bf16[384,256]{1,0:T(8,128)(2,1)S(1)} %bitcast.21, bf16[9,1024,128]{2,1,0:T(8,128)(2,1)} %pad_maximum_fusion.1.query), custom_call_target="tpu_custom_call" | custom-call | flops 5242880 | bytes 5120 | tf_op jit(solution)/shard_map/near/pallas_call | solution.py:216
  131.4 3.5 %collective-permute-start.8 = (bf16[3,144,1024]{2,1,0:T(8,128)(2,1)}, bf16[3,144,1024]{2,1,0:T(8,128)(2,1)}, u32[]{:S(2)}, u32[]{:S(2)}) collective-permute-start(bf16[3,144,1024]{2,1,0:T(8,128)(2,1)} %get-tuple-element.69), channel_id=1, source_target_pairs={{0,8},{8,16},{16,24},{24,32},{32,40},{40,48},{48,56},{56,0},{1,9},... | collective-permute-start | bytes 2654216 | tf_op jit(solution)/shard_map/ppermute | solution.py:310
  136.0 9.6 %far.1 = (bf16[3,144,1024]{2,1,0:T(8,128)(2,1)S(1)}, bf16[3,144,1024]{2,1,0:T(8,128)(2,1)S(1)}) custom-call(s32[8]{0:T(128)S(1)} %slice.40.tags, bf16[4,5,512,256]{3,2,1,0:T(8,128)(2,1)} %all-to-all-done.here, bf16[6,1024,128]{2,1,0:T(8,128)(2,1)S(1)} %constant_dynamic-update-slice_fusion.query), custom_call_target="tpu_custom_call" | custom-call | flops 3145728 | bytes 3072 | tf_op jit(solution)/shard_map/far/pallas_call | solution.py:216
  147.5 11.0 %collective-permute-done.8.refs_1_ = bf16[3,144,1024]{2,1,0:T(8,128)(2,1)} collective-permute-done((bf16[3,144,1024]{2,1,0:T(8,128)(2,1)}, bf16[3,144,1024]{2,1,0:T(8,128)(2,1)}, u32[]{:S(2)}, u32[]{:S(2)}) %collective-permute-start.8) | collective-permute-done | bytes 884768 | tf_op jit(solution)/shard_map/ppermute | solution.py:310
  163.6 13.9 %move.1 = (bf16[3,144,1024]{2,1,0:T(8,128)(2,1)S(1)}, bf16[3,144,1024]{2,1,0:T(8,128)(2,1)S(1)}) custom-call(s32[12]{0:T(128)S(1)} %get-tuple-element.83.tags, bf16[4,3,512,256]{3,2,1,0:T(8,128)(2,1)} %all-to-all-done.1.moved, bf16[6,1024,128]{2,1,0:T(8,128)(2,1)} %copy-done, bf16[3,144,1024]{2,1,0:T(8,128)(2,1)S(1)} %copy-done.2, ...), custom_call_target="tpu_custom_call" | custom-call | flops 4718592 | bytes 4608 | tf_op jit(solution)/shard_map/move/pallas_call | solution.py:216
  177.5 2.9 collective-permute-start.12
  180.4 4.1 %collective-permute-start.13 = (bf16[3,144,1024]{2,1,0:T(8,128)(2,1)S(1)}, bf16[3,144,1024]{2,1,0:T(8,128)(2,1)S(1)}, u32[]{:S(2)}, u32[]{:S(2)}) collective-permute-start(bf16[3,144,1024]{2,1,0:T(8,128)(2,1)S(1)} %get-tuple-element.78), channel_id=1, source_target_pairs={{0,48},{8,56},{16,0},{24,8},{32,16},{40,24},{48,32},{56,40},{1,49}... | collective-permute-start | bytes 2654216 | tf_op jit(solution)/shard_map/ppermute | solution.py:310
  184.4 35.7 %collective-permute-done.12.refs_3_ = bf16[3,144,1024]{2,1,0:T(8,128)(2,1)S(1)} collective-permute-done((bf16[3,144,1024]{2,1,0:T(8,128)(2,1)S(1)}, bf16[3,144,1024]{2,1,0:T(8,128)(2,1)S(1)}, u32[]{:S(2)}, u32[]{:S(2)}) %collective-permute-start.12) | collective-permute-done | bytes 884768 | tf_op jit(solution)/shard_map/ppermute | solution.py:310
  224.1 2.9 collective-permute-start.15
  227.0 3.1 %last.1.context_ref = bf16[384,1024]{1,0:T(8,128)(2,1)S(1)} custom-call(bf16[3,144,1024]{2,1,0:T(8,128)(2,1)S(1)} %get-tuple-element.62.refs_0_, bf16[3,144,1024]{2,1,0:T(8,128)(2,1)} %collective-permute-done.8.refs_1_, bf16[3,144,1024]{2,1,0:T(8,128)(2,1)} %collective-permute-done.9.refs_2_, bf16[3,144,1024]{2,1,0:T(8,128)(2,1)} %copy-done.13, ...), custom_call_target="tpu_custom_call" | custom-call | tf_op jit(solution)/shard_map/last/pallas_call | solution.py:299
  230.1 18.0 %collective-permute-done.14.top_ref = bf16[512,1024]{1,0:T(8,128)(2,1)S(1)} collective-permute-done((bf16[512,1024]{1,0:T(8,128)(2,1)}, bf16[512,1024]{1,0:T(8,128)(2,1)S(1)}, u32[]{:S(2)}, u32[]{:S(2)}) %collective-permute-start.14) | collective-permute-done | bytes 1048608 | tf_op jit(solution)/shard_map/ppermute | solution.py:314
  249.2 5.0 %theirs.1 = bf16[4,384,512]{2,1,0:T(8,128)(2,1)} custom-call(s32[2]{0:T(128)S(1)} %pad_add_fusion.1.place, bf16[384,1024]{1,0:T(8,128)(2,1)S(1)} %last.1.context_ref, bf16[1024,1024]{1,0:T(8,128)(2,1)} %all-gather.2.cloned.1.call-done.own_ref, bf16[1024,1024]{1,0:T(8,128)(2,1)} %copy-done.6, bf16[1024,1024]{1,0:T(8,128)(2,1)} %copy-done.7, ...), custom_call_target="tpu_custom_call" | custom-call | flops 1610612736 | bytes 4194304 | tf_op jit(solution)/shard_map/theirs/pallas_call | solution.py:277
  255.7 4.9 %ours.1 = bf16[4,384,512]{2,1,0:T(8,128)(2,1)} custom-call(s32[2]{0:T(128)S(1)} %pad_add_fusion.place, bf16[384,1024]{1,0:T(8,128)(2,1)S(1)} %last.1.context_ref, bf16[1024,1024]{1,0:T(8,128)(2,1)} %all-gather.2.cloned.1.call-done.own_ref, bf16[1024,1024]{1,0:T(8,128)(2,1)} %copy-done.6, bf16[1024,1024]{1,0:T(8,128)(2,1)} %copy-done.7, ...), custom_call_target="tpu_custom_call" | custom-call | flops 1610612736 | bytes 4194304 | tf_op jit(solution)/shard_map/ours/pallas_call | solution.py:277
  262.5 23.9 %all_to_all.15 = bf16[4,384,512]{2,1,0:T(8,128)(2,1)S(1)} all-to-all(bf16[4,384,512]{2,1,0:T(8,128)(2,1)S(1)} %add_convert_fusion), channel_id=1, replica_groups=mesh['x'=4,'z'=8,'y'=4,'core'=2] {'y'}, dimensions={0} | all-to-all | bytes 3145728 | tf_op jit(solution)/shard_map/all_to_all | solution.py:442
  (106 shorter events, 42.2 us)
Async XLA Ops:
  22.5 65.2 %all-to-all-start = ((bf16[4,5,512,256]{3,2,1,0:T(8,128)(2,1)}), bf16[4,5,512,256]{3,2,1,0:T(8,128)(2,1)}, u32[]{:S(2)}, u32[]{:S(2)}) async-start(bf16[4,5,512,256]{3,2,1,0:T(8,128)(2,1)} %bitcast.22), calls=%async_computation | async-start | bytes 10485760 | tf_op jit(solution)/shard_map/all_to_all | solution.py:318
  27.8 119.7 %all-gather.2.cloned.1.call-start = ((), (), s32[]{:S(2)}) async-start(), calls=%async_computation.3 | async-start | bytes 2359296 | tf_op jit(solution)/shard_map/all_gather | solution.py:354
  27.8 50.6 %collective-permute-start = (bf16[4,512,256]{2,1,0:T(8,128)(2,1)S(1)}, bf16[4,512,256]{2,1,0:T(8,128)(2,1)S(1)}, u32[]{:S(2)}, u32[]{:S(2)}) collective-permute-start(bf16[4,512,256]{2,1,0:T(8,128)(2,1)S(1)} %get-tuple-element.48), channel_id=1, source_target_pairs={{0,8},{8,16},{16,24},{24,32},{32,40},{40,48},{48,56},{56,0},{1,9},... | collective-permute-start | bytes 3145736 | tf_op jit(solution)/shard_map/ppermute | solution.py:310
  30.3 48.1 %collective-permute-start.1 = (bf16[4,512,256]{2,1,0:T(8,128)(2,1)S(1)}, bf16[4,512,256]{2,1,0:T(8,128)(2,1)S(1)}, u32[]{:S(2)}, u32[]{:S(2)}) collective-permute-start(bf16[4,512,256]{2,1,0:T(8,128)(2,1)S(1)} %get-tuple-element.49), channel_id=1, source_target_pairs={{0,56},{8,0},{16,8},{24,16},{32,24},{40,32},{48,40},{56,48},{1,57}... | collective-permute-start | bytes 3145736 | tf_op jit(solution)/shard_map/ppermute | solution.py:310
  34.0 35.5 %collective-permute-start.2 = (bf16[2,512,256]{2,1,0:T(8,128)(2,1)S(1)}, bf16[2,512,256]{2,1,0:T(8,128)(2,1)S(1)}, u32[]{:S(2)}, u32[]{:S(2)}) collective-permute-start(bf16[2,512,256]{2,1,0:T(8,128)(2,1)S(1)} %get-tuple-element.50), channel_id=1, source_target_pairs={{0,16},{8,24},{16,32},{24,40},{32,48},{40,56},{48,0},{56,8},{1,17}... | collective-permute-start | bytes 1572872 | tf_op jit(solution)/shard_map/ppermute | solution.py:310
  34.0 44.4 %collective-permute-start.3 = (bf16[2,512,256]{2,1,0:T(8,128)(2,1)S(1)}, bf16[2,512,256]{2,1,0:T(8,128)(2,1)S(1)}, u32[]{:S(2)}, u32[]{:S(2)}) collective-permute-start(bf16[2,512,256]{2,1,0:T(8,128)(2,1)S(1)} %get-tuple-element.51), channel_id=1, source_target_pairs={{0,48},{8,56},{16,0},{24,8},{32,16},{40,24},{48,32},{56,40},{1,49}... | collective-permute-start | bytes 1572872 | tf_op jit(solution)/shard_map/ppermute | solution.py:310
  69.5 8.9 %copy-start.15 = (bf16[2,512,256]{2,1,0:T(8,128)(2,1)}, bf16[2,512,256]{2,1,0:T(8,128)(2,1)S(1)}, u32[]{:S(2)}) copy-start(bf16[2,512,256]{2,1,0:T(8,128)(2,1)S(1)} %collective-permute-done.2) | copy-start | bytes 1572868
  80.7 22.1 %collective-permute-start.4 = (bf16[3,1024,128]{2,1,0:T(8,128)(2,1)}, bf16[3,1024,128]{2,1,0:T(8,128)(2,1)S(1)}, u32[]{:S(2)}, u32[]{:S(2)}) collective-permute-start(bf16[3,1024,128]{2,1,0:T(8,128)(2,1)} %bitcast.25), channel_id=1, source_target_pairs={{0,56},{8,0},{16,8},{24,16},{32,24},{40,32},{48,40},{56,48},{1,57}... | collective-permute-start | bytes 2359304 | tf_op jit(solution)/shard_map/ppermute | solution.py:310
  84.3 21.9 %collective-permute-start.5 = (bf16[3,1024,128]{2,1,0:T(8,128)(2,1)}, bf16[3,1024,128]{2,1,0:T(8,128)(2,1)}, u32[]{:S(2)}, u32[]{:S(2)}) collective-permute-start(bf16[3,1024,128]{2,1,0:T(8,128)(2,1)} %bitcast.26), channel_id=1, source_target_pairs={{0,8},{8,16},{16,24},{24,32},{32,40},{40,48},{48,56},{56,0},{1,9},... | collective-permute-start | bytes 2359304 | tf_op jit(solution)/shard_map/ppermute | solution.py:310
  87.7 18.6 %copy-start.20 = (s32[32]{0:T(128)S(1)}, s32[32]{0:T(128)}, u32[]{:S(2)}) copy-start(s32[32]{0:T(128)} %constant.119) | copy-start | bytes 388
  87.7 18.7 %copy-start.8 = (bf16[3,128,8,128]{3,1,2,0:T(8,128)(2,1)S(1)}, bf16[3,128,8,128]{3,1,2,0:T(8,128)(2,1)}, u32[]{:S(2)}) copy-start(bf16[3,128,8,128]{3,1,2,0:T(8,128)(2,1)} %copy.17) | copy-start | bytes 2359300
  87.7 70.8 %all-to-all-start.1 = ((bf16[4,3,512,256]{3,2,1,0:T(8,128)(2,1)}), bf16[4,3,512,256]{3,2,1,0:T(8,128)(2,1)}, u32[]{:S(2)}, u32[]{:S(2)}) async-start(bf16[4,3,512,256]{3,2,1,0:T(8,128)(2,1)} %pad_maximum_fusion), calls=%async_computation.1 | async-start | bytes 6291456 | tf_op jit(solution)/shard_map/all_to_all | solution.py:318
  102.8 27.7 %collective-permute-start.6 = (bf16[3,1024,128]{2,1,0:T(8,128)(2,1)S(1)}, bf16[3,1024,128]{2,1,0:T(8,128)(2,1)S(1)}, u32[]{:S(2)}, u32[]{:S(2)}) collective-permute-start(bf16[3,1024,128]{2,1,0:T(8,128)(2,1)S(1)} %collective-permute-done.4), channel_id=1, source_target_pairs={{0,56},{8,0},{16,8},{24,16},{32,24},{40,32},{48,40},{56,48},{1,57}... | collective-permute-start | bytes 2359304 | tf_op jit(solution)/shard_map/ppermute | solution.py:310
  106.2 25.2 %collective-permute-start.7 = (bf16[3,1024,128]{2,1,0:T(8,128)(2,1)}, bf16[3,1024,128]{2,1,0:T(8,128)(2,1)S(1)}, u32[]{:S(2)}, u32[]{:S(2)}) collective-permute-start(bf16[3,1024,128]{2,1,0:T(8,128)(2,1)} %collective-permute-done.5), channel_id=1, source_target_pairs={{0,8},{8,16},{16,24},{24,32},{32,40},{40,48},{48,56},{56,0},{1,9},... | collective-permute-start | bytes 2359304 | tf_op jit(solution)/shard_map/ppermute | solution.py:310
  131.4 27.1 %collective-permute-start.8 = (bf16[3,144,1024]{2,1,0:T(8,128)(2,1)}, bf16[3,144,1024]{2,1,0:T(8,128)(2,1)}, u32[]{:S(2)}, u32[]{:S(2)}) collective-permute-start(bf16[3,144,1024]{2,1,0:T(8,128)(2,1)} %get-tuple-element.69), channel_id=1, source_target_pairs={{0,8},{8,16},{16,24},{24,32},{32,40},{40,48},{48,56},{56,0},{1,9},... | collective-permute-start | bytes 2654216 | tf_op jit(solution)/shard_map/ppermute | solution.py:310
  135.0 23.6 %collective-permute-start.9 = (bf16[3,144,1024]{2,1,0:T(8,128)(2,1)}, bf16[3,144,1024]{2,1,0:T(8,128)(2,1)}, u32[]{:S(2)}, u32[]{:S(2)}) collective-permute-start(bf16[3,144,1024]{2,1,0:T(8,128)(2,1)} %get-tuple-element.70), channel_id=1, source_target_pairs={{0,56},{8,0},{16,8},{24,16},{32,24},{40,32},{48,40},{56,48},{1,57}... | collective-permute-start | bytes 2654216 | tf_op jit(solution)/shard_map/ppermute | solution.py:310
  136.0 9.6 %copy-start = (bf16[6,1024,128]{2,1,0:T(8,128)(2,1)}, bf16[6,1024,128]{2,1,0:T(8,128)(2,1)S(1)}, u32[]{:S(2)}) copy-start(bf16[6,1024,128]{2,1,0:T(8,128)(2,1)S(1)} %constant_dynamic-update-slice_fusion.query) | copy-start | bytes 4718596
  158.6 62.7 %collective-permute-start.10 = (bf16[1024,1024]{1,0:T(8,128)(2,1)}, bf16[1024,1024]{1,0:T(8,128)(2,1)S(1)}, u32[]{:S(2)}, u32[]{:S(2)}) collective-permute-start(bf16[1024,1024]{1,0:T(8,128)(2,1)} %all-gather.2.cloned.1.call-done.own_ref), channel_id=1, source_target_pairs={{0,64},{64,128},{128,192},{192,0},{1,65},{65,129},{129,193},{193,1... | collective-permute-start | bytes 6291464 | tf_op jit(solution)/shard_map/ppermute | solution.py:314
  159.0 62.3 %collective-permute-start.11 = (bf16[1024,1024]{1,0:T(8,128)(2,1)}, bf16[1024,1024]{1,0:T(8,128)(2,1)S(1)}, u32[]{:S(2)}, u32[]{:S(2)}) collective-permute-start(bf16[1024,1024]{1,0:T(8,128)(2,1)} %all-gather.2.cloned.1.call-done.own_ref), channel_id=1, source_target_pairs={{0,192},{64,0},{128,64},{192,128},{1,193},{65,1},{129,65},{193,129... | collective-permute-start | bytes 6291464 | tf_op jit(solution)/shard_map/ppermute | solution.py:314
  177.5 42.6 %collective-permute-start.12 = (bf16[3,144,1024]{2,1,0:T(8,128)(2,1)S(1)}, bf16[3,144,1024]{2,1,0:T(8,128)(2,1)S(1)}, u32[]{:S(2)}, u32[]{:S(2)}) collective-permute-start(bf16[3,144,1024]{2,1,0:T(8,128)(2,1)S(1)} %get-tuple-element.77), channel_id=1, source_target_pairs={{0,16},{8,24},{16,32},{24,40},{32,48},{40,56},{48,0},{56,8},{1,17}... | collective-permute-start | bytes 2654216 | tf_op jit(solution)/shard_map/ppermute | solution.py:310
  180.4 40.9 %collective-permute-start.13 = (bf16[3,144,1024]{2,1,0:T(8,128)(2,1)S(1)}, bf16[3,144,1024]{2,1,0:T(8,128)(2,1)S(1)}, u32[]{:S(2)}, u32[]{:S(2)}) collective-permute-start(bf16[3,144,1024]{2,1,0:T(8,128)(2,1)S(1)} %get-tuple-element.78), channel_id=1, source_target_pairs={{0,48},{8,56},{16,0},{24,8},{32,16},{40,24},{48,32},{56,40},{1,49}... | collective-permute-start | bytes 2654216 | tf_op jit(solution)/shard_map/ppermute | solution.py:310
  222.4 25.6 %collective-permute-start.14 = (bf16[512,1024]{1,0:T(8,128)(2,1)}, bf16[512,1024]{1,0:T(8,128)(2,1)S(1)}, u32[]{:S(2)}, u32[]{:S(2)}) collective-permute-start(bf16[512,1024]{1,0:T(8,128)(2,1)} %slice.42), channel_id=1, source_target_pairs={{0,64},{64,128},{128,192},{192,0},{1,65},{65,129},{129,193},{193,1... | collective-permute-start | bytes 3145736 | tf_op jit(solution)/shard_map/ppermute | solution.py:314
  224.1 25.1 %collective-permute-start.15 = (bf16[512,1024]{1,0:T(8,128)(2,1)}, bf16[512,1024]{1,0:T(8,128)(2,1)S(1)}, u32[]{:S(2)}, u32[]{:S(2)}) collective-permute-start(bf16[512,1024]{1,0:T(8,128)(2,1)} %slice.43), channel_id=1, source_target_pairs={{0,192},{64,0},{128,64},{192,128},{1,193},{65,1},{129,65},{193,129... | collective-permute-start | bytes 3145736 | tf_op jit(solution)/shard_map/ppermute | solution.py:314
  254.1 6.5 %collective-permute-start.16 = (bf16[4,384,512]{2,1,0:T(8,128)(2,1)}, bf16[4,384,512]{2,1,0:T(8,128)(2,1)S(1)}, u32[]{:S(2)}, u32[]{:S(2)}) collective-permute-start(bf16[4,384,512]{2,1,0:T(8,128)(2,1)} %theirs.1), channel_id=1, source_target_pairs={{0,1},{1,0},{2,3},{3,2},{4,5},{5,4},{6,7},{7,6},{8,9},{9,8},{10,11... | collective-permute-start | bytes 4718600 | tf_op jit(solution)/shard_map/ppermute | solution.py:439
  (17 other events, 45.9 us)
Sparse Core Ops, SparseCore 0:
  80.8 65.4 all-gather.1

commit v6 on v5

--- a/solution.py
+++ b/solution.py
@@ -338,17 +338,18 @@
     moving = take_rows(cache, rows[:, stay:].T.reshape(-1), (4, 4, 2, 2))
     moving, staying = lax.optimization_barrier((moving, rows[:, :stay].reshape(-1)))
     (here,) = take_rows(cache, staying, (NX * stay,))
+    q_up = along_z(q_own, -1)
+    q_down = along_z(q_own, 1)
+    here, q_up, q_down = lax.optimization_barrier((here, q_up, q_down))
     here = over_x(here.reshape(NX, stay, PLEN, 2 * HD))
     up3, down3, up4, down4 = moving
     up3 = along_z(up3, 1)
     down3 = along_z(down3, -1)
     up4 = along_z(up4, 2)
     down4 = along_z(down4, -2)
-    up3, down3, up4, down4, q_own, out_weight = lax.optimization_barrier(
-        (up3, down3, up4, down4, q_own, out_weight)
-    )
-    q_up = along_z(q_own, -1)
-    q_down = along_z(q_own, 1)
+    up3, down3, up4, down4, q_up, q_down = lax.optimization_barrier(
+        (up3, down3, up4, down4, q_up, q_down)
+    )
     q_up2 = along_z(q_up, -1)
     q_down2 = along_z(q_down, 1)
     weight = lax.all_gather(out_weight, "z", axis=1, tiled=True)

time: 295 us -> 291 us (0.986)
  waiting for transfers between devices: 117 us -> 93.1 us
  starting transfers between devices: 45.4 us -> 65.2 us
    ppermute x12, waiting for transfers between devices: 97.4 us -> 71.5 us  [along_z(): return lax.ppermute(array, 'z', [(i, (i + shift) % NZ) for i in range(NZ)])]
    ppermute x4, starting transfers between devices: 5.79 us -> 25.1 us  [along_x(): return lax.ppermute(array, 'x', [(i, (i + shift) % NX) for i in range(NX)])]
    unnamed x44 -> x38, local copies, waits for them, and re-layouts: 7.79 us -> 5.69 us
  transfers between devices with their start and end apart: 20 -> 20, of which waited for: 9 -> 11; matrix products, arithmetic and copies ran while one was open for 4% -> 5% of each run, Pallas kernels for 18% -> 22%
where the time goes in v6:
time: 291 us; the launch traced here: 290 us
  waiting for transfers between devices  93.1 us (32%)
  Pallas kernels  67.5 us (23%)
  starting transfers between devices  65.2 us (22%)
  blocking collectives  24.9 us (9%)
  other arithmetic  15.5 us (5%)
  between operations  13.7 us (5%)
  local copies, waits for them, and re-layouts  9.78 us (3%)
    ppermute x12, waiting for transfers between devices, along_z(): return lax.ppermute(array, 'z', [(i, (i + shift) % NZ) for i in range(NZ)])  71.5 us
    pallas_call x3, Pallas kernels, attention(): pl.pallas_call(kernel, out_shape=(jax.ShapeDtypeStruct((n, HD + PACK, ROW...  45.9 us
    ppermute x12, starting transfers between devices, along_z(): return lax.ppermute(array, 'z', [(i, (i + shift) % NZ) for i in range(NZ)])  27 us
    ppermute x4, starting transfers between devices, along_x(): return lax.ppermute(array, 'x', [(i, (i + shift) % NX) for i in range(NX)])  25.1 us
    all_to_all x1, blocking collectives, body(): chips = lax.all_to_all(chip, 'y', split_axis=0, concat_axis=0, tiled=True)  24.9 us
    ppermute x4, waiting for transfers between devices, along_x(): return lax.ppermute(array, 'x', [(i, (i + shift) % NX) for i in range(NX)])  21.5 us
    pallas_call x2, Pallas kernels, project(): pl.pallas_call(project_kernel, out_shape=jax.ShapeDtypeStruct((NX, contex...  9.86 us
    all_to_all x2, starting transfers between devices, over_x(): return lax.all_to_all(items, 'x', split_axis=0, concat_axis=0, tiled=True)  9.84 us
  transfers between devices with their start and end apart: 20, of which 11 were waited for; matrix products, arithmetic and copies ran while one was open for 5% of the time, Pallas kernels for 22%

profile of v6, /device:TPU:1, one launch (start us, length us, event | category | flops | bytes accessed | tf_op | source)
XLA Modules:
  0.0 289.6 jit_solution(12685084065959835251)
XLA Ops:
  8.9 6.4 %collective-permute-start.4 = (bf16[3,1024,128]{2,1,0:T(8,128)(2,1)}, bf16[3,1024,128]{2,1,0:T(8,128)(2,1)}, u32[]{:S(2)}, u32[]{:S(2)}) collective-permute-start(bf16[3,1024,128]{2,1,0:T(8,128)(2,1)} %bitcast.6), channel_id=1, source_target_pairs={{0,56},{8,0},{16,8},{24,16},{32,24},{40,32},{48,40},{56,48},{1,57}... | collective-permute-start | bytes 2359304 | tf_op jit(solution)/shard_map/ppermute | solution.py:310
  22.6 6.0 %take_rows.3 = bf16[20,512,256]{2,1,0:T(8,128)(2,1)} custom-call(s32[20]{0:T(128)S(1)} %reshape.163.rows_ref, bf16[16,512,256]{2,1,0:T(8,128)(2,1)} %bitcast.24), custom_call_target="tpu_custom_call" | custom-call | tf_op jit(solution)/shard_map/take_rows/pallas_call | solution.py:61
  28.6 3.2 %collective-permute-done.4 = bf16[3,1024,128]{2,1,0:T(8,128)(2,1)} collective-permute-done((bf16[3,1024,128]{2,1,0:T(8,128)(2,1)}, bf16[3,1024,128]{2,1,0:T(8,128)(2,1)}, u32[]{:S(2)}, u32[]{:S(2)}) %collective-permute-start.4) | collective-permute-done | bytes 786464 | tf_op jit(solution)/shard_map/ppermute | solution.py:310
  31.9 3.1 %collective-permute-done.5 = bf16[3,1024,128]{2,1,0:T(8,128)(2,1)} collective-permute-done((bf16[3,1024,128]{2,1,0:T(8,128)(2,1)}, bf16[3,1024,128]{2,1,0:T(8,128)(2,1)}, u32[]{:S(2)}, u32[]{:S(2)}) %collective-permute-start.5) | collective-permute-done | bytes 786464 | tf_op jit(solution)/shard_map/ppermute | solution.py:310
  35.0 5.0 %all-to-all-start = ((bf16[4,5,512,256]{3,2,1,0:T(8,128)(2,1)}), bf16[4,5,512,256]{3,2,1,0:T(8,128)(2,1)}, u32[]{:S(2)}, u32[]{:S(2)}) async-start(bf16[4,5,512,256]{3,2,1,0:T(8,128)(2,1)} %bitcast.22), calls=%async_computation | async-start | bytes 10485760 | tf_op jit(solution)/shard_map/all_to_all | solution.py:318
  42.9 3.6 %collective-permute-start.3 = (bf16[2,512,256]{2,1,0:T(8,128)(2,1)S(1)}, bf16[2,512,256]{2,1,0:T(8,128)(2,1)}, u32[]{:S(2)}, u32[]{:S(2)}) collective-permute-start(bf16[2,512,256]{2,1,0:T(8,128)(2,1)S(1)} %get-tuple-element.54), channel_id=1, source_target_pairs={{0,48},{8,56},{16,0},{24,8},{32,16},{40,24},{48,32},{56,40},{1,49}... | collective-permute-start | bytes 1572872 | tf_op jit(solution)/shard_map/ppermute | solution.py:310
  46.6 41.4 %collective-permute-done.2 = bf16[2,512,256]{2,1,0:T(8,128)(2,1)} collective-permute-done((bf16[2,512,256]{2,1,0:T(8,128)(2,1)S(1)}, bf16[2,512,256]{2,1,0:T(8,128)(2,1)}, u32[]{:S(2)}, u32[]{:S(2)}) %collective-permute-start.2) | collective-permute-done | bytes 524320 | tf_op jit(solution)/shard_map/ppermute | solution.py:310
  88.0 5.6 %collective-permute-done.3 = bf16[2,512,256]{2,1,0:T(8,128)(2,1)} collective-permute-done((bf16[2,512,256]{2,1,0:T(8,128)(2,1)S(1)}, bf16[2,512,256]{2,1,0:T(8,128)(2,1)}, u32[]{:S(2)}, u32[]{:S(2)}) %collective-permute-start.3) | collective-permute-done | bytes 524320 | tf_op jit(solution)/shard_map/ppermute | solution.py:310
  94.9 3.7 %pad_maximum_fusion = bf16[4,3,512,256]{3,2,1,0:T(8,128)(2,1)} fusion(bf16[4,1,512,256]{3,2,1,0:T(8,128)(2,1)S(1)} %maximum_bitcast_fusion, bf16[4,1,512,256]{3,2,1,0:T(8,128)(2,1)} %bitcast.9, bf16[4,1,512,256]{3,2,1,0:T(8,128)(2,1)} %bitcast.8), kind=kLoop, calls=%fused_computation | loop fusion | flops 3145728 | bytes 6291456 | tf_op jit(solution)/shard_map/stack | solution.py:356
  98.6 4.8 %all-to-all-start.1 = ((bf16[4,3,512,256]{3,2,1,0:T(8,128)(2,1)}), bf16[4,3,512,256]{3,2,1,0:T(8,128)(2,1)}, u32[]{:S(2)}, u32[]{:S(2)}) async-start(bf16[4,3,512,256]{3,2,1,0:T(8,128)(2,1)} %pad_maximum_fusion), calls=%async_computation.1 | async-start | bytes 6291456 | tf_op jit(solution)/shard_map/all_to_all | solution.py:318
  103.5 4.3 %collective-permute-start.6 = (bf16[3,1024,128]{2,1,0:T(8,128)(2,1)}, bf16[3,1024,128]{2,1,0:T(8,128)(2,1)S(1)}, u32[]{:S(2)}, u32[]{:S(2)}) collective-permute-start(bf16[3,1024,128]{2,1,0:T(8,128)(2,1)} %collective-permute-done.4), channel_id=1, source_target_pairs={{0,56},{8,0},{16,8},{24,16},{32,24},{40,32},{48,40},{56,48},{1,57}... | collective-permute-start | bytes 2359304 | tf_op jit(solution)/shard_map/ppermute | solution.py:310
  109.6 3.3 %pad_maximum_fusion.1.query = bf16[9,1024,128]{2,1,0:T(8,128)(2,1)} fusion(bf16[3,1024,128]{2,1,0:T(8,128)(2,1)} %collective-permute-done.5, bf16[3,1024,128]{2,1,0:T(8,128)(2,1)} %collective-permute-done.4, bf16[3,1024,128]{2,1,0:T(8,128)(2,1)} %bitcast.6), kind=kLoop, calls=%fused_computation.2 | loop fusion | flops 2359296 | bytes 4718592 | tf_op jit(solution)/shard_map/concatenate | solution.py:385
  112.9 23.6 %near.1 = (bf16[3,144,1024]{2,1,0:T(8,128)(2,1)S(1)}, bf16[3,144,1024]{2,1,0:T(8,128)(2,1)}, bf16[3,144,1024]{2,1,0:T(8,128)(2,1)}) custom-call(s32[12]{0:T(128)S(1)} %get-tuple-element.90.tags, bf16[4,5,512,256]{3,2,1,0:T(8,128)(2,1)} %all-to-all-done.here, bf16[384,256]{1,0:T(8,128)(2,1)S(1)} %bitcast.21, bf16[9,1024,128]{2,1,0:T(8,128)(2,1)} %pad_maximum_fusion.1.query), custom_call_target="tpu_custom_call" | custom-call | flops 5242880 | bytes 5120 | tf_op jit(solution)/shard_map/near/pallas_call | solution.py:216
  139.5 9.6 %far.1 = (bf16[3,144,1024]{2,1,0:T(8,128)(2,1)S(1)}, bf16[3,144,1024]{2,1,0:T(8,128)(2,1)S(1)}) custom-call(s32[8]{0:T(128)S(1)} %slice.40.tags, bf16[4,5,512,256]{3,2,1,0:T(8,128)(2,1)} %all-to-all-done.here, bf16[6,1024,128]{2,1,0:T(8,128)(2,1)S(1)} %constant_dynamic-update-slice_fusion.query), custom_call_target="tpu_custom_call" | custom-call | flops 3145728 | bytes 3072 | tf_op jit(solution)/shard_map/far/pallas_call | solution.py:216
  158.4 12.7 %move.1 = (bf16[3,144,1024]{2,1,0:T(8,128)(2,1)S(1)}, bf16[3,144,1024]{2,1,0:T(8,128)(2,1)S(1)}) custom-call(s32[12]{0:T(128)S(1)} %get-tuple-element.89.tags, bf16[4,3,512,256]{3,2,1,0:T(8,128)(2,1)} %all-to-all-done.1.moved, bf16[6,1024,128]{2,1,0:T(8,128)(2,1)} %copy-done, bf16[3,144,1024]{2,1,0:T(8,128)(2,1)S(1)} %copy-done.2, ...), custom_call_target="tpu_custom_call" | custom-call | flops 4718592 | bytes 4608 | tf_op jit(solution)/shard_map/move/pallas_call | solution.py:216
  171.1 5.6 %collective-permute-start.12 = (bf16[3,144,1024]{2,1,0:T(8,128)(2,1)S(1)}, bf16[3,144,1024]{2,1,0:T(8,128)(2,1)S(1)}, u32[]{:S(2)}, u32[]{:S(2)}) collective-permute-start(bf16[3,144,1024]{2,1,0:T(8,128)(2,1)S(1)} %get-tuple-element.83), channel_id=1, source_target_pairs={{0,16},{8,24},{16,32},{24,40},{32,48},{40,56},{48,0},{56,8},{1,17}... | collective-permute-start | bytes 2654216 | tf_op jit(solution)/shard_map/ppermute | solution.py:310
  176.7 12.3 %collective-permute-done.12.refs_3_ = bf16[3,144,1024]{2,1,0:T(8,128)(2,1)S(1)} collective-permute-done((bf16[3,144,1024]{2,1,0:T(8,128)(2,1)S(1)}, bf16[3,144,1024]{2,1,0:T(8,128)(2,1)S(1)}, u32[]{:S(2)}, u32[]{:S(2)}) %collective-permute-start.12) | collective-permute-done | bytes 884768 | tf_op jit(solution)/shard_map/ppermute | solution.py:310
  189.0 3.5 %collective-permute-done.13.refs_4_ = bf16[3,144,1024]{2,1,0:T(8,128)(2,1)S(1)} collective-permute-done((bf16[3,144,1024]{2,1,0:T(8,128)(2,1)S(1)}, bf16[3,144,1024]{2,1,0:T(8,128)(2,1)S(1)}, u32[]{:S(2)}, u32[]{:S(2)}) %collective-permute-start.13) | collective-permute-done | bytes 884768 | tf_op jit(solution)/shard_map/ppermute | solution.py:310
  196.4 21.6 %collective-permute-start.14 = (bf16[512,1024]{1,0:T(8,128)(2,1)}, bf16[512,1024]{1,0:T(8,128)(2,1)S(1)}, u32[]{:S(2)}, u32[]{:S(2)}) collective-permute-start(bf16[512,1024]{1,0:T(8,128)(2,1)} %slice.42), channel_id=1, source_target_pairs={{0,64},{64,128},{128,192},{192,0},{1,65},{65,129},{129,193},{193,1... | collective-permute-start | bytes 3145736 | tf_op jit(solution)/shard_map/ppermute | solution.py:314
  222.9 16.2 %collective-permute-done.14.top_ref = bf16[512,1024]{1,0:T(8,128)(2,1)S(1)} collective-permute-done((bf16[512,1024]{1,0:T(8,128)(2,1)}, bf16[512,1024]{1,0:T(8,128)(2,1)S(1)}, u32[]{:S(2)}, u32[]{:S(2)}) %collective-permute-start.14) | collective-permute-done | bytes 1048608 | tf_op jit(solution)/shard_map/ppermute | solution.py:314
  241.8 4.9 %theirs.1 = bf16[4,384,512]{2,1,0:T(8,128)(2,1)} custom-call(s32[2]{0:T(128)S(1)} %pad_add_fusion.1.place, bf16[384,1024]{1,0:T(8,128)(2,1)S(1)} %last.1.context_ref, bf16[1024,1024]{1,0:T(8,128)(2,1)} %all-gather.2.cloned.1.call-done.own_ref, bf16[1024,1024]{1,0:T(8,128)(2,1)} %copy-done.6, bf16[1024,1024]{1,0:T(8,128)(2,1)} %copy-done.7, ...), custom_call_target="tpu_custom_call" | custom-call | flops 1610612736 | bytes 4194304 | tf_op jit(solution)/shard_map/theirs/pallas_call | solution.py:277
  246.7 3.3 %collective-permute-start.16 = (bf16[4,384,512]{2,1,0:T(8,128)(2,1)}, bf16[4,384,512]{2,1,0:T(8,128)(2,1)S(1)}, u32[]{:S(2)}, u32[]{:S(2)}) collective-permute-start(bf16[4,384,512]{2,1,0:T(8,128)(2,1)} %theirs.1), channel_id=1, source_target_pairs={{0,1},{1,0},{2,3},{3,2},{4,5},{5,4},{6,7},{7,6},{8,9},{9,8},{10,11... | collective-permute-start | bytes 4718600 | tf_op jit(solution)/shard_map/ppermute | solution.py:440
  250.1 4.9 %ours.1 = bf16[4,384,512]{2,1,0:T(8,128)(2,1)} custom-call(s32[2]{0:T(128)S(1)} %pad_add_fusion.place, bf16[384,1024]{1,0:T(8,128)(2,1)S(1)} %last.1.context_ref, bf16[1024,1024]{1,0:T(8,128)(2,1)} %all-gather.2.cloned.1.call-done.own_ref, bf16[1024,1024]{1,0:T(8,128)(2,1)} %copy-done.6, bf16[1024,1024]{1,0:T(8,128)(2,1)} %copy-done.7, ...), custom_call_target="tpu_custom_call" | custom-call | flops 1610612736 | bytes 4194304 | tf_op jit(solution)/shard_map/ours/pallas_call | solution.py:277
  256.9 24.9 %all_to_all.15 = bf16[4,384,512]{2,1,0:T(8,128)(2,1)S(1)} all-to-all(bf16[4,384,512]{2,1,0:T(8,128)(2,1)S(1)} %add_convert_fusion), channel_id=1, replica_groups=mesh['x'=4,'z'=8,'y'=4,'core'=2] {'y'}, dimensions={0} | all-to-all | bytes 3145728 | tf_op jit(solution)/shard_map/all_to_all | solution.py:443
  (100 shorter events, 42.4 us)
Async XLA Ops:
  8.9 22.9 %collective-permute-start.4 = (bf16[3,1024,128]{2,1,0:T(8,128)(2,1)}, bf16[3,1024,128]{2,1,0:T(8,128)(2,1)}, u32[]{:S(2)}, u32[]{:S(2)}) collective-permute-start(bf16[3,1024,128]{2,1,0:T(8,128)(2,1)} %bitcast.6), channel_id=1, source_target_pairs={{0,56},{8,0},{16,8},{24,16},{32,24},{40,32},{48,40},{56,48},{1,57}... | collective-permute-start | bytes 2359304 | tf_op jit(solution)/shard_map/ppermute | solution.py:310
  15.4 19.6 %collective-permute-start.5 = (bf16[3,1024,128]{2,1,0:T(8,128)(2,1)}, bf16[3,1024,128]{2,1,0:T(8,128)(2,1)}, u32[]{:S(2)}, u32[]{:S(2)}) collective-permute-start(bf16[3,1024,128]{2,1,0:T(8,128)(2,1)} %bitcast.6), channel_id=1, source_target_pairs={{0,8},{8,16},{16,24},{24,32},{32,40},{40,48},{48,56},{56,0},{1,9},... | collective-permute-start | bytes 2359304 | tf_op jit(solution)/shard_map/ppermute | solution.py:310
  35.0 63.6 %all-to-all-start = ((bf16[4,5,512,256]{3,2,1,0:T(8,128)(2,1)}), bf16[4,5,512,256]{3,2,1,0:T(8,128)(2,1)}, u32[]{:S(2)}, u32[]{:S(2)}) async-start(bf16[4,5,512,256]{3,2,1,0:T(8,128)(2,1)} %bitcast.22), calls=%async_computation | async-start | bytes 10485760 | tf_op jit(solution)/shard_map/all_to_all | solution.py:318
  40.0 111.0 %all-gather.2.cloned.1.call-start = ((), (), s32[]{:S(2)}) async-start(), calls=%async_computation.3 | async-start | bytes 2359296 | tf_op jit(solution)/shard_map/all_gather | solution.py:355
  40.1 53.6 %collective-permute-start = (bf16[4,512,256]{2,1,0:T(8,128)(2,1)S(1)}, bf16[4,512,256]{2,1,0:T(8,128)(2,1)}, u32[]{:S(2)}, u32[]{:S(2)}) collective-permute-start(bf16[4,512,256]{2,1,0:T(8,128)(2,1)S(1)} %get-tuple-element.51), channel_id=1, source_target_pairs={{0,8},{8,16},{16,24},{24,32},{32,40},{40,48},{48,56},{56,0},{1,9},... | collective-permute-start | bytes 3145736 | tf_op jit(solution)/shard_map/ppermute | solution.py:310
  40.2 53.5 %collective-permute-start.1 = (bf16[4,512,256]{2,1,0:T(8,128)(2,1)S(1)}, bf16[4,512,256]{2,1,0:T(8,128)(2,1)}, u32[]{:S(2)}, u32[]{:S(2)}) collective-permute-start(bf16[4,512,256]{2,1,0:T(8,128)(2,1)S(1)} %get-tuple-element.52), channel_id=1, source_target_pairs={{0,56},{8,0},{16,8},{24,16},{32,24},{40,32},{48,40},{56,48},{1,57}... | collective-permute-start | bytes 3145736 | tf_op jit(solution)/shard_map/ppermute | solution.py:310
  42.9 45.2 %collective-permute-start.2 = (bf16[2,512,256]{2,1,0:T(8,128)(2,1)S(1)}, bf16[2,512,256]{2,1,0:T(8,128)(2,1)}, u32[]{:S(2)}, u32[]{:S(2)}) collective-permute-start(bf16[2,512,256]{2,1,0:T(8,128)(2,1)S(1)} %get-tuple-element.53), channel_id=1, source_target_pairs={{0,16},{8,24},{16,32},{24,40},{32,48},{40,56},{48,0},{56,8},{1,17}... | collective-permute-start | bytes 1572872 | tf_op jit(solution)/shard_map/ppermute | solution.py:310
  42.9 50.7 %collective-permute-start.3 = (bf16[2,512,256]{2,1,0:T(8,128)(2,1)S(1)}, bf16[2,512,256]{2,1,0:T(8,128)(2,1)}, u32[]{:S(2)}, u32[]{:S(2)}) collective-permute-start(bf16[2,512,256]{2,1,0:T(8,128)(2,1)S(1)} %get-tuple-element.54), channel_id=1, source_target_pairs={{0,48},{8,56},{16,0},{24,8},{32,16},{40,24},{48,32},{56,40},{1,49}... | collective-permute-start | bytes 1572872 | tf_op jit(solution)/shard_map/ppermute | solution.py:310
  98.6 54.8 %all-to-all-start.1 = ((bf16[4,3,512,256]{3,2,1,0:T(8,128)(2,1)}), bf16[4,3,512,256]{3,2,1,0:T(8,128)(2,1)}, u32[]{:S(2)}, u32[]{:S(2)}) async-start(bf16[4,3,512,256]{3,2,1,0:T(8,128)(2,1)} %pad_maximum_fusion), calls=%async_computation.1 | async-start | bytes 6291456 | tf_op jit(solution)/shard_map/all_to_all | solution.py:318
  103.5 33.0 %collective-permute-start.6 = (bf16[3,1024,128]{2,1,0:T(8,128)(2,1)}, bf16[3,1024,128]{2,1,0:T(8,128)(2,1)S(1)}, u32[]{:S(2)}, u32[]{:S(2)}) collective-permute-start(bf16[3,1024,128]{2,1,0:T(8,128)(2,1)} %collective-permute-done.4), channel_id=1, source_target_pairs={{0,56},{8,0},{16,8},{24,16},{32,24},{40,32},{48,40},{56,48},{1,57}... | collective-permute-start | bytes 2359304 | tf_op jit(solution)/shard_map/ppermute | solution.py:310
  107.8 28.7 %collective-permute-start.7 = (bf16[3,1024,128]{2,1,0:T(8,128)(2,1)}, bf16[3,1024,128]{2,1,0:T(8,128)(2,1)S(1)}, u32[]{:S(2)}, u32[]{:S(2)}) collective-permute-start(bf16[3,1024,128]{2,1,0:T(8,128)(2,1)} %collective-permute-done.5), channel_id=1, source_target_pairs={{0,8},{8,16},{16,24},{24,32},{32,40},{40,48},{48,56},{56,0},{1,9},... | collective-permute-start | bytes 2359304 | tf_op jit(solution)/shard_map/ppermute | solution.py:310
  136.5 16.8 %collective-permute-start.8 = (bf16[3,144,1024]{2,1,0:T(8,128)(2,1)}, bf16[3,144,1024]{2,1,0:T(8,128)(2,1)}, u32[]{:S(2)}, u32[]{:S(2)}) collective-permute-start(bf16[3,144,1024]{2,1,0:T(8,128)(2,1)} %get-tuple-element.75), channel_id=1, source_target_pairs={{0,8},{8,16},{16,24},{24,32},{32,40},{40,48},{48,56},{56,0},{1,9},... | collective-permute-start | bytes 2654216 | tf_op jit(solution)/shard_map/ppermute | solution.py:310
  136.6 16.8 %collective-permute-start.9 = (bf16[3,144,1024]{2,1,0:T(8,128)(2,1)}, bf16[3,144,1024]{2,1,0:T(8,128)(2,1)}, u32[]{:S(2)}, u32[]{:S(2)}) collective-permute-start(bf16[3,144,1024]{2,1,0:T(8,128)(2,1)} %get-tuple-element.76), channel_id=1, source_target_pairs={{0,56},{8,0},{16,8},{24,16},{32,24},{40,32},{48,40},{56,48},{1,57}... | collective-permute-start | bytes 2654216 | tf_op jit(solution)/shard_map/ppermute | solution.py:310
  153.4 41.7 %collective-permute-start.10 = (bf16[1024,1024]{1,0:T(8,128)(2,1)}, bf16[1024,1024]{1,0:T(8,128)(2,1)S(1)}, u32[]{:S(2)}, u32[]{:S(2)}) collective-permute-start(bf16[1024,1024]{1,0:T(8,128)(2,1)} %all-gather.2.cloned.1.call-done.own_ref), channel_id=1, source_target_pairs={{0,64},{64,128},{128,192},{192,0},{1,65},{65,129},{129,193},{193,1... | collective-permute-start | bytes 6291464 | tf_op jit(solution)/shard_map/ppermute | solution.py:314
  155.2 40.0 %collective-permute-start.11 = (bf16[1024,1024]{1,0:T(8,128)(2,1)}, bf16[1024,1024]{1,0:T(8,128)(2,1)S(1)}, u32[]{:S(2)}, u32[]{:S(2)}) collective-permute-start(bf16[1024,1024]{1,0:T(8,128)(2,1)} %all-gather.2.cloned.1.call-done.own_ref), channel_id=1, source_target_pairs={{0,192},{64,0},{128,64},{192,128},{1,193},{65,1},{129,65},{193,129... | collective-permute-start | bytes 6291464 | tf_op jit(solution)/shard_map/ppermute | solution.py:314
  171.1 17.9 %collective-permute-start.12 = (bf16[3,144,1024]{2,1,0:T(8,128)(2,1)S(1)}, bf16[3,144,1024]{2,1,0:T(8,128)(2,1)S(1)}, u32[]{:S(2)}, u32[]{:S(2)}) collective-permute-start(bf16[3,144,1024]{2,1,0:T(8,128)(2,1)S(1)} %get-tuple-element.83), channel_id=1, source_target_pairs={{0,16},{8,24},{16,32},{24,40},{32,48},{40,56},{48,0},{56,8},{1,17}... | collective-permute-start | bytes 2654216 | tf_op jit(solution)/shard_map/ppermute | solution.py:310
  176.7 15.8 %collective-permute-start.13 = (bf16[3,144,1024]{2,1,0:T(8,128)(2,1)S(1)}, bf16[3,144,1024]{2,1,0:T(8,128)(2,1)S(1)}, u32[]{:S(2)}, u32[]{:S(2)}) collective-permute-start(bf16[3,144,1024]{2,1,0:T(8,128)(2,1)S(1)} %get-tuple-element.84), channel_id=1, source_target_pairs={{0,48},{8,56},{16,0},{24,8},{32,16},{40,24},{48,32},{56,40},{1,49}... | collective-permute-start | bytes 2654216 | tf_op jit(solution)/shard_map/ppermute | solution.py:310
  189.0 28.9 %copy-start.8 = (bf16[3,144,1024]{2,1,0:T(8,128)(2,1)}, bf16[3,144,1024]{2,1,0:T(8,128)(2,1)S(1)}, u32[]{:S(2)}) copy-start(bf16[3,144,1024]{2,1,0:T(8,128)(2,1)S(1)} %collective-permute-done.12.refs_3_) | copy-start | bytes 2654212
  192.5 26.4 %copy-start.9 = (bf16[3,144,1024]{2,1,0:T(8,128)(2,1)}, bf16[3,144,1024]{2,1,0:T(8,128)(2,1)S(1)}, u32[]{:S(2)}) copy-start(bf16[3,144,1024]{2,1,0:T(8,128)(2,1)S(1)} %collective-permute-done.13.refs_4_) | copy-start | bytes 2654212
  195.1 23.9 %copy-start.6 = (bf16[1024,1024]{1,0:T(8,128)(2,1)}, bf16[1024,1024]{1,0:T(8,128)(2,1)S(1)}, u32[]{:S(2)}) copy-start(bf16[1024,1024]{1,0:T(8,128)(2,1)S(1)} %collective-permute-done.10.before_ref) | copy-start | bytes 6291460
  195.2 23.8 %copy-start.7 = (bf16[1024,1024]{1,0:T(8,128)(2,1)}, bf16[1024,1024]{1,0:T(8,128)(2,1)S(1)}, u32[]{:S(2)}) copy-start(bf16[1024,1024]{1,0:T(8,128)(2,1)S(1)} %collective-permute-done.11.after_ref) | copy-start | bytes 6291460
  196.4 42.7 %collective-permute-start.14 = (bf16[512,1024]{1,0:T(8,128)(2,1)}, bf16[512,1024]{1,0:T(8,128)(2,1)S(1)}, u32[]{:S(2)}, u32[]{:S(2)}) collective-permute-start(bf16[512,1024]{1,0:T(8,128)(2,1)} %slice.42), channel_id=1, source_target_pairs={{0,64},{64,128},{128,192},{192,0},{1,65},{65,129},{129,193},{193,1... | collective-permute-start | bytes 3145736 | tf_op jit(solution)/shard_map/ppermute | solution.py:314
  219.0 22.8 %collective-permute-start.15 = (bf16[512,1024]{1,0:T(8,128)(2,1)}, bf16[512,1024]{1,0:T(8,128)(2,1)S(1)}, u32[]{:S(2)}, u32[]{:S(2)}) collective-permute-start(bf16[512,1024]{1,0:T(8,128)(2,1)} %slice.43), channel_id=1, source_target_pairs={{0,192},{64,0},{128,64},{192,128},{1,193},{65,1},{129,65},{193,129... | collective-permute-start | bytes 3145736 | tf_op jit(solution)/shard_map/ppermute | solution.py:314
  246.7 8.3 %collective-permute-start.16 = (bf16[4,384,512]{2,1,0:T(8,128)(2,1)}, bf16[4,384,512]{2,1,0:T(8,128)(2,1)S(1)}, u32[]{:S(2)}, u32[]{:S(2)}) collective-permute-start(bf16[4,384,512]{2,1,0:T(8,128)(2,1)} %theirs.1), channel_id=1, source_target_pairs={{0,1},{1,0},{2,3},{3,2},{4,5},{5,4},{6,7},{7,6},{8,9},{9,8},{10,11... | collective-permute-start | bytes 4718600 | tf_op jit(solution)/shard_map/ppermute | solution.py:440
  (14 other events, 83.7 us)
Sparse Core Ops, SparseCore 0:
  43.0 71.4 all-gather.1

commit v7 on v6

--- a/solution.py
+++ b/solution.py
@@ -17,7 +17,7 @@
 ROWS = GROUP * LQ
 SCALE = math.log2(math.e) / math.sqrt(HD)
 NEG = -1e30
-WIDTH = 512
+WIDTH = 1024
 PACK = 16
 VMEM_LIMIT = 50 << 20
 
@@ -73,7 +73,7 @@
     )(rows, cache)
 
 
-def absorb(keys, values_t, query_ref, group, cols, acc, top, total, causal=False):
+def absorb(keys, values_t, query_ref, group, cols, acc, top, causal=False):
     scores = lax.dot_general(
         keys,
         query_ref[group, cols, :],
@@ -89,16 +89,19 @@
     weights = jnp.exp2((scores - new) * SCALE)
     keep = jnp.exp2((old - new) * SCALE)
     top[group, :, cols] = new
-    total[group, :, cols] = total[group, :, cols] * keep + jnp.sum(weights, axis=0, keepdims=True)
     acc[group, :, cols] = acc[group, :, cols] * keep + jnp.dot(
         values_t, weights.astype(jnp.bfloat16), preferred_element_type=jnp.float32
     )
 
 
-def start(acc, top, total):
+def start(acc, top):
     acc[...] = jnp.zeros_like(acc)
     top[...] = jnp.full_like(top, NEG)
-    total[...] = jnp.zeros_like(total)
+
+
+def with_ones(values):
+    ones = jnp.ones((PACK, values.shape[0]), values.dtype)
+    return jnp.concatenate([values.T, ones], axis=0)
 
 
 def fetches(items_ref, picks, buffer, sems):
@@ -108,7 +111,7 @@
     ]
 
 
-def absorb_all(tag_ref, copies, buffer, query_ref, acc, top, total):
+def absorb_all(tag_ref, copies, buffer, query_ref, acc, top):
     for copy in copies:
         copy.wait()
 
@@ -118,10 +121,10 @@
         @pl.when(tag >= 0)
         def _():
             keys = buffer[i, :, 0:HD]
-            values_t = buffer[i, :, HD : 2 * HD].T
+            values_t = with_ones(buffer[i, :, HD : 2 * HD])
             for part in range(ROWS // WIDTH):
                 cols = pl.ds(part * WIDTH, WIDTH)
-                absorb(keys, values_t, query_ref, tag, cols, acc, top, total)
+                absorb(keys, values_t, query_ref, tag, cols, acc, top)
 
         return carry
 
@@ -149,9 +152,9 @@
     return ref[j, 0:HD, :].astype(jnp.float32), level
 
 
-def state_of(group, acc, top, total):
-    sums = jnp.maximum(total[group], 1e-30)
-    return acc[group] / sums, top[group] * SCALE + jnp.log2(sums)
+def state_of(group, acc, top):
+    sums = jnp.maximum(acc[group, HD : HD + 1, :], 1e-30)
+    return acc[group, 0:HD, :] / sums, top[group] * SCALE + jnp.log2(sums)
 
 
 def merge(pairs):
@@ -173,7 +176,7 @@
     for j in range(n):
         rows = slice(j * LQ, (j + 1) * LQ)
         keys = own[rows, 0:HD]
-        values_t = own[rows, HD : 2 * HD].T
+        values_t = with_ones(own[rows, HD : 2 * HD])
 
         def head(part, carry, j=j, keys=keys, values_t=values_t):
             cols = pl.ds(pl.multiple_of(part * LQ, LQ), LQ)
@@ -222,8 +225,7 @@
         scratch_shapes=[
             pltpu.VMEM((slots, PLEN, 2 * HD), jnp.bfloat16),
             pltpu.SemaphoreType.DMA((slots,)),
-            pltpu.VMEM((groups * n, HD, ROWS), jnp.float32),
-            pltpu.VMEM((groups * n, 1, ROWS), jnp.float32),
+            pltpu.VMEM((groups * n, HD + PACK, ROWS), jnp.float32),
             pltpu.VMEM((groups * n, 1, ROWS), jnp.float32),
         ],
         compiler_params=pltpu.CompilerParams(vmem_limit_bytes=VMEM_LIMIT),
@@ -247,51 +249,36 @@
             )
 
 
-def project_kernel(place, context_ref, own_ref, before_ref, after_ref, top_ref, bottom_ref, out_ref):
-    x = place[1]
-
-    def put(index, products):
-        out_ref[lax.rem(index, NX)] = functools.reduce(jnp.add, products).astype(jnp.bfloat16)
-
-    def times(cols, weight_ref):
-        return jnp.dot(
-            context_ref[:, cols], weight_ref[...], preferred_element_type=jnp.float32
-        )
-
-    half = top_ref.shape[0]
-    everything = slice(None)
-    put(x, [times(everything, own_ref)])
-    put(x + NX - 1, [times(everything, before_ref)])
-    put(x + 1, [times(everything, after_ref)])
-    put(x + 2, [times(slice(0, half), top_ref), times(slice(half, None), bottom_ref)])
-
-
-def project(context, weights, core, x, name):
-    tile = 256
-    width = weights[0].shape[1] // NC
-    steps = width // tile
-
-    def tiles(weight):
-        return pl.BlockSpec((weight.shape[0], tile), lambda i, place: (0, steps * place[0] + i))
-
+def project_kernel(core_ref, context_ref, weight_ref, out_ref):
+    out_ref[0] = jnp.dot(
+        context_ref[...], weight_ref[...], preferred_element_type=jnp.float32
+    ).astype(jnp.bfloat16)
+
+
+def project(context, weight, core, name):
+    width = weight.shape[1] // (NY * NC)
     return pl.pallas_call(
         project_kernel,
-        out_shape=jax.ShapeDtypeStruct((NX, context.shape[0], width), jnp.bfloat16),
+        out_shape=jax.ShapeDtypeStruct((NY, context.shape[0], width), jnp.bfloat16),
         grid_spec=pltpu.PrefetchScalarGridSpec(
             num_scalar_prefetch=1,
-            grid=(steps,),
-            in_specs=[pl.BlockSpec(context.shape, lambda i, place: (0, 0))]
-            + [tiles(weight) for weight in weights],
-            out_specs=pl.BlockSpec((NX, context.shape[0], tile), lambda i, place: (0, 0, i)),
+            grid=(NY,),
+            in_specs=[
+                pl.BlockSpec(context.shape, lambda i, core_ref: (0, 0)),
+                pl.BlockSpec(
+                    (weight.shape[0], width), lambda i, core_ref: (0, NC * i + core_ref[0])
+                ),
+            ],
+            out_specs=pl.BlockSpec((1, context.shape[0], width), lambda i, core_ref: (i, 0, 0)),
         ),
         compiler_params=pltpu.CompilerParams(vmem_limit_bytes=VMEM_LIMIT),
         cost_estimate=pl.CostEstimate(
-            flops=2 * context.shape[0] * context.shape[1] * width * NX,
-            bytes_accessed=context.shape[1] * width * NX * 2,
+            flops=2 * context.shape[0] * weight.shape[0] * width * NY,
+            bytes_accessed=weight.shape[0] * width * NY * 2,
             transcendentals=0,
         ),
         name=name,
-    )(jnp.stack([core, x]), context, *weights)
+    )(core.reshape(1), context, weight)
 
 
 def in_vmem(kernel, name, out, *arrays):
@@ -308,10 +295,6 @@
 
 def along_z(array, shift):
     return lax.ppermute(array, "z", [(i, (i + shift) % NZ) for i in range(NZ)])
-
-
-def along_x(array, shift):
-    return lax.ppermute(array, "x", [(i, (i + shift) % NX) for i in range(NX)])
 
 
 def over_x(items):
@@ -388,7 +371,8 @@
         3 * NX,
         10,
     )
-    near, q_up2, q_down2 = lax.optimization_barrier((near, q_up2, q_down2))
+    near, q_up2, q_down2, weight = lax.optimization_barrier((near, q_up2, q_down2, weight))
+    weight = lax.all_gather(weight, "x", axis=1, tiled=True)
     own_part, near_up, near_down = near
     home_up = along_z(near_up, 1)
     home_down = along_z(near_down, -1)
@@ -404,11 +388,7 @@
         2 * NX,
         6,
     )
-    weight, moved, far, home_up, home_down = lax.optimization_barrier(
-        (weight, moved, far, home_up, home_down)
-    )
-    before = along_x(weight, 1)
-    after = along_x(weight, -1)
+    moved, far, home_up, home_down = lax.optimization_barrier((moved, far, home_up, home_down))
     far_up, far_down = attention(
         move_kernel,
         "move",
@@ -418,11 +398,10 @@
         per_device,
         2,
         3 * NX,
-        9,
+        400000,
     )
     far_up = along_z(far_up, 2)
     far_down = along_z(far_down, -2)
-    before, after, far_up, far_down = lax.optimization_barrier((before, after, far_up, far_down))
     context = in_vmem(
         last_kernel,
         "last",
@@ -434,11 +413,9 @@
         far_down,
     )
     core = lax.axis_index("core")
-    half = weight.shape[0] // 2
-    weights = (weight, before, after, along_x(before[:half], 1), along_x(after[half:], -1))
-    theirs = project(context, weights, 1 - core, x, "theirs")
+    theirs = project(context, weight, 1 - core, "theirs")
     theirs = lax.ppermute(theirs, "core", [(0, 1), (1, 0)])
-    ours = project(context, weights, core, x, "ours")
+    ours = project(context, weight, core, "ours")
     chip = (ours.astype(jnp.float32) + theirs.astype(jnp.float32)).astype(jnp.bfloat16)
     chips = lax.all_to_all(chip, "y", split_axis=0, concat_axis=0, tiled=True)
     return jnp.sum(chips.astype(jnp.float32), axis=0).astype(jnp.bfloat16)

time: 291 us -> 274 us (0.942)
  starting transfers between devices: 65.2 us -> 35.9 us
  waiting for transfers between devices: 93.1 us -> 112 us
  Pallas kernels: 67.5 us -> 64.1 us
    all_gather x0 -> x1, waiting for transfers between devices: none -> 30.2 us  [body(): weight = lax.all_gather(weight, 'x', axis=1, tiled=True)]
    ppermute x4 -> x0, starting transfers between devices: 25.1 us -> none  [along_x(): return lax.ppermute(array, 'x', [(i, (i + shift) % NX) for i in range(NX)])]
    ppermute x4 -> x0, waiting for transfers between devices: 21.5 us -> none  [along_x(): return lax.ppermute(array, 'x', [(i, (i + shift) % NX) for i in range(NX)])]
    ppermute x12, waiting for transfers between devices: 71.5 us -> 81 us  [along_z(): return lax.ppermute(array, 'z', [(i, (i + shift) % NZ) for i in range(NZ)])]
    unnamed x38 -> x32, local copies, waits for them, and re-layouts: 5.69 us -> 6.95 us
  transfers between devices with their start and end apart: 20 -> 17, of which waited for: 11 -> 8; matrix products, arithmetic and copies ran while one was open for 5% -> 5% of each run, Pallas kernels for 22% -> 22%
where the time goes in v7:
time: 274 us; the launch traced here: 273 us
  waiting for transfers between devices  112 us (41%)
  Pallas kernels  64.1 us (23%)
  starting transfers between devices  35.9 us (13%)
  blocking collectives  24.4 us (9%)
  other arithmetic  13.9 us (5%)
  between operations  13.8 us (5%)
  local copies, waits for them, and re-layouts  8.85 us (3%)
    ppermute x12, waiting for transfers between devices, along_z(): return lax.ppermute(array, 'z', [(i, (i + shift) % NZ) for i in range(NZ)])  81 us
    pallas_call x3, Pallas kernels, attention(): pl.pallas_call(kernel, out_shape=(jax.ShapeDtypeStruct((n, HD + PACK, ROW...  43.7 us
    all_gather x1, waiting for transfers between devices, body(): weight = lax.all_gather(weight, 'x', axis=1, tiled=True)  30.2 us
    ppermute x12, starting transfers between devices, along_z(): return lax.ppermute(array, 'z', [(i, (i + shift) % NZ) for i in range(NZ)])  25.1 us
    all_to_all x1, blocking collectives, body(): chips = lax.all_to_all(chip, 'y', split_axis=0, concat_axis=0, tiled=True)  24.4 us
    all_to_all x2, starting transfers between devices, over_x(): return lax.all_to_all(items, 'x', split_axis=0, concat_axis=0, tiled=True)  9.91 us
    pallas_call x2, Pallas kernels, take_rows(): pl.pallas_call(row_copies, out_shape=tuple((jax.ShapeDtypeStruct((n,) + c...  8.99 us
    pallas_call x2, Pallas kernels, project(): pl.pallas_call(project_kernel, out_shape=jax.ShapeDtypeStruct((NY, contex...  8.6 us
  transfers between devices with their start and end apart: 17, of which 8 were waited for; matrix products, arithmetic and copies ran while one was open for 5% of the time, Pallas kernels for 22%

profile of v7, /device:TPU:1, one launch (start us, length us, event | category | flops | bytes accessed | tf_op | source)
XLA Modules:
  0.0 272.8 jit_solution(12994472898542805916)
XLA Ops:
  9.0 6.4 %collective-permute-start.4 = (bf16[3,1024,128]{2,1,0:T(8,128)(2,1)}, bf16[3,1024,128]{2,1,0:T(8,128)(2,1)}, u32[]{:S(2)}, u32[]{:S(2)}) collective-permute-start(bf16[3,1024,128]{2,1,0:T(8,128)(2,1)} %bitcast.5), channel_id=1, source_target_pairs={{0,56},{8,0},{16,8},{24,16},{32,24},{40,32},{48,40},{56,48},{1,57}... | collective-permute-start | bytes 2359304 | tf_op jit(solution)/shard_map/ppermute | solution.py:297
  20.0 2.8 %take_rows.2 = (bf16[4,512,256]{2,1,0:T(8,128)(2,1)S(1)}, bf16[4,512,256]{2,1,0:T(8,128)(2,1)S(1)}, bf16[2,512,256]{2,1,0:T(8,128)(2,1)S(1)}, bf16[2,512,256]{2,1,0:T(8,128)(2,1)S(1)}) custom-call(s32[12]{0:T(128)S(1)} %reshape.168.rows_ref, bf16[16,512,256]{2,1,0:T(8,128)(2,1)} %bitcast.22), custom_call_target="tpu_custom_call" | custom-call | tf_op jit(solution)/shard_map/take_rows/pallas_call | solution.py:61
  22.8 6.2 %take_rows.3 = bf16[20,512,256]{2,1,0:T(8,128)(2,1)} custom-call(s32[20]{0:T(128)S(1)} %reshape.170.rows_ref, bf16[16,512,256]{2,1,0:T(8,128)(2,1)} %bitcast.23), custom_call_target="tpu_custom_call" | custom-call | tf_op jit(solution)/shard_map/take_rows/pallas_call | solution.py:61
  29.0 2.9 %collective-permute-done.4 = bf16[3,1024,128]{2,1,0:T(8,128)(2,1)} collective-permute-done((bf16[3,1024,128]{2,1,0:T(8,128)(2,1)}, bf16[3,1024,128]{2,1,0:T(8,128)(2,1)}, u32[]{:S(2)}, u32[]{:S(2)}) %collective-permute-start.4) | collective-permute-done | bytes 786464 | tf_op jit(solution)/shard_map/ppermute | solution.py:297
  31.9 3.1 %collective-permute-done.5 = bf16[3,1024,128]{2,1,0:T(8,128)(2,1)} collective-permute-done((bf16[3,1024,128]{2,1,0:T(8,128)(2,1)}, bf16[3,1024,128]{2,1,0:T(8,128)(2,1)}, u32[]{:S(2)}, u32[]{:S(2)}) %collective-permute-start.5) | collective-permute-done | bytes 786464 | tf_op jit(solution)/shard_map/ppermute | solution.py:297
  35.0 5.1 %all-to-all-start = ((bf16[4,5,512,256]{3,2,1,0:T(8,128)(2,1)}), bf16[4,5,512,256]{3,2,1,0:T(8,128)(2,1)}, u32[]{:S(2)}, u32[]{:S(2)}) async-start(bf16[4,5,512,256]{3,2,1,0:T(8,128)(2,1)} %bitcast.21), calls=%async_computation | async-start | bytes 10485760 | tf_op jit(solution)/shard_map/all_to_all | solution.py:301
  43.6 3.6 %collective-permute-start.3 = (bf16[2,512,256]{2,1,0:T(8,128)(2,1)S(1)}, bf16[2,512,256]{2,1,0:T(8,128)(2,1)}, u32[]{:S(2)}, u32[]{:S(2)}) collective-permute-start(bf16[2,512,256]{2,1,0:T(8,128)(2,1)S(1)} %get-tuple-element.50), channel_id=1, source_target_pairs={{0,48},{8,56},{16,0},{24,8},{32,16},{40,24},{48,32},{56,40},{1,49}... | collective-permute-start | bytes 1572872 | tf_op jit(solution)/shard_map/ppermute | solution.py:297
  47.3 43.0 %collective-permute-done.2 = bf16[2,512,256]{2,1,0:T(8,128)(2,1)} collective-permute-done((bf16[2,512,256]{2,1,0:T(8,128)(2,1)S(1)}, bf16[2,512,256]{2,1,0:T(8,128)(2,1)}, u32[]{:S(2)}, u32[]{:S(2)}) %collective-permute-start.2) | collective-permute-done | bytes 524320 | tf_op jit(solution)/shard_map/ppermute | solution.py:297
  90.3 6.7 %collective-permute-done.3 = bf16[2,512,256]{2,1,0:T(8,128)(2,1)} collective-permute-done((bf16[2,512,256]{2,1,0:T(8,128)(2,1)S(1)}, bf16[2,512,256]{2,1,0:T(8,128)(2,1)}, u32[]{:S(2)}, u32[]{:S(2)}) %collective-permute-start.3) | collective-permute-done | bytes 524320 | tf_op jit(solution)/shard_map/ppermute | solution.py:297
  98.3 3.5 %pad_maximum_fusion = bf16[4,3,512,256]{3,2,1,0:T(8,128)(2,1)} fusion(bf16[4,1,512,256]{3,2,1,0:T(8,128)(2,1)S(1)} %maximum_bitcast_fusion, bf16[4,1,512,256]{3,2,1,0:T(8,128)(2,1)} %bitcast.8, bf16[4,1,512,256]{3,2,1,0:T(8,128)(2,1)} %bitcast.7), kind=kLoop, calls=%fused_computation | loop fusion | flops 3145728 | bytes 6291456 | tf_op jit(solution)/shard_map/stack | solution.py:339
  101.9 4.8 %all-to-all-start.1 = ((bf16[4,3,512,256]{3,2,1,0:T(8,128)(2,1)}), bf16[4,3,512,256]{3,2,1,0:T(8,128)(2,1)}, u32[]{:S(2)}, u32[]{:S(2)}) async-start(bf16[4,3,512,256]{3,2,1,0:T(8,128)(2,1)} %pad_maximum_fusion), calls=%async_computation.1 | async-start | bytes 6291456 | tf_op jit(solution)/shard_map/all_to_all | solution.py:301
  106.8 3.6 %collective-permute-start.6 = (bf16[3,1024,128]{2,1,0:T(8,128)(2,1)}, bf16[3,1024,128]{2,1,0:T(8,128)(2,1)S(1)}, u32[]{:S(2)}, u32[]{:S(2)}) collective-permute-start(bf16[3,1024,128]{2,1,0:T(8,128)(2,1)} %collective-permute-done.4), channel_id=1, source_target_pairs={{0,56},{8,0},{16,8},{24,16},{32,24},{40,32},{48,40},{56,48},{1,57}... | collective-permute-start | bytes 2359304 | tf_op jit(solution)/shard_map/ppermute | solution.py:297
  113.0 3.3 %pad_maximum_fusion.1.query = bf16[9,1024,128]{2,1,0:T(8,128)(2,1)} fusion(bf16[3,1024,128]{2,1,0:T(8,128)(2,1)} %collective-permute-done.5, bf16[3,1024,128]{2,1,0:T(8,128)(2,1)} %collective-permute-done.4, bf16[3,1024,128]{2,1,0:T(8,128)(2,1)} %bitcast.5), kind=kLoop, calls=%fused_computation.2 | loop fusion | flops 2359296 | bytes 4718592 | tf_op jit(solution)/shard_map/concatenate | solution.py:368
  116.3 21.6 %near.1 = (bf16[3,144,1024]{2,1,0:T(8,128)(2,1)S(1)}, bf16[3,144,1024]{2,1,0:T(8,128)(2,1)}, bf16[3,144,1024]{2,1,0:T(8,128)(2,1)}) custom-call(s32[12]{0:T(128)S(1)} %get-tuple-element.82.tags, bf16[4,5,512,256]{3,2,1,0:T(8,128)(2,1)} %all-to-all-done.here, bf16[384,256]{1,0:T(8,128)(2,1)S(1)} %bitcast.20, bf16[9,1024,128]{2,1,0:T(8,128)(2,1)} %pad_maximum_fusion.1.query), custom_call_target="tpu_custom_call" | custom-call | flops 5242880 | bytes 5120 | tf_op jit(solution)/shard_map/near/pallas_call | solution.py:219
  141.0 6.6 %far.1 = (bf16[3,144,1024]{2,1,0:T(8,128)(2,1)S(1)}, bf16[3,144,1024]{2,1,0:T(8,128)(2,1)S(1)}) custom-call(s32[8]{0:T(128)S(1)} %slice.34.tags, bf16[4,5,512,256]{3,2,1,0:T(8,128)(2,1)} %all-to-all-done.here, bf16[6,1024,128]{2,1,0:T(8,128)(2,1)S(1)} %constant_dynamic-update-slice_fusion.query), custom_call_target="tpu_custom_call" | custom-call | flops 3145728 | bytes 3072 | tf_op jit(solution)/shard_map/far/pallas_call | solution.py:219
  149.5 6.3 %collective-permute-done.8.refs_1_ = bf16[3,144,1024]{2,1,0:T(8,128)(2,1)S(1)} collective-permute-done((bf16[3,144,1024]{2,1,0:T(8,128)(2,1)}, bf16[3,144,1024]{2,1,0:T(8,128)(2,1)S(1)}, u32[]{:S(2)}, u32[]{:S(2)}) %collective-permute-start.8) | collective-permute-done | bytes 884768 | tf_op jit(solution)/shard_map/ppermute | solution.py:297
  158.7 15.6 %move.1 = (bf16[3,144,1024]{2,1,0:T(8,128)(2,1)}, bf16[3,144,1024]{2,1,0:T(8,128)(2,1)S(1)}) custom-call(s32[12]{0:T(128)S(1)} %get-tuple-element.81.tags, bf16[4,3,512,256]{3,2,1,0:T(8,128)(2,1)} %all-to-all-done.1.moved, bf16[6,1024,128]{2,1,0:T(8,128)(2,1)} %copy-done, bf16[3,144,1024]{2,1,0:T(8,128)(2,1)S(1)} %copy-done.3, ...), custom_call_target="tpu_custom_call" | custom-call | flops 209715200000 | bytes 204800000 | tf_op jit(solution)/shard_map/move/pallas_call | solution.py:219
  174.4 3.6 %collective-permute-start.11 = (bf16[3,144,1024]{2,1,0:T(8,128)(2,1)S(1)}, bf16[3,144,1024]{2,1,0:T(8,128)(2,1)}, u32[]{:S(2)}, u32[]{:S(2)}) collective-permute-start(bf16[3,144,1024]{2,1,0:T(8,128)(2,1)S(1)} %get-tuple-element.79), channel_id=1, source_target_pairs={{0,48},{8,56},{16,0},{24,8},{32,16},{40,24},{48,32},{56,40},{1,49}... | collective-permute-start | bytes 2654216 | tf_op jit(solution)/shard_map/ppermute | solution.py:297
  178.0 18.6 %collective-permute-done.10.refs_3_ = bf16[3,144,1024]{2,1,0:T(8,128)(2,1)S(1)} collective-permute-done((bf16[3,144,1024]{2,1,0:T(8,128)(2,1)}, bf16[3,144,1024]{2,1,0:T(8,128)(2,1)S(1)}, u32[]{:S(2)}, u32[]{:S(2)}) %collective-permute-start.10) | collective-permute-done | bytes 884768 | tf_op jit(solution)/shard_map/ppermute | solution.py:297
  197.6 2.8 %last.1.context_ref = bf16[384,1024]{1,0:T(8,128)(2,1)S(1)} custom-call(bf16[3,144,1024]{2,1,0:T(8,128)(2,1)S(1)} %get-tuple-element.65.refs_0_, bf16[3,144,1024]{2,1,0:T(8,128)(2,1)S(1)} %collective-permute-done.8.refs_1_, bf16[3,144,1024]{2,1,0:T(8,128)(2,1)} %collective-permute-done.9.refs_2_, bf16[3,144,1024]{2,1,0:T(8,128)(2,1)} %copy-done.6, ...), custom_call_target="tpu_custom_call" | custom-call | tf_op jit(solution)/shard_map/last/pallas_call | solution.py:286
  200.5 30.2 %all-gather.5.cloned.1.call-done.weight_ref = bf16[1024,4096]{1,0:T(8,128)(2,1)} async-done(((bf16[1024,1024]{1,0:T(8,128)(2,1)}), bf16[1024,4096]{1,0:T(8,128)(2,1)}) %all-gather.5.cloned.1.call-update) | async-done | bytes 8388624 | tf_op jit(solution)/shard_map/all_gather | solution.py:375
  230.6 4.3 %theirs.1 = bf16[4,384,512]{2,1,0:T(8,128)(2,1)S(1)} custom-call(s32[1]{0:T(128)} %bitcast.12.core_ref, bf16[384,1024]{1,0:T(8,128)(2,1)S(1)} %last.1.context_ref, bf16[1024,4096]{1,0:T(8,128)(2,1)} %all-gather.5.cloned.1.call-done.weight_ref), custom_call_target="tpu_custom_call" | custom-call | flops 1610612736 | bytes 4194304 | tf_op jit(solution)/shard_map/theirs/pallas_call | solution.py:260
  235.7 4.3 %ours.1 = bf16[4,384,512]{2,1,0:T(8,128)(2,1)S(1)} custom-call(s32[1]{0:T(128)} %bitcast.core_ref, bf16[384,1024]{1,0:T(8,128)(2,1)S(1)} %last.1.context_ref, bf16[1024,4096]{1,0:T(8,128)(2,1)} %all-gather.5.cloned.1.call-done.weight_ref), custom_call_target="tpu_custom_call" | custom-call | flops 1610612736 | bytes 4194304 | tf_op jit(solution)/shard_map/ours/pallas_call | solution.py:260
  240.5 24.4 %all_to_all.15 = bf16[4,384,512]{2,1,0:T(8,128)(2,1)S(1)} all-to-all(bf16[4,384,512]{2,1,0:T(8,128)(2,1)S(1)} %add_convert_fusion), channel_id=1, replica_groups=mesh['x'=4,'z'=8,'y'=4,'core'=2] {'y'}, dimensions={0} | all-to-all | bytes 3145728 | tf_op jit(solution)/shard_map/all_to_all | solution.py:420
  (85 shorter events, 25.8 us)
Async XLA Ops:
  6.5 12.8 %copy-start.14 = (s32[8]{0:T(128)S(1)}, s32[8]{0:T(128)}, u32[]{:S(2)}) copy-start(s32[8]{0:T(128)} %constant.107.clone) | copy-start | bytes 100
  6.5 8.8 %copy-start.9 = (s32[96]{0:T(128)S(1)}, s32[96]{0:T(128)}, u32[]{:S(2)}) copy-start(s32[96]{0:T(128)} %param.15) | copy-start | bytes 1156
  6.5 8.9 %copy-start.7 = (s32[96,8]{0,1:T(8,128)S(1)}, s32[96,8]{0,1:T(8,128)}, u32[]{:S(2)}) copy-start(s32[96,8]{0,1:T(8,128)} %param.13) | copy-start | bytes 9220
  6.5 10.6 %copy-start.8 = (s32[512]{0:T(512)S(1)}, s32[512]{0:T(512)}, u32[]{:S(2)}) copy-start(s32[512]{0:T(512)} %param.14) | copy-start | bytes 6148
  9.0 22.9 %collective-permute-start.4 = (bf16[3,1024,128]{2,1,0:T(8,128)(2,1)}, bf16[3,1024,128]{2,1,0:T(8,128)(2,1)}, u32[]{:S(2)}, u32[]{:S(2)}) collective-permute-start(bf16[3,1024,128]{2,1,0:T(8,128)(2,1)} %bitcast.5), channel_id=1, source_target_pairs={{0,56},{8,0},{16,8},{24,16},{32,24},{40,32},{48,40},{56,48},{1,57}... | collective-permute-start | bytes 2359304 | tf_op jit(solution)/shard_map/ppermute | solution.py:297
  15.4 19.6 %collective-permute-start.5 = (bf16[3,1024,128]{2,1,0:T(8,128)(2,1)}, bf16[3,1024,128]{2,1,0:T(8,128)(2,1)}, u32[]{:S(2)}, u32[]{:S(2)}) collective-permute-start(bf16[3,1024,128]{2,1,0:T(8,128)(2,1)} %bitcast.5), channel_id=1, source_target_pairs={{0,8},{8,16},{16,24},{24,32},{32,40},{40,48},{48,56},{56,0},{1,9},... | collective-permute-start | bytes 2359304 | tf_op jit(solution)/shard_map/ppermute | solution.py:297
  35.0 66.9 %all-to-all-start = ((bf16[4,5,512,256]{3,2,1,0:T(8,128)(2,1)}), bf16[4,5,512,256]{3,2,1,0:T(8,128)(2,1)}, u32[]{:S(2)}, u32[]{:S(2)}) async-start(bf16[4,5,512,256]{3,2,1,0:T(8,128)(2,1)} %bitcast.21), calls=%async_computation | async-start | bytes 10485760 | tf_op jit(solution)/shard_map/all_to_all | solution.py:301
  40.1 97.8 %all-gather.3.cloned.1.call-start = ((), (), s32[]{:S(2)}) async-start(), calls=%async_computation.3 | async-start | bytes 2359296 | tf_op jit(solution)/shard_map/all_gather | solution.py:338
  40.8 56.1 %collective-permute-start = (bf16[4,512,256]{2,1,0:T(8,128)(2,1)S(1)}, bf16[4,512,256]{2,1,0:T(8,128)(2,1)}, u32[]{:S(2)}, u32[]{:S(2)}) collective-permute-start(bf16[4,512,256]{2,1,0:T(8,128)(2,1)S(1)} %get-tuple-element.47), channel_id=1, source_target_pairs={{0,8},{8,16},{16,24},{24,32},{32,40},{40,48},{48,56},{56,0},{1,9},... | collective-permute-start | bytes 3145736 | tf_op jit(solution)/shard_map/ppermute | solution.py:297
  40.9 56.1 %collective-permute-start.1 = (bf16[4,512,256]{2,1,0:T(8,128)(2,1)S(1)}, bf16[4,512,256]{2,1,0:T(8,128)(2,1)}, u32[]{:S(2)}, u32[]{:S(2)}) collective-permute-start(bf16[4,512,256]{2,1,0:T(8,128)(2,1)S(1)} %get-tuple-element.48), channel_id=1, source_target_pairs={{0,56},{8,0},{16,8},{24,16},{32,24},{40,32},{48,40},{56,48},{1,57}... | collective-permute-start | bytes 3145736 | tf_op jit(solution)/shard_map/ppermute | solution.py:297
  43.6 46.7 %collective-permute-start.2 = (bf16[2,512,256]{2,1,0:T(8,128)(2,1)S(1)}, bf16[2,512,256]{2,1,0:T(8,128)(2,1)}, u32[]{:S(2)}, u32[]{:S(2)}) collective-permute-start(bf16[2,512,256]{2,1,0:T(8,128)(2,1)S(1)} %get-tuple-element.49), channel_id=1, source_target_pairs={{0,16},{8,24},{16,32},{24,40},{32,48},{40,56},{48,0},{56,8},{1,17}... | collective-permute-start | bytes 1572872 | tf_op jit(solution)/shard_map/ppermute | solution.py:297
  43.6 53.4 %collective-permute-start.3 = (bf16[2,512,256]{2,1,0:T(8,128)(2,1)S(1)}, bf16[2,512,256]{2,1,0:T(8,128)(2,1)}, u32[]{:S(2)}, u32[]{:S(2)}) collective-permute-start(bf16[2,512,256]{2,1,0:T(8,128)(2,1)S(1)} %get-tuple-element.50), channel_id=1, source_target_pairs={{0,48},{8,56},{16,0},{24,8},{32,16},{40,24},{48,32},{56,40},{1,49}... | collective-permute-start | bytes 1572872 | tf_op jit(solution)/shard_map/ppermute | solution.py:297
  101.8 5.0 %copy-start.12 = (s32[32]{0:T(128)S(1)}, s32[32]{0:T(128)}, u32[]{:S(2)}) copy-start(s32[32]{0:T(128)} %constant.117) | copy-start | bytes 388
  101.8 11.0 %copy-start.13 = (s32[32]{0:T(128)S(1)}, s32[32]{0:T(128)}, u32[]{:S(2)}) copy-start(s32[32]{0:T(128)} %constant.119) | copy-start | bytes 388
  101.9 54.3 %all-to-all-start.1 = ((bf16[4,3,512,256]{3,2,1,0:T(8,128)(2,1)}), bf16[4,3,512,256]{3,2,1,0:T(8,128)(2,1)}, u32[]{:S(2)}, u32[]{:S(2)}) async-start(bf16[4,3,512,256]{3,2,1,0:T(8,128)(2,1)} %pad_maximum_fusion), calls=%async_computation.1 | async-start | bytes 6291456 | tf_op jit(solution)/shard_map/all_to_all | solution.py:301
  106.7 123.9 %all-gather.5.cloned.1.call-start = ((), (), s32[]{:S(2)}) async-start(), calls=%async_computation.4 | async-start | bytes 10485760 | tf_op jit(solution)/shard_map/all_gather | solution.py:375
  106.8 31.1 %collective-permute-start.6 = (bf16[3,1024,128]{2,1,0:T(8,128)(2,1)}, bf16[3,1024,128]{2,1,0:T(8,128)(2,1)S(1)}, u32[]{:S(2)}, u32[]{:S(2)}) collective-permute-start(bf16[3,1024,128]{2,1,0:T(8,128)(2,1)} %collective-permute-done.4), channel_id=1, source_target_pairs={{0,56},{8,0},{16,8},{24,16},{32,24},{40,32},{48,40},{56,48},{1,57}... | collective-permute-start | bytes 2359304 | tf_op jit(solution)/shard_map/ppermute | solution.py:297
  110.5 27.4 %collective-permute-start.7 = (bf16[3,1024,128]{2,1,0:T(8,128)(2,1)}, bf16[3,1024,128]{2,1,0:T(8,128)(2,1)S(1)}, u32[]{:S(2)}, u32[]{:S(2)}) collective-permute-start(bf16[3,1024,128]{2,1,0:T(8,128)(2,1)} %collective-permute-done.5), channel_id=1, source_target_pairs={{0,8},{8,16},{16,24},{24,32},{32,40},{40,48},{48,56},{56,0},{1,9},... | collective-permute-start | bytes 2359304 | tf_op jit(solution)/shard_map/ppermute | solution.py:297
  138.0 17.8 %collective-permute-start.8 = (bf16[3,144,1024]{2,1,0:T(8,128)(2,1)}, bf16[3,144,1024]{2,1,0:T(8,128)(2,1)S(1)}, u32[]{:S(2)}, u32[]{:S(2)}) collective-permute-start(bf16[3,144,1024]{2,1,0:T(8,128)(2,1)} %get-tuple-element.71), channel_id=1, source_target_pairs={{0,8},{8,16},{16,24},{24,32},{32,40},{40,48},{48,56},{56,0},{1,9},... | collective-permute-start | bytes 2654216 | tf_op jit(solution)/shard_map/ppermute | solution.py:297
  138.1 18.1 %collective-permute-start.9 = (bf16[3,144,1024]{2,1,0:T(8,128)(2,1)}, bf16[3,144,1024]{2,1,0:T(8,128)(2,1)}, u32[]{:S(2)}, u32[]{:S(2)}) collective-permute-start(bf16[3,144,1024]{2,1,0:T(8,128)(2,1)} %get-tuple-element.72), channel_id=1, source_target_pairs={{0,56},{8,0},{16,8},{24,16},{32,24},{40,32},{48,40},{56,48},{1,57}... | collective-permute-start | bytes 2654216 | tf_op jit(solution)/shard_map/ppermute | solution.py:297
  141.0 6.6 %copy-start = (bf16[6,1024,128]{2,1,0:T(8,128)(2,1)}, bf16[6,1024,128]{2,1,0:T(8,128)(2,1)S(1)}, u32[]{:S(2)}) copy-start(bf16[6,1024,128]{2,1,0:T(8,128)(2,1)S(1)} %constant_dynamic-update-slice_fusion.query) | copy-start | bytes 4718596
  174.3 22.3 %collective-permute-start.10 = (bf16[3,144,1024]{2,1,0:T(8,128)(2,1)}, bf16[3,144,1024]{2,1,0:T(8,128)(2,1)S(1)}, u32[]{:S(2)}, u32[]{:S(2)}) collective-permute-start(bf16[3,144,1024]{2,1,0:T(8,128)(2,1)} %get-tuple-element.78), channel_id=1, source_target_pairs={{0,16},{8,24},{16,32},{24,40},{32,48},{40,56},{48,0},{56,8},{1,17}... | collective-permute-start | bytes 2654216 | tf_op jit(solution)/shard_map/ppermute | solution.py:297
  174.4 22.2 %collective-permute-start.11 = (bf16[3,144,1024]{2,1,0:T(8,128)(2,1)S(1)}, bf16[3,144,1024]{2,1,0:T(8,128)(2,1)}, u32[]{:S(2)}, u32[]{:S(2)}) collective-permute-start(bf16[3,144,1024]{2,1,0:T(8,128)(2,1)S(1)} %get-tuple-element.79), channel_id=1, source_target_pairs={{0,48},{8,56},{16,0},{24,8},{32,16},{40,24},{48,32},{56,40},{1,49}... | collective-permute-start | bytes 2654216 | tf_op jit(solution)/shard_map/ppermute | solution.py:297
  234.9 5.1 %collective-permute-start.12 = (bf16[4,384,512]{2,1,0:T(8,128)(2,1)S(1)}, bf16[4,384,512]{2,1,0:T(8,128)(2,1)S(1)}, u32[]{:S(2)}, u32[]{:S(2)}) collective-permute-start(bf16[4,384,512]{2,1,0:T(8,128)(2,1)S(1)} %theirs.1), channel_id=1, source_target_pairs={{0,1},{1,0},{2,3},{3,2},{4,5},{5,4},{6,7},{7,6},{8,9},{9,8},{10,11... | collective-permute-start | bytes 4718600 | tf_op jit(solution)/shard_map/ppermute | solution.py:417
  (8 other events, 18.7 us)
Sparse Core Ops, SparseCore 0:
  42.7 70.7 all-gather.2
  140.9 89.6 all-gather.4

commit v8 on v7

--- a/solution.py
+++ b/solution.py
@@ -37,14 +37,10 @@
     return cache_rows // pass_dev, cache_rows % pass_dev
 
 
-def row_copies(rows_ref, cache_ref, *refs):
-    outs, (buffer, read_sems, write_sems) = refs[:-3], refs[-3:]
-    places = [out_ref.at[i] for out_ref in outs for i in range(out_ref.shape[0])]
+def staged(sources, places, buffer, read_sems, write_sems):
     reads, writes = [], []
-    for n, place in enumerate(places):
-        reads.append(
-            pltpu.make_async_copy(cache_ref.at[rows_ref[n]], buffer.at[n], read_sems.at[n])
-        )
+    for n, (source, place) in enumerate(zip(sources, places)):
+        reads.append(pltpu.make_async_copy(source, buffer.at[n], read_sems.at[n]))
         writes.append(pltpu.make_async_copy(buffer.at[n], place, write_sems.at[n]))
     for read in reads:
         read.start()
@@ -53,6 +49,36 @@
         write.start()
     for write in writes:
         write.wait()
+
+
+def row_copies(rows_ref, cache_ref, *refs):
+    outs, scratch = refs[:-3], refs[-3:]
+    places = [out_ref.at[i] for out_ref in outs for i in range(out_ref.shape[0])]
+    staged([cache_ref.at[rows_ref[n]] for n in range(len(places))], places, *scratch)
+
+
+def assemble_copies(up3, down3, up4, down4, out_ref, *scratch):
+    sources = [ref.at[i] for ref in (up3, down3, up4, down4) for i in range(ref.shape[0])]
+    places = [out_ref.at[i, k] for k in range(3) for i in range(NX)]
+    staged(sources, places, *scratch)
+
+
+def assemble(parts):
+    anywhere = pl.BlockSpec(memory_space=pl.ANY)
+    shape, dtype = parts[0].shape[1:], parts[0].dtype
+    return pl.pallas_call(
+        assemble_copies,
+        out_shape=jax.ShapeDtypeStruct((NX, 3) + shape, dtype),
+        in_specs=[anywhere] * len(parts),
+        out_specs=anywhere,
+        scratch_shapes=[
+            pltpu.VMEM((3 * NX,) + shape, dtype),
+            pltpu.SemaphoreType.DMA((3 * NX,)),
+            pltpu.SemaphoreType.DMA((3 * NX,)),
+        ],
+        compiler_params=pltpu.CompilerParams(vmem_limit_bytes=VMEM_LIMIT),
+        name="assemble",
+    )(*parts)
 
 
 def take_rows(cache, rows, counts):
@@ -167,11 +193,27 @@
     return mixed / whole, level + jnp.log2(whole)
 
 
-def near_kernel(tags, here, own, query, o0, o1, o2, buffer, sems, *state):
+def queries_of(refs, query, sems):
+    n = refs[0].shape[0]
+    copies = [
+        pltpu.make_async_copy(ref, query.at[pl.ds(k * n, n)], sems.at[k])
+        for k, ref in enumerate(refs)
+    ]
+    for copy in copies:
+        copy.start()
+    return copies
+
+
+def near_kernel(
+    tags, here, q0, q1, q2, own, o0, o1, o2, buffer, sems, query, query_sems, *state
+):
+    arriving = queries_of((q0, q1, q2), query, query_sems)
     copies = fetches(here, [(i, k) for k in range(3) for i in range(NX)], buffer, sems)
     for copy in copies:
         copy.start()
     start(*state)
+    for copy in arriving:
+        copy.wait()
     n = o0.shape[0]
     for j in range(n):
         rows = slice(j * LQ, (j + 1) * LQ)
@@ -190,11 +232,14 @@
             store(out_ref, j, *state_of(k * n + j, *state))
 
 
-def far_kernel(tags, here, query, o_up, o_down, buffer, sems, *state):
+def far_kernel(tags, here, q0, q1, o_up, o_down, buffer, sems, query, query_sems, *state):
+    arriving = queries_of((q0, q1), query, query_sems)
     copies = fetches(here, [(i, k) for k in (3, 4) for i in range(NX)], buffer, sems)
     for copy in copies:
         copy.start()
     start(*state)
+    for copy in arriving:
+        copy.wait()
     absorb_all(tags, copies, buffer, query, *state)
     n = o_up.shape[0]
     for j in range(n):
@@ -202,11 +247,28 @@
         store(o_down, j, *state_of(n + j, *state))
 
 
-def move_kernel(tags, moved, query, so_far_up, so_far_down, o_up, o_down, buffer, sems, *state):
+def move_kernel(
+    tags,
+    moved,
+    q0,
+    q1,
+    so_far_up,
+    so_far_down,
+    o_up,
+    o_down,
+    buffer,
+    sems,
+    query,
+    query_sems,
+    *state,
+):
+    arriving = queries_of((q0, q1), query, query_sems)
     copies = fetches(moved, [(i, k) for k in range(3) for i in range(NX)], buffer, sems)
     for copy in copies:
         copy.start()
     start(*state)
+    for copy in arriving:
+        copy.wait()
     absorb_all(tags, copies, buffer, query, *state)
     n = o_up.shape[0]
     for j in range(n):
@@ -214,17 +276,21 @@
         store(o_down, j, *merge([state_of(n + j, *state), load(so_far_down, j)]))
 
 
-def attention(kernel, name, tags, items, arrays, n, groups, slots, work):
-    vmem = pl.BlockSpec(memory_space=pltpu.VMEM)
+def attention(kernel, name, tags, items, queries, arrays, groups, slots, work):
+    vmem, anywhere = pl.BlockSpec(memory_space=pltpu.VMEM), pl.BlockSpec(memory_space=pl.ANY)
+    n = queries[0].shape[0]
     return pl.pallas_call(
         kernel,
         out_shape=(jax.ShapeDtypeStruct((n, HD + PACK, ROWS), jnp.bfloat16),) * groups,
-        in_specs=[pl.BlockSpec(memory_space=pltpu.SMEM), pl.BlockSpec(memory_space=pl.ANY)]
+        in_specs=[pl.BlockSpec(memory_space=pltpu.SMEM), anywhere]
+        + [anywhere] * len(queries)
         + [vmem] * len(arrays),
         out_specs=(vmem,) * groups,
         scratch_shapes=[
             pltpu.VMEM((slots, PLEN, 2 * HD), jnp.bfloat16),
             pltpu.SemaphoreType.DMA((slots,)),
+            pltpu.VMEM((groups * n, ROWS, HD), jnp.bfloat16),
+            pltpu.SemaphoreType.DMA((groups,)),
             pltpu.VMEM((groups * n, HD + PACK, ROWS), jnp.float32),
             pltpu.VMEM((groups * n, 1, ROWS), jnp.float32),
         ],
@@ -235,7 +301,7 @@
             transcendentals=0,
         ),
         name=name,
-    )(tags, items, *arrays)
+    )(tags, items, *queries, *arrays)
 
 
 def last_kernel(*refs):
@@ -249,14 +315,16 @@
             )
 
 
-def project_kernel(core_ref, context_ref, weight_ref, out_ref):
-    out_ref[0] = jnp.dot(
-        context_ref[...], weight_ref[...], preferred_element_type=jnp.float32
-    ).astype(jnp.bfloat16)
-
-
-def project(context, weight, core, name):
-    width = weight.shape[1] // (NY * NC)
+def project_kernel(place, context_ref, most_ref, rest_ref, out_ref):
+    cut = most_ref.shape[0]
+    products = jnp.dot(
+        context_ref[:, :cut], most_ref[...], preferred_element_type=jnp.float32
+    ) + jnp.dot(context_ref[:, cut:], rest_ref[0], preferred_element_type=jnp.float32)
+    out_ref[0] = products.astype(jnp.bfloat16)
+
+
+def project(context, most, rest, core, x, name):
+    width = most.shape[1] // (NY * NC)
     return pl.pallas_call(
         project_kernel,
         out_shape=jax.ShapeDtypeStruct((NY, context.shape[0], width), jnp.bfloat16),
@@ -264,21 +332,23 @@
             num_scalar_prefetch=1,
             grid=(NY,),
             in_specs=[
-                pl.BlockSpec(context.shape, lambda i, core_ref: (0, 0)),
+                pl.BlockSpec(context.shape, lambda i, place: (0, 0)),
+                pl.BlockSpec((most.shape[0], width), lambda i, place: (0, NC * i + place[0])),
                 pl.BlockSpec(
-                    (weight.shape[0], width), lambda i, core_ref: (0, NC * i + core_ref[0])
+                    (1, rest.shape[1], width),
+                    lambda i, place: (lax.rem(i + NX - place[1], NX), 0, place[0]),
                 ),
             ],
-            out_specs=pl.BlockSpec((1, context.shape[0], width), lambda i, core_ref: (i, 0, 0)),
+            out_specs=pl.BlockSpec((1, context.shape[0], width), lambda i, place: (i, 0, 0)),
         ),
         compiler_params=pltpu.CompilerParams(vmem_limit_bytes=VMEM_LIMIT),
         cost_estimate=pl.CostEstimate(
-            flops=2 * context.shape[0] * weight.shape[0] * width * NY,
-            bytes_accessed=weight.shape[0] * width * NY * 2,
+            flops=2 * context.shape[0] * context.shape[1] * width * NY,
+            bytes_accessed=context.shape[1] * width * NY * 2,
             transcendentals=0,
         ),
         name=name,
-    )(core.reshape(1), context, weight)
+    )(jnp.stack([core, x]), context, most, rest)
 
 
 def in_vmem(kernel, name, out, *arrays):
@@ -297,6 +367,10 @@
     return lax.ppermute(array, "z", [(i, (i + shift) % NZ) for i in range(NZ)])
 
 
+def along_x(array, shift):
+    return lax.ppermute(array, "x", [(i, (i + shift) % NX) for i in range(NX)])
+
+
 def over_x(items):
     return lax.all_to_all(items, "x", split_axis=0, concat_axis=0, tiled=True)
 
@@ -323,7 +397,12 @@
     (here,) = take_rows(cache, staying, (NX * stay,))
     q_up = along_z(q_own, -1)
     q_down = along_z(q_own, 1)
-    here, q_up, q_down = lax.optimization_barrier((here, q_up, q_down))
+    cut = out_weight.shape[0] * 3 // 4
+    most = lax.all_gather(out_weight[:cut], "z", axis=1, tiled=True)
+    rest = out_weight[cut:]
+    rest = jnp.stack([rest] + [along_x(rest, -distance) for distance in range(1, NX)])
+    here, q_up, q_down, rest = lax.optimization_barrier((here, q_up, q_down, rest))
+    rest = lax.all_gather(rest, "z", axis=2, tiled=True)
     here = over_x(here.reshape(NX, stay, PLEN, 2 * HD))
     up3, down3, up4, down4 = moving
     up3 = along_z(up3, 1)
@@ -335,8 +414,7 @@
     )
     q_up2 = along_z(q_up, -1)
     q_down2 = along_z(q_down, 1)
-    weight = lax.all_gather(out_weight, "z", axis=1, tiled=True)
-    moved = jnp.stack([up3, down3, jnp.concatenate([up4, down4], axis=0)], axis=1)
+    moved = assemble((up3, down3, up4, down4))
     moved, here = lax.optimization_barrier((moved, here))
     moved = over_x(moved)
 
@@ -365,37 +443,35 @@
         "near",
         tags[: 3 * NX],
         here,
-        [own, jnp.concatenate([q_own, q_up, q_down])],
-        per_device,
+        [q_own, q_up, q_down],
+        [own],
         3,
         3 * NX,
         10,
     )
-    near, q_up2, q_down2, weight = lax.optimization_barrier((near, q_up2, q_down2, weight))
-    weight = lax.all_gather(weight, "x", axis=1, tiled=True)
+    near, q_up2, q_down2, most, rest = lax.optimization_barrier((near, q_up2, q_down2, most, rest))
+    most = lax.all_gather(most, "x", axis=1, tiled=True)
     own_part, near_up, near_down = near
     home_up = along_z(near_up, 1)
     home_down = along_z(near_down, -1)
-    q_far = jnp.concatenate([q_up2, q_down2])
     far = attention(
         far_kernel,
         "far",
         tags[3 * NX : split],
         here,
-        [q_far],
-        per_device,
+        [q_up2, q_down2],
+        [],
         2,
         2 * NX,
         6,
     )
-    moved, far, home_up, home_down = lax.optimization_barrier((moved, far, home_up, home_down))
     far_up, far_down = attention(
         move_kernel,
         "move",
         tags[split:],
         moved,
-        [q_far, *far],
-        per_device,
+        [q_up2, q_down2],
+        far,
         2,
         3 * NX,
         400000,
@@ -413,9 +489,9 @@
         far_down,
     )
     core = lax.axis_index("core")
-    theirs = project(context, weight, 1 - core, "theirs")
+    theirs = project(context, most, rest, 1 - core, x, "theirs")
     theirs = lax.ppermute(theirs, "core", [(0, 1), (1, 0)])
-    ours = project(context, weight, core, "ours")
+    ours = project(context, most, rest, core, x, "ours")
     chip = (ours.astype(jnp.float32) + theirs.astype(jnp.float32)).astype(jnp.bfloat16)
     chips = lax.all_to_all(chip, "y", split_axis=0, concat_axis=0, tiled=True)
     return jnp.sum(chips.astype(jnp.float32), axis=0).astype(jnp.bfloat16)

time: 274 us -> 263 us (0.960)
  waiting for transfers between devices: 112 us -> 101 us
  other arithmetic: 13.9 us -> 7.52 us
  starting transfers between devices: 35.9 us -> 39.1 us
    all_gather x2 -> x3, waiting for transfers between devices: 30.2 us -> 0.02 us  [the longest x1 0.02 us: body(): most = lax.all_gather(most, 'x', axis=1, tiled=True)]
    ppermute x12, waiting for transfers between devices: 81 us -> 100 us  [along_z(): return lax.ppermute(array, 'z', [(i, (i + shift) % NZ) for i in range(NZ)])]
    ppermute x0 -> x3, starting transfers between devices: none -> 6.25 us  [along_x(): return lax.ppermute(array, 'x', [(i, (i + shift) % NX) for i in range(NX)])]
    ppermute x12, starting transfers between devices: 25.1 us -> 21.3 us  [along_z(): return lax.ppermute(array, 'z', [(i, (i + shift) % NZ) for i in range(NZ)])]
    concatenate x1 -> x0, other arithmetic: 3.34 us -> none  [body(): jnp.concatenate([q_own, q_up, q_down])]
    another operation x2 -> x3, other arithmetic: 4.84 us -> 1.79 us  [the longest x1 1.64 us: body(): jnp.stack([rest] + [along_x(rest, -distance) for distance in range(1, NX)])]
    unnamed x32 -> x43, local copies, waits for them, and re-layouts: 6.95 us -> 6.12 us
  transfers between devices with their start and end apart: 17 -> 21, of which waited for: 8 -> 5; matrix products, arithmetic and copies ran while one was open for 5% -> 3% of each run, Pallas kernels for 22% -> 24%
where the time goes in v8:
time: 263 us; the launch traced here: 261 us
  waiting for transfers between devices  101 us (38%)
  Pallas kernels  66.4 us (25%)
  starting transfers between devices  39.1 us (15%)
  blocking collectives  24.2 us (9%)
  between operations  13.6 us (5%)
  local copies, waits for them, and re-layouts  9.24 us (4%)
  other arithmetic  7.52 us (3%)
    ppermute x12, waiting for transfers between devices, along_z(): return lax.ppermute(array, 'z', [(i, (i + shift) % NZ) for i in range(NZ)])  100 us
    pallas_call x3, Pallas kernels, attention(): pl.pallas_call(kernel, out_shape=(jax.ShapeDtypeStruct((n, HD + PACK, ROW...  43.2 us
    all_to_all x1, blocking collectives, body(): chips = lax.all_to_all(chip, 'y', split_axis=0, concat_axis=0, tiled=True)  24.2 us
    ppermute x12, starting transfers between devices, along_z(): return lax.ppermute(array, 'z', [(i, (i + shift) % NZ) for i in range(NZ)])  21.3 us
    all_to_all x2, starting transfers between devices, over_x(): return lax.all_to_all(items, 'x', split_axis=0, concat_axis=0, tiled=True)  10.4 us
    pallas_call x2, Pallas kernels, project(): pl.pallas_call(project_kernel, out_shape=jax.ShapeDtypeStruct((NY, contex...  9.67 us
    pallas_call x2, Pallas kernels, take_rows(): pl.pallas_call(row_copies, out_shape=tuple((jax.ShapeDtypeStruct((n,) + c...  8.37 us
    ppermute x3, starting transfers between devices, along_x(): return lax.ppermute(array, 'x', [(i, (i + shift) % NX) for i in range(NX)])  6.25 us
  transfers between devices with their start and end apart: 21, of which 5 were waited for; matrix products, arithmetic and copies ran while one was open for 3% of the time, Pallas kernels for 24%

profile of v8, /device:TPU:1, one launch (start us, length us, event | category | flops | bytes accessed | tf_op | source)
XLA Modules:
  0.0 260.8 jit_solution(12486166886278125441)
XLA Ops:
  8.0 3.6 %collective-permute-start.7 = (bf16[256,128]{1,0:T(8,128)(2,1)}, bf16[256,128]{1,0:T(8,128)(2,1)}, u32[]{:S(2)}, u32[]{:S(2)}) collective-permute-start(bf16[256,128]{1,0:T(8,128)(2,1)} %get-tuple-element.76), channel_id=1, source_target_pairs={{0,128},{64,192},{128,0},{192,64},{1,129},{65,193},{129,1},{193,65... | collective-permute-start | bytes 196616 | tf_op jit(solution)/shard_map/ppermute | solution.py:371
  11.9 2.4 collective-permute-start.6
  15.8 5.7 %collective-permute-start.4 = (bf16[3,1024,128]{2,1,0:T(8,128)(2,1)S(1)}, bf16[3,1024,128]{2,1,0:T(8,128)(2,1)S(1)}, u32[]{:S(2)}, u32[]{:S(2)}) collective-permute-start(bf16[3,1024,128]{2,1,0:T(8,128)(2,1)S(1)} %bitcast.22), channel_id=1, source_target_pairs={{0,56},{8,0},{16,8},{24,16},{32,24},{40,32},{48,40},{56,48},{1,57}... | collective-permute-start | bytes 2359304 | tf_op jit(solution)/shard_map/ppermute | solution.py:367
  26.9 2.7 %take_rows.2 = (bf16[4,512,256]{2,1,0:T(8,128)(2,1)S(1)}, bf16[4,512,256]{2,1,0:T(8,128)(2,1)S(1)}, bf16[2,512,256]{2,1,0:T(8,128)(2,1)S(1)}, bf16[2,512,256]{2,1,0:T(8,128)(2,1)S(1)}) custom-call(s32[12]{0:T(128)S(1)} %reshape.161.rows_ref, bf16[16,512,256]{2,1,0:T(8,128)(2,1)} %bitcast.27), custom_call_target="tpu_custom_call" | custom-call | tf_op jit(solution)/shard_map/take_rows/pallas_call | solution.py:87
  29.6 5.7 %take_rows.3 = bf16[20,512,256]{2,1,0:T(8,128)(2,1)} custom-call(s32[20]{0:T(128)S(1)} %reshape.163.rows_ref, bf16[16,512,256]{2,1,0:T(8,128)(2,1)} %bitcast.28), custom_call_target="tpu_custom_call" | custom-call | tf_op jit(solution)/shard_map/take_rows/pallas_call | solution.py:87
  38.9 3.1 %collective-permute-done.5.q2 = bf16[3,1024,128]{2,1,0:T(8,128)(2,1)S(1)} collective-permute-done((bf16[3,1024,128]{2,1,0:T(8,128)(2,1)S(1)}, bf16[3,1024,128]{2,1,0:T(8,128)(2,1)S(1)}, u32[]{:S(2)}, u32[]{:S(2)}) %collective-permute-start.5) | collective-permute-done | bytes 786464 | tf_op jit(solution)/shard_map/ppermute | solution.py:367
  42.1 5.0 %all-to-all-start = ((bf16[4,5,512,256]{3,2,1,0:T(8,128)(2,1)}), bf16[4,5,512,256]{3,2,1,0:T(8,128)(2,1)}, u32[]{:S(2)}, u32[]{:S(2)}) async-start(bf16[4,5,512,256]{3,2,1,0:T(8,128)(2,1)} %bitcast.26), calls=%async_computation | async-start | bytes 10485760 | tf_op jit(solution)/shard_map/all_to_all | solution.py:375
  48.0 2.7 %collective-permute-start.1 = (bf16[4,512,256]{2,1,0:T(8,128)(2,1)S(1)}, bf16[4,512,256]{2,1,0:T(8,128)(2,1)S(1)}, u32[]{:S(2)}, u32[]{:S(2)}) collective-permute-start(bf16[4,512,256]{2,1,0:T(8,128)(2,1)S(1)} %get-tuple-element.45), channel_id=1, source_target_pairs={{0,56},{8,0},{16,8},{24,16},{32,24},{40,32},{48,40},{56,48},{1,57}... | collective-permute-start | bytes 3145736 | tf_op jit(solution)/shard_map/ppermute | solution.py:367
  50.6 3.6 %collective-permute-start.3 = (bf16[2,512,256]{2,1,0:T(8,128)(2,1)}, bf16[2,512,256]{2,1,0:T(8,128)(2,1)S(1)}, u32[]{:S(2)}, u32[]{:S(2)}) collective-permute-start(bf16[2,512,256]{2,1,0:T(8,128)(2,1)} %copy-done.8), channel_id=1, source_target_pairs={{0,48},{8,56},{16,0},{24,8},{32,16},{40,24},{48,32},{56,40},{1,49}... | collective-permute-start | bytes 1572872 | tf_op jit(solution)/shard_map/ppermute | solution.py:367
  54.2 50.5 %collective-permute-done.2.up4 = bf16[2,512,256]{2,1,0:T(8,128)(2,1)S(1)} collective-permute-done((bf16[2,512,256]{2,1,0:T(8,128)(2,1)}, bf16[2,512,256]{2,1,0:T(8,128)(2,1)S(1)}, u32[]{:S(2)}, u32[]{:S(2)}) %collective-permute-start.2) | collective-permute-done | bytes 524320 | tf_op jit(solution)/shard_map/ppermute | solution.py:367
  104.7 2.1 assemble.1
  106.9 5.4 %all-to-all-start.1 = ((bf16[4,3,512,256]{3,2,1,0:T(8,128)(2,1)}), bf16[4,3,512,256]{3,2,1,0:T(8,128)(2,1)}, u32[]{:S(2)}, u32[]{:S(2)}) async-start(bf16[4,3,512,256]{3,2,1,0:T(8,128)(2,1)} %assemble.1), calls=%async_computation.1 | async-start | bytes 6291456 | tf_op jit(solution)/shard_map/all_to_all | solution.py:375
  112.7 2.7 %collective-permute-start.9 = (bf16[3,1024,128]{2,1,0:T(8,128)(2,1)S(1)}, bf16[3,1024,128]{2,1,0:T(8,128)(2,1)S(1)}, u32[]{:S(2)}, u32[]{:S(2)}) collective-permute-start(bf16[3,1024,128]{2,1,0:T(8,128)(2,1)S(1)} %collective-permute-done.4.q1), channel_id=1, source_target_pairs={{0,56},{8,0},{16,8},{24,16},{32,24},{40,32},{48,40},{56,48},{1,57}... | collective-permute-start | bytes 2359304 | tf_op jit(solution)/shard_map/ppermute | solution.py:367
  115.7 20.6 %near.1 = (bf16[3,144,1024]{2,1,0:T(8,128)(2,1)S(1)}, bf16[3,144,1024]{2,1,0:T(8,128)(2,1)}, bf16[3,144,1024]{2,1,0:T(8,128)(2,1)}) custom-call(s32[12]{0:T(128)S(1)} %get-tuple-element.78.tags, bf16[4,5,512,256]{3,2,1,0:T(8,128)(2,1)} %all-to-all-done.here, bf16[3,1024,128]{2,1,0:T(8,128)(2,1)S(1)} %bitcast.24, ...), custom_call_target="tpu_custom_call" | custom-call | flops 5242880 | bytes 5120 | tf_op jit(solution)/shard_map/near/pallas_call | solution.py:282
  136.3 5.7 %collective-permute-done.10.q1 = bf16[3,1024,128]{2,1,0:T(8,128)(2,1)S(1)} collective-permute-done((bf16[3,1024,128]{2,1,0:T(8,128)(2,1)S(1)}, bf16[3,1024,128]{2,1,0:T(8,128)(2,1)S(1)}, u32[]{:S(2)}, u32[]{:S(2)}) %collective-permute-start.10) | collective-permute-done | bytes 786464 | tf_op jit(solution)/shard_map/ppermute | solution.py:367
  144.0 2.7 %collective-permute-start.12 = (bf16[3,144,1024]{2,1,0:T(8,128)(2,1)}, bf16[3,144,1024]{2,1,0:T(8,128)(2,1)}, u32[]{:S(2)}, u32[]{:S(2)}) collective-permute-start(bf16[3,144,1024]{2,1,0:T(8,128)(2,1)} %get-tuple-element.65), channel_id=1, source_target_pairs={{0,56},{8,0},{16,8},{24,16},{32,24},{40,32},{48,40},{56,48},{1,57}... | collective-permute-start | bytes 2654216 | tf_op jit(solution)/shard_map/ppermute | solution.py:367
  146.7 6.7 %far.1 = (bf16[3,144,1024]{2,1,0:T(8,128)(2,1)S(1)}, bf16[3,144,1024]{2,1,0:T(8,128)(2,1)S(1)}) custom-call(s32[8]{0:T(128)S(1)} %slice.43.tags, bf16[4,5,512,256]{3,2,1,0:T(8,128)(2,1)} %all-to-all-done.here, bf16[3,1024,128]{2,1,0:T(8,128)(2,1)S(1)} %copy-done.3, bf16[3,1024,128]{2,1,0:T(8,128)(2,1)S(1)} %copy-done.1), custom_call_target="tpu_custom_call" | custom-call | flops 3145728 | bytes 3072 | tf_op jit(solution)/shard_map/far/pallas_call | solution.py:282
  155.3 15.9 %move.1 = (bf16[3,144,1024]{2,1,0:T(8,128)(2,1)}, bf16[3,144,1024]{2,1,0:T(8,128)(2,1)}) custom-call(s32[12]{0:T(128)S(1)} %get-tuple-element.77.tags, bf16[4,3,512,256]{3,2,1,0:T(8,128)(2,1)} %all-to-all-done.1.moved, bf16[3,1024,128]{2,1,0:T(8,128)(2,1)S(1)} %copy-done.3, bf16[3,1024,128]{2,1,0:T(8,128)(2,1)S(1)} %copy-done.1, ...), custom_call_target="tpu_custom_call" | custom-call | flops 209715200000 | bytes 204800000 | tf_op jit(solution)/shard_map/move/pallas_call | solution.py:282
  172.6 2.3 collective-permute-start.14
  175.0 38.7 %collective-permute-done.13.refs_3_ = bf16[3,144,1024]{2,1,0:T(8,128)(2,1)S(1)} collective-permute-done((bf16[3,144,1024]{2,1,0:T(8,128)(2,1)}, bf16[3,144,1024]{2,1,0:T(8,128)(2,1)S(1)}, u32[]{:S(2)}, u32[]{:S(2)}) %collective-permute-start.13) | collective-permute-done | bytes 884768 | tf_op jit(solution)/shard_map/ppermute | solution.py:367
  214.6 3.1 %last.1.context_ref = bf16[384,1024]{1,0:T(8,128)(2,1)S(1)} custom-call(bf16[3,144,1024]{2,1,0:T(8,128)(2,1)S(1)} %get-tuple-element.63.refs_0_, bf16[3,144,1024]{2,1,0:T(8,128)(2,1)} %collective-permute-done.11.refs_1_, bf16[3,144,1024]{2,1,0:T(8,128)(2,1)} %collective-permute-done.12.refs_2_, bf16[3,144,1024]{2,1,0:T(8,128)(2,1)} %copy-done.10, ...), custom_call_target="tpu_custom_call" | custom-call | tf_op jit(solution)/shard_map/last/pallas_call | solution.py:356
  217.7 4.8 %theirs.1 = bf16[4,384,512]{2,1,0:T(8,128)(2,1)S(1)} custom-call(s32[2]{0:T(128)S(1)} %pad_add_fusion.1.place, bf16[384,1024]{1,0:T(8,128)(2,1)S(1)} %last.1.context_ref, bf16[768,4096]{1,0:T(8,128)(2,1)} %all-gather.8.cloned.1.call-done.most_ref, bf16[4,256,1024]{2,1,0:T(8,128)(2,1)} %all-gather.6.cloned.1.call-done.rest_ref), custom_call_target="tpu_custom_call" | custom-call | flops 1610612736 | bytes 4194304 | tf_op jit(solution)/shard_map/theirs/pallas_call | solution.py:328
  223.6 4.8 %ours.1 = bf16[4,384,512]{2,1,0:T(8,128)(2,1)S(1)} custom-call(s32[2]{0:T(128)S(1)} %pad_add_fusion.place, bf16[384,1024]{1,0:T(8,128)(2,1)S(1)} %last.1.context_ref, bf16[768,4096]{1,0:T(8,128)(2,1)} %all-gather.8.cloned.1.call-done.most_ref, bf16[4,256,1024]{2,1,0:T(8,128)(2,1)} %all-gather.6.cloned.1.call-done.rest_ref), custom_call_target="tpu_custom_call" | custom-call | flops 1610612736 | bytes 4194304 | tf_op jit(solution)/shard_map/ours/pallas_call | solution.py:328
  229.0 24.2 %all_to_all.15 = bf16[4,384,512]{2,1,0:T(8,128)(2,1)S(1)} all-to-all(bf16[4,384,512]{2,1,0:T(8,128)(2,1)S(1)} %add_convert_fusion), channel_id=1, replica_groups=mesh['x'=4,'z'=8,'y'=4,'core'=2] {'y'}, dimensions={0} | all-to-all | bytes 3145728 | tf_op jit(solution)/shard_map/all_to_all | solution.py:496
  (107 shorter events, 22.7 us)
Async XLA Ops:
  6.5 137.3 %all-gather.4.cloned.1.call-start = ((), (), s32[]{:S(2)}) async-start(), calls=%async_computation.3 | async-start | bytes 1769472 | tf_op jit(solution)/shard_map/all_gather | solution.py:401
  8.0 27.3 %collective-permute-start.7 = (bf16[256,128]{1,0:T(8,128)(2,1)}, bf16[256,128]{1,0:T(8,128)(2,1)}, u32[]{:S(2)}, u32[]{:S(2)}) collective-permute-start(bf16[256,128]{1,0:T(8,128)(2,1)} %get-tuple-element.76), channel_id=1, source_target_pairs={{0,128},{64,192},{128,0},{192,64},{1,129},{65,193},{129,1},{193,65... | collective-permute-start | bytes 196616 | tf_op jit(solution)/shard_map/ppermute | solution.py:371
  11.6 23.7 %collective-permute-start.8 = (bf16[256,128]{1,0:T(8,128)(2,1)}, bf16[256,128]{1,0:T(8,128)(2,1)}, u32[]{:S(2)}, u32[]{:S(2)}) collective-permute-start(bf16[256,128]{1,0:T(8,128)(2,1)} %get-tuple-element.76), channel_id=1, source_target_pairs={{0,64},{64,128},{128,192},{192,0},{1,65},{65,129},{129,193},{193,1... | collective-permute-start | bytes 196616 | tf_op jit(solution)/shard_map/ppermute | solution.py:371
  11.9 23.4 %collective-permute-start.6 = (bf16[256,128]{1,0:T(8,128)(2,1)}, bf16[256,128]{1,0:T(8,128)(2,1)}, u32[]{:S(2)}, u32[]{:S(2)}) collective-permute-start(bf16[256,128]{1,0:T(8,128)(2,1)} %get-tuple-element.76), channel_id=1, source_target_pairs={{0,192},{64,0},{128,64},{192,128},{1,193},{65,1},{129,65},{193,129... | collective-permute-start | bytes 196616 | tf_op jit(solution)/shard_map/ppermute | solution.py:371
  14.3 9.7 %copy-start.14 = (s32[512]{0:T(512)S(1)}, s32[512]{0:T(512)}, u32[]{:S(2)}) copy-start(s32[512]{0:T(512)} %param.14) | copy-start | bytes 6148
  15.8 23.1 %collective-permute-start.4 = (bf16[3,1024,128]{2,1,0:T(8,128)(2,1)S(1)}, bf16[3,1024,128]{2,1,0:T(8,128)(2,1)S(1)}, u32[]{:S(2)}, u32[]{:S(2)}) collective-permute-start(bf16[3,1024,128]{2,1,0:T(8,128)(2,1)S(1)} %bitcast.22), channel_id=1, source_target_pairs={{0,56},{8,0},{16,8},{24,16},{32,24},{40,32},{48,40},{56,48},{1,57}... | collective-permute-start | bytes 2359304 | tf_op jit(solution)/shard_map/ppermute | solution.py:367
  21.5 20.6 %collective-permute-start.5 = (bf16[3,1024,128]{2,1,0:T(8,128)(2,1)S(1)}, bf16[3,1024,128]{2,1,0:T(8,128)(2,1)S(1)}, u32[]{:S(2)}, u32[]{:S(2)}) collective-permute-start(bf16[3,1024,128]{2,1,0:T(8,128)(2,1)S(1)} %bitcast.23), channel_id=1, source_target_pairs={{0,8},{8,16},{16,24},{24,32},{32,40},{40,48},{48,56},{56,0},{1,9},... | collective-permute-start | bytes 2359304 | tf_op jit(solution)/shard_map/ppermute | solution.py:367
  42.1 64.8 %all-to-all-start = ((bf16[4,5,512,256]{3,2,1,0:T(8,128)(2,1)}), bf16[4,5,512,256]{3,2,1,0:T(8,128)(2,1)}, u32[]{:S(2)}, u32[]{:S(2)}) async-start(bf16[4,5,512,256]{3,2,1,0:T(8,128)(2,1)} %bitcast.26), calls=%async_computation | async-start | bytes 10485760 | tf_op jit(solution)/shard_map/all_to_all | solution.py:375
  47.1 96.8 %all-gather.6.cloned.1.call-start = ((), (), s32[]{:S(2)}) async-start(), calls=%async_computation.4 | async-start | bytes 2359296 | tf_op jit(solution)/shard_map/all_gather | solution.py:405
  47.9 56.9 %collective-permute-start = (bf16[4,512,256]{2,1,0:T(8,128)(2,1)}, bf16[4,512,256]{2,1,0:T(8,128)(2,1)S(1)}, u32[]{:S(2)}, u32[]{:S(2)}) collective-permute-start(bf16[4,512,256]{2,1,0:T(8,128)(2,1)} %copy-done.5), channel_id=1, source_target_pairs={{0,8},{8,16},{16,24},{24,32},{32,40},{40,48},{48,56},{56,0},{1,9},... | collective-permute-start | bytes 3145736 | tf_op jit(solution)/shard_map/ppermute | solution.py:367
  48.0 56.8 %collective-permute-start.1 = (bf16[4,512,256]{2,1,0:T(8,128)(2,1)S(1)}, bf16[4,512,256]{2,1,0:T(8,128)(2,1)S(1)}, u32[]{:S(2)}, u32[]{:S(2)}) collective-permute-start(bf16[4,512,256]{2,1,0:T(8,128)(2,1)S(1)} %get-tuple-element.45), channel_id=1, source_target_pairs={{0,56},{8,0},{16,8},{24,16},{32,24},{40,32},{48,40},{56,48},{1,57}... | collective-permute-start | bytes 3145736 | tf_op jit(solution)/shard_map/ppermute | solution.py:367
  50.6 54.1 %collective-permute-start.2 = (bf16[2,512,256]{2,1,0:T(8,128)(2,1)}, bf16[2,512,256]{2,1,0:T(8,128)(2,1)S(1)}, u32[]{:S(2)}, u32[]{:S(2)}) collective-permute-start(bf16[2,512,256]{2,1,0:T(8,128)(2,1)} %copy-done.9), channel_id=1, source_target_pairs={{0,16},{8,24},{16,32},{24,40},{32,48},{40,56},{48,0},{56,8},{1,17}... | collective-permute-start | bytes 1572872 | tf_op jit(solution)/shard_map/ppermute | solution.py:367
  50.6 54.1 %collective-permute-start.3 = (bf16[2,512,256]{2,1,0:T(8,128)(2,1)}, bf16[2,512,256]{2,1,0:T(8,128)(2,1)S(1)}, u32[]{:S(2)}, u32[]{:S(2)}) collective-permute-start(bf16[2,512,256]{2,1,0:T(8,128)(2,1)} %copy-done.8), channel_id=1, source_target_pairs={{0,48},{8,56},{16,0},{24,8},{32,16},{40,24},{48,32},{56,40},{1,49}... | collective-permute-start | bytes 1572872 | tf_op jit(solution)/shard_map/ppermute | solution.py:367
  106.9 8.7 %copy-start.19 = (s32[32]{0:T(128)S(1)}, s32[32]{0:T(128)}, u32[]{:S(2)}) copy-start(s32[32]{0:T(128)} %constant.119) | copy-start | bytes 388
  106.9 8.8 %copy-start.4 = (bf16[384,1,256]{2,0,1:T(8,128)(2,1)S(1)}, bf16[384,1,256]{2,0,1:T(8,128)(2,1)}, u32[]{:S(2)}) copy-start(bf16[384,1,256]{2,0,1:T(8,128)(2,1)} %param.10) | copy-start | bytes 589828
  106.9 48.4 %all-to-all-start.1 = ((bf16[4,3,512,256]{3,2,1,0:T(8,128)(2,1)}), bf16[4,3,512,256]{3,2,1,0:T(8,128)(2,1)}, u32[]{:S(2)}, u32[]{:S(2)}) async-start(bf16[4,3,512,256]{3,2,1,0:T(8,128)(2,1)} %assemble.1), calls=%async_computation.1 | async-start | bytes 6291456 | tf_op jit(solution)/shard_map/all_to_all | solution.py:375
  112.3 105.4 %all-gather.8.cloned.1.call-start = ((), (), s32[]{:S(2)}) async-start(), calls=%async_computation.5 | async-start | bytes 7864320 | tf_op jit(solution)/shard_map/all_gather | solution.py:453
  112.5 29.6 %collective-permute-start.10 = (bf16[3,1024,128]{2,1,0:T(8,128)(2,1)S(1)}, bf16[3,1024,128]{2,1,0:T(8,128)(2,1)S(1)}, u32[]{:S(2)}, u32[]{:S(2)}) collective-permute-start(bf16[3,1024,128]{2,1,0:T(8,128)(2,1)S(1)} %collective-permute-done.5.q2), channel_id=1, source_target_pairs={{0,8},{8,16},{16,24},{24,32},{32,40},{40,48},{48,56},{56,0},{1,9},... | collective-permute-start | bytes 2359304 | tf_op jit(solution)/shard_map/ppermute | solution.py:367
  112.7 30.2 %collective-permute-start.9 = (bf16[3,1024,128]{2,1,0:T(8,128)(2,1)S(1)}, bf16[3,1024,128]{2,1,0:T(8,128)(2,1)S(1)}, u32[]{:S(2)}, u32[]{:S(2)}) collective-permute-start(bf16[3,1024,128]{2,1,0:T(8,128)(2,1)S(1)} %collective-permute-done.4.q1), channel_id=1, source_target_pairs={{0,56},{8,0},{16,8},{24,16},{32,24},{40,32},{48,40},{56,48},{1,57}... | collective-permute-start | bytes 2359304 | tf_op jit(solution)/shard_map/ppermute | solution.py:367
  143.9 31.1 %collective-permute-start.11 = (bf16[3,144,1024]{2,1,0:T(8,128)(2,1)}, bf16[3,144,1024]{2,1,0:T(8,128)(2,1)}, u32[]{:S(2)}, u32[]{:S(2)}) collective-permute-start(bf16[3,144,1024]{2,1,0:T(8,128)(2,1)} %get-tuple-element.64), channel_id=1, source_target_pairs={{0,8},{8,16},{16,24},{24,32},{32,40},{40,48},{48,56},{56,0},{1,9},... | collective-permute-start | bytes 2654216 | tf_op jit(solution)/shard_map/ppermute | solution.py:367
  144.0 31.0 %collective-permute-start.12 = (bf16[3,144,1024]{2,1,0:T(8,128)(2,1)}, bf16[3,144,1024]{2,1,0:T(8,128)(2,1)}, u32[]{:S(2)}, u32[]{:S(2)}) collective-permute-start(bf16[3,144,1024]{2,1,0:T(8,128)(2,1)} %get-tuple-element.65), channel_id=1, source_target_pairs={{0,56},{8,0},{16,8},{24,16},{32,24},{40,32},{48,40},{56,48},{1,57}... | collective-permute-start | bytes 2654216 | tf_op jit(solution)/shard_map/ppermute | solution.py:367
  171.2 42.4 %collective-permute-start.13 = (bf16[3,144,1024]{2,1,0:T(8,128)(2,1)}, bf16[3,144,1024]{2,1,0:T(8,128)(2,1)S(1)}, u32[]{:S(2)}, u32[]{:S(2)}) collective-permute-start(bf16[3,144,1024]{2,1,0:T(8,128)(2,1)} %get-tuple-element.71), channel_id=1, source_target_pairs={{0,16},{8,24},{16,32},{24,40},{32,48},{40,56},{48,0},{56,8},{1,17}... | collective-permute-start | bytes 2654216 | tf_op jit(solution)/shard_map/ppermute | solution.py:367
  172.6 42.0 %collective-permute-start.14 = (bf16[3,144,1024]{2,1,0:T(8,128)(2,1)}, bf16[3,144,1024]{2,1,0:T(8,128)(2,1)}, u32[]{:S(2)}, u32[]{:S(2)}) collective-permute-start(bf16[3,144,1024]{2,1,0:T(8,128)(2,1)} %get-tuple-element.72), channel_id=1, source_target_pairs={{0,48},{8,56},{16,0},{24,8},{32,16},{40,24},{48,32},{56,40},{1,49}... | collective-permute-start | bytes 2654216 | tf_op jit(solution)/shard_map/ppermute | solution.py:367
  222.5 5.9 %collective-permute-start.15 = (bf16[4,384,512]{2,1,0:T(8,128)(2,1)S(1)}, bf16[4,384,512]{2,1,0:T(8,128)(2,1)S(1)}, u32[]{:S(2)}, u32[]{:S(2)}) collective-permute-start(bf16[4,384,512]{2,1,0:T(8,128)(2,1)S(1)} %theirs.1), channel_id=1, source_target_pairs={{0,1},{1,0},{2,3},{3,2},{4,5},{5,4},{6,7},{7,6},{8,9},{9,8},{10,11... | collective-permute-start | bytes 4718600 | tf_op jit(solution)/shard_map/ppermute | solution.py:493
  (18 other events, 81.2 us)
Sparse Core Ops, SparseCore 0:
  22.4 50.3 all-gather.3
  74.5 65.0 all-gather.5
  146.8 68.5 all-gather.7

commit v9 on v8

--- a/solution.py
+++ b/solution.py
@@ -204,9 +204,24 @@
     return copies
 
 
-def near_kernel(
-    tags, here, q0, q1, q2, own, o0, o1, o2, buffer, sems, query, query_sems, *state
-):
+def self_kernel(q_own, own, out_ref, *state):
+    start(*state)
+    n = q_own.shape[0]
+    for j in range(n):
+        rows = slice(j * LQ, (j + 1) * LQ)
+        keys = own[rows, 0:HD]
+        values_t = with_ones(own[rows, HD : 2 * HD])
+
+        def head(part, carry, j=j, keys=keys, values_t=values_t):
+            cols = pl.ds(pl.multiple_of(part * LQ, LQ), LQ)
+            absorb(keys, values_t, q_own, j, cols, *state, causal=True)
+            return carry
+
+        lax.fori_loop(0, GROUP, head, 0)
+        store(out_ref, j, *state_of(j, *state))
+
+
+def near_kernel(tags, here, q0, q1, q2, o0, o1, o2, buffer, sems, query, query_sems, *state):
     arriving = queries_of((q0, q1, q2), query, query_sems)
     copies = fetches(here, [(i, k) for k in range(3) for i in range(NX)], buffer, sems)
     for copy in copies:
@@ -214,19 +229,8 @@
     start(*state)
     for copy in arriving:
         copy.wait()
+    absorb_all(tags, copies, buffer, query, *state)
     n = o0.shape[0]
-    for j in range(n):
-        rows = slice(j * LQ, (j + 1) * LQ)
-        keys = own[rows, 0:HD]
-        values_t = with_ones(own[rows, HD : 2 * HD])
-
-        def head(part, carry, j=j, keys=keys, values_t=values_t):
-            cols = pl.ds(pl.multiple_of(part * LQ, LQ), LQ)
-            absorb(keys, values_t, query, j, cols, *state, causal=True)
-            return carry
-
-        lax.fori_loop(0, GROUP, head, 0)
-    absorb_all(tags, copies, buffer, query, *state)
     for k, out_ref in enumerate((o0, o1, o2)):
         for j in range(n):
             store(out_ref, j, *state_of(k * n + j, *state))
@@ -351,13 +355,14 @@
     )(jnp.stack([core, x]), context, most, rest)
 
 
-def in_vmem(kernel, name, out, *arrays):
+def in_vmem(kernel, name, out, *arrays, scratch=()):
     vmem = pl.BlockSpec(memory_space=pltpu.VMEM)
     return pl.pallas_call(
         kernel,
         out_shape=out,
         in_specs=[vmem] * len(arrays),
         out_specs=jax.tree.map(lambda _: vmem, out),
+        scratch_shapes=scratch,
         compiler_params=pltpu.CompilerParams(vmem_limit_bytes=VMEM_LIMIT),
         name=name,
     )(*arrays)
@@ -395,13 +400,11 @@
     moving = take_rows(cache, rows[:, stay:].T.reshape(-1), (4, 4, 2, 2))
     moving, staying = lax.optimization_barrier((moving, rows[:, :stay].reshape(-1)))
     (here,) = take_rows(cache, staying, (NX * stay,))
-    q_up = along_z(q_own, -1)
-    q_down = along_z(q_own, 1)
     cut = out_weight.shape[0] * 3 // 4
     most = lax.all_gather(out_weight[:cut], "z", axis=1, tiled=True)
     rest = out_weight[cut:]
     rest = jnp.stack([rest] + [along_x(rest, -distance) for distance in range(1, NX)])
-    here, q_up, q_down, rest = lax.optimization_barrier((here, q_up, q_down, rest))
+    here, rest = lax.optimization_barrier((here, rest))
     rest = lax.all_gather(rest, "z", axis=2, tiled=True)
     here = over_x(here.reshape(NX, stay, PLEN, 2 * HD))
     up3, down3, up4, down4 = moving
@@ -409,9 +412,9 @@
     down3 = along_z(down3, -1)
     up4 = along_z(up4, 2)
     down4 = along_z(down4, -2)
-    up3, down3, up4, down4, q_up, q_down = lax.optimization_barrier(
-        (up3, down3, up4, down4, q_up, q_down)
-    )
+    up3, down3, up4, down4, q_own = lax.optimization_barrier((up3, down3, up4, down4, q_own))
+    q_up = along_z(q_own, -1)
+    q_down = along_z(q_own, 1)
     q_up2 = along_z(q_up, -1)
     q_down2 = along_z(q_down, 1)
     moved = assemble((up3, down3, up4, down4))
@@ -438,13 +441,24 @@
     tags = jnp.where(tags < 0, -1, tags + base)
 
     split = NX * stay
+    itself = in_vmem(
+        self_kernel,
+        "itself",
+        jax.ShapeDtypeStruct((per_device, HD + PACK, ROWS), jnp.bfloat16),
+        q_own,
+        own,
+        scratch=[
+            pltpu.VMEM((per_device, HD + PACK, ROWS), jnp.float32),
+            pltpu.VMEM((per_device, 1, ROWS), jnp.float32),
+        ],
+    )
     near = attention(
         near_kernel,
         "near",
         tags[: 3 * NX],
         here,
         [q_own, q_up, q_down],
-        [own],
+        [],
         3,
         3 * NX,
         10,
@@ -482,6 +496,7 @@
         last_kernel,
         "last",
         jax.ShapeDtypeStruct(queries.shape, jnp.bfloat16),
+        itself,
         own_part,
         home_up,
         home_down,

time: 263 us -> 279 us (1.061)
  waiting for transfers between devices: 101 us -> 110 us
    pallas_call x1 -> x2, Pallas kernels: 3.06 us -> 12.2 us  [in_vmem(): pl.pallas_call(kernel, out_shape=out, in_specs=[vmem] * len(arrays), out_...]
    ppermute x12, waiting for transfers between devices: 100 us -> 109 us  [along_z(): return lax.ppermute(array, 'z', [(i, (i + shift) % NZ) for i in range(NZ)])]
    pallas_call x3, Pallas kernels: 43.2 us -> 35.1 us  [attention(): pl.pallas_call(kernel, out_shape=(jax.ShapeDtypeStruct((n, HD + PACK, ROW...]
    ppermute x12, starting transfers between devices: 21.3 us -> 24.3 us  [along_z(): return lax.ppermute(array, 'z', [(i, (i + shift) % NZ) for i in range(NZ)])]
    unnamed x43 -> x25, local copies, waits for them, and re-layouts: 6.12 us -> 3.92 us
  transfers between devices with their start and end apart: 21 -> 21, of which waited for: 5 -> 7; matrix products, arithmetic and copies ran while one was open for 3% -> 4% of each run, Pallas kernels for 24% -> 23%
where the time goes in v9:
time: 279 us; the launch traced here: 275 us
  waiting for transfers between devices  110 us (39%)
  Pallas kernels  68.6 us (25%)
  starting transfers between devices  41.5 us (15%)
  blocking collectives  24.5 us (9%)
  between operations  13.5 us (5%)
  other arithmetic  10.1 us (4%)
  local copies, waits for them, and re-layouts  7.29 us (3%)
    ppermute x12, waiting for transfers between devices, along_z(): return lax.ppermute(array, 'z', [(i, (i + shift) % NZ) for i in range(NZ)])  109 us
    pallas_call x3, Pallas kernels, attention(): pl.pallas_call(kernel, out_shape=(jax.ShapeDtypeStruct((n, HD + PACK, ROW...  35.1 us
    all_to_all x1, blocking collectives, body(): chips = lax.all_to_all(chip, 'y', split_axis=0, concat_axis=0, tiled=True)  24.5 us
    ppermute x12, starting transfers between devices, along_z(): return lax.ppermute(array, 'z', [(i, (i + shift) % NZ) for i in range(NZ)])  24.3 us
    pallas_call x2, Pallas kernels, in_vmem(): pl.pallas_call(kernel, out_shape=out, in_specs=[vmem] * len(arrays), out_...  12.2 us
    all_to_all x2, starting transfers between devices, over_x(): return lax.all_to_all(items, 'x', split_axis=0, concat_axis=0, tiled=True)  9.84 us
    pallas_call x2, Pallas kernels, take_rows(): pl.pallas_call(row_copies, out_shape=tuple((jax.ShapeDtypeStruct((n,) + c...  9.63 us
    pallas_call x2, Pallas kernels, project(): pl.pallas_call(project_kernel, out_shape=jax.ShapeDtypeStruct((NY, contex...  9.6 us
  transfers between devices with their start and end apart: 21, of which 7 were waited for; matrix products, arithmetic and copies ran while one was open for 4% of the time, Pallas kernels for 23%

profile of v9, /device:TPU:1, one launch (start us, length us, event | category | flops | bytes accessed | tf_op | source)
XLA Modules:
  0.0 275.1 jit_solution(16126556591892546458)
XLA Ops:
  7.4 3.7 %collective-permute-start.5 = (bf16[256,128]{1,0:T(8,128)(2,1)S(1)}, bf16[256,128]{1,0:T(8,128)(2,1)S(1)}, u32[]{:S(2)}, u32[]{:S(2)}) collective-permute-start(bf16[256,128]{1,0:T(8,128)(2,1)S(1)} %get-tuple-element.70), channel_id=1, source_target_pairs={{0,128},{64,192},{128,0},{192,64},{1,129},{65,193},{129,1},{193,65... | collective-permute-start | bytes 196616 | tf_op jit(solution)/shard_map/ppermute | solution.py:376
  16.0 2.4 multiply_reduce_fusion
  18.4 2.5 select_reduce_fusion
  22.6 3.6 %take_rows.2 = (bf16[4,512,256]{2,1,0:T(8,128)(2,1)S(1)}, bf16[4,512,256]{2,1,0:T(8,128)(2,1)S(1)}, bf16[2,512,256]{2,1,0:T(8,128)(2,1)}, bf16[2,512,256]{2,1,0:T(8,128)(2,1)S(1)}) custom-call(s32[12]{0:T(128)S(1)} %reshape.160.rows_ref, bf16[16,512,256]{2,1,0:T(8,128)(2,1)} %bitcast.28), custom_call_target="tpu_custom_call" | custom-call | tf_op jit(solution)/shard_map/take_rows/pallas_call | solution.py:87
  26.2 6.0 %take_rows.3 = bf16[20,512,256]{2,1,0:T(8,128)(2,1)} custom-call(s32[20]{0:T(128)S(1)} %reshape.162.rows_ref, bf16[16,512,256]{2,1,0:T(8,128)(2,1)} %bitcast.29), custom_call_target="tpu_custom_call" | custom-call | tf_op jit(solution)/shard_map/take_rows/pallas_call | solution.py:87
  33.9 5.2 %all-to-all-start = ((bf16[4,5,512,256]{3,2,1,0:T(8,128)(2,1)}), bf16[4,5,512,256]{3,2,1,0:T(8,128)(2,1)}, u32[]{:S(2)}, u32[]{:S(2)}) async-start(bf16[4,5,512,256]{3,2,1,0:T(8,128)(2,1)} %bitcast.27), calls=%async_computation | async-start | bytes 10485760 | tf_op jit(solution)/shard_map/all_to_all | solution.py:380
  40.8 4.3 %collective-permute-start.1 = (bf16[4,512,256]{2,1,0:T(8,128)(2,1)S(1)}, bf16[4,512,256]{2,1,0:T(8,128)(2,1)S(1)}, u32[]{:S(2)}, u32[]{:S(2)}) collective-permute-start(bf16[4,512,256]{2,1,0:T(8,128)(2,1)S(1)} %get-tuple-element.42), channel_id=1, source_target_pairs={{0,56},{8,0},{16,8},{24,16},{32,24},{40,32},{48,40},{56,48},{1,57}... | collective-permute-start | bytes 3145736 | tf_op jit(solution)/shard_map/ppermute | solution.py:372
  45.2 3.6 %collective-permute-start.3 = (bf16[2,512,256]{2,1,0:T(8,128)(2,1)S(1)}, bf16[2,512,256]{2,1,0:T(8,128)(2,1)S(1)}, u32[]{:S(2)}, u32[]{:S(2)}) collective-permute-start(bf16[2,512,256]{2,1,0:T(8,128)(2,1)S(1)} %get-tuple-element.44), channel_id=1, source_target_pairs={{0,48},{8,56},{16,0},{24,8},{32,16},{40,24},{48,32},{56,40},{1,49}... | collective-permute-start | bytes 1572872 | tf_op jit(solution)/shard_map/ppermute | solution.py:372
  49.1 41.5 %collective-permute-done.2.up4 = bf16[2,512,256]{2,1,0:T(8,128)(2,1)S(1)} collective-permute-done((bf16[2,512,256]{2,1,0:T(8,128)(2,1)}, bf16[2,512,256]{2,1,0:T(8,128)(2,1)S(1)}, u32[]{:S(2)}, u32[]{:S(2)}) %collective-permute-start.2) | collective-permute-done | bytes 524320 | tf_op jit(solution)/shard_map/ppermute | solution.py:372
  90.6 10.6 %collective-permute-done.3.down4 = bf16[2,512,256]{2,1,0:T(8,128)(2,1)S(1)} collective-permute-done((bf16[2,512,256]{2,1,0:T(8,128)(2,1)S(1)}, bf16[2,512,256]{2,1,0:T(8,128)(2,1)S(1)}, u32[]{:S(2)}, u32[]{:S(2)}) %collective-permute-start.3) | collective-permute-done | bytes 524320 | tf_op jit(solution)/shard_map/ppermute | solution.py:372
  103.3 4.7 %all-to-all-start.1 = ((bf16[4,3,512,256]{3,2,1,0:T(8,128)(2,1)}), bf16[4,3,512,256]{3,2,1,0:T(8,128)(2,1)}, u32[]{:S(2)}, u32[]{:S(2)}) async-start(bf16[4,3,512,256]{3,2,1,0:T(8,128)(2,1)} %assemble.1), calls=%async_computation.1 | async-start | bytes 6291456 | tf_op jit(solution)/shard_map/all_to_all | solution.py:380
  111.9 24.0 %collective-permute-done.8.q2 = bf16[3,1024,128]{2,1,0:T(8,128)(2,1)S(1)} collective-permute-done((bf16[3,1024,128]{2,1,0:T(8,128)(2,1)S(1)}, bf16[3,1024,128]{2,1,0:T(8,128)(2,1)S(1)}, u32[]{:S(2)}, u32[]{:S(2)}) %collective-permute-start.8) | collective-permute-done | bytes 786464 | tf_op jit(solution)/shard_map/ppermute | solution.py:372
  138.2 2.7 collective-permute-start.9
  141.2 12.4 %near.1 = (bf16[3,144,1024]{2,1,0:T(8,128)(2,1)S(1)}, bf16[3,144,1024]{2,1,0:T(8,128)(2,1)}, bf16[3,144,1024]{2,1,0:T(8,128)(2,1)}) custom-call(s32[12]{0:T(128)S(1)} %get-tuple-element.72.tags, bf16[4,5,512,256]{3,2,1,0:T(8,128)(2,1)} %all-to-all-done.here, bf16[3,1024,128]{2,1,0:T(8,128)(2,1)S(1)} %bitcast.24, ...), custom_call_target="tpu_custom_call" | custom-call | flops 5242880 | bytes 5120 | tf_op jit(solution)/shard_map/near/pallas_call | solution.py:286
  160.9 7.7 %far.1 = (bf16[3,144,1024]{2,1,0:T(8,128)(2,1)S(1)}, bf16[3,144,1024]{2,1,0:T(8,128)(2,1)S(1)}) custom-call(s32[8]{0:T(128)S(1)} %slice.43.tags, bf16[4,5,512,256]{3,2,1,0:T(8,128)(2,1)} %all-to-all-done.here, bf16[3,1024,128]{2,1,0:T(8,128)(2,1)S(1)} %copy-done.3, bf16[3,1024,128]{2,1,0:T(8,128)(2,1)S(1)} %copy-done.1), custom_call_target="tpu_custom_call" | custom-call | flops 3145728 | bytes 3072 | tf_op jit(solution)/shard_map/far/pallas_call | solution.py:286
  170.5 15.0 %move.1 = (bf16[3,144,1024]{2,1,0:T(8,128)(2,1)}, bf16[3,144,1024]{2,1,0:T(8,128)(2,1)}) custom-call(s32[12]{0:T(128)S(1)} %get-tuple-element.71.tags, bf16[4,3,512,256]{3,2,1,0:T(8,128)(2,1)} %all-to-all-done.1.moved, bf16[3,1024,128]{2,1,0:T(8,128)(2,1)S(1)} %copy-done.3, bf16[3,1024,128]{2,1,0:T(8,128)(2,1)S(1)} %copy-done.1, ...), custom_call_target="tpu_custom_call" | custom-call | flops 209715200000 | bytes 204800000 | tf_op jit(solution)/shard_map/move/pallas_call | solution.py:286
  186.3 2.9 %collective-permute-start.14 = (bf16[3,144,1024]{2,1,0:T(8,128)(2,1)}, bf16[3,144,1024]{2,1,0:T(8,128)(2,1)}, u32[]{:S(2)}, u32[]{:S(2)}) collective-permute-start(bf16[3,144,1024]{2,1,0:T(8,128)(2,1)} %get-tuple-element.66), channel_id=1, source_target_pairs={{0,48},{8,56},{16,0},{24,8},{32,16},{40,24},{48,32},{56,40},{1,49}... | collective-permute-start | bytes 2654216 | tf_op jit(solution)/shard_map/ppermute | solution.py:372
  189.3 8.9 %itself.1.refs_0_ = bf16[3,144,1024]{2,1,0:T(8,128)(2,1)S(1)} custom-call(bf16[3,1024,128]{2,1,0:T(8,128)(2,1)S(1)} %bitcast.25, bf16[384,256]{1,0:T(8,128)(2,1)S(1)} %bitcast.26), custom_call_target="tpu_custom_call" | custom-call | tf_op jit(solution)/shard_map/itself/pallas_call | solution.py:360
  198.2 15.3 %collective-permute-done.13.refs_4_ = bf16[3,144,1024]{2,1,0:T(8,128)(2,1)} collective-permute-done((bf16[3,144,1024]{2,1,0:T(8,128)(2,1)}, bf16[3,144,1024]{2,1,0:T(8,128)(2,1)}, u32[]{:S(2)}, u32[]{:S(2)}) %collective-permute-start.13) | collective-permute-done | bytes 884768 | tf_op jit(solution)/shard_map/ppermute | solution.py:372
  213.5 15.2 %collective-permute-done.14.refs_5_ = bf16[3,144,1024]{2,1,0:T(8,128)(2,1)} collective-permute-done((bf16[3,144,1024]{2,1,0:T(8,128)(2,1)}, bf16[3,144,1024]{2,1,0:T(8,128)(2,1)}, u32[]{:S(2)}, u32[]{:S(2)}) %collective-permute-start.14) | collective-permute-done | bytes 884768 | tf_op jit(solution)/shard_map/ppermute | solution.py:372
  228.7 3.2 %last.1.context_ref = bf16[384,1024]{1,0:T(8,128)(2,1)S(1)} custom-call(bf16[3,144,1024]{2,1,0:T(8,128)(2,1)S(1)} %itself.1.refs_0_, bf16[3,144,1024]{2,1,0:T(8,128)(2,1)S(1)} %get-tuple-element.57.refs_1_, bf16[3,144,1024]{2,1,0:T(8,128)(2,1)} %collective-permute-done.11.refs_2_, bf16[3,144,1024]{2,1,0:T(8,128)(2,1)} %collective-permute-done.12.refs_3_, ...), custom_call_target="tpu_custom_call" | custom-call | tf_op jit(solution)/shard_map/last/pallas_call | solution.py:360
  231.9 4.8 %theirs.1 = bf16[4,384,512]{2,1,0:T(8,128)(2,1)S(1)} custom-call(s32[2]{0:T(128)S(1)} %pad_add_fusion.1.place, bf16[384,1024]{1,0:T(8,128)(2,1)S(1)} %last.1.context_ref, bf16[768,4096]{1,0:T(8,128)(2,1)} %all-gather.8.cloned.1.call-done.most_ref, bf16[4,256,1024]{2,1,0:T(8,128)(2,1)} %all-gather.6.cloned.1.call-done.rest_ref), custom_call_target="tpu_custom_call" | custom-call | flops 1610612736 | bytes 4194304 | tf_op jit(solution)/shard_map/theirs/pallas_call | solution.py:332
  237.8 4.8 %ours.1 = bf16[4,384,512]{2,1,0:T(8,128)(2,1)S(1)} custom-call(s32[2]{0:T(128)S(1)} %pad_add_fusion.place, bf16[384,1024]{1,0:T(8,128)(2,1)S(1)} %last.1.context_ref, bf16[768,4096]{1,0:T(8,128)(2,1)} %all-gather.8.cloned.1.call-done.most_ref, bf16[4,256,1024]{2,1,0:T(8,128)(2,1)} %all-gather.6.cloned.1.call-done.rest_ref), custom_call_target="tpu_custom_call" | custom-call | flops 1610612736 | bytes 4194304 | tf_op jit(solution)/shard_map/ours/pallas_call | solution.py:332
  243.1 24.5 %all_to_all.15 = bf16[4,384,512]{2,1,0:T(8,128)(2,1)S(1)} all-to-all(bf16[4,384,512]{2,1,0:T(8,128)(2,1)S(1)} %add_convert_fusion), channel_id=1, replica_groups=mesh['x'=4,'z'=8,'y'=4,'core'=2] {'y'}, dimensions={0} | all-to-all | bytes 3145728 | tf_op jit(solution)/shard_map/all_to_all | solution.py:511
  (90 shorter events, 32.3 us)
Async XLA Ops:
  6.5 151.3 %all-gather.4.cloned.1.call-start = ((), (), s32[]{:S(2)}) async-start(), calls=%async_computation.3 | async-start | bytes 1769472 | tf_op jit(solution)/shard_map/all_gather | solution.py:404
  7.4 24.9 %collective-permute-start.5 = (bf16[256,128]{1,0:T(8,128)(2,1)S(1)}, bf16[256,128]{1,0:T(8,128)(2,1)S(1)}, u32[]{:S(2)}, u32[]{:S(2)}) collective-permute-start(bf16[256,128]{1,0:T(8,128)(2,1)S(1)} %get-tuple-element.70), channel_id=1, source_target_pairs={{0,128},{64,192},{128,0},{192,64},{1,129},{65,193},{129,1},{193,65... | collective-permute-start | bytes 196616 | tf_op jit(solution)/shard_map/ppermute | solution.py:376
  11.1 21.2 %collective-permute-start.6 = (bf16[256,128]{1,0:T(8,128)(2,1)S(1)}, bf16[256,128]{1,0:T(8,128)(2,1)S(1)}, u32[]{:S(2)}, u32[]{:S(2)}) collective-permute-start(bf16[256,128]{1,0:T(8,128)(2,1)S(1)} %get-tuple-element.70), channel_id=1, source_target_pairs={{0,64},{64,128},{128,192},{192,0},{1,65},{65,129},{129,193},{193,1... | collective-permute-start | bytes 196616 | tf_op jit(solution)/shard_map/ppermute | solution.py:376
  11.4 20.9 %collective-permute-start.4 = (bf16[256,128]{1,0:T(8,128)(2,1)S(1)}, bf16[256,128]{1,0:T(8,128)(2,1)}, u32[]{:S(2)}, u32[]{:S(2)}) collective-permute-start(bf16[256,128]{1,0:T(8,128)(2,1)S(1)} %get-tuple-element.70), channel_id=1, source_target_pairs={{0,192},{64,0},{128,64},{192,128},{1,193},{65,1},{129,65},{193,129... | collective-permute-start | bytes 196616 | tf_op jit(solution)/shard_map/ppermute | solution.py:376
  33.9 14.9 %copy-start.7 = (bf16[384,1024]{1,0:T(8,128)(2,1)S(1)}, bf16[384,1024]{1,0:T(8,128)(2,1)}, u32[]{:S(2)}) copy-start(bf16[384,1024]{1,0:T(8,128)(2,1)} %param.9) | copy-start | bytes 2359300
  33.9 69.4 %all-to-all-start = ((bf16[4,5,512,256]{3,2,1,0:T(8,128)(2,1)}), bf16[4,5,512,256]{3,2,1,0:T(8,128)(2,1)}, u32[]{:S(2)}, u32[]{:S(2)}) async-start(bf16[4,5,512,256]{3,2,1,0:T(8,128)(2,1)} %bitcast.27), calls=%async_computation | async-start | bytes 10485760 | tf_op jit(solution)/shard_map/all_to_all | solution.py:380
  39.1 118.8 %all-gather.6.cloned.1.call-start = ((), (), s32[]{:S(2)}) async-start(), calls=%async_computation.4 | async-start | bytes 2359296 | tf_op jit(solution)/shard_map/all_gather | solution.py:408
  39.8 61.4 %collective-permute-start = (bf16[4,512,256]{2,1,0:T(8,128)(2,1)S(1)}, bf16[4,512,256]{2,1,0:T(8,128)(2,1)S(1)}, u32[]{:S(2)}, u32[]{:S(2)}) collective-permute-start(bf16[4,512,256]{2,1,0:T(8,128)(2,1)S(1)} %get-tuple-element.41), channel_id=1, source_target_pairs={{0,8},{8,16},{16,24},{24,32},{32,40},{40,48},{48,56},{56,0},{1,9},... | collective-permute-start | bytes 3145736 | tf_op jit(solution)/shard_map/ppermute | solution.py:372
  40.8 60.3 %collective-permute-start.1 = (bf16[4,512,256]{2,1,0:T(8,128)(2,1)S(1)}, bf16[4,512,256]{2,1,0:T(8,128)(2,1)S(1)}, u32[]{:S(2)}, u32[]{:S(2)}) collective-permute-start(bf16[4,512,256]{2,1,0:T(8,128)(2,1)S(1)} %get-tuple-element.42), channel_id=1, source_target_pairs={{0,56},{8,0},{16,8},{24,16},{32,24},{40,32},{48,40},{56,48},{1,57}... | collective-permute-start | bytes 3145736 | tf_op jit(solution)/shard_map/ppermute | solution.py:372
  45.2 45.4 %collective-permute-start.2 = (bf16[2,512,256]{2,1,0:T(8,128)(2,1)}, bf16[2,512,256]{2,1,0:T(8,128)(2,1)S(1)}, u32[]{:S(2)}, u32[]{:S(2)}) collective-permute-start(bf16[2,512,256]{2,1,0:T(8,128)(2,1)} %get-tuple-element.43), channel_id=1, source_target_pairs={{0,16},{8,24},{16,32},{24,40},{32,48},{40,56},{48,0},{56,8},{1,17}... | collective-permute-start | bytes 1572872 | tf_op jit(solution)/shard_map/ppermute | solution.py:372
  45.2 56.0 %collective-permute-start.3 = (bf16[2,512,256]{2,1,0:T(8,128)(2,1)S(1)}, bf16[2,512,256]{2,1,0:T(8,128)(2,1)S(1)}, u32[]{:S(2)}, u32[]{:S(2)}) collective-permute-start(bf16[2,512,256]{2,1,0:T(8,128)(2,1)S(1)} %get-tuple-element.44), channel_id=1, source_target_pairs={{0,48},{8,56},{16,0},{24,8},{32,16},{40,24},{48,32},{56,40},{1,49}... | collective-permute-start | bytes 1572872 | tf_op jit(solution)/shard_map/ppermute | solution.py:372
  103.3 37.8 %copy-start.11 = (s32[32]{0:T(128)S(1)}, s32[32]{0:T(128)}, u32[]{:S(2)}) copy-start(s32[32]{0:T(128)} %constant.119) | copy-start | bytes 388
  103.3 67.2 %all-to-all-start.1 = ((bf16[4,3,512,256]{3,2,1,0:T(8,128)(2,1)}), bf16[4,3,512,256]{3,2,1,0:T(8,128)(2,1)}, u32[]{:S(2)}, u32[]{:S(2)}) async-start(bf16[4,3,512,256]{3,2,1,0:T(8,128)(2,1)} %assemble.1), calls=%async_computation.1 | async-start | bytes 6291456 | tf_op jit(solution)/shard_map/all_to_all | solution.py:380
  108.0 123.9 %all-gather.8.cloned.1.call-start = ((), (), s32[]{:S(2)}) async-start(), calls=%async_computation.5 | async-start | bytes 7864320 | tf_op jit(solution)/shard_map/all_gather | solution.py:467
  108.0 30.2 %collective-permute-start.7 = (bf16[3,1024,128]{2,1,0:T(8,128)(2,1)S(1)}, bf16[3,1024,128]{2,1,0:T(8,128)(2,1)S(1)}, u32[]{:S(2)}, u32[]{:S(2)}) collective-permute-start(bf16[3,1024,128]{2,1,0:T(8,128)(2,1)S(1)} %bitcast.22), channel_id=1, source_target_pairs={{0,56},{8,0},{16,8},{24,16},{32,24},{40,32},{48,40},{56,48},{1,57}... | collective-permute-start | bytes 2359304 | tf_op jit(solution)/shard_map/ppermute | solution.py:372
  109.8 26.1 %collective-permute-start.8 = (bf16[3,1024,128]{2,1,0:T(8,128)(2,1)S(1)}, bf16[3,1024,128]{2,1,0:T(8,128)(2,1)S(1)}, u32[]{:S(2)}, u32[]{:S(2)}) collective-permute-start(bf16[3,1024,128]{2,1,0:T(8,128)(2,1)S(1)} %bitcast.23), channel_id=1, source_target_pairs={{0,8},{8,16},{16,24},{24,32},{32,40},{40,48},{48,56},{56,0},{1,9},... | collective-permute-start | bytes 2359304 | tf_op jit(solution)/shard_map/ppermute | solution.py:372
  135.9 18.3 %collective-permute-start.10 = (bf16[3,1024,128]{2,1,0:T(8,128)(2,1)S(1)}, bf16[3,1024,128]{2,1,0:T(8,128)(2,1)S(1)}, u32[]{:S(2)}, u32[]{:S(2)}) collective-permute-start(bf16[3,1024,128]{2,1,0:T(8,128)(2,1)S(1)} %collective-permute-done.8.q2), channel_id=1, source_target_pairs={{0,8},{8,16},{16,24},{24,32},{32,40},{40,48},{48,56},{56,0},{1,9},... | collective-permute-start | bytes 2359304 | tf_op jit(solution)/shard_map/ppermute | solution.py:372
  138.2 18.7 %collective-permute-start.9 = (bf16[3,1024,128]{2,1,0:T(8,128)(2,1)S(1)}, bf16[3,1024,128]{2,1,0:T(8,128)(2,1)S(1)}, u32[]{:S(2)}, u32[]{:S(2)}) collective-permute-start(bf16[3,1024,128]{2,1,0:T(8,128)(2,1)S(1)} %collective-permute-done.7.q1), channel_id=1, source_target_pairs={{0,56},{8,0},{16,8},{24,16},{32,24},{40,32},{48,40},{56,48},{1,57}... | collective-permute-start | bytes 2359304 | tf_op jit(solution)/shard_map/ppermute | solution.py:372
  157.9 40.3 %collective-permute-start.11 = (bf16[3,144,1024]{2,1,0:T(8,128)(2,1)}, bf16[3,144,1024]{2,1,0:T(8,128)(2,1)}, u32[]{:S(2)}, u32[]{:S(2)}) collective-permute-start(bf16[3,144,1024]{2,1,0:T(8,128)(2,1)} %get-tuple-element.58), channel_id=1, source_target_pairs={{0,8},{8,16},{16,24},{24,32},{32,40},{40,48},{48,56},{56,0},{1,9},... | collective-permute-start | bytes 2654216 | tf_op jit(solution)/shard_map/ppermute | solution.py:372
  159.4 38.8 %collective-permute-start.12 = (bf16[3,144,1024]{2,1,0:T(8,128)(2,1)}, bf16[3,144,1024]{2,1,0:T(8,128)(2,1)}, u32[]{:S(2)}, u32[]{:S(2)}) collective-permute-start(bf16[3,144,1024]{2,1,0:T(8,128)(2,1)} %get-tuple-element.59), channel_id=1, source_target_pairs={{0,56},{8,0},{16,8},{24,16},{32,24},{40,32},{48,40},{56,48},{1,57}... | collective-permute-start | bytes 2654216 | tf_op jit(solution)/shard_map/ppermute | solution.py:372
  170.5 18.8 %copy-start.4 = (bf16[384,1,256]{2,0,1:T(8,128)(2,1)S(1)}, bf16[384,1,256]{2,0,1:T(8,128)(2,1)}, u32[]{:S(2)}) copy-start(bf16[384,1,256]{2,0,1:T(8,128)(2,1)} %param.10) | copy-start | bytes 589828
  185.6 28.0 %collective-permute-start.13 = (bf16[3,144,1024]{2,1,0:T(8,128)(2,1)}, bf16[3,144,1024]{2,1,0:T(8,128)(2,1)}, u32[]{:S(2)}, u32[]{:S(2)}) collective-permute-start(bf16[3,144,1024]{2,1,0:T(8,128)(2,1)} %get-tuple-element.65), channel_id=1, source_target_pairs={{0,16},{8,24},{16,32},{24,40},{32,48},{40,56},{48,0},{56,8},{1,17}... | collective-permute-start | bytes 2654216 | tf_op jit(solution)/shard_map/ppermute | solution.py:372
  186.3 42.4 %collective-permute-start.14 = (bf16[3,144,1024]{2,1,0:T(8,128)(2,1)}, bf16[3,144,1024]{2,1,0:T(8,128)(2,1)}, u32[]{:S(2)}, u32[]{:S(2)}) collective-permute-start(bf16[3,144,1024]{2,1,0:T(8,128)(2,1)} %get-tuple-element.66), channel_id=1, source_target_pairs={{0,48},{8,56},{16,0},{24,8},{32,16},{40,24},{48,32},{56,40},{1,49}... | collective-permute-start | bytes 2654216 | tf_op jit(solution)/shard_map/ppermute | solution.py:372
  236.8 5.8 %collective-permute-start.15 = (bf16[4,384,512]{2,1,0:T(8,128)(2,1)S(1)}, bf16[4,384,512]{2,1,0:T(8,128)(2,1)S(1)}, u32[]{:S(2)}, u32[]{:S(2)}) collective-permute-start(bf16[4,384,512]{2,1,0:T(8,128)(2,1)S(1)} %theirs.1), channel_id=1, source_target_pairs={{0,1},{1,0},{2,3},{3,2},{4,5},{5,4},{6,7},{7,6},{8,9},{9,8},{10,11... | collective-permute-start | bytes 4718600 | tf_op jit(solution)/shard_map/ppermute | solution.py:508
  (9 other events, 35.6 us)
Sparse Core Ops, SparseCore 0:
  15.5 48.8 all-gather.3
  66.1 69.4 all-gather.5
  161.0 69.1 all-gather.7

commit v10 on v9

--- a/solution.py
+++ b/solution.py
@@ -400,11 +400,13 @@
     moving = take_rows(cache, rows[:, stay:].T.reshape(-1), (4, 4, 2, 2))
     moving, staying = lax.optimization_barrier((moving, rows[:, :stay].reshape(-1)))
     (here,) = take_rows(cache, staying, (NX * stay,))
+    q_up = along_z(q_own, -1)
+    q_down = along_z(q_own, 1)
     cut = out_weight.shape[0] * 3 // 4
     most = lax.all_gather(out_weight[:cut], "z", axis=1, tiled=True)
     rest = out_weight[cut:]
     rest = jnp.stack([rest] + [along_x(rest, -distance) for distance in range(1, NX)])
-    here, rest = lax.optimization_barrier((here, rest))
+    here, q_up, q_down, rest = lax.optimization_barrier((here, q_up, q_down, rest))
     rest = lax.all_gather(rest, "z", axis=2, tiled=True)
     here = over_x(here.reshape(NX, stay, PLEN, 2 * HD))
     up3, down3, up4, down4 = moving
@@ -412,9 +414,9 @@
     down3 = along_z(down3, -1)
     up4 = along_z(up4, 2)
     down4 = along_z(down4, -2)
-    up3, down3, up4, down4, q_own = lax.optimization_barrier((up3, down3, up4, down4, q_own))
-    q_up = along_z(q_own, -1)
-    q_down = along_z(q_own, 1)
+    up3, down3, up4, down4, q_up, q_down = lax.optimization_barrier(
+        (up3, down3, up4, down4, q_up, q_down)
+    )
     q_up2 = along_z(q_up, -1)
     q_down2 = along_z(q_down, 1)
     moved = assemble((up3, down3, up4, down4))
@@ -463,7 +465,8 @@
         3 * NX,
         10,
     )
-    near, q_up2, q_down2, most, rest = lax.optimization_barrier((near, q_up2, q_down2, most, rest))
+    near, most, rest = lax.optimization_barrier((near, most, rest))
+    near, q_up2, q_down2 = lax.optimization_barrier((near, q_up2, q_down2))
     most = lax.all_gather(most, "x", axis=1, tiled=True)
     own_part, near_up, near_down = near
     home_up = along_z(near_up, 1)

time: 279 us -> 263 us (0.943)
  waiting for transfers between devices: 110 us -> 103 us
  starting transfers between devices: 41.5 us -> 38.7 us
    ppermute x12, waiting for transfers between devices: 109 us -> 85.8 us  [along_z(): return lax.ppermute(array, 'z', [(i, (i + shift) % NZ) for i in range(NZ)])]
    all_gather x1, waiting for transfers between devices: 0.01 us -> 16 us  [body(): rest = lax.all_gather(rest, 'z', axis=2, tiled=True)]
  transfers between devices with their start and end apart: 21 -> 21, of which waited for: 7 -> 7; matrix products, arithmetic and copies ran while one was open for 4% -> 3% of each run, Pallas kernels for 23% -> 24%
where the time goes in v10:
time: 263 us; the launch traced here: 260 us
  waiting for transfers between devices  103 us (39%)
  Pallas kernels  67 us (25%)
  starting transfers between devices  38.7 us (15%)
  blocking collectives  24.6 us (9%)
  between operations  13.5 us (5%)
  other arithmetic  7.53 us (3%)
  local copies, waits for them, and re-layouts  6.37 us (2%)
    ppermute x12, waiting for transfers between devices, along_z(): return lax.ppermute(array, 'z', [(i, (i + shift) % NZ) for i in range(NZ)])  85.8 us
    pallas_call x3, Pallas kernels, attention(): pl.pallas_call(kernel, out_shape=(jax.ShapeDtypeStruct((n, HD + PACK, ROW...  34.3 us
    all_to_all x1, blocking collectives, body(): chips = lax.all_to_all(chip, 'y', split_axis=0, concat_axis=0, tiled=True)  24.6 us
    ppermute x12, starting transfers between devices, along_z(): return lax.ppermute(array, 'z', [(i, (i + shift) % NZ) for i in range(NZ)])  23.2 us
    all_gather x1, waiting for transfers between devices, body(): rest = lax.all_gather(rest, 'z', axis=2, tiled=True)  16 us
    pallas_call x2, Pallas kernels, in_vmem(): pl.pallas_call(kernel, out_shape=out, in_specs=[vmem] * len(arrays), out_...  12.2 us
    all_to_all x2, starting transfers between devices, over_x(): return lax.all_to_all(items, 'x', split_axis=0, concat_axis=0, tiled=True)  9.72 us
    pallas_call x2, Pallas kernels, project(): pl.pallas_call(project_kernel, out_shape=jax.ShapeDtypeStruct((NY, contex...  9.6 us
  transfers between devices with their start and end apart: 21, of which 7 were waited for; matrix products, arithmetic and copies ran while one was open for 3% of the time, Pallas kernels for 24%

profile of v10, /device:TPU:1, one launch (start us, length us, event | category | flops | bytes accessed | tf_op | source)
XLA Modules:
  0.0 260.2 jit_solution(16360174698004559156)
XLA Ops:
  8.0 3.3 %collective-permute-start.6 = (bf16[256,128]{1,0:T(8,128)(2,1)}, bf16[256,128]{1,0:T(8,128)(2,1)}, u32[]{:S(2)}, u32[]{:S(2)}) collective-permute-start(bf16[256,128]{1,0:T(8,128)(2,1)} %get-tuple-element.82), channel_id=1, source_target_pairs={{0,192},{64,0},{128,64},{192,128},{1,193},{65,1},{129,65},{193,129... | collective-permute-start | bytes 196616 | tf_op jit(solution)/shard_map/ppermute | solution.py:376
  14.0 5.7 %collective-permute-start.4 = (bf16[3,1024,128]{2,1,0:T(8,128)(2,1)S(1)}, bf16[3,1024,128]{2,1,0:T(8,128)(2,1)S(1)}, u32[]{:S(2)}, u32[]{:S(2)}) collective-permute-start(bf16[3,1024,128]{2,1,0:T(8,128)(2,1)S(1)} %bitcast.22), channel_id=1, source_target_pairs={{0,56},{8,0},{16,8},{24,16},{32,24},{40,32},{48,40},{56,48},{1,57}... | collective-permute-start | bytes 2359304 | tf_op jit(solution)/shard_map/ppermute | solution.py:372
  25.0 2.8 %take_rows.2 = (bf16[4,512,256]{2,1,0:T(8,128)(2,1)S(1)}, bf16[4,512,256]{2,1,0:T(8,128)(2,1)S(1)}, bf16[2,512,256]{2,1,0:T(8,128)(2,1)S(1)}, bf16[2,512,256]{2,1,0:T(8,128)(2,1)S(1)}) custom-call(s32[12]{0:T(128)S(1)} %reshape.164.rows_ref, bf16[16,512,256]{2,1,0:T(8,128)(2,1)} %bitcast.28), custom_call_target="tpu_custom_call" | custom-call | tf_op jit(solution)/shard_map/take_rows/pallas_call | solution.py:87
  27.9 6.0 %take_rows.3 = bf16[20,512,256]{2,1,0:T(8,128)(2,1)} custom-call(s32[20]{0:T(128)S(1)} %reshape.166.rows_ref, bf16[16,512,256]{2,1,0:T(8,128)(2,1)} %bitcast.29), custom_call_target="tpu_custom_call" | custom-call | tf_op jit(solution)/shard_map/take_rows/pallas_call | solution.py:87
  37.1 3.1 %collective-permute-done.5.q2 = bf16[3,1024,128]{2,1,0:T(8,128)(2,1)S(1)} collective-permute-done((bf16[3,1024,128]{2,1,0:T(8,128)(2,1)S(1)}, bf16[3,1024,128]{2,1,0:T(8,128)(2,1)S(1)}, u32[]{:S(2)}, u32[]{:S(2)}) %collective-permute-start.5) | collective-permute-done | bytes 786464 | tf_op jit(solution)/shard_map/ppermute | solution.py:372
  40.2 5.0 %all-to-all-start = ((bf16[4,5,512,256]{3,2,1,0:T(8,128)(2,1)}), bf16[4,5,512,256]{3,2,1,0:T(8,128)(2,1)}, u32[]{:S(2)}, u32[]{:S(2)}) async-start(bf16[4,5,512,256]{3,2,1,0:T(8,128)(2,1)} %bitcast.27), calls=%async_computation | async-start | bytes 10485760 | tf_op jit(solution)/shard_map/all_to_all | solution.py:380
  48.8 3.6 %collective-permute-start.3 = (bf16[2,512,256]{2,1,0:T(8,128)(2,1)}, bf16[2,512,256]{2,1,0:T(8,128)(2,1)S(1)}, u32[]{:S(2)}, u32[]{:S(2)}) collective-permute-start(bf16[2,512,256]{2,1,0:T(8,128)(2,1)} %copy-done.4), channel_id=1, source_target_pairs={{0,48},{8,56},{16,0},{24,8},{32,16},{40,24},{48,32},{56,40},{1,49}... | collective-permute-start | bytes 1572872 | tf_op jit(solution)/shard_map/ppermute | solution.py:372
  52.3 40.9 %collective-permute-done.2.up4 = bf16[2,512,256]{2,1,0:T(8,128)(2,1)S(1)} collective-permute-done((bf16[2,512,256]{2,1,0:T(8,128)(2,1)}, bf16[2,512,256]{2,1,0:T(8,128)(2,1)S(1)}, u32[]{:S(2)}, u32[]{:S(2)}) %collective-permute-start.2) | collective-permute-done | bytes 524320 | tf_op jit(solution)/shard_map/ppermute | solution.py:372
  93.2 9.4 %collective-permute-done.3.down4 = bf16[2,512,256]{2,1,0:T(8,128)(2,1)S(1)} collective-permute-done((bf16[2,512,256]{2,1,0:T(8,128)(2,1)}, bf16[2,512,256]{2,1,0:T(8,128)(2,1)S(1)}, u32[]{:S(2)}, u32[]{:S(2)}) %collective-permute-start.3) | collective-permute-done | bytes 524320 | tf_op jit(solution)/shard_map/ppermute | solution.py:372
  104.8 4.7 %all-to-all-start.1 = ((bf16[4,3,512,256]{3,2,1,0:T(8,128)(2,1)}), bf16[4,3,512,256]{3,2,1,0:T(8,128)(2,1)}, u32[]{:S(2)}, u32[]{:S(2)}) async-start(bf16[4,3,512,256]{3,2,1,0:T(8,128)(2,1)} %assemble.1), calls=%async_computation.1 | async-start | bytes 6291456 | tf_op jit(solution)/shard_map/all_to_all | solution.py:380
  109.7 3.9 %collective-permute-start.10 = (bf16[3,1024,128]{2,1,0:T(8,128)(2,1)S(1)}, bf16[3,1024,128]{2,1,0:T(8,128)(2,1)}, u32[]{:S(2)}, u32[]{:S(2)}) collective-permute-start(bf16[3,1024,128]{2,1,0:T(8,128)(2,1)S(1)} %collective-permute-done.5.q2), channel_id=1, source_target_pairs={{0,8},{8,16},{16,24},{24,32},{32,40},{40,48},{48,56},{56,0},{1,9},... | collective-permute-start | bytes 2359304 | tf_op jit(solution)/shard_map/ppermute | solution.py:372
  113.9 10.3 %near.1 = (bf16[3,144,1024]{2,1,0:T(8,128)(2,1)S(1)}, bf16[3,144,1024]{2,1,0:T(8,128)(2,1)}, bf16[3,144,1024]{2,1,0:T(8,128)(2,1)}) custom-call(s32[12]{0:T(128)S(1)} %get-tuple-element.84.tags, bf16[4,5,512,256]{3,2,1,0:T(8,128)(2,1)} %all-to-all-done.here, bf16[3,1024,128]{2,1,0:T(8,128)(2,1)S(1)} %bitcast.24, ...), custom_call_target="tpu_custom_call" | custom-call | flops 5242880 | bytes 5120 | tf_op jit(solution)/shard_map/near/pallas_call | solution.py:286
  124.2 16.0 %all-gather.6.cloned.1.call-done.rest_ref = bf16[4,256,1024]{2,1,0:T(8,128)(2,1)} async-done(((bf16[4,256,128]{2,1,0:T(8,128)(2,1)}), bf16[4,256,1024]{2,1,0:T(8,128)(2,1)}) %all-gather.6.cloned.1.call-update) | async-done | bytes 2097168 | tf_op jit(solution)/shard_map/all_gather | solution.py:410
  140.2 2.8 %collective-permute-start.11 = (bf16[3,144,1024]{2,1,0:T(8,128)(2,1)}, bf16[3,144,1024]{2,1,0:T(8,128)(2,1)}, u32[]{:S(2)}, u32[]{:S(2)}) collective-permute-start(bf16[3,144,1024]{2,1,0:T(8,128)(2,1)} %get-tuple-element.70), channel_id=1, source_target_pairs={{0,8},{8,16},{16,24},{24,32},{32,40},{40,48},{48,56},{56,0},{1,9},... | collective-permute-start | bytes 2654216 | tf_op jit(solution)/shard_map/ppermute | solution.py:372
  143.9 9.1 %far.1 = (bf16[3,144,1024]{2,1,0:T(8,128)(2,1)S(1)}, bf16[3,144,1024]{2,1,0:T(8,128)(2,1)S(1)}) custom-call(s32[8]{0:T(128)S(1)} %slice.43.tags, bf16[4,5,512,256]{3,2,1,0:T(8,128)(2,1)} %all-to-all-done.here, bf16[3,1024,128]{2,1,0:T(8,128)(2,1)} %collective-permute-done.9.q0, bf16[3,1024,128]{2,1,0:T(8,128)(2,1)} %collective-permute-done.10.q1), custom_call_target="tpu_custom_call" | custom-call | flops 3145728 | bytes 3072 | tf_op jit(solution)/shard_map/far/pallas_call | solution.py:286
  154.9 14.9 %move.1 = (bf16[3,144,1024]{2,1,0:T(8,128)(2,1)}, bf16[3,144,1024]{2,1,0:T(8,128)(2,1)}) custom-call(s32[12]{0:T(128)S(1)} %get-tuple-element.83.tags, bf16[4,3,512,256]{3,2,1,0:T(8,128)(2,1)} %all-to-all-done.1.moved, bf16[3,1024,128]{2,1,0:T(8,128)(2,1)} %collective-permute-done.9.q0, bf16[3,1024,128]{2,1,0:T(8,128)(2,1)} %collective-permute-done.10.q1, ...), custom_call_target="tpu_custom_call" | custom-call | flops 209715200000 | bytes 204800000 | tf_op jit(solution)/shard_map/move/pallas_call | solution.py:286
  169.8 3.2 %collective-permute-start.13 = (bf16[3,144,1024]{2,1,0:T(8,128)(2,1)}, bf16[3,144,1024]{2,1,0:T(8,128)(2,1)}, u32[]{:S(2)}, u32[]{:S(2)}) collective-permute-start(bf16[3,144,1024]{2,1,0:T(8,128)(2,1)} %get-tuple-element.77), channel_id=1, source_target_pairs={{0,16},{8,24},{16,32},{24,40},{32,48},{40,56},{48,0},{56,8},{1,17}... | collective-permute-start | bytes 2654216 | tf_op jit(solution)/shard_map/ppermute | solution.py:372
  173.5 8.9 %itself.1.refs_0_ = bf16[3,144,1024]{2,1,0:T(8,128)(2,1)S(1)} custom-call(bf16[3,1024,128]{2,1,0:T(8,128)(2,1)S(1)} %bitcast.25, bf16[384,256]{1,0:T(8,128)(2,1)S(1)} %bitcast.26), custom_call_target="tpu_custom_call" | custom-call | tf_op jit(solution)/shard_map/itself/pallas_call | solution.py:360
  182.5 11.2 %collective-permute-done.13.refs_4_ = bf16[3,144,1024]{2,1,0:T(8,128)(2,1)} collective-permute-done((bf16[3,144,1024]{2,1,0:T(8,128)(2,1)}, bf16[3,144,1024]{2,1,0:T(8,128)(2,1)}, u32[]{:S(2)}, u32[]{:S(2)}) %collective-permute-start.13) | collective-permute-done | bytes 884768 | tf_op jit(solution)/shard_map/ppermute | solution.py:372
  193.7 19.6 %collective-permute-done.14.refs_5_ = bf16[3,144,1024]{2,1,0:T(8,128)(2,1)} collective-permute-done((bf16[3,144,1024]{2,1,0:T(8,128)(2,1)}, bf16[3,144,1024]{2,1,0:T(8,128)(2,1)}, u32[]{:S(2)}, u32[]{:S(2)}) %collective-permute-start.14) | collective-permute-done | bytes 884768 | tf_op jit(solution)/shard_map/ppermute | solution.py:372
  213.3 3.2 %last.1.context_ref = bf16[384,1024]{1,0:T(8,128)(2,1)S(1)} custom-call(bf16[3,144,1024]{2,1,0:T(8,128)(2,1)S(1)} %itself.1.refs_0_, bf16[3,144,1024]{2,1,0:T(8,128)(2,1)S(1)} %get-tuple-element.69.refs_1_, bf16[3,144,1024]{2,1,0:T(8,128)(2,1)} %collective-permute-done.11.refs_2_, bf16[3,144,1024]{2,1,0:T(8,128)(2,1)} %collective-permute-done.12.refs_3_, ...), custom_call_target="tpu_custom_call" | custom-call | tf_op jit(solution)/shard_map/last/pallas_call | solution.py:360
  216.6 4.8 %theirs.1 = bf16[4,384,512]{2,1,0:T(8,128)(2,1)S(1)} custom-call(s32[2]{0:T(128)S(1)} %pad_add_fusion.1.place, bf16[384,1024]{1,0:T(8,128)(2,1)S(1)} %last.1.context_ref, bf16[768,4096]{1,0:T(8,128)(2,1)} %all-gather.8.cloned.1.call-done.most_ref, bf16[4,256,1024]{2,1,0:T(8,128)(2,1)} %all-gather.6.cloned.1.call-done.rest_ref), custom_call_target="tpu_custom_call" | custom-call | flops 1610612736 | bytes 4194304 | tf_op jit(solution)/shard_map/theirs/pallas_call | solution.py:332
  222.8 4.8 %ours.1 = bf16[4,384,512]{2,1,0:T(8,128)(2,1)S(1)} custom-call(s32[2]{0:T(128)S(1)} %pad_add_fusion.place, bf16[384,1024]{1,0:T(8,128)(2,1)S(1)} %last.1.context_ref, bf16[768,4096]{1,0:T(8,128)(2,1)} %all-gather.8.cloned.1.call-done.most_ref, bf16[4,256,1024]{2,1,0:T(8,128)(2,1)} %all-gather.6.cloned.1.call-done.rest_ref), custom_call_target="tpu_custom_call" | custom-call | flops 1610612736 | bytes 4194304 | tf_op jit(solution)/shard_map/ours/pallas_call | solution.py:332
  228.1 24.6 %all_to_all.15 = bf16[4,384,512]{2,1,0:T(8,128)(2,1)S(1)} all-to-all(bf16[4,384,512]{2,1,0:T(8,128)(2,1)S(1)} %add_convert_fusion), channel_id=1, replica_groups=mesh['x'=4,'z'=8,'y'=4,'core'=2] {'y'}, dimensions={0} | all-to-all | bytes 3145728 | tf_op jit(solution)/shard_map/all_to_all | solution.py:514
  (96 shorter events, 24.8 us)
Async XLA Ops:
  6.5 117.7 %all-gather.4.cloned.1.call-start = ((), (), s32[]{:S(2)}) async-start(), calls=%async_computation.3 | async-start | bytes 1769472 | tf_op jit(solution)/shard_map/all_gather | solution.py:406
  8.0 25.9 %collective-permute-start.6 = (bf16[256,128]{1,0:T(8,128)(2,1)}, bf16[256,128]{1,0:T(8,128)(2,1)}, u32[]{:S(2)}, u32[]{:S(2)}) collective-permute-start(bf16[256,128]{1,0:T(8,128)(2,1)} %get-tuple-element.82), channel_id=1, source_target_pairs={{0,192},{64,0},{128,64},{192,128},{1,193},{65,1},{129,65},{193,129... | collective-permute-start | bytes 196616 | tf_op jit(solution)/shard_map/ppermute | solution.py:376
  11.3 22.6 %collective-permute-start.7 = (bf16[256,128]{1,0:T(8,128)(2,1)}, bf16[256,128]{1,0:T(8,128)(2,1)}, u32[]{:S(2)}, u32[]{:S(2)}) collective-permute-start(bf16[256,128]{1,0:T(8,128)(2,1)} %get-tuple-element.82), channel_id=1, source_target_pairs={{0,128},{64,192},{128,0},{192,64},{1,129},{65,193},{129,1},{193,65... | collective-permute-start | bytes 196616 | tf_op jit(solution)/shard_map/ppermute | solution.py:376
  11.9 22.1 %collective-permute-start.8 = (bf16[256,128]{1,0:T(8,128)(2,1)}, bf16[256,128]{1,0:T(8,128)(2,1)}, u32[]{:S(2)}, u32[]{:S(2)}) collective-permute-start(bf16[256,128]{1,0:T(8,128)(2,1)} %get-tuple-element.82), channel_id=1, source_target_pairs={{0,64},{64,128},{128,192},{192,0},{1,65},{65,129},{129,193},{193,1... | collective-permute-start | bytes 196616 | tf_op jit(solution)/shard_map/ppermute | solution.py:376
  12.5 9.7 %copy-start.8 = (s32[512]{0:T(512)S(1)}, s32[512]{0:T(512)}, u32[]{:S(2)}) copy-start(s32[512]{0:T(512)} %param.14) | copy-start | bytes 6148
  14.0 23.1 %collective-permute-start.4 = (bf16[3,1024,128]{2,1,0:T(8,128)(2,1)S(1)}, bf16[3,1024,128]{2,1,0:T(8,128)(2,1)S(1)}, u32[]{:S(2)}, u32[]{:S(2)}) collective-permute-start(bf16[3,1024,128]{2,1,0:T(8,128)(2,1)S(1)} %bitcast.22), channel_id=1, source_target_pairs={{0,56},{8,0},{16,8},{24,16},{32,24},{40,32},{48,40},{56,48},{1,57}... | collective-permute-start | bytes 2359304 | tf_op jit(solution)/shard_map/ppermute | solution.py:372
  19.7 20.6 %collective-permute-start.5 = (bf16[3,1024,128]{2,1,0:T(8,128)(2,1)S(1)}, bf16[3,1024,128]{2,1,0:T(8,128)(2,1)S(1)}, u32[]{:S(2)}, u32[]{:S(2)}) collective-permute-start(bf16[3,1024,128]{2,1,0:T(8,128)(2,1)S(1)} %bitcast.23), channel_id=1, source_target_pairs={{0,8},{8,16},{16,24},{24,32},{32,40},{40,48},{48,56},{56,0},{1,9},... | collective-permute-start | bytes 2359304 | tf_op jit(solution)/shard_map/ppermute | solution.py:372
  40.2 64.5 %all-to-all-start = ((bf16[4,5,512,256]{3,2,1,0:T(8,128)(2,1)}), bf16[4,5,512,256]{3,2,1,0:T(8,128)(2,1)}, u32[]{:S(2)}, u32[]{:S(2)}) async-start(bf16[4,5,512,256]{3,2,1,0:T(8,128)(2,1)} %bitcast.27), calls=%async_computation | async-start | bytes 10485760 | tf_op jit(solution)/shard_map/all_to_all | solution.py:380
  45.3 95.0 %all-gather.6.cloned.1.call-start = ((), (), s32[]{:S(2)}) async-start(), calls=%async_computation.4 | async-start | bytes 2359296 | tf_op jit(solution)/shard_map/all_gather | solution.py:410
  46.0 56.6 %collective-permute-start = (bf16[4,512,256]{2,1,0:T(8,128)(2,1)}, bf16[4,512,256]{2,1,0:T(8,128)(2,1)S(1)}, u32[]{:S(2)}, u32[]{:S(2)}) collective-permute-start(bf16[4,512,256]{2,1,0:T(8,128)(2,1)} %copy-done.1), channel_id=1, source_target_pairs={{0,8},{8,16},{16,24},{24,32},{32,40},{40,48},{48,56},{56,0},{1,9},... | collective-permute-start | bytes 3145736 | tf_op jit(solution)/shard_map/ppermute | solution.py:372
  46.1 56.5 %collective-permute-start.1 = (bf16[4,512,256]{2,1,0:T(8,128)(2,1)S(1)}, bf16[4,512,256]{2,1,0:T(8,128)(2,1)S(1)}, u32[]{:S(2)}, u32[]{:S(2)}) collective-permute-start(bf16[4,512,256]{2,1,0:T(8,128)(2,1)S(1)} %get-tuple-element.48), channel_id=1, source_target_pairs={{0,56},{8,0},{16,8},{24,16},{32,24},{40,32},{48,40},{56,48},{1,57}... | collective-permute-start | bytes 3145736 | tf_op jit(solution)/shard_map/ppermute | solution.py:372
  48.8 44.4 %collective-permute-start.2 = (bf16[2,512,256]{2,1,0:T(8,128)(2,1)}, bf16[2,512,256]{2,1,0:T(8,128)(2,1)S(1)}, u32[]{:S(2)}, u32[]{:S(2)}) collective-permute-start(bf16[2,512,256]{2,1,0:T(8,128)(2,1)} %copy-done.5), channel_id=1, source_target_pairs={{0,16},{8,24},{16,32},{24,40},{32,48},{40,56},{48,0},{56,8},{1,17}... | collective-permute-start | bytes 1572872 | tf_op jit(solution)/shard_map/ppermute | solution.py:372
  48.8 53.8 %collective-permute-start.3 = (bf16[2,512,256]{2,1,0:T(8,128)(2,1)}, bf16[2,512,256]{2,1,0:T(8,128)(2,1)S(1)}, u32[]{:S(2)}, u32[]{:S(2)}) collective-permute-start(bf16[2,512,256]{2,1,0:T(8,128)(2,1)} %copy-done.4), channel_id=1, source_target_pairs={{0,48},{8,56},{16,0},{24,8},{32,16},{40,24},{48,32},{56,40},{1,49}... | collective-permute-start | bytes 1572872 | tf_op jit(solution)/shard_map/ppermute | solution.py:372
  104.7 9.0 %copy-start.13 = (s32[32]{0:T(128)S(1)}, s32[32]{0:T(128)}, u32[]{:S(2)}) copy-start(s32[32]{0:T(128)} %constant.119) | copy-start | bytes 388
  104.8 50.2 %all-to-all-start.1 = ((bf16[4,3,512,256]{3,2,1,0:T(8,128)(2,1)}), bf16[4,3,512,256]{3,2,1,0:T(8,128)(2,1)}, u32[]{:S(2)}, u32[]{:S(2)}) async-start(bf16[4,3,512,256]{3,2,1,0:T(8,128)(2,1)} %assemble.1), calls=%async_computation.1 | async-start | bytes 6291456 | tf_op jit(solution)/shard_map/all_to_all | solution.py:380
  109.4 107.1 %all-gather.8.cloned.1.call-start = ((), (), s32[]{:S(2)}) async-start(), calls=%async_computation.5 | async-start | bytes 7864320 | tf_op jit(solution)/shard_map/all_gather | solution.py:470
  109.7 30.6 %collective-permute-start.10 = (bf16[3,1024,128]{2,1,0:T(8,128)(2,1)S(1)}, bf16[3,1024,128]{2,1,0:T(8,128)(2,1)}, u32[]{:S(2)}, u32[]{:S(2)}) collective-permute-start(bf16[3,1024,128]{2,1,0:T(8,128)(2,1)S(1)} %collective-permute-done.5.q2), channel_id=1, source_target_pairs={{0,8},{8,16},{16,24},{24,32},{32,40},{40,48},{48,56},{56,0},{1,9},... | collective-permute-start | bytes 2359304 | tf_op jit(solution)/shard_map/ppermute | solution.py:372
  113.6 26.7 %collective-permute-start.9 = (bf16[3,1024,128]{2,1,0:T(8,128)(2,1)S(1)}, bf16[3,1024,128]{2,1,0:T(8,128)(2,1)}, u32[]{:S(2)}, u32[]{:S(2)}) collective-permute-start(bf16[3,1024,128]{2,1,0:T(8,128)(2,1)S(1)} %collective-permute-done.4.q1), channel_id=1, source_target_pairs={{0,56},{8,0},{16,8},{24,16},{32,24},{40,32},{48,40},{56,48},{1,57}... | collective-permute-start | bytes 2359304 | tf_op jit(solution)/shard_map/ppermute | solution.py:372
  140.2 42.2 %collective-permute-start.11 = (bf16[3,144,1024]{2,1,0:T(8,128)(2,1)}, bf16[3,144,1024]{2,1,0:T(8,128)(2,1)}, u32[]{:S(2)}, u32[]{:S(2)}) collective-permute-start(bf16[3,144,1024]{2,1,0:T(8,128)(2,1)} %get-tuple-element.70), channel_id=1, source_target_pairs={{0,8},{8,16},{16,24},{24,32},{32,40},{40,48},{48,56},{56,0},{1,9},... | collective-permute-start | bytes 2654216 | tf_op jit(solution)/shard_map/ppermute | solution.py:372
  143.0 39.4 %collective-permute-start.12 = (bf16[3,144,1024]{2,1,0:T(8,128)(2,1)}, bf16[3,144,1024]{2,1,0:T(8,128)(2,1)}, u32[]{:S(2)}, u32[]{:S(2)}) collective-permute-start(bf16[3,144,1024]{2,1,0:T(8,128)(2,1)} %get-tuple-element.71), channel_id=1, source_target_pairs={{0,56},{8,0},{16,8},{24,16},{32,24},{40,32},{48,40},{56,48},{1,57}... | collective-permute-start | bytes 2654216 | tf_op jit(solution)/shard_map/ppermute | solution.py:372
  154.9 18.5 %copy-start = (bf16[384,1,256]{2,0,1:T(8,128)(2,1)S(1)}, bf16[384,1,256]{2,0,1:T(8,128)(2,1)}, u32[]{:S(2)}) copy-start(bf16[384,1,256]{2,0,1:T(8,128)(2,1)} %param.10) | copy-start | bytes 589828
  169.8 23.9 %collective-permute-start.13 = (bf16[3,144,1024]{2,1,0:T(8,128)(2,1)}, bf16[3,144,1024]{2,1,0:T(8,128)(2,1)}, u32[]{:S(2)}, u32[]{:S(2)}) collective-permute-start(bf16[3,144,1024]{2,1,0:T(8,128)(2,1)} %get-tuple-element.77), channel_id=1, source_target_pairs={{0,16},{8,24},{16,32},{24,40},{32,48},{40,56},{48,0},{56,8},{1,17}... | collective-permute-start | bytes 2654216 | tf_op jit(solution)/shard_map/ppermute | solution.py:372
  173.0 40.3 %collective-permute-start.14 = (bf16[3,144,1024]{2,1,0:T(8,128)(2,1)}, bf16[3,144,1024]{2,1,0:T(8,128)(2,1)}, u32[]{:S(2)}, u32[]{:S(2)}) collective-permute-start(bf16[3,144,1024]{2,1,0:T(8,128)(2,1)} %get-tuple-element.78), channel_id=1, source_target_pairs={{0,48},{8,56},{16,0},{24,8},{32,16},{40,24},{48,32},{56,40},{1,49}... | collective-permute-start | bytes 2654216 | tf_op jit(solution)/shard_map/ppermute | solution.py:372
  221.4 6.2 %collective-permute-start.15 = (bf16[4,384,512]{2,1,0:T(8,128)(2,1)S(1)}, bf16[4,384,512]{2,1,0:T(8,128)(2,1)S(1)}, u32[]{:S(2)}, u32[]{:S(2)}) collective-permute-start(bf16[4,384,512]{2,1,0:T(8,128)(2,1)S(1)} %theirs.1), channel_id=1, source_target_pairs={{0,1},{1,0},{2,3},{3,2},{4,5},{5,4},{6,7},{7,6},{8,9},{9,8},{10,11... | collective-permute-start | bytes 4718600 | tf_op jit(solution)/shard_map/ppermute | solution.py:511
  (12 other events, 65.8 us)
Sparse Core Ops, SparseCore 0:
  20.5 52.8 all-gather.3
  75.1 65.0 all-gather.5
  144.0 68.8 all-gather.7

commit v11 on v10

--- a/solution.py
+++ b/solution.py
@@ -465,9 +465,7 @@
         3 * NX,
         10,
     )
-    near, most, rest = lax.optimization_barrier((near, most, rest))
     near, q_up2, q_down2 = lax.optimization_barrier((near, q_up2, q_down2))
-    most = lax.all_gather(most, "x", axis=1, tiled=True)
     own_part, near_up, near_down = near
     home_up = along_z(near_up, 1)
     home_down = along_z(near_down, -1)
@@ -482,6 +480,8 @@
         2 * NX,
         6,
     )
+    far, most, rest = lax.optimization_barrier((far, most, rest))
+    most = lax.all_gather(most, "x", axis=1, tiled=True)
     far_up, far_down = attention(
         move_kernel,
         "move",

time: 263 us -> 270 us (1.027)
  Pallas kernels: 67 us -> 72.7 us
    all_gather x1, waiting for transfers between devices: 16 us -> 0.01 us  [body(): rest = lax.all_gather(rest, 'z', axis=2, tiled=True)]
    ppermute x12, waiting for transfers between devices: 85.8 us -> 95.9 us  [along_z(): return lax.ppermute(array, 'z', [(i, (i + shift) % NZ) for i in range(NZ)])]
    all_gather x1, waiting for transfers between devices: 0.02 us -> 8.39 us  [body(): most = lax.all_gather(most, 'x', axis=1, tiled=True)]
    pallas_call x3, Pallas kernels: 34.3 us -> 39.9 us  [attention(): pl.pallas_call(kernel, out_shape=(jax.ShapeDtypeStruct((n, HD + PACK, ROW...]
  transfers between devices with their start and end apart: 21 -> 21, of which waited for: 7 -> 9; matrix products, arithmetic and copies ran while one was open for 3% -> 3% of each run, Pallas kernels for 24% -> 25%
where the time goes in v11:
time: 270 us; the launch traced here: 269 us
  waiting for transfers between devices  105 us (39%)
  Pallas kernels  72.7 us (27%)
  starting transfers between devices  37.4 us (14%)
  blocking collectives  24.4 us (9%)
  between operations  13.6 us (5%)
  local copies, waits for them, and re-layouts  8.13 us (3%)
  other arithmetic  7.53 us (3%)
    ppermute x12, waiting for transfers between devices, along_z(): return lax.ppermute(array, 'z', [(i, (i + shift) % NZ) for i in range(NZ)])  95.9 us
    pallas_call x3, Pallas kernels, attention(): pl.pallas_call(kernel, out_shape=(jax.ShapeDtypeStruct((n, HD + PACK, ROW...  39.9 us
    all_to_all x1, blocking collectives, body(): chips = lax.all_to_all(chip, 'y', split_axis=0, concat_axis=0, tiled=True)  24.4 us
    ppermute x12, starting transfers between devices, along_z(): return lax.ppermute(array, 'z', [(i, (i + shift) % NZ) for i in range(NZ)])  22.4 us
    pallas_call x2, Pallas kernels, in_vmem(): pl.pallas_call(kernel, out_shape=out, in_specs=[vmem] * len(arrays), out_...  12.2 us
    all_to_all x2, starting transfers between devices, over_x(): return lax.all_to_all(items, 'x', split_axis=0, concat_axis=0, tiled=True)  9.72 us
    pallas_call x2, Pallas kernels, project(): pl.pallas_call(project_kernel, out_shape=jax.ShapeDtypeStruct((NY, contex...  9.6 us
    pallas_call x2, Pallas kernels, take_rows(): pl.pallas_call(row_copies, out_shape=tuple((jax.ShapeDtypeStruct((n,) + c...  8.84 us
  transfers between devices with their start and end apart: 21, of which 9 were waited for; matrix products, arithmetic and copies ran while one was open for 3% of the time, Pallas kernels for 25%

profile of v11, /device:TPU:1, one launch (start us, length us, event | category | flops | bytes accessed | tf_op | source)
XLA Modules:
  0.0 268.6 jit_solution(12967309542329637013)
XLA Ops:
  8.0 3.3 %collective-permute-start.6 = (bf16[256,128]{1,0:T(8,128)(2,1)}, bf16[256,128]{1,0:T(8,128)(2,1)}, u32[]{:S(2)}, u32[]{:S(2)}) collective-permute-start(bf16[256,128]{1,0:T(8,128)(2,1)} %get-tuple-element.80), channel_id=1, source_target_pairs={{0,192},{64,0},{128,64},{192,128},{1,193},{65,1},{129,65},{193,129... | collective-permute-start | bytes 196616 | tf_op jit(solution)/shard_map/ppermute | solution.py:376
  14.0 5.7 %collective-permute-start.4 = (bf16[3,1024,128]{2,1,0:T(8,128)(2,1)S(1)}, bf16[3,1024,128]{2,1,0:T(8,128)(2,1)S(1)}, u32[]{:S(2)}, u32[]{:S(2)}) collective-permute-start(bf16[3,1024,128]{2,1,0:T(8,128)(2,1)S(1)} %bitcast.22), channel_id=1, source_target_pairs={{0,56},{8,0},{16,8},{24,16},{32,24},{40,32},{48,40},{56,48},{1,57}... | collective-permute-start | bytes 2359304 | tf_op jit(solution)/shard_map/ppermute | solution.py:372
  25.0 2.9 %take_rows.2 = (bf16[4,512,256]{2,1,0:T(8,128)(2,1)S(1)}, bf16[4,512,256]{2,1,0:T(8,128)(2,1)S(1)}, bf16[2,512,256]{2,1,0:T(8,128)(2,1)S(1)}, bf16[2,512,256]{2,1,0:T(8,128)(2,1)S(1)}) custom-call(s32[12]{0:T(128)S(1)} %reshape.164.rows_ref, bf16[16,512,256]{2,1,0:T(8,128)(2,1)} %bitcast.28), custom_call_target="tpu_custom_call" | custom-call | tf_op jit(solution)/shard_map/take_rows/pallas_call | solution.py:87
  28.0 5.9 %take_rows.3 = bf16[20,512,256]{2,1,0:T(8,128)(2,1)} custom-call(s32[20]{0:T(128)S(1)} %reshape.166.rows_ref, bf16[16,512,256]{2,1,0:T(8,128)(2,1)} %bitcast.29), custom_call_target="tpu_custom_call" | custom-call | tf_op jit(solution)/shard_map/take_rows/pallas_call | solution.py:87
  37.1 3.1 %collective-permute-done.5.q2 = bf16[3,1024,128]{2,1,0:T(8,128)(2,1)S(1)} collective-permute-done((bf16[3,1024,128]{2,1,0:T(8,128)(2,1)S(1)}, bf16[3,1024,128]{2,1,0:T(8,128)(2,1)S(1)}, u32[]{:S(2)}, u32[]{:S(2)}) %collective-permute-start.5) | collective-permute-done | bytes 786464 | tf_op jit(solution)/shard_map/ppermute | solution.py:372
  40.2 5.1 %all-to-all-start = ((bf16[4,5,512,256]{3,2,1,0:T(8,128)(2,1)}), bf16[4,5,512,256]{3,2,1,0:T(8,128)(2,1)}, u32[]{:S(2)}, u32[]{:S(2)}) async-start(bf16[4,5,512,256]{3,2,1,0:T(8,128)(2,1)} %bitcast.27), calls=%async_computation | async-start | bytes 10485760 | tf_op jit(solution)/shard_map/all_to_all | solution.py:380
  48.8 3.6 %collective-permute-start.3 = (bf16[2,512,256]{2,1,0:T(8,128)(2,1)}, bf16[2,512,256]{2,1,0:T(8,128)(2,1)S(1)}, u32[]{:S(2)}, u32[]{:S(2)}) collective-permute-start(bf16[2,512,256]{2,1,0:T(8,128)(2,1)} %copy-done.8), channel_id=1, source_target_pairs={{0,48},{8,56},{16,0},{24,8},{32,16},{40,24},{48,32},{56,40},{1,49}... | collective-permute-start | bytes 1572872 | tf_op jit(solution)/shard_map/ppermute | solution.py:372
  52.4 41.0 %collective-permute-done.2.up4 = bf16[2,512,256]{2,1,0:T(8,128)(2,1)S(1)} collective-permute-done((bf16[2,512,256]{2,1,0:T(8,128)(2,1)}, bf16[2,512,256]{2,1,0:T(8,128)(2,1)S(1)}, u32[]{:S(2)}, u32[]{:S(2)}) %collective-permute-start.2) | collective-permute-done | bytes 524320 | tf_op jit(solution)/shard_map/ppermute | solution.py:372
  93.4 9.1 %collective-permute-done.3.down4 = bf16[2,512,256]{2,1,0:T(8,128)(2,1)S(1)} collective-permute-done((bf16[2,512,256]{2,1,0:T(8,128)(2,1)}, bf16[2,512,256]{2,1,0:T(8,128)(2,1)S(1)}, u32[]{:S(2)}, u32[]{:S(2)}) %collective-permute-start.3) | collective-permute-done | bytes 524320 | tf_op jit(solution)/shard_map/ppermute | solution.py:372
  104.8 4.7 %all-to-all-start.1 = ((bf16[4,3,512,256]{3,2,1,0:T(8,128)(2,1)}), bf16[4,3,512,256]{3,2,1,0:T(8,128)(2,1)}, u32[]{:S(2)}, u32[]{:S(2)}) async-start(bf16[4,3,512,256]{3,2,1,0:T(8,128)(2,1)} %assemble.1), calls=%async_computation.1 | async-start | bytes 6291456 | tf_op jit(solution)/shard_map/all_to_all | solution.py:380
  109.7 4.0 %collective-permute-start.10 = (bf16[3,1024,128]{2,1,0:T(8,128)(2,1)S(1)}, bf16[3,1024,128]{2,1,0:T(8,128)(2,1)S(1)}, u32[]{:S(2)}, u32[]{:S(2)}) collective-permute-start(bf16[3,1024,128]{2,1,0:T(8,128)(2,1)S(1)} %collective-permute-done.5.q2), channel_id=1, source_target_pairs={{0,8},{8,16},{16,24},{24,32},{32,40},{40,48},{48,56},{56,0},{1,9},... | collective-permute-start | bytes 2359304 | tf_op jit(solution)/shard_map/ppermute | solution.py:372
  114.0 13.4 %near.1 = (bf16[3,144,1024]{2,1,0:T(8,128)(2,1)S(1)}, bf16[3,144,1024]{2,1,0:T(8,128)(2,1)}, bf16[3,144,1024]{2,1,0:T(8,128)(2,1)}) custom-call(s32[12]{0:T(128)S(1)} %get-tuple-element.82.tags, bf16[4,5,512,256]{3,2,1,0:T(8,128)(2,1)} %all-to-all-done.here, bf16[3,1024,128]{2,1,0:T(8,128)(2,1)S(1)} %bitcast.24, ...), custom_call_target="tpu_custom_call" | custom-call | flops 5242880 | bytes 5120 | tf_op jit(solution)/shard_map/near/pallas_call | solution.py:286
  127.3 7.9 %collective-permute-done.10.q1 = bf16[3,1024,128]{2,1,0:T(8,128)(2,1)S(1)} collective-permute-done((bf16[3,1024,128]{2,1,0:T(8,128)(2,1)S(1)}, bf16[3,1024,128]{2,1,0:T(8,128)(2,1)S(1)}, u32[]{:S(2)}, u32[]{:S(2)}) %collective-permute-start.10) | collective-permute-done | bytes 786464 | tf_op jit(solution)/shard_map/ppermute | solution.py:372
  137.5 9.7 %far.1 = (bf16[3,144,1024]{2,1,0:T(8,128)(2,1)S(1)}, bf16[3,144,1024]{2,1,0:T(8,128)(2,1)S(1)}) custom-call(s32[8]{0:T(128)S(1)} %slice.42.tags, bf16[4,5,512,256]{3,2,1,0:T(8,128)(2,1)} %all-to-all-done.here, bf16[3,1024,128]{2,1,0:T(8,128)(2,1)S(1)} %collective-permute-done.9.q0, bf16[3,1024,128]{2,1,0:T(8,128)(2,1)S(1)} %collective-permute-done.10.q1), custom_call_target="tpu_custom_call" | custom-call | flops 3145728 | bytes 3072 | tf_op jit(solution)/shard_map/far/pallas_call | solution.py:286
  153.7 16.8 %move.1 = (bf16[3,144,1024]{2,1,0:T(8,128)(2,1)}, bf16[3,144,1024]{2,1,0:T(8,128)(2,1)}) custom-call(s32[12]{0:T(128)S(1)} %get-tuple-element.81.tags, bf16[4,3,512,256]{3,2,1,0:T(8,128)(2,1)} %all-to-all-done.1.moved, bf16[3,1024,128]{2,1,0:T(8,128)(2,1)S(1)} %copy-done.3, bf16[3,1024,128]{2,1,0:T(8,128)(2,1)S(1)} %copy-done.1, ...), custom_call_target="tpu_custom_call" | custom-call | flops 209715200000 | bytes 204800000 | tf_op jit(solution)/shard_map/move/pallas_call | solution.py:286
  170.6 2.9 %collective-permute-start.13 = (bf16[3,144,1024]{2,1,0:T(8,128)(2,1)}, bf16[3,144,1024]{2,1,0:T(8,128)(2,1)}, u32[]{:S(2)}, u32[]{:S(2)}) collective-permute-start(bf16[3,144,1024]{2,1,0:T(8,128)(2,1)} %get-tuple-element.75), channel_id=1, source_target_pairs={{0,16},{8,24},{16,32},{24,40},{32,48},{40,56},{48,0},{56,8},{1,17}... | collective-permute-start | bytes 2654216 | tf_op jit(solution)/shard_map/ppermute | solution.py:372
  174.2 8.9 %itself.1.refs_0_ = bf16[3,144,1024]{2,1,0:T(8,128)(2,1)S(1)} custom-call(bf16[3,1024,128]{2,1,0:T(8,128)(2,1)S(1)} %bitcast.25, bf16[384,256]{1,0:T(8,128)(2,1)S(1)} %bitcast.26), custom_call_target="tpu_custom_call" | custom-call | tf_op jit(solution)/shard_map/itself/pallas_call | solution.py:360
  183.2 27.1 %collective-permute-done.13.refs_4_ = bf16[3,144,1024]{2,1,0:T(8,128)(2,1)} collective-permute-done((bf16[3,144,1024]{2,1,0:T(8,128)(2,1)}, bf16[3,144,1024]{2,1,0:T(8,128)(2,1)}, u32[]{:S(2)}, u32[]{:S(2)}) %collective-permute-start.13) | collective-permute-done | bytes 884768 | tf_op jit(solution)/shard_map/ppermute | solution.py:372
  210.3 3.8 %collective-permute-done.14.refs_5_ = bf16[3,144,1024]{2,1,0:T(8,128)(2,1)} collective-permute-done((bf16[3,144,1024]{2,1,0:T(8,128)(2,1)}, bf16[3,144,1024]{2,1,0:T(8,128)(2,1)}, u32[]{:S(2)}, u32[]{:S(2)}) %collective-permute-start.14) | collective-permute-done | bytes 884768 | tf_op jit(solution)/shard_map/ppermute | solution.py:372
  214.1 3.2 %last.1.context_ref = bf16[384,1024]{1,0:T(8,128)(2,1)S(1)} custom-call(bf16[3,144,1024]{2,1,0:T(8,128)(2,1)S(1)} %itself.1.refs_0_, bf16[3,144,1024]{2,1,0:T(8,128)(2,1)S(1)} %get-tuple-element.64.refs_1_, bf16[3,144,1024]{2,1,0:T(8,128)(2,1)} %collective-permute-done.11.refs_2_, bf16[3,144,1024]{2,1,0:T(8,128)(2,1)} %collective-permute-done.12.refs_3_, ...), custom_call_target="tpu_custom_call" | custom-call | tf_op jit(solution)/shard_map/last/pallas_call | solution.py:360
  217.4 8.4 %all-gather.8.cloned.1.call-done.most_ref = bf16[768,4096]{1,0:T(8,128)(2,1)} async-done(((bf16[768,1024]{1,0:T(8,128)(2,1)}), bf16[768,4096]{1,0:T(8,128)(2,1)}) %all-gather.8.cloned.1.call-update) | async-done | bytes 6291472 | tf_op jit(solution)/shard_map/all_gather | solution.py:484
  225.8 4.8 %theirs.1 = bf16[4,384,512]{2,1,0:T(8,128)(2,1)S(1)} custom-call(s32[2]{0:T(128)S(1)} %pad_add_fusion.1.place, bf16[384,1024]{1,0:T(8,128)(2,1)S(1)} %last.1.context_ref, bf16[768,4096]{1,0:T(8,128)(2,1)} %all-gather.8.cloned.1.call-done.most_ref, bf16[4,256,1024]{2,1,0:T(8,128)(2,1)} %all-gather.6.cloned.1.call-done.rest_ref), custom_call_target="tpu_custom_call" | custom-call | flops 1610612736 | bytes 4194304 | tf_op jit(solution)/shard_map/theirs/pallas_call | solution.py:332
  231.4 4.8 %ours.1 = bf16[4,384,512]{2,1,0:T(8,128)(2,1)S(1)} custom-call(s32[2]{0:T(128)S(1)} %pad_add_fusion.place, bf16[384,1024]{1,0:T(8,128)(2,1)S(1)} %last.1.context_ref, bf16[768,4096]{1,0:T(8,128)(2,1)} %all-gather.8.cloned.1.call-done.most_ref, bf16[4,256,1024]{2,1,0:T(8,128)(2,1)} %all-gather.6.cloned.1.call-done.rest_ref), custom_call_target="tpu_custom_call" | custom-call | flops 1610612736 | bytes 4194304 | tf_op jit(solution)/shard_map/ours/pallas_call | solution.py:332
  236.7 24.4 %all_to_all.15 = bf16[4,384,512]{2,1,0:T(8,128)(2,1)S(1)} all-to-all(bf16[4,384,512]{2,1,0:T(8,128)(2,1)S(1)} %add_convert_fusion), channel_id=1, replica_groups=mesh['x'=4,'z'=8,'y'=4,'core'=2] {'y'}, dimensions={0} | all-to-all | bytes 3145728 | tf_op jit(solution)/shard_map/all_to_all | solution.py:514
  (104 shorter events, 30.6 us)
Async XLA Ops:
  6.5 144.4 %all-gather.4.cloned.1.call-start = ((), (), s32[]{:S(2)}) async-start(), calls=%async_computation.3 | async-start | bytes 1769472 | tf_op jit(solution)/shard_map/all_gather | solution.py:406
  8.0 25.9 %collective-permute-start.6 = (bf16[256,128]{1,0:T(8,128)(2,1)}, bf16[256,128]{1,0:T(8,128)(2,1)}, u32[]{:S(2)}, u32[]{:S(2)}) collective-permute-start(bf16[256,128]{1,0:T(8,128)(2,1)} %get-tuple-element.80), channel_id=1, source_target_pairs={{0,192},{64,0},{128,64},{192,128},{1,193},{65,1},{129,65},{193,129... | collective-permute-start | bytes 196616 | tf_op jit(solution)/shard_map/ppermute | solution.py:376
  11.3 22.6 %collective-permute-start.7 = (bf16[256,128]{1,0:T(8,128)(2,1)}, bf16[256,128]{1,0:T(8,128)(2,1)}, u32[]{:S(2)}, u32[]{:S(2)}) collective-permute-start(bf16[256,128]{1,0:T(8,128)(2,1)} %get-tuple-element.80), channel_id=1, source_target_pairs={{0,128},{64,192},{128,0},{192,64},{1,129},{65,193},{129,1},{193,65... | collective-permute-start | bytes 196616 | tf_op jit(solution)/shard_map/ppermute | solution.py:376
  11.9 22.1 %collective-permute-start.8 = (bf16[256,128]{1,0:T(8,128)(2,1)}, bf16[256,128]{1,0:T(8,128)(2,1)}, u32[]{:S(2)}, u32[]{:S(2)}) collective-permute-start(bf16[256,128]{1,0:T(8,128)(2,1)} %get-tuple-element.80), channel_id=1, source_target_pairs={{0,64},{64,128},{128,192},{192,0},{1,65},{65,129},{129,193},{193,1... | collective-permute-start | bytes 196616 | tf_op jit(solution)/shard_map/ppermute | solution.py:376
  12.5 9.7 %copy-start.12 = (s32[512]{0:T(512)S(1)}, s32[512]{0:T(512)}, u32[]{:S(2)}) copy-start(s32[512]{0:T(512)} %param.14) | copy-start | bytes 6148
  14.0 23.1 %collective-permute-start.4 = (bf16[3,1024,128]{2,1,0:T(8,128)(2,1)S(1)}, bf16[3,1024,128]{2,1,0:T(8,128)(2,1)S(1)}, u32[]{:S(2)}, u32[]{:S(2)}) collective-permute-start(bf16[3,1024,128]{2,1,0:T(8,128)(2,1)S(1)} %bitcast.22), channel_id=1, source_target_pairs={{0,56},{8,0},{16,8},{24,16},{32,24},{40,32},{48,40},{56,48},{1,57}... | collective-permute-start | bytes 2359304 | tf_op jit(solution)/shard_map/ppermute | solution.py:372
  19.7 20.6 %collective-permute-start.5 = (bf16[3,1024,128]{2,1,0:T(8,128)(2,1)S(1)}, bf16[3,1024,128]{2,1,0:T(8,128)(2,1)S(1)}, u32[]{:S(2)}, u32[]{:S(2)}) collective-permute-start(bf16[3,1024,128]{2,1,0:T(8,128)(2,1)S(1)} %bitcast.23), channel_id=1, source_target_pairs={{0,8},{8,16},{16,24},{24,32},{32,40},{40,48},{48,56},{56,0},{1,9},... | collective-permute-start | bytes 2359304 | tf_op jit(solution)/shard_map/ppermute | solution.py:372
  40.2 64.6 %all-to-all-start = ((bf16[4,5,512,256]{3,2,1,0:T(8,128)(2,1)}), bf16[4,5,512,256]{3,2,1,0:T(8,128)(2,1)}, u32[]{:S(2)}, u32[]{:S(2)}) async-start(bf16[4,5,512,256]{3,2,1,0:T(8,128)(2,1)} %bitcast.27), calls=%async_computation | async-start | bytes 10485760 | tf_op jit(solution)/shard_map/all_to_all | solution.py:380
  45.3 105.6 %all-gather.6.cloned.1.call-start = ((), (), s32[]{:S(2)}) async-start(), calls=%async_computation.4 | async-start | bytes 2359296 | tf_op jit(solution)/shard_map/all_gather | solution.py:410
  46.0 56.5 %collective-permute-start = (bf16[4,512,256]{2,1,0:T(8,128)(2,1)}, bf16[4,512,256]{2,1,0:T(8,128)(2,1)S(1)}, u32[]{:S(2)}, u32[]{:S(2)}) collective-permute-start(bf16[4,512,256]{2,1,0:T(8,128)(2,1)} %copy-done.5), channel_id=1, source_target_pairs={{0,8},{8,16},{16,24},{24,32},{32,40},{40,48},{48,56},{56,0},{1,9},... | collective-permute-start | bytes 3145736 | tf_op jit(solution)/shard_map/ppermute | solution.py:372
  46.1 56.4 %collective-permute-start.1 = (bf16[4,512,256]{2,1,0:T(8,128)(2,1)S(1)}, bf16[4,512,256]{2,1,0:T(8,128)(2,1)S(1)}, u32[]{:S(2)}, u32[]{:S(2)}) collective-permute-start(bf16[4,512,256]{2,1,0:T(8,128)(2,1)S(1)} %get-tuple-element.47), channel_id=1, source_target_pairs={{0,56},{8,0},{16,8},{24,16},{32,24},{40,32},{48,40},{56,48},{1,57}... | collective-permute-start | bytes 3145736 | tf_op jit(solution)/shard_map/ppermute | solution.py:372
  48.8 44.6 %collective-permute-start.2 = (bf16[2,512,256]{2,1,0:T(8,128)(2,1)}, bf16[2,512,256]{2,1,0:T(8,128)(2,1)S(1)}, u32[]{:S(2)}, u32[]{:S(2)}) collective-permute-start(bf16[2,512,256]{2,1,0:T(8,128)(2,1)} %copy-done.9), channel_id=1, source_target_pairs={{0,16},{8,24},{16,32},{24,40},{32,48},{40,56},{48,0},{56,8},{1,17}... | collective-permute-start | bytes 1572872 | tf_op jit(solution)/shard_map/ppermute | solution.py:372
  48.8 53.8 %collective-permute-start.3 = (bf16[2,512,256]{2,1,0:T(8,128)(2,1)}, bf16[2,512,256]{2,1,0:T(8,128)(2,1)S(1)}, u32[]{:S(2)}, u32[]{:S(2)}) collective-permute-start(bf16[2,512,256]{2,1,0:T(8,128)(2,1)} %copy-done.8), channel_id=1, source_target_pairs={{0,48},{8,56},{16,0},{24,8},{32,16},{40,24},{48,32},{56,40},{1,49}... | collective-permute-start | bytes 1572872 | tf_op jit(solution)/shard_map/ppermute | solution.py:372
  104.8 9.0 %copy-start.17 = (s32[32]{0:T(128)S(1)}, s32[32]{0:T(128)}, u32[]{:S(2)}) copy-start(s32[32]{0:T(128)} %constant.119) | copy-start | bytes 388
  104.8 48.9 %all-to-all-start.1 = ((bf16[4,3,512,256]{3,2,1,0:T(8,128)(2,1)}), bf16[4,3,512,256]{3,2,1,0:T(8,128)(2,1)}, u32[]{:S(2)}, u32[]{:S(2)}) async-start(bf16[4,3,512,256]{3,2,1,0:T(8,128)(2,1)} %assemble.1), calls=%async_computation.1 | async-start | bytes 6291456 | tf_op jit(solution)/shard_map/all_to_all | solution.py:380
  109.5 116.3 %all-gather.8.cloned.1.call-start = ((), (), s32[]{:S(2)}) async-start(), calls=%async_computation.5 | async-start | bytes 7864320 | tf_op jit(solution)/shard_map/all_gather | solution.py:484
  109.7 25.5 %collective-permute-start.10 = (bf16[3,1024,128]{2,1,0:T(8,128)(2,1)S(1)}, bf16[3,1024,128]{2,1,0:T(8,128)(2,1)S(1)}, u32[]{:S(2)}, u32[]{:S(2)}) collective-permute-start(bf16[3,1024,128]{2,1,0:T(8,128)(2,1)S(1)} %collective-permute-done.5.q2), channel_id=1, source_target_pairs={{0,8},{8,16},{16,24},{24,32},{32,40},{40,48},{48,56},{56,0},{1,9},... | collective-permute-start | bytes 2359304 | tf_op jit(solution)/shard_map/ppermute | solution.py:372
  113.7 23.8 %collective-permute-start.9 = (bf16[3,1024,128]{2,1,0:T(8,128)(2,1)S(1)}, bf16[3,1024,128]{2,1,0:T(8,128)(2,1)S(1)}, u32[]{:S(2)}, u32[]{:S(2)}) collective-permute-start(bf16[3,1024,128]{2,1,0:T(8,128)(2,1)S(1)} %collective-permute-done.4.q1), channel_id=1, source_target_pairs={{0,56},{8,0},{16,8},{24,16},{32,24},{40,32},{48,40},{56,48},{1,57}... | collective-permute-start | bytes 2359304 | tf_op jit(solution)/shard_map/ppermute | solution.py:372
  150.9 32.3 %collective-permute-start.11 = (bf16[3,144,1024]{2,1,0:T(8,128)(2,1)}, bf16[3,144,1024]{2,1,0:T(8,128)(2,1)}, u32[]{:S(2)}, u32[]{:S(2)}) collective-permute-start(bf16[3,144,1024]{2,1,0:T(8,128)(2,1)} %get-tuple-element.65), channel_id=1, source_target_pairs={{0,8},{8,16},{16,24},{24,32},{32,40},{40,48},{48,56},{56,0},{1,9},... | collective-permute-start | bytes 2654216 | tf_op jit(solution)/shard_map/ppermute | solution.py:372
  153.4 29.8 %collective-permute-start.12 = (bf16[3,144,1024]{2,1,0:T(8,128)(2,1)}, bf16[3,144,1024]{2,1,0:T(8,128)(2,1)}, u32[]{:S(2)}, u32[]{:S(2)}) collective-permute-start(bf16[3,144,1024]{2,1,0:T(8,128)(2,1)} %get-tuple-element.66), channel_id=1, source_target_pairs={{0,56},{8,0},{16,8},{24,16},{32,24},{40,32},{48,40},{56,48},{1,57}... | collective-permute-start | bytes 2654216 | tf_op jit(solution)/shard_map/ppermute | solution.py:372
  153.7 20.5 %copy-start.4 = (bf16[384,1,256]{2,0,1:T(8,128)(2,1)S(1)}, bf16[384,1,256]{2,0,1:T(8,128)(2,1)}, u32[]{:S(2)}) copy-start(bf16[384,1,256]{2,0,1:T(8,128)(2,1)} %param.10) | copy-start | bytes 589828
  170.6 39.8 %collective-permute-start.13 = (bf16[3,144,1024]{2,1,0:T(8,128)(2,1)}, bf16[3,144,1024]{2,1,0:T(8,128)(2,1)}, u32[]{:S(2)}, u32[]{:S(2)}) collective-permute-start(bf16[3,144,1024]{2,1,0:T(8,128)(2,1)} %get-tuple-element.75), channel_id=1, source_target_pairs={{0,16},{8,24},{16,32},{24,40},{32,48},{40,56},{48,0},{56,8},{1,17}... | collective-permute-start | bytes 2654216 | tf_op jit(solution)/shard_map/ppermute | solution.py:372
  173.4 40.7 %collective-permute-start.14 = (bf16[3,144,1024]{2,1,0:T(8,128)(2,1)}, bf16[3,144,1024]{2,1,0:T(8,128)(2,1)}, u32[]{:S(2)}, u32[]{:S(2)}) collective-permute-start(bf16[3,144,1024]{2,1,0:T(8,128)(2,1)} %get-tuple-element.76), channel_id=1, source_target_pairs={{0,48},{8,56},{16,0},{24,8},{32,16},{40,24},{48,32},{56,40},{1,49}... | collective-permute-start | bytes 2654216 | tf_op jit(solution)/shard_map/ppermute | solution.py:372
  230.6 5.6 %collective-permute-start.15 = (bf16[4,384,512]{2,1,0:T(8,128)(2,1)S(1)}, bf16[4,384,512]{2,1,0:T(8,128)(2,1)S(1)}, u32[]{:S(2)}, u32[]{:S(2)}) collective-permute-start(bf16[4,384,512]{2,1,0:T(8,128)(2,1)S(1)} %theirs.1), channel_id=1, source_target_pairs={{0,1},{1,0},{2,3},{3,2},{4,5},{5,4},{6,7},{7,6},{8,9},{9,8},{10,11... | collective-permute-start | bytes 4718600 | tf_op jit(solution)/shard_map/ppermute | solution.py:511
  (16 other events, 72.9 us)
Sparse Core Ops, SparseCore 0:
  20.5 52.2 all-gather.3
  74.5 65.4 all-gather.5
  153.8 71.9 all-gather.7

commit v12 on v10

--- a/solution.py
+++ b/solution.py
@@ -402,7 +402,7 @@
     (here,) = take_rows(cache, staying, (NX * stay,))
     q_up = along_z(q_own, -1)
     q_down = along_z(q_own, 1)
-    cut = out_weight.shape[0] * 3 // 4
+    cut = out_weight.shape[0] * 7 // 8
     most = lax.all_gather(out_weight[:cut], "z", axis=1, tiled=True)
     rest = out_weight[cut:]
     rest = jnp.stack([rest] + [along_x(rest, -distance) for distance in range(1, NX)])

time: 263 us -> 279 us (1.061)
  waiting for transfers between devices: 103 us -> 113 us
  Pallas kernels: 67 us -> 74 us
  local copies, waits for them, and re-layouts: 6.37 us -> 9.71 us
    all_gather x1, waiting for transfers between devices: 0.02 us -> 26.6 us  [body(): most = lax.all_gather(out_weight[:cut], 'z', axis=1, tiled=True)]
    all_gather x1, waiting for transfers between devices: 16 us -> 0.01 us  [body(): rest = lax.all_gather(rest, 'z', axis=2, tiled=True)]
    ppermute x12, waiting for transfers between devices: 85.8 us -> 75.3 us  [along_z(): return lax.ppermute(array, 'z', [(i, (i + shift) % NZ) for i in range(NZ)])]
    all_gather x1, waiting for transfers between devices: 0.02 us -> 7.51 us  [body(): most = lax.all_gather(most, 'x', axis=1, tiled=True)]
    pallas_call x3, Pallas kernels: 34.3 us -> 40.4 us  [attention(): pl.pallas_call(kernel, out_shape=(jax.ShapeDtypeStruct((n, HD + PACK, ROW...]
    all_to_all x2, waiting for transfers between devices: 0.01 us -> 3.16 us  [over_x(): return lax.all_to_all(items, 'x', split_axis=0, concat_axis=0, tiled=True)]
    unnamed x31 -> x41, local copies, waits for them, and re-layouts: 3.29 us -> 6.4 us
  transfers between devices with their start and end apart: 21 -> 21, of which waited for: 7 -> 8; matrix products, arithmetic and copies ran while one was open for 3% -> 3% of each run, Pallas kernels for 24% -> 25%
where the time goes in v12:
time: 279 us; the launch traced here: 278 us
  waiting for transfers between devices  113 us (41%)
  Pallas kernels  74 us (27%)
  starting transfers between devices  36.5 us (13%)
  blocking collectives  24.4 us (9%)
  between operations  13.5 us (5%)
  local copies, waits for them, and re-layouts  9.71 us (3%)
  other arithmetic  6.54 us (2%)
    ppermute x12, waiting for transfers between devices, along_z(): return lax.ppermute(array, 'z', [(i, (i + shift) % NZ) for i in range(NZ)])  75.3 us
    pallas_call x3, Pallas kernels, attention(): pl.pallas_call(kernel, out_shape=(jax.ShapeDtypeStruct((n, HD + PACK, ROW...  40.4 us
    all_gather x1, waiting for transfers between devices, body(): most = lax.all_gather(out_weight[:cut], 'z', axis=1, tiled=True)  26.6 us
    all_to_all x1, blocking collectives, body(): chips = lax.all_to_all(chip, 'y', split_axis=0, concat_axis=0, tiled=True)  24.4 us
    ppermute x12, starting transfers between devices, along_z(): return lax.ppermute(array, 'z', [(i, (i + shift) % NZ) for i in range(NZ)])  21.3 us
    pallas_call x2, Pallas kernels, in_vmem(): pl.pallas_call(kernel, out_shape=out, in_specs=[vmem] * len(arrays), out_...  12.2 us
    pallas_call x2, Pallas kernels, project(): pl.pallas_call(project_kernel, out_shape=jax.ShapeDtypeStruct((NY, contex...  10.1 us
    all_to_all x2, starting transfers between devices, over_x(): return lax.all_to_all(items, 'x', split_axis=0, concat_axis=0, tiled=True)  9.79 us
  transfers between devices with their start and end apart: 21, of which 8 were waited for; matrix products, arithmetic and copies ran while one was open for 3% of the time, Pallas kernels for 25%

profile of v12, /device:TPU:1, one launch (start us, length us, event | category | flops | bytes accessed | tf_op | source)
XLA Modules:
  0.0 278.0 jit_solution(11258443178050772678)
XLA Ops:
  7.3 3.4 %collective-permute-start.6 = (bf16[128,128]{1,0:T(8,128)(2,1)S(1)}, bf16[128,128]{1,0:T(8,128)(2,1)S(1)}, u32[]{:S(2)}, u32[]{:S(2)}) collective-permute-start(bf16[128,128]{1,0:T(8,128)(2,1)S(1)} %get-tuple-element.82), channel_id=1, source_target_pairs={{0,192},{64,0},{128,64},{192,128},{1,193},{65,1},{129,65},{193,129... | collective-permute-start | bytes 98312 | tf_op jit(solution)/shard_map/ppermute | solution.py:376
  13.4 5.7 %collective-permute-start.4 = (bf16[3,1024,128]{2,1,0:T(8,128)(2,1)S(1)}, bf16[3,1024,128]{2,1,0:T(8,128)(2,1)S(1)}, u32[]{:S(2)}, u32[]{:S(2)}) collective-permute-start(bf16[3,1024,128]{2,1,0:T(8,128)(2,1)S(1)} %bitcast.22), channel_id=1, source_target_pairs={{0,56},{8,0},{16,8},{24,16},{32,24},{40,32},{48,40},{56,48},{1,57}... | collective-permute-start | bytes 2359304 | tf_op jit(solution)/shard_map/ppermute | solution.py:372
  23.6 3.4 %take_rows.2 = (bf16[4,512,256]{2,1,0:T(8,128)(2,1)}, bf16[4,512,256]{2,1,0:T(8,128)(2,1)S(1)}, bf16[2,512,256]{2,1,0:T(8,128)(2,1)S(1)}, bf16[2,512,256]{2,1,0:T(8,128)(2,1)S(1)}) custom-call(s32[12]{0:T(128)S(1)} %reshape.164.rows_ref, bf16[16,512,256]{2,1,0:T(8,128)(2,1)} %bitcast.28), custom_call_target="tpu_custom_call" | custom-call | tf_op jit(solution)/shard_map/take_rows/pallas_call | solution.py:87
  27.1 5.8 %take_rows.3 = bf16[20,512,256]{2,1,0:T(8,128)(2,1)} custom-call(s32[20]{0:T(128)S(1)} %reshape.166.rows_ref, bf16[16,512,256]{2,1,0:T(8,128)(2,1)} %bitcast.29), custom_call_target="tpu_custom_call" | custom-call | tf_op jit(solution)/shard_map/take_rows/pallas_call | solution.py:87
  34.3 3.1 %collective-permute-done.5.q2 = bf16[3,1024,128]{2,1,0:T(8,128)(2,1)S(1)} collective-permute-done((bf16[3,1024,128]{2,1,0:T(8,128)(2,1)S(1)}, bf16[3,1024,128]{2,1,0:T(8,128)(2,1)S(1)}, u32[]{:S(2)}, u32[]{:S(2)}) %collective-permute-start.5) | collective-permute-done | bytes 786464 | tf_op jit(solution)/shard_map/ppermute | solution.py:372
  38.3 5.1 %all-to-all-start = ((bf16[4,5,512,256]{3,2,1,0:T(8,128)(2,1)}), bf16[4,5,512,256]{3,2,1,0:T(8,128)(2,1)}, u32[]{:S(2)}, u32[]{:S(2)}) async-start(bf16[4,5,512,256]{3,2,1,0:T(8,128)(2,1)} %bitcast.27), calls=%async_computation | async-start | bytes 10485760 | tf_op jit(solution)/shard_map/all_to_all | solution.py:380
  44.3 2.7 collective-permute-start.1
  48.8 3.6 %collective-permute-start.3 = (bf16[2,512,256]{2,1,0:T(8,128)(2,1)S(1)}, bf16[2,512,256]{2,1,0:T(8,128)(2,1)S(1)}, u32[]{:S(2)}, u32[]{:S(2)}) collective-permute-start(bf16[2,512,256]{2,1,0:T(8,128)(2,1)S(1)} %get-tuple-element.50), channel_id=1, source_target_pairs={{0,48},{8,56},{16,0},{24,8},{32,16},{40,24},{48,32},{56,40},{1,49}... | collective-permute-start | bytes 1572872 | tf_op jit(solution)/shard_map/ppermute | solution.py:372
  52.3 38.2 %collective-permute-done.2.up4 = bf16[2,512,256]{2,1,0:T(8,128)(2,1)S(1)} collective-permute-done((bf16[2,512,256]{2,1,0:T(8,128)(2,1)}, bf16[2,512,256]{2,1,0:T(8,128)(2,1)S(1)}, u32[]{:S(2)}, u32[]{:S(2)}) %collective-permute-start.2) | collective-permute-done | bytes 524320 | tf_op jit(solution)/shard_map/ppermute | solution.py:372
  90.5 5.0 %collective-permute-done.3.down4 = bf16[2,512,256]{2,1,0:T(8,128)(2,1)S(1)} collective-permute-done((bf16[2,512,256]{2,1,0:T(8,128)(2,1)S(1)}, bf16[2,512,256]{2,1,0:T(8,128)(2,1)S(1)}, u32[]{:S(2)}, u32[]{:S(2)}) %collective-permute-start.3) | collective-permute-done | bytes 524320 | tf_op jit(solution)/shard_map/ppermute | solution.py:372
  97.7 3.2 %all-to-all-done.here = bf16[4,5,512,256]{3,2,1,0:T(8,128)(2,1)} async-done(((bf16[4,5,512,256]{3,2,1,0:T(8,128)(2,1)}), bf16[4,5,512,256]{3,2,1,0:T(8,128)(2,1)}, u32[]{:S(2)}, u32[]{:S(2)}) %all-to-all-start) | async-done | bytes 5242912 | tf_op jit(solution)/shard_map/all_to_all | solution.py:380
  100.9 4.7 %all-to-all-start.1 = ((bf16[4,3,512,256]{3,2,1,0:T(8,128)(2,1)}), bf16[4,3,512,256]{3,2,1,0:T(8,128)(2,1)}, u32[]{:S(2)}, u32[]{:S(2)}) async-start(bf16[4,3,512,256]{3,2,1,0:T(8,128)(2,1)} %assemble.1), calls=%async_computation.1 | async-start | bytes 6291456 | tf_op jit(solution)/shard_map/all_to_all | solution.py:380
  109.0 14.5 %near.1 = (bf16[3,144,1024]{2,1,0:T(8,128)(2,1)S(1)}, bf16[3,144,1024]{2,1,0:T(8,128)(2,1)}, bf16[3,144,1024]{2,1,0:T(8,128)(2,1)}) custom-call(s32[12]{0:T(128)S(1)} %get-tuple-element.84.tags, bf16[4,5,512,256]{3,2,1,0:T(8,128)(2,1)} %all-to-all-done.here, bf16[3,1024,128]{2,1,0:T(8,128)(2,1)S(1)} %bitcast.24, bf16[3,1024,128]{2,1,0:T(8,128)(2,1)S(1)} %copy-done.4, ...), custom_call_target="tpu_custom_call" | custom-call | flops 5242880 | bytes 5120 | tf_op jit(solution)/shard_map/near/pallas_call | solution.py:286
  124.4 26.6 %all-gather.4.cloned.1.call-done = bf16[896,1024]{1,0:T(8,128)(2,1)} async-done(((bf16[896,128]{1,0:T(8,128)(2,1)}), bf16[896,1024]{1,0:T(8,128)(2,1)}) %all-gather.4.cloned.1.call-update) | async-done | bytes 1835024 | tf_op jit(solution)/shard_map/all_gather | solution.py:406
  153.8 9.9 %far.1 = (bf16[3,144,1024]{2,1,0:T(8,128)(2,1)S(1)}, bf16[3,144,1024]{2,1,0:T(8,128)(2,1)S(1)}) custom-call(s32[8]{0:T(128)S(1)} %slice.43.tags, bf16[4,5,512,256]{3,2,1,0:T(8,128)(2,1)} %all-to-all-done.here, bf16[3,1024,128]{2,1,0:T(8,128)(2,1)} %collective-permute-done.9.q0, bf16[3,1024,128]{2,1,0:T(8,128)(2,1)S(1)} %collective-permute-done.10.q1), custom_call_target="tpu_custom_call" | custom-call | flops 3145728 | bytes 3072 | tf_op jit(solution)/shard_map/far/pallas_call | solution.py:286
  165.7 16.1 %move.1 = (bf16[3,144,1024]{2,1,0:T(8,128)(2,1)}, bf16[3,144,1024]{2,1,0:T(8,128)(2,1)}) custom-call(s32[12]{0:T(128)S(1)} %get-tuple-element.83.tags, bf16[4,3,512,256]{3,2,1,0:T(8,128)(2,1)} %all-to-all-done.1.moved, bf16[3,1024,128]{2,1,0:T(8,128)(2,1)} %collective-permute-done.9.q0, bf16[3,1024,128]{2,1,0:T(8,128)(2,1)S(1)} %collective-permute-done.10.q1, ...), custom_call_target="tpu_custom_call" | custom-call | flops 209715200000 | bytes 204800000 | tf_op jit(solution)/shard_map/move/pallas_call | solution.py:286
  181.8 3.6 %collective-permute-start.14 = (bf16[3,144,1024]{2,1,0:T(8,128)(2,1)}, bf16[3,144,1024]{2,1,0:T(8,128)(2,1)}, u32[]{:S(2)}, u32[]{:S(2)}) collective-permute-start(bf16[3,144,1024]{2,1,0:T(8,128)(2,1)} %get-tuple-element.78), channel_id=1, source_target_pairs={{0,48},{8,56},{16,0},{24,8},{32,16},{40,24},{48,32},{56,40},{1,49}... | collective-permute-start | bytes 2654216 | tf_op jit(solution)/shard_map/ppermute | solution.py:372
  185.4 8.9 %itself.1.refs_0_ = bf16[3,144,1024]{2,1,0:T(8,128)(2,1)S(1)} custom-call(bf16[3,1024,128]{2,1,0:T(8,128)(2,1)S(1)} %bitcast.25, bf16[384,256]{1,0:T(8,128)(2,1)S(1)} %bitcast.26), custom_call_target="tpu_custom_call" | custom-call | tf_op jit(solution)/shard_map/itself/pallas_call | solution.py:360
  194.4 28.3 %collective-permute-done.13.refs_4_ = bf16[3,144,1024]{2,1,0:T(8,128)(2,1)} collective-permute-done((bf16[3,144,1024]{2,1,0:T(8,128)(2,1)}, bf16[3,144,1024]{2,1,0:T(8,128)(2,1)}, u32[]{:S(2)}, u32[]{:S(2)}) %collective-permute-start.13) | collective-permute-done | bytes 884768 | tf_op jit(solution)/shard_map/ppermute | solution.py:372
  223.9 3.2 %last.1.context_ref = bf16[384,1024]{1,0:T(8,128)(2,1)S(1)} custom-call(bf16[3,144,1024]{2,1,0:T(8,128)(2,1)S(1)} %itself.1.refs_0_, bf16[3,144,1024]{2,1,0:T(8,128)(2,1)S(1)} %copy-done.2, bf16[3,144,1024]{2,1,0:T(8,128)(2,1)} %collective-permute-done.11.refs_2_, bf16[3,144,1024]{2,1,0:T(8,128)(2,1)} %collective-permute-done.12.refs_3_, ...), custom_call_target="tpu_custom_call" | custom-call | tf_op jit(solution)/shard_map/last/pallas_call | solution.py:360
  227.1 7.5 %all-gather.8.cloned.1.call-done.most_ref = bf16[896,4096]{1,0:T(8,128)(2,1)} async-done(((bf16[896,1024]{1,0:T(8,128)(2,1)}), bf16[896,4096]{1,0:T(8,128)(2,1)}) %all-gather.8.cloned.1.call-update) | async-done | bytes 7340048 | tf_op jit(solution)/shard_map/all_gather | solution.py:470
  234.6 5.0 %theirs.1 = bf16[4,384,512]{2,1,0:T(8,128)(2,1)S(1)} custom-call(s32[2]{0:T(128)S(1)} %pad_add_fusion.1.place, bf16[384,1024]{1,0:T(8,128)(2,1)S(1)} %last.1.context_ref, bf16[896,4096]{1,0:T(8,128)(2,1)} %all-gather.8.cloned.1.call-done.most_ref, bf16[4,128,1024]{2,1,0:T(8,128)(2,1)S(1)} %copy-done), custom_call_target="tpu_custom_call" | custom-call | flops 1610612736 | bytes 4194304 | tf_op jit(solution)/shard_map/theirs/pallas_call | solution.py:332
  240.5 5.0 %ours.1 = bf16[4,384,512]{2,1,0:T(8,128)(2,1)S(1)} custom-call(s32[2]{0:T(128)S(1)} %pad_add_fusion.place, bf16[384,1024]{1,0:T(8,128)(2,1)S(1)} %last.1.context_ref, bf16[896,4096]{1,0:T(8,128)(2,1)} %all-gather.8.cloned.1.call-done.most_ref, bf16[4,128,1024]{2,1,0:T(8,128)(2,1)S(1)} %copy-done), custom_call_target="tpu_custom_call" | custom-call | flops 1610612736 | bytes 4194304 | tf_op jit(solution)/shard_map/ours/pallas_call | solution.py:332
  246.0 24.4 %all_to_all.15 = bf16[4,384,512]{2,1,0:T(8,128)(2,1)S(1)} all-to-all(bf16[4,384,512]{2,1,0:T(8,128)(2,1)S(1)} %add_convert_fusion), channel_id=1, replica_groups=mesh['x'=4,'z'=8,'y'=4,'core'=2] {'y'}, dimensions={0} | all-to-all | bytes 3145728 | tf_op jit(solution)/shard_map/all_to_all | solution.py:514
  (106 shorter events, 27.7 us)
Async XLA Ops:
  7.3 25.7 %collective-permute-start.6 = (bf16[128,128]{1,0:T(8,128)(2,1)S(1)}, bf16[128,128]{1,0:T(8,128)(2,1)S(1)}, u32[]{:S(2)}, u32[]{:S(2)}) collective-permute-start(bf16[128,128]{1,0:T(8,128)(2,1)S(1)} %get-tuple-element.82), channel_id=1, source_target_pairs={{0,192},{64,0},{128,64},{192,128},{1,193},{65,1},{129,65},{193,129... | collective-permute-start | bytes 98312 | tf_op jit(solution)/shard_map/ppermute | solution.py:376
  10.7 22.3 %collective-permute-start.7 = (bf16[128,128]{1,0:T(8,128)(2,1)S(1)}, bf16[128,128]{1,0:T(8,128)(2,1)S(1)}, u32[]{:S(2)}, u32[]{:S(2)}) collective-permute-start(bf16[128,128]{1,0:T(8,128)(2,1)S(1)} %get-tuple-element.82), channel_id=1, source_target_pairs={{0,128},{64,192},{128,0},{192,64},{1,129},{65,193},{129,1},{193,65... | collective-permute-start | bytes 98312 | tf_op jit(solution)/shard_map/ppermute | solution.py:376
  11.2 21.8 %collective-permute-start.8 = (bf16[128,128]{1,0:T(8,128)(2,1)S(1)}, bf16[128,128]{1,0:T(8,128)(2,1)S(1)}, u32[]{:S(2)}, u32[]{:S(2)}) collective-permute-start(bf16[128,128]{1,0:T(8,128)(2,1)S(1)} %get-tuple-element.82), channel_id=1, source_target_pairs={{0,64},{64,128},{128,192},{192,0},{1,65},{65,129},{129,193},{193,1... | collective-permute-start | bytes 98312 | tf_op jit(solution)/shard_map/ppermute | solution.py:376
  13.4 21.0 %collective-permute-start.4 = (bf16[3,1024,128]{2,1,0:T(8,128)(2,1)S(1)}, bf16[3,1024,128]{2,1,0:T(8,128)(2,1)S(1)}, u32[]{:S(2)}, u32[]{:S(2)}) collective-permute-start(bf16[3,1024,128]{2,1,0:T(8,128)(2,1)S(1)} %bitcast.22), channel_id=1, source_target_pairs={{0,56},{8,0},{16,8},{24,16},{32,24},{40,32},{48,40},{56,48},{1,57}... | collective-permute-start | bytes 2359304 | tf_op jit(solution)/shard_map/ppermute | solution.py:372
  19.0 18.4 %collective-permute-start.5 = (bf16[3,1024,128]{2,1,0:T(8,128)(2,1)S(1)}, bf16[3,1024,128]{2,1,0:T(8,128)(2,1)S(1)}, u32[]{:S(2)}, u32[]{:S(2)}) collective-permute-start(bf16[3,1024,128]{2,1,0:T(8,128)(2,1)S(1)} %bitcast.23), channel_id=1, source_target_pairs={{0,8},{8,16},{16,24},{24,32},{32,40},{40,48},{48,56},{56,0},{1,9},... | collective-permute-start | bytes 2359304 | tf_op jit(solution)/shard_map/ppermute | solution.py:372
  38.3 62.5 %all-to-all-start = ((bf16[4,5,512,256]{3,2,1,0:T(8,128)(2,1)}), bf16[4,5,512,256]{3,2,1,0:T(8,128)(2,1)}, u32[]{:S(2)}, u32[]{:S(2)}) async-start(bf16[4,5,512,256]{3,2,1,0:T(8,128)(2,1)} %bitcast.27), calls=%async_computation | async-start | bytes 10485760 | tf_op jit(solution)/shard_map/all_to_all | solution.py:380
  43.5 81.0 %all-gather.6.cloned.1.call-start = ((), (), s32[]{:S(2)}) async-start(), calls=%async_computation.4 | async-start | bytes 1179648 | tf_op jit(solution)/shard_map/all_gather | solution.py:410
  44.2 106.8 %all-gather.4.cloned.1.call-start = ((), (), s32[]{:S(2)}) async-start(), calls=%async_computation.3 | async-start | bytes 2064384 | tf_op jit(solution)/shard_map/all_gather | solution.py:406
  44.3 51.3 %collective-permute-start = (bf16[4,512,256]{2,1,0:T(8,128)(2,1)}, bf16[4,512,256]{2,1,0:T(8,128)(2,1)S(1)}, u32[]{:S(2)}, u32[]{:S(2)}) collective-permute-start(bf16[4,512,256]{2,1,0:T(8,128)(2,1)} %get-tuple-element.47), channel_id=1, source_target_pairs={{0,8},{8,16},{16,24},{24,32},{32,40},{40,48},{48,56},{56,0},{1,9},... | collective-permute-start | bytes 3145736 | tf_op jit(solution)/shard_map/ppermute | solution.py:372
  44.3 51.2 %collective-permute-start.1 = (bf16[4,512,256]{2,1,0:T(8,128)(2,1)}, bf16[4,512,256]{2,1,0:T(8,128)(2,1)S(1)}, u32[]{:S(2)}, u32[]{:S(2)}) collective-permute-start(bf16[4,512,256]{2,1,0:T(8,128)(2,1)} %copy-done.8), channel_id=1, source_target_pairs={{0,56},{8,0},{16,8},{24,16},{32,24},{40,32},{48,40},{56,48},{1,57}... | collective-permute-start | bytes 3145736 | tf_op jit(solution)/shard_map/ppermute | solution.py:372
  48.7 41.8 %collective-permute-start.2 = (bf16[2,512,256]{2,1,0:T(8,128)(2,1)}, bf16[2,512,256]{2,1,0:T(8,128)(2,1)S(1)}, u32[]{:S(2)}, u32[]{:S(2)}) collective-permute-start(bf16[2,512,256]{2,1,0:T(8,128)(2,1)} %copy-done.11), channel_id=1, source_target_pairs={{0,16},{8,24},{16,32},{24,40},{32,48},{40,56},{48,0},{56,8},{1,17}... | collective-permute-start | bytes 1572872 | tf_op jit(solution)/shard_map/ppermute | solution.py:372
  48.8 46.7 %collective-permute-start.3 = (bf16[2,512,256]{2,1,0:T(8,128)(2,1)S(1)}, bf16[2,512,256]{2,1,0:T(8,128)(2,1)S(1)}, u32[]{:S(2)}, u32[]{:S(2)}) collective-permute-start(bf16[2,512,256]{2,1,0:T(8,128)(2,1)S(1)} %get-tuple-element.50), channel_id=1, source_target_pairs={{0,48},{8,56},{16,0},{24,8},{32,16},{40,24},{48,32},{56,40},{1,49}... | collective-permute-start | bytes 1572872 | tf_op jit(solution)/shard_map/ppermute | solution.py:372
  97.7 11.1 %copy-start.18 = (s32[32]{0:T(128)S(1)}, s32[32]{0:T(128)}, u32[]{:S(2)}) copy-start(s32[32]{0:T(128)} %constant.119) | copy-start | bytes 388
  100.9 64.8 %all-to-all-start.1 = ((bf16[4,3,512,256]{3,2,1,0:T(8,128)(2,1)}), bf16[4,3,512,256]{3,2,1,0:T(8,128)(2,1)}, u32[]{:S(2)}, u32[]{:S(2)}) async-start(bf16[4,3,512,256]{3,2,1,0:T(8,128)(2,1)} %assemble.1), calls=%async_computation.1 | async-start | bytes 6291456 | tf_op jit(solution)/shard_map/all_to_all | solution.py:380
  105.6 129.1 %all-gather.8.cloned.1.call-start = ((), (), s32[]{:S(2)}) async-start(), calls=%async_computation.5 | async-start | bytes 9175040 | tf_op jit(solution)/shard_map/all_gather | solution.py:470
  105.8 45.3 %collective-permute-start.10 = (bf16[3,1024,128]{2,1,0:T(8,128)(2,1)S(1)}, bf16[3,1024,128]{2,1,0:T(8,128)(2,1)S(1)}, u32[]{:S(2)}, u32[]{:S(2)}) collective-permute-start(bf16[3,1024,128]{2,1,0:T(8,128)(2,1)S(1)} %copy-done.6), channel_id=1, source_target_pairs={{0,8},{8,16},{16,24},{24,32},{32,40},{40,48},{48,56},{56,0},{1,9},... | collective-permute-start | bytes 2359304 | tf_op jit(solution)/shard_map/ppermute | solution.py:372
  106.8 44.2 %collective-permute-start.9 = (bf16[3,1024,128]{2,1,0:T(8,128)(2,1)S(1)}, bf16[3,1024,128]{2,1,0:T(8,128)(2,1)}, u32[]{:S(2)}, u32[]{:S(2)}) collective-permute-start(bf16[3,1024,128]{2,1,0:T(8,128)(2,1)S(1)} %copy-done.4), channel_id=1, source_target_pairs={{0,56},{8,0},{16,8},{24,16},{32,24},{40,32},{48,40},{56,48},{1,57}... | collective-permute-start | bytes 2359304 | tf_op jit(solution)/shard_map/ppermute | solution.py:372
  151.1 43.4 %collective-permute-start.11 = (bf16[3,144,1024]{2,1,0:T(8,128)(2,1)}, bf16[3,144,1024]{2,1,0:T(8,128)(2,1)}, u32[]{:S(2)}, u32[]{:S(2)}) collective-permute-start(bf16[3,144,1024]{2,1,0:T(8,128)(2,1)} %get-tuple-element.70), channel_id=1, source_target_pairs={{0,8},{8,16},{16,24},{24,32},{32,40},{40,48},{48,56},{56,0},{1,9},... | collective-permute-start | bytes 2654216 | tf_op jit(solution)/shard_map/ppermute | solution.py:372
  151.5 42.9 %collective-permute-start.12 = (bf16[3,144,1024]{2,1,0:T(8,128)(2,1)}, bf16[3,144,1024]{2,1,0:T(8,128)(2,1)}, u32[]{:S(2)}, u32[]{:S(2)}) collective-permute-start(bf16[3,144,1024]{2,1,0:T(8,128)(2,1)} %get-tuple-element.71), channel_id=1, source_target_pairs={{0,56},{8,0},{16,8},{24,16},{32,24},{40,32},{48,40},{56,48},{1,57}... | collective-permute-start | bytes 2654216 | tf_op jit(solution)/shard_map/ppermute | solution.py:372
  165.7 19.7 %copy-start.7 = (bf16[384,1,256]{2,0,1:T(8,128)(2,1)S(1)}, bf16[384,1,256]{2,0,1:T(8,128)(2,1)}, u32[]{:S(2)}) copy-start(bf16[384,1,256]{2,0,1:T(8,128)(2,1)} %param.10) | copy-start | bytes 589828
  181.8 40.9 %collective-permute-start.13 = (bf16[3,144,1024]{2,1,0:T(8,128)(2,1)}, bf16[3,144,1024]{2,1,0:T(8,128)(2,1)}, u32[]{:S(2)}, u32[]{:S(2)}) collective-permute-start(bf16[3,144,1024]{2,1,0:T(8,128)(2,1)} %get-tuple-element.77), channel_id=1, source_target_pairs={{0,16},{8,24},{16,32},{24,40},{32,48},{40,56},{48,0},{56,8},{1,17}... | collective-permute-start | bytes 2654216 | tf_op jit(solution)/shard_map/ppermute | solution.py:372
  181.8 40.9 %collective-permute-start.14 = (bf16[3,144,1024]{2,1,0:T(8,128)(2,1)}, bf16[3,144,1024]{2,1,0:T(8,128)(2,1)}, u32[]{:S(2)}, u32[]{:S(2)}) collective-permute-start(bf16[3,144,1024]{2,1,0:T(8,128)(2,1)} %get-tuple-element.78), channel_id=1, source_target_pairs={{0,48},{8,56},{16,0},{24,8},{32,16},{40,24},{48,32},{56,40},{1,49}... | collective-permute-start | bytes 2654216 | tf_op jit(solution)/shard_map/ppermute | solution.py:372
  194.4 40.2 %copy-start = (bf16[4,128,1024]{2,1,0:T(8,128)(2,1)S(1)}, bf16[4,128,1024]{2,1,0:T(8,128)(2,1)}, u32[]{:S(2)}) copy-start(bf16[4,128,1024]{2,1,0:T(8,128)(2,1)} %all-gather.6.cloned.1.call-done.rest_ref) | copy-start | bytes 3145732
  239.7 5.9 %collective-permute-start.15 = (bf16[4,384,512]{2,1,0:T(8,128)(2,1)S(1)}, bf16[4,384,512]{2,1,0:T(8,128)(2,1)S(1)}, u32[]{:S(2)}, u32[]{:S(2)}) collective-permute-start(bf16[4,384,512]{2,1,0:T(8,128)(2,1)S(1)} %theirs.1), channel_id=1, source_target_pairs={{0,1},{1,0},{2,3},{3,2},{4,5},{5,4},{6,7},{7,6},{8,9},{9,8},{10,11... | collective-permute-start | bytes 4718600 | tf_op jit(solution)/shard_map/ppermute | solution.py:511
  (17 other events, 92.0 us)
Sparse Core Ops, SparseCore 0:
  46.0 56.2 all-gather.5
  104.1 46.9 all-gather.3
  153.9 80.7 all-gather.7
